TPU v7x, 32 devices: a whole 2x2x4 slice. The times are simulated.
32 devices in a mesh: grp: 2 (over x), mode: 4 (over y, core), space: 4 (over z).
Axes of the slice: x: 2, y: 2, z: 4, core: 2. Of those that a mesh axis runs over, the one named last changes fastest.
Arguments:
- electrons: bfloat16 [1024, 64, 128], P('mode', ('grp', 'space')), parts along dimension 1, may hold values from -6 to 6
- phonons: bfloat16 [2048, 64, 128], P('mode', ('grp', 'space')), parts along dimension 1, may hold values from -6 to 6
- emission: bfloat16 [2048, 1024], P('mode'), may hold values from -0.1875 to 0.1875
- absorption: bfloat16 [1024, 2048], P('mode'), may hold values from -0.125 to 0.125
- block_coupling: bfloat16 [2048, 12, 128], P('mode'), may hold values from -0.15625 to 0.15625
- block_cols: int32 [16, 12], P('mode'), may hold values from -1 to 15, as said below
- upwind: int32 [64, 128], P(('grp', 'space')), parts along dimension 0, may hold values from 0 to 1
- speed: float32 [1024], P('mode'), may hold values from 0.1 to 0.9
- diffusion: float32 [2048], P('mode'), may hold values from 0.02 to 0.24
- electron_rate: float32 [1024], P('mode'), may hold values from 0.2 to 2
- phonon_rate: float32 [2048], P('mode'), may hold values from 0.2 to 2
Outputs:
- electrons_out: bfloat16 [1024, 64, 128], P('mode', ('grp', 'space')), parts along dimension 1
- phonons_out: bfloat16 [2048, 64, 128], P('mode', ('grp', 'space')), parts along dimension 1
There are 2 independent parts, one for each index of `grp`. A program takes and returns all parts, laid end to end along the dimension named above; an argument that names none is the same for every part. Nothing has to cross between parts.
Inputs may be any that keep to these rules, and one draw needn't show every extreme that they name: `block_cols`: each row lists distinct block indices in its first slots and -1 in all later slots; every row has at least one block, one row fills all 12 slots, one of them naming block 15, and one row has a single block.
All inputs are finite; a program needn't handle non-finite values.
Results may differ from a plain program's by a relative error of at most 0.0065.
Values may be sent and summed in bfloat16 or wider, within the bound.
No kernel may reach another device: no remote copies, remote signals or barrier semaphores. Data moves between devices by JAX's collectives and lax.ppermute only.
A program may use at most 64 MiB of HBM per device.

v0:
```python
import jax
import jax.numpy as jnp
from jax import lax
from jax.sharding import PartitionSpec as P

NM = 2048
BLK = 128
ITERS = 2


def extended(x, sides, width):
    for axis, dim in sides:
        count, length = (lax.axis_size(axis), x.shape[dim])
        up = [(i, (i + 1) % count) for i in range(count - 1)]
        down = [(j, i) for i, j in up]
        last = lax.slice_in_dim(x, length - width, length, axis=dim)
        first = lax.slice_in_dim(x, 0, width, axis=dim)
        before = lax.ppermute(last, axis, up)
        after = lax.ppermute(first, axis, down)
        x = jnp.concatenate([before, x, after], axis=dim)
    return x


def on_device(
    electrons,
    phonons,
    emission,
    absorption,
    block_coupling,
    block_cols,
    upwind,
    speed,
    diffusion,
    electron_rate,
    phonon_rate,
):
    e_rows, width_x, width_y = electrons.shape
    m_rows = phonons.shape[0]
    cells = width_x * width_y
    slots = block_coupling.shape[1]
    b_rows = m_rows // BLK
    total_blocks = NM // BLK
    kernel = block_coupling.reshape(b_rows, BLK, slots, BLK)
    upward = (upwind == 1)[None]
    block_ids = jnp.arange(total_blocks, dtype=jnp.int32)
    hits = (block_cols[:, :, None] == block_ids[None, None, :]).astype(jnp.bfloat16)
    dense_all = jnp.einsum(
        "bsk,bisj->bikj", hits, kernel, preferred_element_type=jnp.float32
    ).astype(jnp.bfloat16)
    dense_all = dense_all.reshape(m_rows, NM)

    def add_gain(piece):
        return jnp.dot(
            absorption, piece.reshape(piece.shape[0], cells), preferred_element_type=jnp.float32
        )

    def add_emit(piece):
        return jnp.dot(
            emission, piece.reshape(piece.shape[0], cells), preferred_element_type=jnp.float32
        )

    state_e = electrons
    state_p = phonons
    for step in range(ITERS):
        rimmed_e = extended(state_e, (("space", 1),), 1)
        rimmed_p = extended(state_p, (("space", 1),), 1)
        field_e = state_e.astype(jnp.float32)
        field_p = state_p.astype(jnp.float32)
        rim_e = rimmed_e.astype(jnp.float32)
        f_up = jnp.where(upward, rim_e[:, :-2], rim_e[:, 2:])
        rim_p = rimmed_p.astype(jnp.float32)
        side_y = jnp.pad(field_p, ((0, 0), (0, 0), (1, 1)))
        lap = rim_p[:, :-2] + rim_p[:, 2:] + side_y[:, :, :-2] + side_y[:, :, 2:] - 4.0 * field_p
        emit = add_emit(lax.all_gather(state_e, "mode", axis=0, tiled=True))
        add_piece = lax.all_gather(state_p, "mode", axis=0, tiled=True)
        count = add_piece.shape[0]
        add_flat = add_piece.reshape(count, cells)
        scatter = jnp.dot(dense_all, add_flat, preferred_element_type=jnp.float32)
        gain = add_gain(lax.all_gather(state_p, "mode", axis=0, tiled=True))
        gain = gain.reshape(e_rows, width_x, width_y)
        sources = (emit + scatter).reshape(m_rows, width_x, width_y)
        new_e = (field_e - speed[:, None, None] * (field_e - f_up) + 0.5 * gain) / (
            1.0 + electron_rate[:, None, None]
        )
        new_p = (field_p + diffusion[:, None, None] * lap + 0.5 * sources) / (
            1.0 + phonon_rate[:, None, None]
        )
        state_e = new_e.astype(jnp.bfloat16)
        state_p = new_p.astype(jnp.bfloat16)
    return (state_e, state_p)


def solution(mesh):
    placed = (
        P("mode", ("grp", "space"), None),
        P("mode", ("grp", "space"), None),
        P("mode", None),
        P("mode", None),
        P("mode", None, None),
        P("mode", None),
        P(("grp", "space"), None),
        P("mode"),
        P("mode"),
        P("mode"),
        P("mode"),
    )
    return jax.shard_map(
        on_device,
        mesh=mesh,
        in_specs=placed,
        out_specs=(P("mode", ("grp", "space"), None), P("mode", ("grp", "space"), None)),
        check_vma=False,
    )
```

profile of v0, /device:TPU:13, one launch (start us, length us, event | category | flops | bytes accessed | tf_op | source)
XLA Modules:
  0.0 156.1 jit_solution(11161160371256622655)
XLA Ops:
  9.9 3.2 %collective-permute-start = (bf16[256,1,128]{2,0,1:T(8,128)(2,1)S(1)}, bf16[256,1,128]{2,0,1:T(8,128)(2,1)S(1)}, u32[]{:S(2)}, u32[]{:S(2)}) collective-permute-start(bf16[256,1,128]{2,0,1:T(8,128)(2,1)S(1)} %get-tuple-element.16), channel_id=1, source_target_pairs={{0,1},{1,2},{2,3},{4,5},{5,6},{6,7},{8,9},{9,10},{10,11},{12,13},{... | collective-permute-start | bytes 196616 | tf_op jit(solution)/shard_map/ppermute | solution.py:18
  13.1 2.1 %collective-permute-start.1 = (bf16[256,1,128]{2,0,1:T(8,128)(2,1)S(1)}, bf16[256,1,128]{2,0,1:T(8,128)(2,1)S(1)}, u32[]{:S(2)}, u32[]{:S(2)}) collective-permute-start(bf16[256,1,128]{2,0,1:T(8,128)(2,1)S(1)} %get-tuple-element.17), channel_id=1, source_target_pairs={{1,0},{2,1},{3,2},{5,4},{6,5},{7,6},{9,8},{10,9},{11,10},{13,12},{... | collective-permute-start | bytes 196616 | tf_op jit(solution)/shard_map/ppermute | solution.py:19
  15.2 2.9 %collective-permute-done.1 = bf16[256,1,128]{2,0,1:T(8,128)(2,1)S(1)} collective-permute-done((bf16[256,1,128]{2,0,1:T(8,128)(2,1)S(1)}, bf16[256,1,128]{2,0,1:T(8,128)(2,1)S(1)}, u32[]{:S(2)}, u32[]{:S(2)}) %collective-permute-start.1) | collective-permute-done | bytes 65568 | tf_op jit(solution)/shard_map/ppermute | solution.py:19
  19.3 25.4 %all-gather.5.cloned.1.call-done = bf16[2048,8,128]{2,1,0:T(8,128)(2,1)} async-done(((bf16[512,8,128]{2,1,0:T(8,128)(2,1)}), bf16[2048,8,128]{2,1,0:T(8,128)(2,1)}) %all-gather.5.cloned.1.call-update) | async-done | bytes 4194320 | tf_op jit(solution)/shard_map/all_gather | solution.py:79
  44.7 5.3 %copy.90 = bf16[256,8,8,128]{3,1,2,0:T(8,128)(2,1)} copy(bf16[256,8,8,128]{3,2,1,0:T(8,128)(2,1)} %bitcast.69) | data formatting | bytes 8388608
  50.1 6.6 %copy.35 = bf16[2048,1024]{0,1:T(8,128)(2,1)} copy(bf16[2048,1024]{1,0:T(8,128)(2,1)} %bitcast.68) | data formatting | bytes 8388608 | tf_op jit(solution)/shard_map/reshape | solution.py:54
  56.7 5.5 %fusion.44 = bf16[256,8,128]{2,0,1:T(8,128)(2,1)} fusion(bf16[8,128,2048]{2,1,0:T(8,128)(2,1)} %bitcast.71, f32[256,10,128]{2,0,1:T(8,128)} %maximum_convert_fusion.2, bf16[256,2048]{1,0:T(8,128)(2,1)} %param.14, f32[256]{0:T(256)S(1)} %broadcast_add_fusion.1, f32[256]{0:T(256)S(1)} %copy-done.18, pred[8,128]{1,0:T(8,128)(4,1)S(1)} %broadcast_compare_fusion, ...), kind=kOutput, calls=%fused_computation.54 | convolution fusion | flops 1076101120 | bytes 8391680 | tf_op jit(solution)/shard_map/dot_general | solution.py:53
  62.6 3.1 %collective-permute-start.4 = (bf16[512,1,128]{2,0,1:T(8,128)(2,1)S(1)}, bf16[512,1,128]{2,0,1:T(8,128)(2,1)S(1)}, u32[]{:S(2)}, u32[]{:S(2)}) collective-permute-start(bf16[512,1,128]{2,0,1:T(8,128)(2,1)S(1)} %copy.51), channel_id=1, source_target_pairs={{0,1},{1,2},{2,3},{4,5},{5,6},{6,7},{8,9},{9,10},{10,11},{12,13},{... | collective-permute-start | bytes 393224 | tf_op jit(solution)/shard_map/ppermute | solution.py:18
  65.8 2.2 %collective-permute-start.5 = (bf16[512,1,128]{2,0,1:T(8,128)(2,1)S(1)}, bf16[512,1,128]{2,0,1:T(8,128)(2,1)S(1)}, u32[]{:S(2)}, u32[]{:S(2)}) collective-permute-start(bf16[512,1,128]{2,0,1:T(8,128)(2,1)S(1)} %copy.52), channel_id=1, source_target_pairs={{1,0},{2,1},{3,2},{5,4},{6,5},{7,6},{9,8},{10,9},{11,10},{13,12},{... | collective-permute-start | bytes 393224 | tf_op jit(solution)/shard_map/ppermute | solution.py:19
  72.4 3.2 %maximum_convert_fusion = f32[512,10,128]{2,1,0:T(8,128)} fusion(bf16[512,1,128]{2,1,0:T(2,128)(2,1)S(1)} %copy.39, bf16[512,8,128]{2,1,0:T(8,128)(2,1)S(1)} %copy-done.4, bf16[512,1,128]{2,1,0:T(2,128)(2,1)S(1)} %copy.38), kind=kLoop, calls=%fused_computation.33 | loop fusion | flops 3932160 | bytes 3932160 | tf_op jit(solution)/shard_map/convert_element_type | solution.py:71
  75.6 3.7 %fusion.21 = f32[512,1024]{1,0:T(8,128)} fusion(bf16[64,8,16,128]{3,2,1,0:T(8,128)(2,1)S(1)} %bitcast.73, bf16[256,8,8,128]{3,2,1,0:T(8,128)(2,1)S(1)} %bitcast.70), kind=kOutput, calls=%fused_computation.26 | convolution fusion | flops 2147483648 | bytes 8388608 | tf_op jit(solution)/shard_map/dot_general | solution.py:78
  79.3 4.0 %multiply_bitcast_fusion = f32[64,8,8,128]{3,1,2,0:T(8,128)S(1)} fusion(f32[512,1024]{1,0:T(8,128)} %fusion.21, bf16[512,1024]{1,0:T(8,128)(2,1)S(1)} %copy-done.22, bf16[128,8,8,128]{3,2,1,0:T(8,128)(2,1)} %bitcast.78), kind=kOutput, calls=%fused_computation.40 | convolution fusion | flops 1074790400 | bytes 7340032 | tf_op jit(solution)/shard_map/dot_general | solution.py:58
  85.5 3.8 %fusion.54 = (f32[512,8,128]{2,1,0:T(8,128)}, bf16[512,8,128]{2,1,0:T(8,128)(2,1)}) fusion(f32[512]{0:T(512)S(1)} %broadcast_add_fusion, f32[64,8,8,128]{3,2,1,0:T(8,128)S(1)} %copy.56, f32[512,8,128]{2,1,0:T(8,128)S(1)} %copy-done.6, f32[512,10,128]{2,1,0:T(8,128)S(1)} %copy-done.3, f32[512]{0:T(512)S(1)} %copy-done.14), kind=kLoop, calls=%fused_computation.71 | loop fusion | flops 5767168 | bytes 11538432 | tf_op jit(solution)/shard_map/convert_element_type | solution.py:68
  89.4 3.1 %collective-permute-start.2 = (bf16[256,1,128]{2,0,1:T(8,128)(2,1)S(1)}, bf16[256,1,128]{2,0,1:T(8,128)(2,1)S(1)}, u32[]{:S(2)}, u32[]{:S(2)}) collective-permute-start(bf16[256,1,128]{2,0,1:T(8,128)(2,1)S(1)} %get-tuple-element.14), channel_id=1, source_target_pairs={{0,1},{1,2},{2,3},{4,5},{5,6},{6,7},{8,9},{9,10},{10,11},{12,13},{... | collective-permute-start | bytes 196616 | tf_op jit(solution)/shard_map/ppermute | solution.py:18
  92.5 2.3 %collective-permute-start.3 = (bf16[256,1,128]{2,0,1:T(8,128)(2,1)S(1)}, bf16[256,1,128]{2,0,1:T(8,128)(2,1)S(1)}, u32[]{:S(2)}, u32[]{:S(2)}) collective-permute-start(bf16[256,1,128]{2,0,1:T(8,128)(2,1)S(1)} %get-tuple-element.15), channel_id=1, source_target_pairs={{1,0},{2,1},{3,2},{5,4},{6,5},{7,6},{9,8},{10,9},{11,10},{13,12},{... | collective-permute-start | bytes 196616 | tf_op jit(solution)/shard_map/ppermute | solution.py:19
  96.8 3.1 %collective-permute-start.6 = (bf16[512,1,128]{2,0,1:T(8,128)(2,1)S(1)}, bf16[512,1,128]{2,0,1:T(8,128)(2,1)S(1)}, u32[]{:S(2)}, u32[]{:S(2)}) collective-permute-start(bf16[512,1,128]{2,0,1:T(8,128)(2,1)S(1)} %copy.42), channel_id=1, source_target_pairs={{0,1},{1,2},{2,3},{4,5},{5,6},{6,7},{8,9},{9,10},{10,11},{12,13},{... | collective-permute-start | bytes 393224 | tf_op jit(solution)/shard_map/ppermute | solution.py:18
  100.0 2.4 %collective-permute-start.7 = (bf16[512,1,128]{2,0,1:T(8,128)(2,1)S(1)}, bf16[512,1,128]{2,0,1:T(8,128)(2,1)S(1)}, u32[]{:S(2)}, u32[]{:S(2)}) collective-permute-start(bf16[512,1,128]{2,0,1:T(8,128)(2,1)S(1)} %copy.43), channel_id=1, source_target_pairs={{1,0},{2,1},{3,2},{5,4},{6,5},{7,6},{9,8},{10,9},{11,10},{13,12},{... | collective-permute-start | bytes 393224 | tf_op jit(solution)/shard_map/ppermute | solution.py:19
  102.7 2.9 %collective-permute-done.7 = bf16[512,1,128]{2,0,1:T(8,128)(2,1)S(1)} collective-permute-done((bf16[512,1,128]{2,0,1:T(8,128)(2,1)S(1)}, bf16[512,1,128]{2,0,1:T(8,128)(2,1)S(1)}, u32[]{:S(2)}, u32[]{:S(2)}) %collective-permute-start.7) | collective-permute-done | bytes 131104 | tf_op jit(solution)/shard_map/ppermute | solution.py:19
  105.9 3.1 %maximum_convert_fusion.1 = f32[512,10,128]{2,1,0:T(8,128)} fusion(bf16[512,1,128]{2,1,0:T(2,128)(2,1)S(1)} %copy.45, bf16[512,8,128]{2,1,0:T(8,128)(2,1)S(1)} %copy-done.5, bf16[512,1,128]{2,1,0:T(2,128)(2,1)S(1)} %copy.44), kind=kLoop, calls=%fused_computation.34 | loop fusion | flops 3932160 | bytes 3932160 | tf_op jit(solution)/shard_map/convert_element_type | solution.py:71
  109.1 4.0 %copy.46 = bf16[1024,8,128]{0,2,1:T(8,128)(2,1)} copy(bf16[1024,8,128]{2,0,1:T(8,128)(2,1)} %all-gather.11.cloned.1.call-done) | data formatting | bytes 4194304 | tf_op jit(solution)/shard_map/all_gather | solution.py:74
  113.1 17.1 %all-gather.9.cloned.1.call-done = bf16[2048,8,128]{2,1,0:T(8,128)(2,1)} async-done(((bf16[512,8,128]{2,1,0:T(8,128)(2,1)}), bf16[2048,8,128]{2,1,0:T(8,128)(2,1)}) %all-gather.9.cloned.1.call-update) | async-done | bytes 4194320 | tf_op jit(solution)/shard_map/all_gather | solution.py:79
  130.2 4.7 %fusion.39 = f32[1024,256]{1,0:T(8,128)} fusion(bf16[256,2048]{1,0:T(8,128)(2,1)S(1)} %copy-done.21, bf16[256,8,8,128]{3,2,1,0:T(8,128)(2,1)} %bitcast.76), kind=kOutput, calls=%fused_computation.47 | convolution fusion | flops 1074003968 | bytes 6291456 | tf_op jit(solution)/shard_map/dot_general | solution.py:53
  134.9 3.7 %fusion = f32[512,1024]{1,0:T(8,128)} fusion(bf16[256,8,8,128]{3,2,1,0:T(8,128)(2,1)S(1)} %bitcast.77, bf16[64,8,16,128]{3,2,1,0:T(8,128)(2,1)S(1)} %bitcast.74), kind=kOutput, calls=%fused_computation.4 | convolution fusion | flops 2147483648 | bytes 8388608 | tf_op jit(solution)/shard_map/dot_general | solution.py:78
  146.4 3.2 %fusion.30 = bf16[512,8,128]{2,1,0:T(8,128)(2,1)} fusion(f32[64,8,8,128]{3,2,1,0:T(8,128)S(1)} %copy.58, f32[512,8,128]{2,1,0:T(8,128)S(1)} %copy-done.7, f32[512,10,128]{2,1,0:T(8,128)S(1)} %copy-done.2, f32[512]{0:T(512)S(1)} %broadcast_add_fusion, f32[512]{0:T(512)S(1)} %copy-done.14), kind=kLoop, calls=%fused_computation.41 | loop fusion | flops 5242880 | bytes 9441280 | tf_op jit(solution)/shard_map/convert_element_type | solution.py:89
  (92 shorter events, 21.3 us)
Async XLA Ops:
  7.2 62.2 %copy-start = (bf16[512,12,128]{2,0,1:T(8,128)(2,1)S(1)}, bf16[512,12,128]{2,0,1:T(8,128)(2,1)}, u32[]{:S(2)}) copy-start(bf16[512,12,128]{2,0,1:T(8,128)(2,1)} %param.15) | copy-start | bytes 4718596
  7.2 8.0 %copy-start.15 = (s32[8,128]{1,0:T(8,128)S(1)}, s32[8,128]{1,0:T(8,128)}, u32[]{:S(2)}) copy-start(s32[8,128]{1,0:T(8,128)} %param.17) | copy-start | bytes 12292
  7.2 8.0 %copy-start.19 = (f32[256]{0:T(256)S(1)}, f32[256]{0:T(256)}, u32[]{:S(2)}) copy-start(f32[256]{0:T(256)} %param.20) | copy-start | bytes 3076
  7.2 37.5 %all-gather.5.cloned.1.call-start = ((), (), s32[]{:S(2)}) async-start(), calls=%async_computation | async-start | bytes 5242880 | tf_op jit(solution)/shard_map/all_gather | solution.py:79
  7.9 71.4 %all-gather.7.cloned.1.call-start = ((), (), s32[]{:S(2)}) async-start(), calls=%async_computation.1 | async-start | bytes 2621440 | tf_op jit(solution)/shard_map/all_gather | solution.py:74
  8.7 100.4 %all-gather.11.cloned.1.call-start = ((), (), s32[]{:S(2)}) async-start(), calls=%async_computation.3 | async-start | bytes 2621440 | tf_op jit(solution)/shard_map/all_gather | solution.py:74
  9.9 5.3 %collective-permute-start = (bf16[256,1,128]{2,0,1:T(8,128)(2,1)S(1)}, bf16[256,1,128]{2,0,1:T(8,128)(2,1)S(1)}, u32[]{:S(2)}, u32[]{:S(2)}) collective-permute-start(bf16[256,1,128]{2,0,1:T(8,128)(2,1)S(1)} %get-tuple-element.16), channel_id=1, source_target_pairs={{0,1},{1,2},{2,3},{4,5},{5,6},{6,7},{8,9},{9,10},{10,11},{12,13},{... | collective-permute-start | bytes 196616 | tf_op jit(solution)/shard_map/ppermute | solution.py:18
  13.1 5.0 %collective-permute-start.1 = (bf16[256,1,128]{2,0,1:T(8,128)(2,1)S(1)}, bf16[256,1,128]{2,0,1:T(8,128)(2,1)S(1)}, u32[]{:S(2)}, u32[]{:S(2)}) collective-permute-start(bf16[256,1,128]{2,0,1:T(8,128)(2,1)S(1)} %get-tuple-element.17), channel_id=1, source_target_pairs={{1,0},{2,1},{3,2},{5,4},{6,5},{7,6},{9,8},{10,9},{11,10},{13,12},{... | collective-permute-start | bytes 196616 | tf_op jit(solution)/shard_map/ppermute | solution.py:19
  50.0 6.7 %copy-start.11 = (bf16[256,8,128]{2,1,0:T(8,128)(2,1)S(1)}, bf16[256,8,128]{2,1,0:T(8,128)(2,1)}, u32[]{:S(2)}) copy-start(bf16[256,8,128]{2,1,0:T(8,128)(2,1)} %param.11) | copy-start | bytes 1572868
  50.0 6.7 %copy-start.18 = (f32[256]{0:T(256)S(1)}, f32[256]{0:T(256)}, u32[]{:S(2)}) copy-start(f32[256]{0:T(256)} %param.18) | copy-start | bytes 3076
  56.7 5.5 %copy-start.4 = (bf16[512,8,128]{2,1,0:T(8,128)(2,1)S(1)}, bf16[512,8,128]{2,1,0:T(8,128)(2,1)}, u32[]{:S(2)}) copy-start(bf16[512,8,128]{2,1,0:T(8,128)(2,1)} %param.12) | copy-start | bytes 3145732
  62.2 68.0 %all-gather.9.cloned.1.call-start = ((), (), s32[]{:S(2)}) async-start(), calls=%async_computation.2 | async-start | bytes 5242880 | tf_op jit(solution)/shard_map/all_gather | solution.py:79
  62.6 6.8 %copy-start.16 = (s32[4,12]{1,0:T(4,128)S(1)}, s32[4,12]{1,0:T(4,128)}, u32[]{:S(2)}) copy-start(s32[4,12]{1,0:T(4,128)} %param.16) | copy-start | bytes 580
  62.6 8.0 %collective-permute-start.4 = (bf16[512,1,128]{2,0,1:T(8,128)(2,1)S(1)}, bf16[512,1,128]{2,0,1:T(8,128)(2,1)S(1)}, u32[]{:S(2)}, u32[]{:S(2)}) collective-permute-start(bf16[512,1,128]{2,0,1:T(8,128)(2,1)S(1)} %copy.51), channel_id=1, source_target_pairs={{0,1},{1,2},{2,3},{4,5},{5,6},{6,7},{8,9},{9,10},{10,11},{12,13},{... | collective-permute-start | bytes 393224 | tf_op jit(solution)/shard_map/ppermute | solution.py:18
  65.8 6.4 %collective-permute-start.5 = (bf16[512,1,128]{2,0,1:T(8,128)(2,1)S(1)}, bf16[512,1,128]{2,0,1:T(8,128)(2,1)S(1)}, u32[]{:S(2)}, u32[]{:S(2)}) collective-permute-start(bf16[512,1,128]{2,0,1:T(8,128)(2,1)S(1)} %copy.52), channel_id=1, source_target_pairs={{1,0},{2,1},{3,2},{5,4},{6,5},{7,6},{9,8},{10,9},{11,10},{13,12},{... | collective-permute-start | bytes 393224 | tf_op jit(solution)/shard_map/ppermute | solution.py:19
  70.6 5.1 %copy-start.12 = (bf16[4,16,128,128]{3,1,2,0:T(8,128)(2,1)}, bf16[4,16,128,128]{3,1,2,0:T(8,128)(2,1)S(1)}, u32[]{:S(2)}) copy-start(bf16[4,16,128,128]{3,1,2,0:T(8,128)(2,1)S(1)} %fusion.32) | copy-start | bytes 6291460
  89.4 12.9 %collective-permute-start.2 = (bf16[256,1,128]{2,0,1:T(8,128)(2,1)S(1)}, bf16[256,1,128]{2,0,1:T(8,128)(2,1)S(1)}, u32[]{:S(2)}, u32[]{:S(2)}) collective-permute-start(bf16[256,1,128]{2,0,1:T(8,128)(2,1)S(1)} %get-tuple-element.14), channel_id=1, source_target_pairs={{0,1},{1,2},{2,3},{4,5},{5,6},{6,7},{8,9},{9,10},{10,11},{12,13},{... | collective-permute-start | bytes 196616 | tf_op jit(solution)/shard_map/ppermute | solution.py:18
  92.5 13.4 %copy-start.5 = (bf16[512,8,128]{2,1,0:T(8,128)(2,1)S(1)}, bf16[512,8,128]{2,1,0:T(8,128)(2,1)}, u32[]{:S(2)}) copy-start(bf16[512,8,128]{2,1,0:T(8,128)(2,1)} %get-tuple-element.9) | copy-start | bytes 3145732
  92.5 9.8 %collective-permute-start.3 = (bf16[256,1,128]{2,0,1:T(8,128)(2,1)S(1)}, bf16[256,1,128]{2,0,1:T(8,128)(2,1)S(1)}, u32[]{:S(2)}, u32[]{:S(2)}) collective-permute-start(bf16[256,1,128]{2,0,1:T(8,128)(2,1)S(1)} %get-tuple-element.15), channel_id=1, source_target_pairs={{1,0},{2,1},{3,2},{5,4},{6,5},{7,6},{9,8},{10,9},{11,10},{13,12},{... | collective-permute-start | bytes 196616 | tf_op jit(solution)/shard_map/ppermute | solution.py:19
  96.8 5.7 %collective-permute-start.6 = (bf16[512,1,128]{2,0,1:T(8,128)(2,1)S(1)}, bf16[512,1,128]{2,0,1:T(8,128)(2,1)S(1)}, u32[]{:S(2)}, u32[]{:S(2)}) collective-permute-start(bf16[512,1,128]{2,0,1:T(8,128)(2,1)S(1)} %copy.42), channel_id=1, source_target_pairs={{0,1},{1,2},{2,3},{4,5},{5,6},{6,7},{8,9},{9,10},{10,11},{12,13},{... | collective-permute-start | bytes 393224 | tf_op jit(solution)/shard_map/ppermute | solution.py:18
  100.0 5.7 %collective-permute-start.7 = (bf16[512,1,128]{2,0,1:T(8,128)(2,1)S(1)}, bf16[512,1,128]{2,0,1:T(8,128)(2,1)S(1)}, u32[]{:S(2)}, u32[]{:S(2)}) collective-permute-start(bf16[512,1,128]{2,0,1:T(8,128)(2,1)S(1)} %copy.43), channel_id=1, source_target_pairs={{1,0},{2,1},{3,2},{5,4},{6,5},{7,6},{9,8},{10,9},{11,10},{13,12},{... | collective-permute-start | bytes 393224 | tf_op jit(solution)/shard_map/ppermute | solution.py:19
  109.0 21.1 %copy-start.21 = (bf16[256,2048]{1,0:T(8,128)(2,1)S(1)}, bf16[256,2048]{1,0:T(8,128)(2,1)}, u32[]{:S(2)}) copy-start(bf16[256,2048]{1,0:T(8,128)(2,1)} %param.14) | copy-start | bytes 3145732
  130.2 4.7 %copy-start.13 = (bf16[4,16,128,128]{3,1,2,0:T(8,128)(2,1)S(1)}, bf16[4,16,128,128]{3,1,2,0:T(8,128)(2,1)}, u32[]{:S(2)}) copy-start(bf16[4,16,128,128]{3,1,2,0:T(8,128)(2,1)} %copy-done.12) | copy-start | bytes 6291460
  130.2 4.7 %copy-start.20 = (bf16[2048,8,128]{2,1,0:T(8,128)(2,1)S(1)}, bf16[2048,8,128]{2,1,0:T(8,128)(2,1)}, u32[]{:S(2)}) copy-start(bf16[2048,8,128]{2,1,0:T(8,128)(2,1)} %all-gather.9.cloned.1.call-done) | copy-start | bytes 12582916
  (13 other events, 36.6 us)
Sparse Core Ops, SparseCore 0:
  9.6 35.0 all-gather.4
  46.3 22.5 all-gather.6
  71.0 22.5 all-gather.10
  95.6 34.4 all-gather.8
where the time goes:
time: 159 us; the launch traced here: 156 us
  waiting for transfers between devices  51.3 us (32%)
  local copies, waits for them, and re-layouts  28.7 us (18%)
  matrix products  23.9 us (15%)
  starting transfers between devices  21.6 us (14%)
  other arithmetic  16.4 us (10%)
  between operations  14.2 us (9%)
    all_gather x2, waiting for transfers between devices, on_device(): gain = add_gain(lax.all_gather(state_p, 'mode', axis=0, tiled=True))  42.6 us
    unnamed x57, local copies, waits for them, and re-layouts  13.4 us
    ppermute x4, starting transfers between devices, extended(): before = lax.ppermute(last, axis, up)  12.5 us
    dot_general x2, matrix products, add_gain(): jnp.dot(absorption, piece.reshape(piece.shape[0], cells), preferred_eleme...  10.1 us
    ppermute x4, starting transfers between devices, extended(): after = lax.ppermute(first, axis, down)  8.91 us
    dot_general x2, matrix products, on_device(): scatter = jnp.dot(dense_all, add_flat, preferred_element_type=jnp.float32)  7.37 us
    ppermute x4, waiting for transfers between devices, extended(): after = lax.ppermute(first, axis, down)  7.22 us
    reshape x1, local copies, waits for them, and re-layouts, add_gain(): piece.reshape(piece.shape[0], cells)  6.65 us
  transfers between devices with their start and end apart: 12, of which 6 were waited for; matrix products, arithmetic and copies ran while one was open for 31% of the time, Pallas kernels for 0%

commit v1 on v0

v1 whole, which is shorter than its diff:
```python
import jax
import jax.numpy as jnp
from jax import lax
from jax.experimental import pallas as pl
from jax.experimental.pallas import tpu as pltpu
from jax.sharding import PartitionSpec as P

NM = 2048
BLK = 128
ITERS = 2
CORES = 2
CHUNKS = 2


def swap_cores(x):
    n = lax.axis_size("mode")
    return lax.ppermute(x, "mode", [(i, i ^ 1) for i in range(n)])


def from_chip(x, offset):
    n = lax.axis_size("mode")
    return lax.ppermute(x, "mode", [((i + CORES * offset) % n, i) for i in range(n)])


def from_space(x, step):
    n = lax.axis_size("space")
    pairs = [(i, i - step) for i in range(n) if 0 <= i - step < n]
    return lax.ppermute(x, "space", pairs)


def step_kernel(e, p, pieces, width, ny, source_ref, *refs):
    piece_refs = refs[:pieces]
    (low_ref, high_ref, up_ref, emission_ref, absorption_ref, dense_ref,
     speed_ref, diffusion_ref, e_rate_ref, p_rate_ref, out_ref, se_ref, sp_ref) = refs[pieces:]
    for j, piece in enumerate(piece_refs):
        owner = source_ref[j]
        se_ref[pl.ds(pl.multiple_of(owner * e, e), e), :] = piece[0:e, :]
        sp_ref[pl.ds(pl.multiple_of(owner * p, p), p), :] = piece[e:, :]
    own_ref = piece_refs[0]
    tile = min(p, 256)

    def around(rows):
        own = own_ref[rows, :].astype(jnp.float32)
        low = low_ref[rows, :].astype(jnp.float32)
        high = high_ref[rows, :].astype(jnp.float32)
        if width == ny:
            return own, low, high
        lower = jnp.concatenate([low, own[:, : width - ny]], axis=1)
        higher = jnp.concatenate([own[:, ny:], high], axis=1)
        return own, lower, higher

    own, lower, higher = around(pl.ds(0, e))
    gain = jnp.dot(absorption_ref[...], sp_ref[...], preferred_element_type=jnp.float32)
    f_up = jnp.where(up_ref[...] == 1, lower, higher)
    out_ref[0:e, :] = (
        (own - speed_ref[...] * (own - f_up) + 0.5 * gain) / (1.0 + e_rate_ref[...])
    ).astype(jnp.bfloat16)

    @pl.loop(0, p // tile)
    def _(i):
        at = pl.multiple_of(i * tile, tile)
        source = jnp.dot(
            emission_ref[pl.ds(at, tile), :], se_ref[...], preferred_element_type=jnp.float32
        ) + jnp.dot(dense_ref[pl.ds(at, tile), :], sp_ref[...], preferred_element_type=jnp.float32)
        own, lower, higher = around(pl.ds(pl.multiple_of(e + at, e), tile))
        column = lax.broadcasted_iota(jnp.int32, (tile, ny), 1)
        left, right = [], []
        for r in range(width // ny):
            row = own[:, r * ny : (r + 1) * ny]
            left.append(jnp.where(column == 0, 0.0, pltpu.roll(row, 1, 1)))
            right.append(jnp.where(column == ny - 1, 0.0, pltpu.roll(row, ny - 1, 1)))
        left, right = jnp.concatenate(left, axis=1), jnp.concatenate(right, axis=1)
        lap = lower + higher + left + right - 4.0 * own
        out_ref[pl.ds(pl.multiple_of(e + at, e), tile), :] = (
            (own + diffusion_ref[pl.ds(at, tile), :] * lap + 0.5 * source)
            / (1.0 + p_rate_ref[pl.ds(at, tile), :])
        ).astype(jnp.bfloat16)


def on_device(
    electrons,
    phonons,
    emission,
    absorption,
    block_coupling,
    block_cols,
    upwind,
    speed,
    diffusion,
    electron_rate,
    phonon_rate,
):
    e, nx, ny = electrons.shape
    p = phonons.shape[0]
    rows = e + p
    n = lax.axis_size("mode")
    chips = n // CORES
    slots = block_coupling.shape[1]
    b_rows = p // BLK
    kernel = block_coupling.reshape(b_rows, BLK, slots, BLK)
    block_ids = jnp.arange(NM // BLK, dtype=jnp.int32)
    hits = (block_cols[:, :, None] == block_ids[None, None, :]).astype(jnp.bfloat16)
    dense = jnp.einsum(
        "bsk,bisj->bikj", hits, kernel, preferred_element_type=jnp.float32
    ).astype(jnp.bfloat16).reshape(p, NM)

    tall = nx // CHUNKS
    width = tall * ny
    me = lax.axis_index("mode")
    chip, core = me // CORES, me % CORES
    sources = jnp.stack(
        [((chip + d) % chips) * CORES + (core ^ c) for d in range(chips) for c in range(CORES)]
    ).astype(jnp.int32)
    speed, diffusion = speed[:, None], diffusion[:, None]
    electron_rate, phonon_rate = electron_rate[:, None], phonon_rate[:, None]
    ups = [upwind[k * tall : (k + 1) * tall].reshape(1, width) for k in range(CHUNKS)]

    def step(pieces, low, high, up):
        whole = pl.BlockSpec(memory_space=pltpu.VMEM)
        operands = (*pieces, low, high, up, emission, absorption, dense, speed, diffusion, electron_rate, phonon_rate)
        return pl.pallas_call(
            lambda *refs: step_kernel(e, p, n, width, ny, *refs),
            out_shape=jax.ShapeDtypeStruct((rows, width), jnp.bfloat16),
            in_specs=[pl.BlockSpec(memory_space=pltpu.SMEM)] + [whole] * len(operands),
            out_specs=whole,
            scratch_shapes=[
                pltpu.VMEM((n * e, width), jnp.bfloat16),
                pltpu.VMEM((n * p, width), jnp.bfloat16),
            ],
            compiler_params=pltpu.CompilerParams(vmem_limit_bytes=32 << 20),
            cost_estimate=pl.CostEstimate(
                flops=2 * width * n * (e * p * 2 + p * p),
                bytes_accessed=2 * ((n + 1) * rows * width + n * (2 * e * p + p * p)),
                transcendentals=0,
            ),
            name="step",
        )(sources, *operands)

    chunks = [
        jnp.concatenate(
            [x[:, k * tall : (k + 1) * tall].reshape(-1, width) for x in (electrons, phonons)], axis=0
        )
        for k in range(CHUNKS)
    ]
    for _ in range(ITERS):
        low = from_space(chunks[-1][:, width - ny :], -1)
        high = from_space(chunks[0][:, :ny], 1)
        edges = [low] + [c[:, width - ny :] for c in chunks[:-1]], [c[:, :ny] for c in chunks[1:]] + [high]
        new = []
        for k, chunk in enumerate(chunks):
            pieces = [chunk, swap_cores(chunk)]
            for d in range(1, chips):
                far = from_chip(chunk, d)
                pieces += [far, swap_cores(far)]
            new.append(step(pieces, edges[0][k], edges[1][k], ups[k]))
        chunks = new
    state = jnp.concatenate([c.reshape(rows, tall, ny) for c in chunks], axis=1)
    return state[:e], state[e:]


def solution(mesh):
    placed = (
        P("mode", ("grp", "space"), None),
        P("mode", ("grp", "space"), None),
        P("mode", None),
        P("mode", None),
        P("mode", None, None),
        P("mode", None),
        P(("grp", "space"), None),
        P("mode"),
        P("mode"),
        P("mode"),
        P("mode"),
    )
    return jax.shard_map(
        on_device,
        mesh=mesh,
        in_specs=placed,
        out_specs=(P("mode", ("grp", "space"), None), P("mode", ("grp", "space"), None)),
        check_vma=False,
    )
```

time: 159 us -> 134 us (0.84)
  matrix products: 23.9 us -> 2.48 us
  Pallas kernels: 0 us -> 19.1 us
  between operations: 14.2 us -> 1.02 us
  other arithmetic: 16.4 us -> 6.41 us
  waiting for transfers between devices: 51.3 us -> 53.8 us
  local copies, waits for them, and re-layouts: 28.7 us -> 26.5 us
    ppermute x8 -> x16, waiting for transfers between devices: 7.29 us -> 53.8 us  [the longest x4 49.3 us: from_chip(): lax.ppermute(x, 'mode', [((i + CORES * offset) % n, i) for i in range(n)])]
    all_gather x4 -> x0, waiting for transfers between devices: 42.6 us -> none  [the longest x2 42.6 us: on_device(): gain = add_gain(lax.all_gather(state_p, 'mode', axis=0, tiled=True))]
    dot_general x6 -> x0, matrix products: 22.7 us -> none  [the longest x2 10.1 us: add_gain(): jnp.dot(absorption, piece.reshape(piece.shape[0], cells), preferred_eleme...]
    pallas_call x0 -> x4, Pallas kernels: none -> 19.1 us  [step(): pl.pallas_call(lambda *refs: step_kernel(e, p, n, width, ny, *refs), out_...]
    convert_element_type x8 -> x0, other arithmetic: 16.4 us -> none  [the longest x2 6.33 us: on_device(): rim_p = rimmed_p.astype(jnp.float32)]
    concatenate x0 -> x5, other arithmetic: none -> 5.26 us  [the longest x4 3.75 us: on_device(): jnp.concatenate([x[:, k * tall:(k + 1) * tall].reshape(-1, width) for x i...]
    all_gather x1 -> x0, local copies, waits for them, and re-layouts: 4 us -> none  [on_device(): emit = add_emit(lax.all_gather(state_e, 'mode', axis=0, tiled=True))]
    slice x6 -> x5, local copies, waits for them, and re-layouts: 2.35 us -> 6.19 us  [the longest x2 4.36 us: on_device(): x[:, k * tall:(k + 1) * tall].reshape(-1, width)]
  transfers between devices with their start and end apart: 12 -> 16, of which waited for: 6 -> 5; matrix products, arithmetic and copies ran while one was open for 31% -> 12% of each run, Pallas kernels for 0% -> 11%
where the time goes in v1:
time: 134 us; the launch traced here: 132 us
  waiting for transfers between devices  53.8 us (40%)
  local copies, waits for them, and re-layouts  26.5 us (20%)
  starting transfers between devices  22.8 us (17%)
  Pallas kernels  19.1 us (14%)
  other arithmetic  6.41 us (5%)
  matrix products  2.48 us (2%)
    ppermute x4, waiting for transfers between devices, from_chip(): lax.ppermute(x, 'mode', [((i + CORES * offset) % n, i) for i in range(n)])  49.3 us
    pallas_call x4, Pallas kernels, step(): pl.pallas_call(lambda *refs: step_kernel(e, p, n, width, ny, *refs), out_...  19.1 us
    unnamed x47, local copies, waits for them, and re-layouts  14.8 us
    ppermute x4, starting transfers between devices, from_space(): return lax.ppermute(x, 'space', pairs)  10.6 us
    ppermute x8, starting transfers between devices, swap_cores(): return lax.ppermute(x, 'mode', [(i, i ^ 1) for i in range(n)])  9.23 us
    ppermute x4, waiting for transfers between devices, from_space(): return lax.ppermute(x, 'space', pairs)  4.46 us
    slice x2, local copies, waits for them, and re-layouts, on_device(): x[:, k * tall:(k + 1) * tall].reshape(-1, width)  4.36 us
    reshape x2, local copies, waits for them, and re-layouts, on_device(): state = jnp.concatenate([c.reshape(rows, tall, ny) for c in chunks], axis=1)  4.26 us
  transfers between devices with their start and end apart: 16, of which 5 were waited for; matrix products, arithmetic and copies ran while one was open for 12% of the time, Pallas kernels for 11%

profile of v1, /device:TPU:13, one launch (start us, length us, event | category | flops | bytes accessed | tf_op | source)
XLA Modules:
  0.0 132.1 jit_solution(6721609418517409365)
XLA Ops:
  0.6 2.1 %fusion.12 = (bf16[512,4,128]{2,1,0:T(4,128)(2,1)S(1)}, bf16[512,4,128]{2,1,0:T(4,128)(2,1)S(1)}) fusion(bf16[512,8,128]{2,1,0:T(8,128)(2,1)} %param.12), kind=kLoop, calls=%fused_computation.24 | loop fusion | bytes 2097152 | tf_op jit(solution)/shard_map/slice | solution.py:141
  3.3 2.3 %fusion.15 = (bf16[256,4,128]{2,1,0:T(4,128)(2,1)S(1)}, bf16[256,4,128]{2,1,0:T(4,128)(2,1)}) fusion(bf16[256,8,128]{2,1,0:T(8,128)(2,1)} %param.11), kind=kLoop, calls=%fused_computation.27 | loop fusion | bytes 1048576 | tf_op jit(solution)/shard_map/slice | solution.py:141
  13.2 3.2 %collective-permute-start.3 = (bf16[768,128]{1,0:T(8,128)(2,1)}, bf16[768,128]{1,0:T(8,128)(2,1)}, u32[]{:S(2)}, u32[]{:S(2)}) collective-permute-start(bf16[768,128]{1,0:T(8,128)(2,1)} %get-tuple-element.9), channel_id=1, source_target_pairs={{0,1},{1,2},{2,3},{4,5},{5,6},{6,7},{8,9},{9,10},{10,11},{12,13},{... | collective-permute-start | bytes 589832 | tf_op jit(solution)/shard_map/ppermute | solution.py:28
  16.4 9.3 %collective-permute-done.1.refs_3_ = bf16[768,512]{1,0:T(8,128)(2,1)} collective-permute-done((bf16[768,512]{1,0:T(8,128)(2,1)}, bf16[768,512]{1,0:T(8,128)(2,1)}, u32[]{:S(2)}, u32[]{:S(2)}) %collective-permute-start.1) | collective-permute-done | bytes 786464 | tf_op jit(solution)/shard_map/ppermute | solution.py:22
  25.6 2.7 %collective-permute-start.2 = (bf16[768,512]{1,0:T(8,128)(2,1)}, bf16[768,512]{1,0:T(8,128)(2,1)}, u32[]{:S(2)}, u32[]{:S(2)}) collective-permute-start(bf16[768,512]{1,0:T(8,128)(2,1)} %collective-permute-done.1.refs_3_), channel_id=1, source_target_pairs={{0,4},{4,0},{8,12},{12,8},{1,5},{5,1},{9,13},{13,9},{2,6},{6,2},{1... | collective-permute-start | bytes 2359304 | tf_op jit(solution)/shard_map/ppermute | solution.py:17
  28.3 14.2 %collective-permute-done.8.refs_3_ = bf16[768,512]{1,0:T(8,128)(2,1)} collective-permute-done((bf16[768,512]{1,0:T(8,128)(2,1)}, bf16[768,512]{1,0:T(8,128)(2,1)}, u32[]{:S(2)}, u32[]{:S(2)}) %collective-permute-start.8) | collective-permute-done | bytes 786464 | tf_op jit(solution)/shard_map/ppermute | solution.py:22
  42.5 1.5 %collective-permute-start.9 = (bf16[768,512]{1,0:T(8,128)(2,1)}, bf16[768,512]{1,0:T(8,128)(2,1)}, u32[]{:S(2)}, u32[]{:S(2)}) collective-permute-start(bf16[768,512]{1,0:T(8,128)(2,1)} %collective-permute-done.8.refs_3_), channel_id=1, source_target_pairs={{0,4},{4,0},{8,12},{12,8},{1,5},{5,1},{9,13},{13,9},{2,6},{6,2},{1... | collective-permute-start | bytes 2359304 | tf_op jit(solution)/shard_map/ppermute | solution.py:17
  44.0 2.5 %fusion.2 = bf16[4,16,128,128]{3,1,2,0:T(8,128)(2,1)} fusion(bf16[4,128,12,128]{3,1,0,2:T(8,128)(2,1)S(1)} %bitcast.26, s32[4,12]{1,0:T(4,128)S(1)} %copy-done.16), kind=kOutput, calls=%fused_computation.3 | convolution fusion | flops 26215168 | bytes 3670208 | tf_op jit(solution)/shard_map/bsk,bisj->bikj/dot_general | solution.py:103
  46.5 3.6 %copy.50 = bf16[64,8,16,128]{3,1,2,0:T(8,128)(2,1)} copy(bf16[64,8,16,128]{3,2,1,0:T(8,128)(2,1)} %bitcast.35) | data formatting | bytes 4194304
  51.9 2.1 %collective-permute-start.10 = (bf16[768,128]{1,0:T(8,128)(2,1)S(1)}, bf16[768,128]{1,0:T(8,128)(2,1)S(1)}, u32[]{:S(2)}, u32[]{:S(2)}) collective-permute-start(bf16[768,128]{1,0:T(8,128)(2,1)S(1)} %get-tuple-element.10), channel_id=1, source_target_pairs={{1,0},{2,1},{3,2},{5,4},{6,5},{7,6},{9,8},{10,9},{11,10},{13,12},{... | collective-permute-start | bytes 589832 | tf_op jit(solution)/shard_map/ppermute | solution.py:28
  54.0 1.6 %copy-done.1 = bf16[64,8,16,128]{3,1,2,0:T(8,128)(2,1)S(1)} copy-done((bf16[64,8,16,128]{3,1,2,0:T(8,128)(2,1)S(1)}, bf16[64,8,16,128]{3,1,2,0:T(8,128)(2,1)}, u32[]{:S(2)}) %copy-start.1) | copy-done | bytes 2097176
  57.8 5.0 %step.4.refs_1_ = bf16[768,512]{1,0:T(8,128)(2,1)S(1)} custom-call(s32[4]{0:T(128)S(1)} %pad_add_fusion.refs_0_, bf16[768,512]{1,0:T(8,128)(2,1)} %pad_maximum_fusion.refs_1_, bf16[768,512]{1,0:T(8,128)(2,1)} %collective-permute-done.refs_2_, bf16[768,512]{1,0:T(8,128)(2,1)} %collective-permute-done.1.refs_3_, ...), custom_call_target="tpu_custom_call" | custom-call | flops 2147483648 | bytes 8126464 | tf_op jit(solution)/shard_map/step/pallas_call | solution.py:121
  63.0 5.8 %step.5.refs_1_ = bf16[768,512]{1,0:T(8,128)(2,1)} custom-call(s32[4]{0:T(128)S(1)} %pad_add_fusion.refs_0_, bf16[768,512]{1,0:T(8,128)(2,1)} %pad_maximum_fusion.1.refs_1_, bf16[768,512]{1,0:T(8,128)(2,1)} %collective-permute-done.7.refs_2_, bf16[768,512]{1,0:T(8,128)(2,1)} %collective-permute-done.8.refs_3_, ...), custom_call_target="tpu_custom_call" | custom-call | flops 2147483648 | bytes 8126464 | tf_op jit(solution)/shard_map/step/pallas_call | solution.py:121
  71.0 10.8 %collective-permute-done.5.refs_3_ = bf16[768,512]{1,0:T(8,128)(2,1)S(1)} collective-permute-done((bf16[768,512]{1,0:T(8,128)(2,1)S(1)}, bf16[768,512]{1,0:T(8,128)(2,1)S(1)}, u32[]{:S(2)}, u32[]{:S(2)}) %collective-permute-start.5) | collective-permute-done | bytes 786464 | tf_op jit(solution)/shard_map/ppermute | solution.py:22
  81.7 1.8 %collective-permute-start.6 = (bf16[768,512]{1,0:T(8,128)(2,1)S(1)}, bf16[768,512]{1,0:T(8,128)(2,1)S(1)}, u32[]{:S(2)}, u32[]{:S(2)}) collective-permute-start(bf16[768,512]{1,0:T(8,128)(2,1)S(1)} %collective-permute-done.5.refs_3_), channel_id=1, source_target_pairs={{0,4},{4,0},{8,12},{12,8},{1,5},{5,1},{9,13},{13,9},{2,6},{6,2},{1... | collective-permute-start | bytes 2359304 | tf_op jit(solution)/shard_map/ppermute | solution.py:17
  83.5 15.1 %collective-permute-done.13.refs_3_ = bf16[768,512]{1,0:T(8,128)(2,1)} collective-permute-done((bf16[768,512]{1,0:T(8,128)(2,1)}, bf16[768,512]{1,0:T(8,128)(2,1)}, u32[]{:S(2)}, u32[]{:S(2)}) %collective-permute-start.13) | collective-permute-done | bytes 786464 | tf_op jit(solution)/shard_map/ppermute | solution.py:22
  100.8 3.2 %collective-permute-start.11 = (bf16[768,128]{1,0:T(8,128)(2,1)S(1)}, bf16[768,128]{1,0:T(8,128)(2,1)S(1)}, u32[]{:S(2)}, u32[]{:S(2)}) collective-permute-start(bf16[768,128]{1,0:T(8,128)(2,1)S(1)} %get-tuple-element.5), channel_id=1, source_target_pairs={{0,1},{1,2},{2,3},{4,5},{5,6},{6,7},{8,9},{9,10},{10,11},{12,13},{... | collective-permute-start | bytes 589832 | tf_op jit(solution)/shard_map/ppermute | solution.py:28
  104.8 4.5 %collective-permute-done.11.refs_5_ = bf16[768,128]{1,0:T(8,128)(2,1)S(1)} collective-permute-done((bf16[768,128]{1,0:T(8,128)(2,1)S(1)}, bf16[768,128]{1,0:T(8,128)(2,1)S(1)}, u32[]{:S(2)}, u32[]{:S(2)}) %collective-permute-start.11) | collective-permute-done | bytes 196640 | tf_op jit(solution)/shard_map/ppermute | solution.py:28
  109.3 2.1 %collective-permute-start.15 = (bf16[768,128]{1,0:T(8,128)(2,1)}, bf16[768,128]{1,0:T(8,128)(2,1)}, u32[]{:S(2)}, u32[]{:S(2)}) collective-permute-start(bf16[768,128]{1,0:T(8,128)(2,1)} %get-tuple-element.6), channel_id=1, source_target_pairs={{1,0},{2,1},{3,2},{5,4},{6,5},{7,6},{9,8},{10,9},{11,10},{13,12},{... | collective-permute-start | bytes 589832 | tf_op jit(solution)/shard_map/ppermute | solution.py:28
  111.4 3.5 %step.6 = bf16[768,512]{1,0:T(8,128)(2,1)S(1)} custom-call(s32[4]{0:T(128)S(1)} %pad_add_fusion.refs_0_, bf16[768,512]{1,0:T(8,128)(2,1)S(1)} %step.4.refs_1_, bf16[768,512]{1,0:T(8,128)(2,1)S(1)} %collective-permute-done.4.refs_2_, bf16[768,512]{1,0:T(8,128)(2,1)S(1)} %collective-permute-done.5.refs_3_, ...), custom_call_target="tpu_custom_call" | custom-call | flops 2147483648 | bytes 8126464 | tf_op jit(solution)/shard_map/step/pallas_call | solution.py:121
  115.8 2.4 %reshape.43 = bf16[768,4,128]{2,1,0:T(4,128)(2,1)} reshape(bf16[768,512]{1,0:T(8,128)(2,1)} %copy-done.9) | data formatting | bytes 1572864 | tf_op jit(solution)/shard_map/reshape | solution.py:157
  118.3 1.6 %copy-done.3 = bf16[64,8,16,128]{3,1,2,0:T(8,128)(2,1)S(1)} copy-done((bf16[64,8,16,128]{3,1,2,0:T(8,128)(2,1)S(1)}, bf16[64,8,16,128]{3,1,2,0:T(8,128)(2,1)}, u32[]{:S(2)}) %copy-start.3) | copy-done | bytes 2097176
  122.0 4.8 %step.7 = bf16[768,512]{1,0:T(8,128)(2,1)S(1)} custom-call(s32[4]{0:T(128)S(1)} %pad_add_fusion.refs_0_, bf16[768,512]{1,0:T(8,128)(2,1)} %step.5.refs_1_, bf16[768,512]{1,0:T(8,128)(2,1)} %collective-permute-done.12.refs_2_, bf16[768,512]{1,0:T(8,128)(2,1)} %collective-permute-done.13.refs_3_, bf16[768,512]{1,0:T(8,128)(2,1)} %collective-permute-done.14.refs_4_, ...), custom_call_target="tpu_custom_call" | custom-call | flops 2147483648 | bytes 8126464 | tf_op jit(solution)/shard_map/step/pallas_call | solution.py:121
  127.7 1.8 %reshape.44 = bf16[768,4,128]{2,1,0:T(4,128)(2,1)S(1)} reshape(bf16[768,512]{1,0:T(8,128)(2,1)} %copy-done.8) | data formatting | bytes 1572864 | tf_op jit(solution)/shard_map/reshape | solution.py:157
  (82 shorter events, 23.7 us)
Async XLA Ops:
  0.6 43.4 %copy-start = (bf16[512,12,128]{2,0,1:T(8,128)(2,1)S(1)}, bf16[512,12,128]{2,0,1:T(8,128)(2,1)}, u32[]{:S(2)}) copy-start(bf16[512,12,128]{2,0,1:T(8,128)(2,1)} %param.15) | copy-start | bytes 4718596
  3.3 4.2 %copy-start.13 = (bf16[512,512]{1,0:T(8,128)(2,1)}, bf16[512,512]{1,0:T(8,128)(2,1)S(1)}, u32[]{:S(2)}) copy-start(bf16[512,512]{1,0:T(8,128)(2,1)S(1)} %copy.17) | copy-start | bytes 1572868
  6.9 18.7 %collective-permute-start.1 = (bf16[768,512]{1,0:T(8,128)(2,1)}, bf16[768,512]{1,0:T(8,128)(2,1)}, u32[]{:S(2)}, u32[]{:S(2)}) collective-permute-start(bf16[768,512]{1,0:T(8,128)(2,1)} %pad_maximum_fusion.refs_1_), channel_id=1, source_target_pairs={{8,0},{12,4},{0,8},{4,12},{9,1},{13,5},{1,9},{5,13},{10,2},{14,6},... | collective-permute-start | bytes 2359304 | tf_op jit(solution)/shard_map/ppermute | solution.py:22
  7.7 36.4 %copy-start.16 = (s32[4,12]{1,0:T(4,128)S(1)}, s32[4,12]{1,0:T(4,128)}, u32[]{:S(2)}) copy-start(s32[4,12]{1,0:T(4,128)} %param.16) | copy-start | bytes 580
  9.9 32.6 %collective-permute-start.8 = (bf16[768,512]{1,0:T(8,128)(2,1)}, bf16[768,512]{1,0:T(8,128)(2,1)}, u32[]{:S(2)}, u32[]{:S(2)}) collective-permute-start(bf16[768,512]{1,0:T(8,128)(2,1)} %pad_maximum_fusion.1.refs_1_), channel_id=1, source_target_pairs={{8,0},{12,4},{0,8},{4,12},{9,1},{13,5},{1,9},{5,13},{10,2},{14,6},... | collective-permute-start | bytes 2359304 | tf_op jit(solution)/shard_map/ppermute | solution.py:22
  11.1 42.9 %collective-permute-start = (bf16[768,512]{1,0:T(8,128)(2,1)}, bf16[768,512]{1,0:T(8,128)(2,1)}, u32[]{:S(2)}, u32[]{:S(2)}) collective-permute-start(bf16[768,512]{1,0:T(8,128)(2,1)} %pad_maximum_fusion.refs_1_), channel_id=1, source_target_pairs={{0,4},{4,0},{8,12},{12,8},{1,5},{5,1},{9,13},{13,9},{2,6},{6,2},{1... | collective-permute-start | bytes 2359304 | tf_op jit(solution)/shard_map/ppermute | solution.py:17
  12.4 50.6 %collective-permute-start.7 = (bf16[768,512]{1,0:T(8,128)(2,1)}, bf16[768,512]{1,0:T(8,128)(2,1)}, u32[]{:S(2)}, u32[]{:S(2)}) collective-permute-start(bf16[768,512]{1,0:T(8,128)(2,1)} %pad_maximum_fusion.1.refs_1_), channel_id=1, source_target_pairs={{0,4},{4,0},{8,12},{12,8},{1,5},{5,1},{9,13},{13,9},{2,6},{6,2},{1... | collective-permute-start | bytes 2359304 | tf_op jit(solution)/shard_map/ppermute | solution.py:17
  13.2 38.7 %collective-permute-start.3 = (bf16[768,128]{1,0:T(8,128)(2,1)}, bf16[768,128]{1,0:T(8,128)(2,1)}, u32[]{:S(2)}, u32[]{:S(2)}) collective-permute-start(bf16[768,128]{1,0:T(8,128)(2,1)} %get-tuple-element.9), channel_id=1, source_target_pairs={{0,1},{1,2},{2,3},{4,5},{5,6},{6,7},{8,9},{9,10},{10,11},{12,13},{... | collective-permute-start | bytes 589832 | tf_op jit(solution)/shard_map/ppermute | solution.py:28
  25.6 28.4 %collective-permute-start.2 = (bf16[768,512]{1,0:T(8,128)(2,1)}, bf16[768,512]{1,0:T(8,128)(2,1)}, u32[]{:S(2)}, u32[]{:S(2)}) collective-permute-start(bf16[768,512]{1,0:T(8,128)(2,1)} %collective-permute-done.1.refs_3_), channel_id=1, source_target_pairs={{0,4},{4,0},{8,12},{12,8},{1,5},{5,1},{9,13},{13,9},{2,6},{6,2},{1... | collective-permute-start | bytes 2359304 | tf_op jit(solution)/shard_map/ppermute | solution.py:17
  42.5 20.5 %collective-permute-start.9 = (bf16[768,512]{1,0:T(8,128)(2,1)}, bf16[768,512]{1,0:T(8,128)(2,1)}, u32[]{:S(2)}, u32[]{:S(2)}) collective-permute-start(bf16[768,512]{1,0:T(8,128)(2,1)} %collective-permute-done.8.refs_3_), channel_id=1, source_target_pairs={{0,4},{4,0},{8,12},{12,8},{1,5},{5,1},{9,13},{13,9},{2,6},{6,2},{1... | collective-permute-start | bytes 2359304 | tf_op jit(solution)/shard_map/ppermute | solution.py:17
  46.5 4.1 %copy-start.20 = (f32[256]{0:T(256)S(1)}, f32[256]{0:T(256)}, u32[]{:S(2)}) copy-start(f32[256]{0:T(256)} %param.20) | copy-start | bytes 3076
  46.5 5.4 %copy-start.15 = (s32[8,128]{1,0:T(8,128)S(1)}, s32[8,128]{1,0:T(8,128)}, u32[]{:S(2)}) copy-start(s32[8,128]{1,0:T(8,128)} %param.17) | copy-start | bytes 12292
  46.5 7.5 %copy-start.4 = (bf16[512,1024]{1,0:T(8,128)(2,1)S(1)}, bf16[512,1024]{1,0:T(8,128)(2,1)}, u32[]{:S(2)}) copy-start(bf16[512,1024]{1,0:T(8,128)(2,1)} %refs_8_.7) | copy-start | bytes 3145732
  51.9 11.0 %collective-permute-start.10 = (bf16[768,128]{1,0:T(8,128)(2,1)S(1)}, bf16[768,128]{1,0:T(8,128)(2,1)S(1)}, u32[]{:S(2)}, u32[]{:S(2)}) collective-permute-start(bf16[768,128]{1,0:T(8,128)(2,1)S(1)} %get-tuple-element.10), channel_id=1, source_target_pairs={{1,0},{2,1},{3,2},{5,4},{6,5},{7,6},{9,8},{10,9},{11,10},{13,12},{... | collective-permute-start | bytes 589832 | tf_op jit(solution)/shard_map/ppermute | solution.py:28
  57.8 5.2 %copy-start.2 = (bf16[64,8,16,128]{3,1,2,0:T(8,128)(2,1)S(1)}, bf16[64,8,16,128]{3,1,2,0:T(8,128)(2,1)}, u32[]{:S(2)}) copy-start(bf16[64,8,16,128]{3,1,2,0:T(8,128)(2,1)} %copy.50) | copy-start | bytes 6291460
  57.8 5.2 %copy-start.6 = (bf16[256,2048]{1,0:T(8,128)(2,1)S(1)}, bf16[256,2048]{1,0:T(8,128)(2,1)}, u32[]{:S(2)}) copy-start(bf16[256,2048]{1,0:T(8,128)(2,1)} %refs_9_.7) | copy-start | bytes 3145732
  62.8 18.9 %collective-permute-start.5 = (bf16[768,512]{1,0:T(8,128)(2,1)S(1)}, bf16[768,512]{1,0:T(8,128)(2,1)S(1)}, u32[]{:S(2)}, u32[]{:S(2)}) collective-permute-start(bf16[768,512]{1,0:T(8,128)(2,1)S(1)} %step.4.refs_1_), channel_id=1, source_target_pairs={{8,0},{12,4},{0,8},{4,12},{9,1},{13,5},{1,9},{5,13},{10,2},{14,6},... | collective-permute-start | bytes 2359304 | tf_op jit(solution)/shard_map/ppermute | solution.py:22
  68.7 29.9 %collective-permute-start.13 = (bf16[768,512]{1,0:T(8,128)(2,1)}, bf16[768,512]{1,0:T(8,128)(2,1)}, u32[]{:S(2)}, u32[]{:S(2)}) collective-permute-start(bf16[768,512]{1,0:T(8,128)(2,1)} %step.5.refs_1_), channel_id=1, source_target_pairs={{8,0},{12,4},{0,8},{4,12},{9,1},{13,5},{1,9},{5,13},{10,2},{14,6},... | collective-permute-start | bytes 2359304 | tf_op jit(solution)/shard_map/ppermute | solution.py:22
  70.1 41.2 %collective-permute-start.4 = (bf16[768,512]{1,0:T(8,128)(2,1)S(1)}, bf16[768,512]{1,0:T(8,128)(2,1)S(1)}, u32[]{:S(2)}, u32[]{:S(2)}) collective-permute-start(bf16[768,512]{1,0:T(8,128)(2,1)S(1)} %step.4.refs_1_), channel_id=1, source_target_pairs={{0,4},{4,0},{8,12},{12,8},{1,5},{5,1},{9,13},{13,9},{2,6},{6,2},{1... | collective-permute-start | bytes 2359304 | tf_op jit(solution)/shard_map/ppermute | solution.py:17
  81.7 29.7 %collective-permute-start.6 = (bf16[768,512]{1,0:T(8,128)(2,1)S(1)}, bf16[768,512]{1,0:T(8,128)(2,1)S(1)}, u32[]{:S(2)}, u32[]{:S(2)}) collective-permute-start(bf16[768,512]{1,0:T(8,128)(2,1)S(1)} %collective-permute-done.5.refs_3_), channel_id=1, source_target_pairs={{0,4},{4,0},{8,12},{12,8},{1,5},{5,1},{9,13},{13,9},{2,6},{6,2},{1... | collective-permute-start | bytes 2359304 | tf_op jit(solution)/shard_map/ppermute | solution.py:17
  83.5 34.7 %collective-permute-start.12 = (bf16[768,512]{1,0:T(8,128)(2,1)}, bf16[768,512]{1,0:T(8,128)(2,1)}, u32[]{:S(2)}, u32[]{:S(2)}) collective-permute-start(bf16[768,512]{1,0:T(8,128)(2,1)} %step.5.refs_1_), channel_id=1, source_target_pairs={{0,4},{4,0},{8,12},{12,8},{1,5},{5,1},{9,13},{13,9},{2,6},{6,2},{1... | collective-permute-start | bytes 2359304 | tf_op jit(solution)/shard_map/ppermute | solution.py:17
  98.7 19.6 %collective-permute-start.14 = (bf16[768,512]{1,0:T(8,128)(2,1)}, bf16[768,512]{1,0:T(8,128)(2,1)}, u32[]{:S(2)}, u32[]{:S(2)}) collective-permute-start(bf16[768,512]{1,0:T(8,128)(2,1)} %collective-permute-done.13.refs_3_), channel_id=1, source_target_pairs={{0,4},{4,0},{8,12},{12,8},{1,5},{5,1},{9,13},{13,9},{2,6},{6,2},{1... | collective-permute-start | bytes 2359304 | tf_op jit(solution)/shard_map/ppermute | solution.py:17
  100.8 8.4 %collective-permute-start.11 = (bf16[768,128]{1,0:T(8,128)(2,1)S(1)}, bf16[768,128]{1,0:T(8,128)(2,1)S(1)}, u32[]{:S(2)}, u32[]{:S(2)}) collective-permute-start(bf16[768,128]{1,0:T(8,128)(2,1)S(1)} %get-tuple-element.5), channel_id=1, source_target_pairs={{0,1},{1,2},{2,3},{4,5},{5,6},{6,7},{8,9},{9,10},{10,11},{12,13},{... | collective-permute-start | bytes 589832 | tf_op jit(solution)/shard_map/ppermute | solution.py:28
  109.3 9.0 %collective-permute-start.15 = (bf16[768,128]{1,0:T(8,128)(2,1)}, bf16[768,128]{1,0:T(8,128)(2,1)}, u32[]{:S(2)}, u32[]{:S(2)}) collective-permute-start(bf16[768,128]{1,0:T(8,128)(2,1)} %get-tuple-element.6), channel_id=1, source_target_pairs={{1,0},{2,1},{3,2},{5,4},{6,5},{7,6},{9,8},{10,9},{11,10},{13,12},{... | collective-permute-start | bytes 589832 | tf_op jit(solution)/shard_map/ppermute | solution.py:28
  (13 other events, 25.3 us)

commit v2 on v1

v2 whole, which is shorter than its diff:
```python
import jax
import jax.numpy as jnp
from jax import lax
from jax.experimental import pallas as pl
from jax.experimental.pallas import tpu as pltpu
from jax.sharding import PartitionSpec as P

NM = 2048
BLK = 128
ITERS = 2
CORES = 2
CHUNKS = 2

VMEM = pl.BlockSpec(memory_space=pltpu.VMEM)


def swap_cores(x):
    n = lax.axis_size("mode")
    return lax.ppermute(x, "mode", [(i, i ^ 1) for i in range(n)])


def from_chip(x, offset):
    n = lax.axis_size("mode")
    return lax.ppermute(x, "mode", [((i + CORES * offset) % n, i) for i in range(n)])


def from_space(x, step):
    n = lax.axis_size("space")
    pairs = [(i, i - step) for i in range(n) if 0 <= i - step < n]
    return lax.ppermute(x, "space", pairs)


def after(x, *others):
    return lax.optimization_barrier((x, *others))[0]


def flatten_kernel(e, p, nx, ny, e_ref, p_ref, *refs):
    outs, low_ref, high_ref, wide_ref = refs[:-3], refs[-3], refs[-2], refs[-1]
    tall = nx // len(outs)
    for x_ref, base, count in ((e_ref, 0, e), (p_ref, e, p)):
        tile = min(count, 64)

        @pl.loop(0, count // tile)
        def _(i):
            at = pl.multiple_of(i * tile, tile)
            wide_ref[0 : tile * nx, :] = x_ref[pl.ds(pl.multiple_of(at * nx, tile * nx), tile * nx), :].astype(jnp.float32)
            to = pl.ds(pl.multiple_of(base + at, tile), tile)
            for r in range(nx):
                row = wide_ref[pl.ds(r, tile, stride=nx), :].astype(jnp.bfloat16)
                k, c = r // tall, r % tall
                outs[k][to, c * ny : (c + 1) * ny] = row
                if r == 0:
                    low_ref[to, :] = row
                if r == nx - 1:
                    high_ref[to, :] = row


def flatten(electrons, phonons):
    e, nx, ny = electrons.shape
    p = phonons.shape[0]
    chunk = jax.ShapeDtypeStruct((e + p, nx // CHUNKS * ny), jnp.bfloat16)
    edge = jax.ShapeDtypeStruct((e + p, ny), jnp.bfloat16)
    out = pl.pallas_call(
        lambda *refs: flatten_kernel(e, p, nx, ny, *refs),
        out_shape=(chunk,) * CHUNKS + (edge, edge),
        in_specs=[VMEM, VMEM],
        out_specs=(VMEM,) * (CHUNKS + 2),
        scratch_shapes=[pltpu.VMEM((64 * nx, ny), jnp.float32)],
        compiler_params=pltpu.CompilerParams(vmem_limit_bytes=8 << 20),
        cost_estimate=pl.CostEstimate(flops=0, bytes_accessed=4 * (e + p) * nx * ny, transcendentals=0),
        name="flatten",
    )(electrons.reshape(e * nx, ny), phonons.reshape(p * nx, ny))
    return list(out[:CHUNKS]), out[-2], out[-1]


def step_kernel(e, p, pieces, width, ny, nx, last, edge, source_ref, *refs):
    piece_refs, refs = refs[:pieces], refs[pieces:]
    (low_ref, high_ref, up_ref, emission_ref, absorption_ref, dense_ref,
     speed_ref, diffusion_ref, e_rate_ref, p_rate_ref), refs = refs[:10], refs[10:]
    if last:
        done_refs, refs = refs[: CHUNKS - 1], refs[CHUNKS - 1 :]
        e_out_ref, p_out_ref, se_ref, sp_ref, wide_ref = refs
    else:
        out_ref, edge_ref, se_ref, sp_ref = refs if edge is not None else (refs[0], None, *refs[1:])
    for j, piece in enumerate(piece_refs):
        owner = source_ref[j]
        se_ref[pl.ds(pl.multiple_of(owner * e, e), e), :] = piece[0:e, :]
        sp_ref[pl.ds(pl.multiple_of(owner * p, p), p), :] = piece[e:, :]
    own_ref = piece_refs[0]
    tile = min(p, 256)

    def around(rows):
        own = own_ref[rows, :].astype(jnp.float32)
        low = low_ref[rows, low_ref.shape[1] - ny :].astype(jnp.float32)
        high = high_ref[rows, :ny].astype(jnp.float32)
        lower = jnp.concatenate([low, own[:, : width - ny]], axis=1) if width > ny else low
        higher = jnp.concatenate([own[:, ny:], high], axis=1) if width > ny else high
        return own, lower, higher

    def store(new, at, count, base):
        rows = pl.ds(pl.multiple_of(base + at, count), count)
        if not last:
            new = new.astype(jnp.bfloat16)
            out_ref[rows, :] = new
            if edge is not None:
                edge_ref[rows, :] = new[:, edge * ny : (edge + 1) * ny]
            return
        tall = width // ny
        for k, done in enumerate(done_refs):
            old = done[rows, :].astype(jnp.float32)
            for r in range(tall):
                wide_ref[pl.ds(k * tall + r, count, stride=nx), :] = old[:, r * ny : (r + 1) * ny]
        for r in range(tall):
            wide_ref[pl.ds(nx - tall + r, count, stride=nx), :] = new[:, r * ny : (r + 1) * ny]
        to = p_out_ref if base else e_out_ref
        to[pl.ds(pl.multiple_of(at * nx, count * nx), count * nx), :] = wide_ref[0 : count * nx, :].astype(jnp.bfloat16)

    own, lower, higher = around(pl.ds(0, e))
    gain = jnp.dot(absorption_ref[...], sp_ref[...], preferred_element_type=jnp.float32)
    f_up = jnp.where(up_ref[...] == 1, lower, higher)
    new = (own - speed_ref[...] * (own - f_up) + 0.5 * gain) / (1.0 + e_rate_ref[...])
    store(new, 0, e, 0)

    @pl.loop(0, p // tile)
    def _(i):
        at = pl.multiple_of(i * tile, tile)
        source = jnp.dot(
            emission_ref[pl.ds(at, tile), :], se_ref[...], preferred_element_type=jnp.float32
        ) + jnp.dot(dense_ref[pl.ds(at, tile), :], sp_ref[...], preferred_element_type=jnp.float32)
        own, lower, higher = around(pl.ds(pl.multiple_of(e + at, e), tile))
        column = lax.broadcasted_iota(jnp.int32, (tile, ny), 1)
        left, right = [], []
        for r in range(width // ny):
            row = own[:, r * ny : (r + 1) * ny]
            left.append(jnp.where(column == 0, 0.0, pltpu.roll(row, 1, 1)))
            right.append(jnp.where(column == ny - 1, 0.0, pltpu.roll(row, ny - 1, 1)))
        left, right = jnp.concatenate(left, axis=1), jnp.concatenate(right, axis=1)
        lap = lower + higher + left + right - 4.0 * own
        new = (own + diffusion_ref[pl.ds(at, tile), :] * lap + 0.5 * source) / (1.0 + p_rate_ref[pl.ds(at, tile), :])
        store(new, at, tile, e)


def on_device(
    electrons,
    phonons,
    emission,
    absorption,
    block_coupling,
    block_cols,
    upwind,
    speed,
    diffusion,
    electron_rate,
    phonon_rate,
):
    e, nx, ny = electrons.shape
    p = phonons.shape[0]
    rows = e + p
    n = lax.axis_size("mode")
    chips = n // CORES
    slots = block_coupling.shape[1]
    b_rows = p // BLK
    tall = nx // CHUNKS
    width = tall * ny

    chunks, first, final = flatten(electrons, phonons)
    block_coupling = after(block_coupling, chunks[0])
    kernel = block_coupling.reshape(b_rows, BLK, slots, BLK)
    block_ids = jnp.arange(NM // BLK, dtype=jnp.int32)
    hits = (block_cols[:, :, None] == block_ids[None, None, :]).astype(jnp.bfloat16)
    dense = jnp.einsum(
        "bsk,bisj->bikj", hits, kernel, preferred_element_type=jnp.float32
    ).astype(jnp.bfloat16).reshape(p, NM)

    me = lax.axis_index("mode").astype(jnp.uint32)
    chip, core = me // CORES, me % CORES
    sources = jnp.stack(
        [((chip + d) % chips) * CORES + (core ^ c) for d in range(chips) for c in range(CORES)]
    ).astype(jnp.int32)
    speed, diffusion = speed[:, None], diffusion[:, None]
    electron_rate, phonon_rate = electron_rate[:, None], phonon_rate[:, None]
    ups = [upwind[k * tall : (k + 1) * tall].reshape(1, width) for k in range(CHUNKS)]

    def step(pieces, low, high, up, edge, done):
        last = bool(done)
        operands = (*pieces, low, high, up, emission, absorption, dense, speed, diffusion, electron_rate, phonon_rate, *done)
        scratch = [pltpu.VMEM((n * e, width), jnp.bfloat16), pltpu.VMEM((n * p, width), jnp.bfloat16)]
        if last:
            out = (jax.ShapeDtypeStruct((e * nx, ny), jnp.bfloat16), jax.ShapeDtypeStruct((p * nx, ny), jnp.bfloat16))
            scratch.append(pltpu.VMEM((max(e, min(p, 256)) * nx, ny), jnp.float32))
        else:
            out = (jax.ShapeDtypeStruct((rows, width), jnp.bfloat16),)
            if edge is not None:
                out += (jax.ShapeDtypeStruct((rows, ny), jnp.bfloat16),)
        return pl.pallas_call(
            lambda *refs: step_kernel(e, p, n, width, ny, nx, last, edge, *refs),
            out_shape=out,
            in_specs=[pl.BlockSpec(memory_space=pltpu.SMEM)] + [VMEM] * len(operands),
            out_specs=(VMEM,) * len(out),
            scratch_shapes=scratch,
            compiler_params=pltpu.CompilerParams(vmem_limit_bytes=20 << 20),
            cost_estimate=pl.CostEstimate(
                flops=1000,
                bytes_accessed=1000,
                transcendentals=0,
            ),
            name="step",
        )(sources, *operands)

    wait_for = dense
    for i in range(ITERS):
        low, high = from_space(final, -1), from_space(first, 1)
        swapped = [swap_cores(c) for c in chunks]
        far = [[from_chip(c, d) for d in range(1, chips)] for c in chunks]
        new = []
        for k, chunk in enumerate(chunks):
            pieces = [chunk, swapped[k]]
            for f in far[k]:
                f = after(f, wait_for)
                pieces += [f, swap_cores(f)]
            before = low if k == 0 else chunks[k - 1]
            behind = high if k == CHUNKS - 1 else chunks[k + 1]
            final_step = i == ITERS - 1
            edge = None if final_step else {0: 0, CHUNKS - 1: tall - 1}.get(k)
            out = step(pieces, before, behind, ups[k], edge, new if final_step and k == CHUNKS - 1 else [])
            if edge is not None:
                first, final = (out[1], final) if k == 0 else (first, out[1])
            new.append(out[0])
            wait_for = out[0]
        chunks = new
    return out[0].reshape(e, nx, ny), out[1].reshape(p, nx, ny)


def solution(mesh):
    placed = (
        P("mode", ("grp", "space"), None),
        P("mode", ("grp", "space"), None),
        P("mode", None),
        P("mode", None),
        P("mode", None, None),
        P("mode", None),
        P(("grp", "space"), None),
        P("mode"),
        P("mode"),
        P("mode"),
        P("mode"),
    )
    return jax.shard_map(
        on_device,
        mesh=mesh,
        in_specs=placed,
        out_specs=(P("mode", ("grp", "space"), None), P("mode", ("grp", "space"), None)),
        check_vma=False,
    )
```

time: 134 us -> 101 us (0.75)
  local copies, waits for them, and re-layouts: 26.5 us -> 8.56 us
  other arithmetic: 6.41 us -> 0.08 us
  starting transfers between devices: 22.8 us -> 17.6 us
  waiting for transfers between devices: 53.8 us -> 50 us
  Pallas kernels: 19.1 us -> 20.5 us
    ppermute x4, waiting for transfers between devices: 49.3 us -> 30.6 us  [from_chip(): lax.ppermute(x, 'mode', [((i + CORES * offset) % n, i) for i in range(n)])]
    ppermute x4, waiting for transfers between devices: 4.46 us -> 19.4 us  [from_space(): return lax.ppermute(x, 'space', pairs)]
    unnamed x47 -> x35, local copies, waits for them, and re-layouts: 14.8 us -> 6.62 us
    slice x4 -> x0, local copies, waits for them, and re-layouts: 6.18 us -> none  [the longest x2 4.36 us: on_device(): x[:, k * tall:(k + 1) * tall].reshape(-1, width)]
    concatenate x5 -> x0, other arithmetic: 5.26 us -> none  [the longest x4 3.75 us: on_device(): jnp.concatenate([x[:, k * tall:(k + 1) * tall].reshape(-1, width) for x i...]
    reshape x6 -> x0, local copies, waits for them, and re-layouts: 4.97 us -> none  [the longest x2 4.26 us: on_device(): state = jnp.concatenate([c.reshape(rows, tall, ny) for c in chunks], axis=1)]
    ppermute x8, starting transfers between devices: 9.23 us -> 6.33 us  [swap_cores(): return lax.ppermute(x, 'mode', [(i, i ^ 1) for i in range(n)])]
    ppermute x4, starting transfers between devices: 3 us -> 0.91 us  [from_chip(): lax.ppermute(x, 'mode', [((i + CORES * offset) % n, i) for i in range(n)])]
  transfers between devices with their start and end apart: 16 -> 16, of which waited for: 5 -> 8; matrix products, arithmetic and copies ran while one was open for 12% -> 4% of each run, Pallas kernels for 11% -> 14%
where the time goes in v2:
time: 101 us; the launch traced here: 99.4 us
  waiting for transfers between devices  50 us (50%)
  Pallas kernels  20.5 us (20%)
  starting transfers between devices  17.6 us (17%)
  local copies, waits for them, and re-layouts  8.56 us (8%)
  matrix products  1.83 us (2%)
    ppermute x4, waiting for transfers between devices, from_chip(): lax.ppermute(x, 'mode', [((i + CORES * offset) % n, i) for i in range(n)])  30.6 us
    ppermute x4, waiting for transfers between devices, from_space(): return lax.ppermute(x, 'space', pairs)  19.4 us
    pallas_call x4, Pallas kernels, step(): pl.pallas_call(lambda *refs: step_kernel(e, p, n, width, ny, nx, last, ed...  18.4 us
    ppermute x4, starting transfers between devices, from_space(): return lax.ppermute(x, 'space', pairs)  10.4 us
    unnamed x35, local copies, waits for them, and re-layouts  6.62 us
    ppermute x8, starting transfers between devices, swap_cores(): return lax.ppermute(x, 'mode', [(i, i ^ 1) for i in range(n)])  6.33 us
    pallas_call x1, Pallas kernels, flatten(): pl.pallas_call(lambda *refs: flatten_kernel(e, p, nx, ny, *refs), out_sha...  2.05 us
  transfers between devices with their start and end apart: 16, of which 8 were waited for; matrix products, arithmetic and copies ran while one was open for 4% of the time, Pallas kernels for 14%

profile of v2, /device:TPU:13, one launch (start us, length us, event | category | flops | bytes accessed | tf_op | source)
XLA Modules:
  0.0 99.4 jit_solution(4699235093155262981)
XLA Ops:
  0.6 1.2 %copy-done.7 = bf16[512,8,128]{2,1,0:T(8,128)(2,1)S(1)} copy-done((bf16[512,8,128]{2,1,0:T(8,128)(2,1)S(1)}, bf16[512,8,128]{2,1,0:T(8,128)(2,1)}, u32[]{:S(2)}) %copy-start.7) | copy-done | bytes 1048600
  1.9 1.0 %copy-done.8 = bf16[256,8,128]{2,1,0:T(8,128)(2,1)S(1)} copy-done((bf16[256,8,128]{2,1,0:T(8,128)(2,1)S(1)}, bf16[256,8,128]{2,1,0:T(8,128)(2,1)}, u32[]{:S(2)}) %copy-start.8) | copy-done | bytes 524312
  2.9 2.1 %flatten.1 = (bf16[768,512]{1,0:T(8,128)(2,1)}, bf16[768,512]{1,0:T(8,128)(2,1)}, bf16[768,128]{1,0:T(8,128)(2,1)S(1)}, bf16[768,128]{1,0:T(8,128)(2,1)}) custom-call(bf16[2048,128]{1,0:T(8,128)(2,1)S(1)} %bitcast.31, bf16[4096,128]{1,0:T(8,128)(2,1)S(1)} %bitcast.30), custom_call_target="tpu_custom_call" | custom-call | bytes 3145728 | tf_op jit(solution)/shard_map/flatten/pallas_call | solution.py:63
  5.9 1.0 collective-permute-start.2
  6.8 1.8 %fusion.2 = bf16[4,128,128,16]{2,3,1,0:T(8,128)(2,1)S(1)} fusion(bf16[4,128,12,128]{3,1,0,2:T(8,128)(2,1)S(1)} %bitcast.37, s32[4,12]{1,0:T(4,128)} %param.16), kind=kOutput, calls=%fused_computation.3 | convolution fusion | flops 26215168 | bytes 3670208 | tf_op jit(solution)/shard_map/bsk,bisj->bikj/dot_general | solution.py:171
  9.3 15.1 %collective-permute-done.3.refs_3_ = bf16[768,512]{1,0:T(8,128)(2,1)} collective-permute-done((bf16[768,512]{1,0:T(8,128)(2,1)}, bf16[768,512]{1,0:T(8,128)(2,1)}, u32[]{:S(2)}, u32[]{:S(2)}) %collective-permute-start.3) | collective-permute-done | bytes 786464 | tf_op jit(solution)/shard_map/ppermute | solution.py:24
  24.4 1.5 %collective-permute-start.4 = (bf16[768,512]{1,0:T(8,128)(2,1)}, bf16[768,512]{1,0:T(8,128)(2,1)}, u32[]{:S(2)}, u32[]{:S(2)}) collective-permute-start(bf16[768,512]{1,0:T(8,128)(2,1)} %collective-permute-done.3.refs_3_), channel_id=1, source_target_pairs={{0,4},{4,0},{8,12},{12,8},{1,5},{5,1},{9,13},{13,9},{2,6},{6,2},{1... | collective-permute-start | bytes 2359304 | tf_op jit(solution)/shard_map/ppermute | solution.py:19
  26.4 3.2 %collective-permute-start.5 = (bf16[768,128]{1,0:T(8,128)(2,1)}, bf16[768,128]{1,0:T(8,128)(2,1)}, u32[]{:S(2)}, u32[]{:S(2)}) collective-permute-start(bf16[768,128]{1,0:T(8,128)(2,1)} %get-tuple-element.21), channel_id=1, source_target_pairs={{0,1},{1,2},{2,3},{4,5},{5,6},{6,7},{8,9},{9,10},{10,11},{12,13},{... | collective-permute-start | bytes 589832 | tf_op jit(solution)/shard_map/ppermute | solution.py:30
  31.7 3.2 %collective-permute-done.5.refs_5_ = bf16[768,128]{1,0:T(8,128)(2,1)} collective-permute-done((bf16[768,128]{1,0:T(8,128)(2,1)}, bf16[768,128]{1,0:T(8,128)(2,1)}, u32[]{:S(2)}, u32[]{:S(2)}) %collective-permute-start.5) | collective-permute-done | bytes 196640 | tf_op jit(solution)/shard_map/ppermute | solution.py:30
  34.9 1.2 %copy-done.1 = bf16[256,2048]{1,0:T(8,128)(2,1)S(1)} copy-done((bf16[256,2048]{1,0:T(8,128)(2,1)S(1)}, bf16[256,2048]{1,0:T(8,128)(2,1)}, u32[]{:S(2)}) %copy-start.1) | copy-done | bytes 1048600
  36.1 0.9 copy-done.3
  38.0 5.2 %step.4 = (bf16[768,512]{1,0:T(8,128)(2,1)S(1)}, bf16[768,128]{1,0:T(8,128)(2,1)S(1)}) custom-call(s32[4]{0:T(128)S(1)} %add_convert_fusion.refs_0_, bf16[768,512]{1,0:T(8,128)(2,1)} %get-tuple-element.18.refs_1_.refs_5_, bf16[768,512]{1,0:T(8,128)(2,1)} %collective-permute-done.2.refs_2_, bf16[768,512]{1,0:T(8,128)(2,1)} %collective-permute-done.3.refs_3_, ...), custom_call_target="tpu_custom_call" | custom-call | flops 1000 | bytes 1000 | tf_op jit(solution)/shard_map/step/pallas_call | solution.py:195
  43.2 2.2 %collective-permute-done.1.refs_3_ = bf16[768,512]{1,0:T(8,128)(2,1)} collective-permute-done((bf16[768,512]{1,0:T(8,128)(2,1)}, bf16[768,512]{1,0:T(8,128)(2,1)}, u32[]{:S(2)}, u32[]{:S(2)}) %collective-permute-start.1) | collective-permute-done | bytes 786464 | tf_op jit(solution)/shard_map/ppermute | solution.py:24
  46.4 1.9 %collective-permute-start.7 = (bf16[768,128]{1,0:T(8,128)(2,1)S(1)}, bf16[768,128]{1,0:T(8,128)(2,1)S(1)}, u32[]{:S(2)}, u32[]{:S(2)}) collective-permute-start(bf16[768,128]{1,0:T(8,128)(2,1)S(1)} %copy-done.10), channel_id=1, source_target_pairs={{1,0},{2,1},{3,2},{5,4},{6,5},{7,6},{9,8},{10,9},{11,10},{13,12},{... | collective-permute-start | bytes 589832 | tf_op jit(solution)/shard_map/ppermute | solution.py:30
  48.9 5.6 %collective-permute-done.7.refs_6_ = bf16[768,128]{1,0:T(8,128)(2,1)S(1)} collective-permute-done((bf16[768,128]{1,0:T(8,128)(2,1)S(1)}, bf16[768,128]{1,0:T(8,128)(2,1)S(1)}, u32[]{:S(2)}, u32[]{:S(2)}) %collective-permute-start.7) | collective-permute-done | bytes 196640 | tf_op jit(solution)/shard_map/ppermute | solution.py:30
  54.5 4.9 %step.5 = (bf16[768,512]{1,0:T(8,128)(2,1)S(1)}, bf16[768,128]{1,0:T(8,128)(2,1)S(1)}) custom-call(s32[4]{0:T(128)S(1)} %add_convert_fusion.refs_0_, bf16[768,512]{1,0:T(8,128)(2,1)} %get-tuple-element.17.refs_6_.refs_1_, bf16[768,512]{1,0:T(8,128)(2,1)} %collective-permute-done.refs_2_, bf16[768,512]{1,0:T(8,128)(2,1)} %collective-permute-done.1.refs_3_, ...), custom_call_target="tpu_custom_call" | custom-call | flops 1000 | bytes 1000 | tf_op jit(solution)/shard_map/step/pallas_call | solution.py:195
  59.4 5.9 %collective-permute-done.11.refs_3_ = bf16[768,512]{1,0:T(8,128)(2,1)S(1)} collective-permute-done((bf16[768,512]{1,0:T(8,128)(2,1)S(1)}, bf16[768,512]{1,0:T(8,128)(2,1)S(1)}, u32[]{:S(2)}, u32[]{:S(2)}) %collective-permute-start.11) | collective-permute-done | bytes 786464 | tf_op jit(solution)/shard_map/ppermute | solution.py:24
  66.4 3.2 %collective-permute-start.13 = (bf16[768,128]{1,0:T(8,128)(2,1)S(1)}, bf16[768,128]{1,0:T(8,128)(2,1)S(1)}, u32[]{:S(2)}, u32[]{:S(2)}) collective-permute-start(bf16[768,128]{1,0:T(8,128)(2,1)S(1)} %get-tuple-element.27), channel_id=1, source_target_pairs={{0,1},{1,2},{2,3},{4,5},{5,6},{6,7},{8,9},{9,10},{10,11},{12,13},{... | collective-permute-start | bytes 589832 | tf_op jit(solution)/shard_map/ppermute | solution.py:30
  70.2 4.3 %collective-permute-done.13.refs_5_ = bf16[768,128]{1,0:T(8,128)(2,1)S(1)} collective-permute-done((bf16[768,128]{1,0:T(8,128)(2,1)S(1)}, bf16[768,128]{1,0:T(8,128)(2,1)S(1)}, u32[]{:S(2)}, u32[]{:S(2)}) %collective-permute-start.13) | collective-permute-done | bytes 196640 | tf_op jit(solution)/shard_map/ppermute | solution.py:30
  74.5 3.5 %step.6.refs_15_ = bf16[768,512]{1,0:T(8,128)(2,1)S(1)} custom-call(s32[4]{0:T(128)S(1)} %add_convert_fusion.refs_0_, bf16[768,512]{1,0:T(8,128)(2,1)S(1)} %get-tuple-element.22.refs_1_.refs_5_, bf16[768,512]{1,0:T(8,128)(2,1)S(1)} %collective-permute-done.10.refs_2_, bf16[768,512]{1,0:T(8,128)(2,1)S(1)} %collective-permute-done.11.refs_3_, ...), custom_call_target="tpu_custom_call" | custom-call | flops 1000 | bytes 1000 | tf_op jit(solution)/shard_map/step/pallas_call | solution.py:195
  78.0 7.3 %collective-permute-done.9.refs_3_ = bf16[768,512]{1,0:T(8,128)(2,1)S(1)} collective-permute-done((bf16[768,512]{1,0:T(8,128)(2,1)S(1)}, bf16[768,512]{1,0:T(8,128)(2,1)S(1)}, u32[]{:S(2)}, u32[]{:S(2)}) %collective-permute-start.9) | collective-permute-done | bytes 786464 | tf_op jit(solution)/shard_map/ppermute | solution.py:24
  86.1 2.1 %collective-permute-start.15 = (bf16[768,128]{1,0:T(8,128)(2,1)S(1)}, bf16[768,128]{1,0:T(8,128)(2,1)S(1)}, u32[]{:S(2)}, u32[]{:S(2)}) collective-permute-start(bf16[768,128]{1,0:T(8,128)(2,1)S(1)} %get-tuple-element.29), channel_id=1, source_target_pairs={{1,0},{2,1},{3,2},{5,4},{6,5},{7,6},{9,8},{10,9},{11,10},{13,12},{... | collective-permute-start | bytes 589832 | tf_op jit(solution)/shard_map/ppermute | solution.py:30
  88.2 6.3 %collective-permute-done.15.refs_6_ = bf16[768,128]{1,0:T(8,128)(2,1)S(1)} collective-permute-done((bf16[768,128]{1,0:T(8,128)(2,1)S(1)}, bf16[768,128]{1,0:T(8,128)(2,1)S(1)}, u32[]{:S(2)}, u32[]{:S(2)}) %collective-permute-start.15) | collective-permute-done | bytes 196640 | tf_op jit(solution)/shard_map/ppermute | solution.py:30
  94.5 4.9 %step.7 = (bf16[2048,128]{1,0:T(8,128)(2,1)}, bf16[4096,128]{1,0:T(8,128)(2,1)}) custom-call(s32[4]{0:T(128)S(1)} %add_convert_fusion.refs_0_, bf16[768,512]{1,0:T(8,128)(2,1)S(1)} %get-tuple-element.25.refs_6_.refs_1_, bf16[768,512]{1,0:T(8,128)(2,1)S(1)} %collective-permute-done.8.refs_2_, bf16[768,512]{1,0:T(8,128)(2,1)S(1)} %collective-permute-done.9.refs_3_, ...), custom_call_target="tpu_custom_call" | custom-call | flops 1000 | bytes 1000 | tf_op jit(solution)/shard_map/step/pallas_call | solution.py:195
  (55 shorter events, 9.0 us)
Async XLA Ops:
  5.6 18.7 %collective-permute-start.3 = (bf16[768,512]{1,0:T(8,128)(2,1)}, bf16[768,512]{1,0:T(8,128)(2,1)}, u32[]{:S(2)}, u32[]{:S(2)}) collective-permute-start(bf16[768,512]{1,0:T(8,128)(2,1)} %get-tuple-element.18.refs_1_.refs_5_), channel_id=1, source_target_pairs={{8,0},{12,4},{0,8},{4,12},{9,1},{13,5},{1,9},{5,13},{10,2},{14,6},... | collective-permute-start | bytes 2359304 | tf_op jit(solution)/shard_map/ppermute | solution.py:24
  5.9 29.0 %collective-permute-start.2 = (bf16[768,512]{1,0:T(8,128)(2,1)}, bf16[768,512]{1,0:T(8,128)(2,1)}, u32[]{:S(2)}, u32[]{:S(2)}) collective-permute-start(bf16[768,512]{1,0:T(8,128)(2,1)} %get-tuple-element.18.refs_1_.refs_5_), channel_id=1, source_target_pairs={{0,4},{4,0},{8,12},{12,8},{1,5},{5,1},{9,13},{13,9},{2,6},{6,2},{1... | collective-permute-start | bytes 2359304 | tf_op jit(solution)/shard_map/ppermute | solution.py:19
  8.7 21.0 %copy-start.13 = (f32[512]{0:T(512)S(1)}, f32[512]{0:T(512)}, u32[]{:S(2)}) copy-start(f32[512]{0:T(512)} %param.19) | copy-start | bytes 6148
  8.7 21.1 %copy-start.14 = (f32[512]{0:T(512)S(1)}, f32[512]{0:T(512)}, u32[]{:S(2)}) copy-start(f32[512]{0:T(512)} %param.21) | copy-start | bytes 6148
  8.7 22.0 %copy-start.15 = (f32[256]{0:T(256)S(1)}, f32[256]{0:T(256)}, u32[]{:S(2)}) copy-start(f32[256]{0:T(256)} %param.18) | copy-start | bytes 3076
  8.7 22.1 %copy-start.16 = (f32[256]{0:T(256)S(1)}, f32[256]{0:T(256)}, u32[]{:S(2)}) copy-start(f32[256]{0:T(256)} %param.20) | copy-start | bytes 3076
  8.7 23.0 %copy-start.12 = (s32[8,128]{1,0:T(8,128)S(1)}, s32[8,128]{1,0:T(8,128)}, u32[]{:S(2)}) copy-start(s32[8,128]{1,0:T(8,128)} %param.17) | copy-start | bytes 12292
  8.7 26.2 %copy-start = (bf16[512,1024]{1,0:T(8,128)(2,1)S(1)}, bf16[512,1024]{1,0:T(8,128)(2,1)}, u32[]{:S(2)}) copy-start(bf16[512,1024]{1,0:T(8,128)(2,1)} %refs_8_.7) | copy-start | bytes 3145732
  24.4 10.5 %collective-permute-start.4 = (bf16[768,512]{1,0:T(8,128)(2,1)}, bf16[768,512]{1,0:T(8,128)(2,1)}, u32[]{:S(2)}, u32[]{:S(2)}) collective-permute-start(bf16[768,512]{1,0:T(8,128)(2,1)} %collective-permute-done.3.refs_3_), channel_id=1, source_target_pairs={{0,4},{4,0},{8,12},{12,8},{1,5},{5,1},{9,13},{13,9},{2,6},{6,2},{1... | collective-permute-start | bytes 2359304 | tf_op jit(solution)/shard_map/ppermute | solution.py:19
  25.9 19.5 %collective-permute-start.1 = (bf16[768,512]{1,0:T(8,128)(2,1)}, bf16[768,512]{1,0:T(8,128)(2,1)}, u32[]{:S(2)}, u32[]{:S(2)}) collective-permute-start(bf16[768,512]{1,0:T(8,128)(2,1)} %get-tuple-element.17.refs_6_.refs_1_), channel_id=1, source_target_pairs={{8,0},{12,4},{0,8},{4,12},{9,1},{13,5},{1,9},{5,13},{10,2},{14,6},... | collective-permute-start | bytes 2359304 | tf_op jit(solution)/shard_map/ppermute | solution.py:24
  26.1 28.4 %collective-permute-start = (bf16[768,512]{1,0:T(8,128)(2,1)}, bf16[768,512]{1,0:T(8,128)(2,1)}, u32[]{:S(2)}, u32[]{:S(2)}) collective-permute-start(bf16[768,512]{1,0:T(8,128)(2,1)} %get-tuple-element.17.refs_6_.refs_1_), channel_id=1, source_target_pairs={{0,4},{4,0},{8,12},{12,8},{1,5},{5,1},{9,13},{13,9},{2,6},{6,2},{1... | collective-permute-start | bytes 2359304 | tf_op jit(solution)/shard_map/ppermute | solution.py:19
  26.4 8.5 %collective-permute-start.5 = (bf16[768,128]{1,0:T(8,128)(2,1)}, bf16[768,128]{1,0:T(8,128)(2,1)}, u32[]{:S(2)}, u32[]{:S(2)}) collective-permute-start(bf16[768,128]{1,0:T(8,128)(2,1)} %get-tuple-element.21), channel_id=1, source_target_pairs={{0,1},{1,2},{2,3},{4,5},{5,6},{6,7},{8,9},{9,10},{10,11},{12,13},{... | collective-permute-start | bytes 589832 | tf_op jit(solution)/shard_map/ppermute | solution.py:30
  45.4 9.1 %collective-permute-start.6 = (bf16[768,512]{1,0:T(8,128)(2,1)}, bf16[768,512]{1,0:T(8,128)(2,1)S(1)}, u32[]{:S(2)}, u32[]{:S(2)}) collective-permute-start(bf16[768,512]{1,0:T(8,128)(2,1)} %collective-permute-done.1.refs_3_), channel_id=1, source_target_pairs={{0,4},{4,0},{8,12},{12,8},{1,5},{5,1},{9,13},{13,9},{2,6},{6,2},{1... | collective-permute-start | bytes 2359304 | tf_op jit(solution)/shard_map/ppermute | solution.py:19
  46.2 19.2 %collective-permute-start.11 = (bf16[768,512]{1,0:T(8,128)(2,1)S(1)}, bf16[768,512]{1,0:T(8,128)(2,1)S(1)}, u32[]{:S(2)}, u32[]{:S(2)}) collective-permute-start(bf16[768,512]{1,0:T(8,128)(2,1)S(1)} %get-tuple-element.22.refs_1_.refs_5_), channel_id=1, source_target_pairs={{8,0},{12,4},{0,8},{4,12},{9,1},{13,5},{1,9},{5,13},{10,2},{14,6},... | collective-permute-start | bytes 2359304 | tf_op jit(solution)/shard_map/ppermute | solution.py:24
  46.4 8.1 %collective-permute-start.7 = (bf16[768,128]{1,0:T(8,128)(2,1)S(1)}, bf16[768,128]{1,0:T(8,128)(2,1)S(1)}, u32[]{:S(2)}, u32[]{:S(2)}) collective-permute-start(bf16[768,128]{1,0:T(8,128)(2,1)S(1)} %copy-done.10), channel_id=1, source_target_pairs={{1,0},{2,1},{3,2},{5,4},{6,5},{7,6},{9,8},{10,9},{11,10},{13,12},{... | collective-permute-start | bytes 589832 | tf_op jit(solution)/shard_map/ppermute | solution.py:30
  48.3 21.9 %collective-permute-start.10 = (bf16[768,512]{1,0:T(8,128)(2,1)S(1)}, bf16[768,512]{1,0:T(8,128)(2,1)S(1)}, u32[]{:S(2)}, u32[]{:S(2)}) collective-permute-start(bf16[768,512]{1,0:T(8,128)(2,1)S(1)} %get-tuple-element.22.refs_1_.refs_5_), channel_id=1, source_target_pairs={{0,4},{4,0},{8,12},{12,8},{1,5},{5,1},{9,13},{13,9},{2,6},{6,2},{1... | collective-permute-start | bytes 2359304 | tf_op jit(solution)/shard_map/ppermute | solution.py:19
  54.5 19.9 %copy-start.4 = (f32[512,1]{1,0:T(8,128)S(1)}, f32[512,1]{1,0:T(8,128)}, u32[]{:S(2)}) copy-start(f32[512,1]{1,0:T(8,128)} %copy.18.refs_14_) | copy-start | bytes 6148
  54.5 19.9 %copy-start.6 = (f32[256,1]{1,0:T(8,128)S(1)}, f32[256,1]{1,0:T(8,128)}, u32[]{:S(2)}) copy-start(f32[256,1]{1,0:T(8,128)} %copy.17.refs_13_) | copy-start | bytes 3076
  65.4 9.1 %collective-permute-start.12 = (bf16[768,512]{1,0:T(8,128)(2,1)S(1)}, bf16[768,512]{1,0:T(8,128)(2,1)S(1)}, u32[]{:S(2)}, u32[]{:S(2)}) collective-permute-start(bf16[768,512]{1,0:T(8,128)(2,1)S(1)} %collective-permute-done.11.refs_3_), channel_id=1, source_target_pairs={{0,4},{4,0},{8,12},{12,8},{1,5},{5,1},{9,13},{13,9},{2,6},{6,2},{1... | collective-permute-start | bytes 2359304 | tf_op jit(solution)/shard_map/ppermute | solution.py:19
  66.1 19.2 %collective-permute-start.9 = (bf16[768,512]{1,0:T(8,128)(2,1)S(1)}, bf16[768,512]{1,0:T(8,128)(2,1)S(1)}, u32[]{:S(2)}, u32[]{:S(2)}) collective-permute-start(bf16[768,512]{1,0:T(8,128)(2,1)S(1)} %get-tuple-element.25.refs_6_.refs_1_), channel_id=1, source_target_pairs={{8,0},{12,4},{0,8},{4,12},{9,1},{13,5},{1,9},{5,13},{10,2},{14,6},... | collective-permute-start | bytes 2359304 | tf_op jit(solution)/shard_map/ppermute | solution.py:24
  66.4 8.1 %collective-permute-start.13 = (bf16[768,128]{1,0:T(8,128)(2,1)S(1)}, bf16[768,128]{1,0:T(8,128)(2,1)S(1)}, u32[]{:S(2)}, u32[]{:S(2)}) collective-permute-start(bf16[768,128]{1,0:T(8,128)(2,1)S(1)} %get-tuple-element.27), channel_id=1, source_target_pairs={{0,1},{1,2},{2,3},{4,5},{5,6},{6,7},{8,9},{9,10},{10,11},{12,13},{... | collective-permute-start | bytes 589832 | tf_op jit(solution)/shard_map/ppermute | solution.py:30
  69.6 24.9 %collective-permute-start.8 = (bf16[768,512]{1,0:T(8,128)(2,1)S(1)}, bf16[768,512]{1,0:T(8,128)(2,1)S(1)}, u32[]{:S(2)}, u32[]{:S(2)}) collective-permute-start(bf16[768,512]{1,0:T(8,128)(2,1)S(1)} %get-tuple-element.25.refs_6_.refs_1_), channel_id=1, source_target_pairs={{0,4},{4,0},{8,12},{12,8},{1,5},{5,1},{9,13},{13,9},{2,6},{6,2},{1... | collective-permute-start | bytes 2359304 | tf_op jit(solution)/shard_map/ppermute | solution.py:19
  85.3 9.2 %collective-permute-start.14 = (bf16[768,512]{1,0:T(8,128)(2,1)S(1)}, bf16[768,512]{1,0:T(8,128)(2,1)S(1)}, u32[]{:S(2)}, u32[]{:S(2)}) collective-permute-start(bf16[768,512]{1,0:T(8,128)(2,1)S(1)} %collective-permute-done.9.refs_3_), channel_id=1, source_target_pairs={{0,4},{4,0},{8,12},{12,8},{1,5},{5,1},{9,13},{13,9},{2,6},{6,2},{1... | collective-permute-start | bytes 2359304 | tf_op jit(solution)/shard_map/ppermute | solution.py:19
  86.1 8.4 %collective-permute-start.15 = (bf16[768,128]{1,0:T(8,128)(2,1)S(1)}, bf16[768,128]{1,0:T(8,128)(2,1)S(1)}, u32[]{:S(2)}, u32[]{:S(2)}) collective-permute-start(bf16[768,128]{1,0:T(8,128)(2,1)S(1)} %get-tuple-element.29), channel_id=1, source_target_pairs={{1,0},{2,1},{3,2},{5,4},{6,5},{7,6},{9,8},{10,9},{11,10},{13,12},{... | collective-permute-start | bytes 589832 | tf_op jit(solution)/shard_map/ppermute | solution.py:30
  (9 other events, 34.9 us)

commit v3 on v1

v3 whole, which is shorter than its diff:
```python
import jax
import jax.numpy as jnp
from jax import lax
from jax.experimental import pallas as pl
from jax.experimental.pallas import tpu as pltpu
from jax.sharding import PartitionSpec as P

NM = 2048
BLK = 128
ITERS = 2
CORES = 2
CHUNKS = 2

VMEM = pl.BlockSpec(memory_space=pltpu.VMEM)
SMEM = pl.BlockSpec(memory_space=pltpu.SMEM)
COST = pl.CostEstimate(flops=1000, bytes_accessed=1000, transcendentals=0)


def swap_cores(x):
    n = lax.axis_size("mode")
    return lax.ppermute(x, "mode", [(i, i ^ 1) for i in range(n)])


def from_chip(x, offset):
    n = lax.axis_size("mode")
    return lax.ppermute(x, "mode", [((i + CORES * offset) % n, i) for i in range(n)])


def from_space(x, step):
    n = lax.axis_size("space")
    pairs = [(i, i - step) for i in range(n) if 0 <= i - step < n]
    return lax.ppermute(x, "space", pairs)


def after(x, *others):
    return lax.optimization_barrier((x, *others))[0]


def bf16(*shape):
    return jax.ShapeDtypeStruct(shape, jnp.bfloat16)


def call(kernel, out, scratch, operands, specs=None, megabytes=20, name="step"):
    return pl.pallas_call(
        kernel,
        out_shape=out,
        in_specs=specs or [VMEM] * len(operands),
        out_specs=(VMEM,) * len(out),
        scratch_shapes=scratch,
        compiler_params=pltpu.CompilerParams(vmem_limit_bytes=megabytes << 20),
        cost_estimate=COST,
        name=name,
    )(*operands)


def flatten_kernel(nx, ny, x_ref, *refs):
    outs, wide_ref = refs[:-1], refs[-1]
    count = x_ref.shape[0] // nx
    tall = nx // len(outs)
    tile = min(count, 64)

    @pl.loop(0, count // tile)
    def _(i):
        at = pl.multiple_of(i * tile, tile)
        wide_ref[0 : tile * nx, :] = x_ref[pl.ds(pl.multiple_of(at * nx, tile * nx), tile * nx), :].astype(jnp.float32)
        for r in range(nx):
            k, c = r // tall, r % tall
            row = wide_ref[pl.ds(r, tile, stride=nx), :].astype(jnp.bfloat16)
            outs[k][pl.ds(at, tile), c * ny : (c + 1) * ny] = row


def flatten_edges_kernel(nx, ny, x_ref, e_ref, *refs):
    *outs, first_ref, final_ref, wide_ref = refs
    flatten_kernel(nx, ny, x_ref, *outs, wide_ref)
    e = e_ref.shape[0]
    first_ref[0:e, :] = e_ref[:, 0:ny]
    first_ref[e:, :] = outs[0][:, 0:ny]
    final_ref[0:e, :] = e_ref[:, (nx - 1) * ny :]
    final_ref[e:, :] = outs[-1][:, outs[-1].shape[1] - ny :]


def step_kernel(n, e, p, width, ny, nx, cols, edge, last, *refs):
    refs = list(refs)

    def take(count):
        taken = refs[:count]
        del refs[:count]
        return taken

    (source_ref,) = take(1)
    e_refs, p_refs = take(n), take(n)
    (low_e_ref, low_p_ref, high_e_ref, high_p_ref), at_e, at_p = take(4), cols[0][0], cols[1][0]
    low_cols, high_cols, halo_low, halo_high = cols[2]
    (up_ref, emission_ref, absorption_ref, dense_ref, speed_ref, diffusion_ref, e_rate_ref, p_rate_ref) = take(8)
    if last:
        done_e, done_p = take(CHUNKS - 1), take(CHUNKS - 1)
        e_out_ref, p_out_ref, se_ref, sp_ref, wide_ref = refs
    elif edge is not None:
        e_out_ref, p_out_ref, edge_ref, se_ref, sp_ref = refs
    else:
        e_out_ref, p_out_ref, se_ref, sp_ref = refs
    for j in range(n):
        owner = source_ref[j]
        se_ref[pl.ds(pl.multiple_of(owner * e, e), e), :] = e_refs[j][:, cols[0][j] : cols[0][j] + width]
        sp_ref[pl.ds(pl.multiple_of(owner * p, p), p), :] = p_refs[j][:, cols[1][j] : cols[1][j] + width]
    tile = min(p, 256)

    def around(own_ref, low_ref, high_ref, rows, col, k):
        own = own_ref[rows, col : col + width].astype(jnp.float32)
        base = e if k else 0
        low_rows = pl.ds(rows.start + base, rows.size) if halo_low else rows
        high_rows = pl.ds(rows.start + base, rows.size) if halo_high else rows
        low = low_ref[low_rows, low_cols[k] : low_cols[k] + ny].astype(jnp.float32)
        high = high_ref[high_rows, high_cols[k] : high_cols[k] + ny].astype(jnp.float32)
        lower = jnp.concatenate([low, own[:, : width - ny]], axis=1) if width > ny else low
        higher = jnp.concatenate([own[:, ny:], high], axis=1) if width > ny else high
        return own, lower, higher

    def store(new, at, count, phonons):
        out_ref = p_out_ref if phonons else e_out_ref
        rows = pl.ds(at, count)
        if not last:
            new = new.astype(jnp.bfloat16)
            out_ref[rows, :] = new
            if edge is not None:
                edge_rows = pl.ds(at + e if phonons else at, count)
                edge_ref[edge_rows, :] = new[:, edge * ny : (edge + 1) * ny]
            return
        tall = width // ny
        for k, done in enumerate(done_p if phonons else done_e):
            old = done[rows, :].astype(jnp.float32)
            for r in range(tall):
                wide_ref[pl.ds(k * tall + r, count, stride=nx), :] = old[:, r * ny : (r + 1) * ny]
        for r in range(tall):
            wide_ref[pl.ds(nx - tall + r, count, stride=nx), :] = new[:, r * ny : (r + 1) * ny]
        start = at * nx if isinstance(at, int) else pl.multiple_of(at * nx, count * nx)
        out_ref[pl.ds(start, count * nx), :] = wide_ref[0 : count * nx, :].astype(jnp.bfloat16)

    own, lower, higher = around(e_refs[0], low_e_ref, high_e_ref, pl.ds(0, e), at_e, 0)
    gain = jnp.dot(absorption_ref[...], sp_ref[...], preferred_element_type=jnp.float32)
    f_up = jnp.where(up_ref[...] == 1, lower, higher)
    new = (own - speed_ref[...] * (own - f_up) + 0.5 * gain) / (1.0 + e_rate_ref[...])
    store(new, 0, e, False)

    for i in range(p // tile):
        at = i * tile
        source = jnp.dot(
            emission_ref[pl.ds(at, tile), :], se_ref[...], preferred_element_type=jnp.float32
        ) + jnp.dot(dense_ref[pl.ds(at, tile), :], sp_ref[...], preferred_element_type=jnp.float32)
        own, lower, higher = around(p_refs[0], low_p_ref, high_p_ref, pl.ds(at, tile), at_p, 1)
        column = lax.broadcasted_iota(jnp.int32, (tile, ny), 1)
        left, right = [], []
        for r in range(width // ny):
            row = own[:, r * ny : (r + 1) * ny]
            left.append(jnp.where(column == 0, 0.0, pltpu.roll(row, 1, 1)))
            right.append(jnp.where(column == ny - 1, 0.0, pltpu.roll(row, ny - 1, 1)))
        left, right = jnp.concatenate(left, axis=1), jnp.concatenate(right, axis=1)
        lap = lower + higher + left + right - 4.0 * own
        new = (own + diffusion_ref[pl.ds(at, tile), :] * lap + 0.5 * source) / (1.0 + p_rate_ref[pl.ds(at, tile), :])
        store(new, at, tile, True)


def on_device(
    electrons,
    phonons,
    emission,
    absorption,
    block_coupling,
    block_cols,
    upwind,
    speed,
    diffusion,
    electron_rate,
    phonon_rate,
):
    e, nx, ny = electrons.shape
    p = phonons.shape[0]
    n = lax.axis_size("mode")
    chips = n // CORES
    slots = block_coupling.shape[1]
    b_rows = p // BLK
    tall = nx // CHUNKS
    width = tall * ny
    lanes = pltpu.VMEM((64 * nx, ny), jnp.float32)

    (e_all,) = call(
        lambda *refs: flatten_kernel(nx, ny, *refs), (bf16(e, nx * ny),), [lanes],
        (electrons.reshape(e * nx, ny),), megabytes=4, name="flatten",
    )
    far_e = [from_chip(e_all, d) for d in range(1, chips)]
    *p_chunks, first, final = call(
        lambda *refs: flatten_edges_kernel(nx, ny, *refs), (bf16(p, width),) * CHUNKS + (bf16(e + p, ny),) * 2, [lanes],
        (phonons.reshape(p * nx, ny), e_all), megabytes=8, name="flatten",
    )
    block_coupling = after(block_coupling, p_chunks[0])
    kernel = block_coupling.reshape(b_rows, BLK, slots, BLK)
    block_ids = jnp.arange(NM // BLK, dtype=jnp.int32)
    hits = (block_cols[:, :, None] == block_ids[None, None, :]).astype(jnp.bfloat16)
    dense = jnp.einsum(
        "bsk,bisj->bikj", hits, kernel, preferred_element_type=jnp.float32
    ).astype(jnp.bfloat16).reshape(p, NM)

    me = lax.axis_index("mode").astype(jnp.uint32)
    chip, core = me // CORES, me % CORES
    sources = jnp.stack(
        [((chip + d) % chips) * CORES + (core ^ c) for d in range(chips) for c in range(CORES)]
    ).astype(jnp.int32)
    speed, diffusion = speed[:, None], diffusion[:, None]
    electron_rate, phonon_rate = electron_rate[:, None], phonon_rate[:, None]
    ups = [upwind[k * tall : (k + 1) * tall].reshape(1, width) for k in range(CHUNKS)]
    weights = (emission, absorption, dense, speed, diffusion, electron_rate, phonon_rate)

    def step(k, es, ps, low, high, done, want_edge):
        last = bool(done)
        edge = {0: 0, CHUNKS - 1: tall - 1}.get(k) if want_edge else None
        cols = (
            [c for _, c in es], [c for _, c in ps],
            ((low[0][1], low[1][1]), (high[0][1], high[1][1]), k == 0, k == CHUNKS - 1),
        )
        operands = (
            sources, *(x for x, _ in es), *(x for x, _ in ps), low[0][0], low[1][0], high[0][0], high[1][0],
            ups[k], *weights, *(d[0] for d in done), *(d[1] for d in done),
        )
        scratch = [pltpu.VMEM((n * e, width), jnp.bfloat16), pltpu.VMEM((n * p, width), jnp.bfloat16)]
        if last:
            out = (bf16(e * nx, ny), bf16(p * nx, ny))
            scratch.append(pltpu.VMEM((max(e, min(p, 256)) * nx, ny), jnp.float32))
        else:
            out = (bf16(e, width), bf16(p, width)) + ((bf16(e + p, ny),) if edge is not None else ())
        return call(
            lambda *refs: step_kernel(n, e, p, width, ny, nx, cols, edge, last, *refs), out, scratch, operands,
            specs=[SMEM] + [VMEM] * (len(operands) - 1),
        )

    def gathered(own, far, wait_for, col):
        arrays = [own, swap_cores(own)]
        for f in far:
            f = after(f, *wait_for)
            arrays += [f, swap_cores(f)]
        return [(x, col) for x in arrays]

    low, high = from_space(final, -1), from_space(first, 1)
    far_p = [[from_chip(c, d) for d in range(1, chips)] for c in p_chunks]
    everyone = [x for x, _ in gathered(e_all, far_e, (p_chunks[0],), 0)]
    new = []
    for k in range(CHUNKS):
        es = [(x, k * width) for x in everyone]
        ps = gathered(p_chunks[k], far_p[k], (new[-1][0],) if k else (dense, low, high), 0)
        before = ((e_all, k * width - ny), (p_chunks[k - 1], width - ny)) if k else ((low, 0), (low, 0))
        behind = ((e_all, (k + 1) * width), (p_chunks[k + 1], 0)) if k + 1 < CHUNKS else ((high, 0), (high, 0))
        new.append(step(k, es, ps, before, behind, [], True))
    first, final = new[0][2], new[-1][2]
    chunks = [(c[0], c[1]) for c in new]

    low, high = from_space(final, -1), from_space(first, 1)
    far = [[[from_chip(x, d) for d in range(1, chips)] for x in c] for c in chunks]
    done = []
    for k in range(CHUNKS):
        wait_for = (done[-1][0],) if k else (chunks[-1][0], low, high)
        es, ps = (gathered(chunks[k][i], far[k][i], wait_for, 0) for i in range(2))
        before = tuple((x, width - ny) for x in chunks[k - 1]) if k else ((low, 0), (low, 0))
        behind = tuple((x, 0) for x in chunks[k + 1]) if k + 1 < CHUNKS else ((high, 0), (high, 0))
        done.append(step(k, es, ps, before, behind, done if k + 1 == CHUNKS else [], False))
    return done[-1][0].reshape(e, nx, ny), done[-1][1].reshape(p, nx, ny)


def solution(mesh):
    placed = (
        P("mode", ("grp", "space"), None),
        P("mode", ("grp", "space"), None),
        P("mode", None),
        P("mode", None),
        P("mode", None, None),
        P("mode", None),
        P(("grp", "space"), None),
        P("mode"),
        P("mode"),
        P("mode"),
        P("mode"),
    )
    return jax.shard_map(
        on_device,
        mesh=mesh,
        in_specs=placed,
        out_specs=(P("mode", ("grp", "space"), None), P("mode", ("grp", "space"), None)),
        check_vma=False,
    )
```

time: 134 us -> 89.6 us (0.67)
  waiting for transfers between devices: 53.8 us -> 31.5 us
  local copies, waits for them, and re-layouts: 26.5 us -> 8.16 us
  other arithmetic: 6.41 us -> 0.08 us
  starting transfers between devices: 22.8 us -> 27 us
    ppermute x4 -> x7, waiting for transfers between devices: 49.3 us -> 24.8 us  [from_chip(): lax.ppermute(x, 'mode', [((i + CORES * offset) % n, i) for i in range(n)])]
    unnamed x47 -> x35, local copies, waits for them, and re-layouts: 14.8 us -> 7.6 us
    slice x4 -> x0, local copies, waits for them, and re-layouts: 6.18 us -> none  [the longest x2 4.36 us: on_device(): x[:, k * tall:(k + 1) * tall].reshape(-1, width)]
    concatenate x5 -> x0, other arithmetic: 5.26 us -> none  [the longest x4 3.75 us: on_device(): jnp.concatenate([x[:, k * tall:(k + 1) * tall].reshape(-1, width) for x i...]
    reshape x6 -> x0, local copies, waits for them, and re-layouts: 4.97 us -> none  [the longest x2 4.26 us: on_device(): state = jnp.concatenate([c.reshape(rows, tall, ny) for c in chunks], axis=1)]
    ppermute x8 -> x14, waiting for transfers between devices: 0.02 us -> 2.71 us  [swap_cores(): return lax.ppermute(x, 'mode', [(i, i ^ 1) for i in range(n)])]
    ppermute x8 -> x14, starting transfers between devices: 9.23 us -> 11.7 us  [swap_cores(): return lax.ppermute(x, 'mode', [(i, i ^ 1) for i in range(n)])]
    ppermute x4 -> x7, starting transfers between devices: 3 us -> 4.62 us  [from_chip(): lax.ppermute(x, 'mode', [((i + CORES * offset) % n, i) for i in range(n)])]
  transfers between devices with their start and end apart: 16 -> 25, of which waited for: 5 -> 12; matrix products, arithmetic and copies ran while one was open for 12% -> 3% of each run, Pallas kernels for 11% -> 14%
where the time goes in v3:
time: 89.6 us; the launch traced here: 88 us
  waiting for transfers between devices  31.5 us (35%)
  starting transfers between devices  27 us (30%)
  Pallas kernels  19.2 us (21%)
  local copies, waits for them, and re-layouts  8.16 us (9%)
  matrix products  1.15 us (1%)
  between operations  0.91 us (1%)
    ppermute x7, waiting for transfers between devices, from_chip(): lax.ppermute(x, 'mode', [((i + CORES * offset) % n, i) for i in range(n)])  24.8 us
    pallas_call x6, Pallas kernels, call(): pl.pallas_call(kernel, out_shape=out, in_specs=specs or [VMEM] * len(oper...  19.2 us
    ppermute x14, starting transfers between devices, swap_cores(): return lax.ppermute(x, 'mode', [(i, i ^ 1) for i in range(n)])  11.7 us
    ppermute x4, starting transfers between devices, from_space(): return lax.ppermute(x, 'space', pairs)  10.7 us
    unnamed x35, local copies, waits for them, and re-layouts  7.6 us
    ppermute x7, starting transfers between devices, from_chip(): lax.ppermute(x, 'mode', [((i + CORES * offset) % n, i) for i in range(n)])  4.62 us
    ppermute x4, waiting for transfers between devices, from_space(): return lax.ppermute(x, 'space', pairs)  3.95 us
    ppermute x14, waiting for transfers between devices, swap_cores(): return lax.ppermute(x, 'mode', [(i, i ^ 1) for i in range(n)])  2.71 us
  transfers between devices with their start and end apart: 25, of which 12 were waited for; matrix products, arithmetic and copies ran while one was open for 3% of the time, Pallas kernels for 14%

profile of v3, /device:TPU:13, one launch (start us, length us, event | category | flops | bytes accessed | tf_op | source)
XLA Modules:
  0.0 88.0 jit_solution(2972592238802533172)
XLA Ops:
  3.2 1.6 %flatten.3 = (bf16[512,512]{1,0:T(8,128)(2,1)}, bf16[512,512]{1,0:T(8,128)(2,1)}, bf16[768,128]{1,0:T(8,128)(2,1)S(1)}, bf16[768,128]{1,0:T(8,128)(2,1)S(1)}) custom-call(bf16[4096,128]{1,0:T(8,128)(2,1)S(1)} %bitcast.30, bf16[256,1024]{1,0:T(8,128)(2,1)S(1)} %flatten.2.refs_1_.refs_11_.refs_9_), custom_call_target="tpu_custom_call" | custom-call | flops 1000 | bytes 1000 | tf_op jit(solution)/shard_map/flatten/pallas_call | solution.py:44
  5.0 1.2 %collective-permute-start.1 = (bf16[256,1024]{1,0:T(8,128)(2,1)S(1)}, bf16[256,1024]{1,0:T(8,128)(2,1)}, u32[]{:S(2)}, u32[]{:S(2)}) collective-permute-start(bf16[256,1024]{1,0:T(8,128)(2,1)S(1)} %flatten.2.refs_1_.refs_11_.refs_9_), channel_id=1, source_target_pairs={{8,0},{12,4},{0,8},{4,12},{9,1},{13,5},{1,9},{5,13},{10,2},{14,6},... | collective-permute-start | bytes 1572872 | tf_op jit(solution)/shard_map/ppermute | solution.py:26
  6.3 1.2 %collective-permute-start.5 = (bf16[512,512]{1,0:T(8,128)(2,1)}, bf16[512,512]{1,0:T(8,128)(2,1)}, u32[]{:S(2)}, u32[]{:S(2)}) collective-permute-start(bf16[512,512]{1,0:T(8,128)(2,1)} %get-tuple-element.24.refs_5_.refs_10_), channel_id=1, source_target_pairs={{0,4},{4,0},{8,12},{12,8},{1,5},{5,1},{9,13},{13,9},{2,6},{6,2},{1... | collective-permute-start | bytes 1572872 | tf_op jit(solution)/shard_map/ppermute | solution.py:21
  7.5 3.2 %collective-permute-start.7 = (bf16[768,128]{1,0:T(8,128)(2,1)S(1)}, bf16[768,128]{1,0:T(8,128)(2,1)S(1)}, u32[]{:S(2)}, u32[]{:S(2)}) collective-permute-start(bf16[768,128]{1,0:T(8,128)(2,1)S(1)} %get-tuple-element.28), channel_id=1, source_target_pairs={{0,1},{1,2},{2,3},{4,5},{5,6},{6,7},{8,9},{9,10},{10,11},{12,13},{... | collective-permute-start | bytes 589832 | tf_op jit(solution)/shard_map/ppermute | solution.py:32
  10.7 2.1 %collective-permute-start.8 = (bf16[768,128]{1,0:T(8,128)(2,1)S(1)}, bf16[768,128]{1,0:T(8,128)(2,1)S(1)}, u32[]{:S(2)}, u32[]{:S(2)}) collective-permute-start(bf16[768,128]{1,0:T(8,128)(2,1)S(1)} %get-tuple-element.29), channel_id=1, source_target_pairs={{1,0},{2,1},{3,2},{5,4},{6,5},{7,6},{9,8},{10,9},{11,10},{13,12},{... | collective-permute-start | bytes 589832 | tf_op jit(solution)/shard_map/ppermute | solution.py:32
  14.6 1.4 %collective-permute-done.7.refs_9_.refs_10_ = bf16[768,128]{1,0:T(8,128)(2,1)S(1)} collective-permute-done((bf16[768,128]{1,0:T(8,128)(2,1)S(1)}, bf16[768,128]{1,0:T(8,128)(2,1)S(1)}, u32[]{:S(2)}, u32[]{:S(2)}) %collective-permute-start.7) | collective-permute-done | bytes 196640 | tf_op jit(solution)/shard_map/ppermute | solution.py:32
  17.4 1.5 %collective-permute-done.8.refs_11_.refs_12_ = bf16[768,128]{1,0:T(8,128)(2,1)S(1)} collective-permute-done((bf16[768,128]{1,0:T(8,128)(2,1)S(1)}, bf16[768,128]{1,0:T(8,128)(2,1)S(1)}, u32[]{:S(2)}, u32[]{:S(2)}) %collective-permute-start.8) | collective-permute-done | bytes 196640 | tf_op jit(solution)/shard_map/ppermute | solution.py:32
  20.6 8.5 %collective-permute-done.1.refs_3_ = bf16[256,1024]{1,0:T(8,128)(2,1)} collective-permute-done((bf16[256,1024]{1,0:T(8,128)(2,1)S(1)}, bf16[256,1024]{1,0:T(8,128)(2,1)}, u32[]{:S(2)}, u32[]{:S(2)}) %collective-permute-start.1) | collective-permute-done | bytes 524320 | tf_op jit(solution)/shard_map/ppermute | solution.py:26
  29.1 1.5 %collective-permute-start.2 = (bf16[256,1024]{1,0:T(8,128)(2,1)}, bf16[256,1024]{1,0:T(8,128)(2,1)}, u32[]{:S(2)}, u32[]{:S(2)}) collective-permute-start(bf16[256,1024]{1,0:T(8,128)(2,1)} %collective-permute-done.1.refs_3_), channel_id=1, source_target_pairs={{0,4},{4,0},{8,12},{12,8},{1,5},{5,1},{9,13},{13,9},{2,6},{6,2},{1... | collective-permute-start | bytes 1572872 | tf_op jit(solution)/shard_map/ppermute | solution.py:21
  32.6 1.2 %copy-done = bf16[512,1024]{1,0:T(8,128)(2,1)S(1)} copy-done((bf16[512,1024]{1,0:T(8,128)(2,1)S(1)}, bf16[512,1024]{1,0:T(8,128)(2,1)}, u32[]{:S(2)}) %copy-start) | copy-done | bytes 1048600
  33.8 1.2 %copy-done.2 = bf16[256,2048]{1,0:T(8,128)(2,1)S(1)} copy-done((bf16[256,2048]{1,0:T(8,128)(2,1)S(1)}, bf16[256,2048]{1,0:T(8,128)(2,1)}, u32[]{:S(2)}) %copy-start.2) | copy-done | bytes 1048600
  35.9 5.0 %step.4 = (bf16[256,512]{1,0:T(8,128)(2,1)S(1)}, bf16[512,512]{1,0:T(8,128)(2,1)S(1)}, bf16[768,128]{1,0:T(8,128)(2,1)S(1)}) custom-call(s32[4]{0:T(128)S(1)} %add_convert_fusion.refs_0_, bf16[256,1024]{1,0:T(8,128)(2,1)S(1)} %flatten.2.refs_1_.refs_11_.refs_9_, bf16[256,1024]{1,0:T(8,128)(2,1)} %collective-permute-done.refs_2_, ...), custom_call_target="tpu_custom_call" | custom-call | flops 1000 | bytes 1000 | tf_op jit(solution)/shard_map/step/pallas_call | solution.py:44
  40.9 3.6 %collective-permute-done.4.refs_7_ = bf16[512,512]{1,0:T(8,128)(2,1)} collective-permute-done((bf16[512,512]{1,0:T(8,128)(2,1)}, bf16[512,512]{1,0:T(8,128)(2,1)}, u32[]{:S(2)}, u32[]{:S(2)}) %collective-permute-start.4) | collective-permute-done | bytes 524320 | tf_op jit(solution)/shard_map/ppermute | solution.py:26
  45.6 1.9 %collective-permute-start.16 = (bf16[768,128]{1,0:T(8,128)(2,1)S(1)}, bf16[768,128]{1,0:T(8,128)(2,1)S(1)}, u32[]{:S(2)}, u32[]{:S(2)}) collective-permute-start(bf16[768,128]{1,0:T(8,128)(2,1)S(1)} %get-tuple-element.35), channel_id=1, source_target_pairs={{1,0},{2,1},{3,2},{5,4},{6,5},{7,6},{9,8},{10,9},{11,10},{13,12},{... | collective-permute-start | bytes 589832 | tf_op jit(solution)/shard_map/ppermute | solution.py:32
  47.5 4.5 %step.5 = (bf16[256,512]{1,0:T(8,128)(2,1)S(1)}, bf16[512,512]{1,0:T(8,128)(2,1)S(1)}, bf16[768,128]{1,0:T(8,128)(2,1)S(1)}) custom-call(s32[4]{0:T(128)S(1)} %add_convert_fusion.refs_0_, bf16[256,1024]{1,0:T(8,128)(2,1)S(1)} %flatten.2.refs_1_.refs_11_.refs_9_, bf16[256,1024]{1,0:T(8,128)(2,1)} %collective-permute-done.refs_2_, ...), custom_call_target="tpu_custom_call" | custom-call | flops 1000 | bytes 1000 | tf_op jit(solution)/shard_map/step/pallas_call | solution.py:44
  52.0 3.5 %collective-permute-start.15 = (bf16[768,128]{1,0:T(8,128)(2,1)S(1)}, bf16[768,128]{1,0:T(8,128)(2,1)S(1)}, u32[]{:S(2)}, u32[]{:S(2)}) collective-permute-start(bf16[768,128]{1,0:T(8,128)(2,1)S(1)} %get-tuple-element.34), channel_id=1, source_target_pairs={{0,1},{1,2},{2,3},{4,5},{5,6},{6,7},{8,9},{9,10},{10,11},{12,13},{... | collective-permute-start | bytes 589832 | tf_op jit(solution)/shard_map/ppermute | solution.py:32
  55.6 1.3 %collective-permute-start.14 = (bf16[256,512]{1,0:T(8,128)(2,1)S(1)}, bf16[256,512]{1,0:T(8,128)(2,1)S(1)}, u32[]{:S(2)}, u32[]{:S(2)}) collective-permute-start(bf16[256,512]{1,0:T(8,128)(2,1)S(1)} %get-tuple-element.31.refs_1_.refs_9_), channel_id=1, source_target_pairs={{8,0},{12,4},{0,8},{4,12},{9,1},{13,5},{1,9},{5,13},{10,2},{14,6},... | collective-permute-start | bytes 786440 | tf_op jit(solution)/shard_map/ppermute | solution.py:26
  59.9 1.3 %collective-permute-start.20 = (bf16[512,512]{1,0:T(8,128)(2,1)S(1)}, bf16[512,512]{1,0:T(8,128)(2,1)S(1)}, u32[]{:S(2)}, u32[]{:S(2)}) collective-permute-start(bf16[512,512]{1,0:T(8,128)(2,1)S(1)} %collective-permute-done.19.refs_7_), channel_id=1, source_target_pairs={{0,4},{4,0},{8,12},{12,8},{1,5},{5,1},{9,13},{13,9},{2,6},{6,2},{1... | collective-permute-start | bytes 1572872 | tf_op jit(solution)/shard_map/ppermute | solution.py:21
  61.2 1.4 %collective-permute-start.23 = (bf16[512,512]{1,0:T(8,128)(2,1)S(1)}, bf16[512,512]{1,0:T(8,128)(2,1)S(1)}, u32[]{:S(2)}, u32[]{:S(2)}) collective-permute-start(bf16[512,512]{1,0:T(8,128)(2,1)S(1)} %get-tuple-element.39.refs_12_.refs_5_), channel_id=1, source_target_pairs={{8,0},{12,4},{0,8},{4,12},{9,1},{13,5},{1,9},{5,13},{10,2},{14,6},... | collective-permute-start | bytes 1572872 | tf_op jit(solution)/shard_map/ppermute | solution.py:26
  62.9 1.6 %collective-permute-done.14.refs_3_ = bf16[256,512]{1,0:T(8,128)(2,1)S(1)} collective-permute-done((bf16[256,512]{1,0:T(8,128)(2,1)S(1)}, bf16[256,512]{1,0:T(8,128)(2,1)S(1)}, u32[]{:S(2)}, u32[]{:S(2)}) %collective-permute-start.14) | collective-permute-done | bytes 262176 | tf_op jit(solution)/shard_map/ppermute | solution.py:26
  66.8 3.2 %step.6 = (bf16[256,512]{1,0:T(8,128)(2,1)S(1)}, bf16[512,512]{1,0:T(8,128)(2,1)S(1)}) custom-call(s32[4]{0:T(128)S(1)} %add_convert_fusion.refs_0_, bf16[256,512]{1,0:T(8,128)(2,1)S(1)} %get-tuple-element.31.refs_1_.refs_9_, bf16[256,512]{1,0:T(8,128)(2,1)S(1)} %collective-permute-done.13.refs_2_, bf16[256,512]{1,0:T(8,128)(2,1)S(1)} %collective-permute-done.14.refs_3_, ...), custom_call_target="tpu_custom_call" | custom-call | flops 1000 | bytes 1000 | tf_op jit(solution)/shard_map/step/pallas_call | solution.py:44
  70.0 5.7 %collective-permute-done.23.refs_7_ = bf16[512,512]{1,0:T(8,128)(2,1)S(1)} collective-permute-done((bf16[512,512]{1,0:T(8,128)(2,1)S(1)}, bf16[512,512]{1,0:T(8,128)(2,1)S(1)}, u32[]{:S(2)}, u32[]{:S(2)}) %collective-permute-start.23) | collective-permute-done | bytes 524320 | tf_op jit(solution)/shard_map/ppermute | solution.py:26
  76.9 4.4 %collective-permute-done.12.refs_3_ = bf16[256,512]{1,0:T(8,128)(2,1)S(1)} collective-permute-done((bf16[256,512]{1,0:T(8,128)(2,1)S(1)}, bf16[256,512]{1,0:T(8,128)(2,1)S(1)}, u32[]{:S(2)}, u32[]{:S(2)}) %collective-permute-start.12) | collective-permute-done | bytes 262176 | tf_op jit(solution)/shard_map/ppermute | solution.py:26
  83.3 4.7 %step.7 = (bf16[2048,128]{1,0:T(8,128)(2,1)}, bf16[4096,128]{1,0:T(8,128)(2,1)}) custom-call(s32[4]{0:T(128)S(1)} %add_convert_fusion.refs_0_, bf16[256,512]{1,0:T(8,128)(2,1)S(1)} %get-tuple-element.33.refs_11_.refs_1_, bf16[256,512]{1,0:T(8,128)(2,1)S(1)} %collective-permute-done.11.refs_2_, bf16[256,512]{1,0:T(8,128)(2,1)S(1)} %collective-permute-done.12.refs_3_, ...), custom_call_target="tpu_custom_call" | custom-call | flops 1000 | bytes 1000 | tf_op jit(solution)/shard_map/step/pallas_call | solution.py:44
  (74 shorter events, 20.1 us)
Async XLA Ops:
  4.8 14.8 %collective-permute-start.6 = (bf16[512,512]{1,0:T(8,128)(2,1)}, bf16[512,512]{1,0:T(8,128)(2,1)}, u32[]{:S(2)}, u32[]{:S(2)}) collective-permute-start(bf16[512,512]{1,0:T(8,128)(2,1)} %get-tuple-element.24.refs_5_.refs_10_), channel_id=1, source_target_pairs={{8,0},{12,4},{0,8},{4,12},{9,1},{13,5},{1,9},{5,13},{10,2},{14,6},... | collective-permute-start | bytes 1572872 | tf_op jit(solution)/shard_map/ppermute | solution.py:26
  5.0 24.1 %collective-permute-start.1 = (bf16[256,1024]{1,0:T(8,128)(2,1)S(1)}, bf16[256,1024]{1,0:T(8,128)(2,1)}, u32[]{:S(2)}, u32[]{:S(2)}) collective-permute-start(bf16[256,1024]{1,0:T(8,128)(2,1)S(1)} %flatten.2.refs_1_.refs_11_.refs_9_), channel_id=1, source_target_pairs={{8,0},{12,4},{0,8},{4,12},{9,1},{13,5},{1,9},{5,13},{10,2},{14,6},... | collective-permute-start | bytes 1572872 | tf_op jit(solution)/shard_map/ppermute | solution.py:26
  6.3 25.4 %collective-permute-start.5 = (bf16[512,512]{1,0:T(8,128)(2,1)}, bf16[512,512]{1,0:T(8,128)(2,1)}, u32[]{:S(2)}, u32[]{:S(2)}) collective-permute-start(bf16[512,512]{1,0:T(8,128)(2,1)} %get-tuple-element.24.refs_5_.refs_10_), channel_id=1, source_target_pairs={{0,4},{4,0},{8,12},{12,8},{1,5},{5,1},{9,13},{13,9},{2,6},{6,2},{1... | collective-permute-start | bytes 1572872 | tf_op jit(solution)/shard_map/ppermute | solution.py:21
  7.5 8.5 %collective-permute-start.7 = (bf16[768,128]{1,0:T(8,128)(2,1)S(1)}, bf16[768,128]{1,0:T(8,128)(2,1)S(1)}, u32[]{:S(2)}, u32[]{:S(2)}) collective-permute-start(bf16[768,128]{1,0:T(8,128)(2,1)S(1)} %get-tuple-element.28), channel_id=1, source_target_pairs={{0,1},{1,2},{2,3},{4,5},{5,6},{6,7},{8,9},{9,10},{10,11},{12,13},{... | collective-permute-start | bytes 589832 | tf_op jit(solution)/shard_map/ppermute | solution.py:32
  10.7 8.2 %collective-permute-start.8 = (bf16[768,128]{1,0:T(8,128)(2,1)S(1)}, bf16[768,128]{1,0:T(8,128)(2,1)S(1)}, u32[]{:S(2)}, u32[]{:S(2)}) collective-permute-start(bf16[768,128]{1,0:T(8,128)(2,1)S(1)} %get-tuple-element.29), channel_id=1, source_target_pairs={{1,0},{2,1},{3,2},{5,4},{6,5},{7,6},{9,8},{10,9},{11,10},{13,12},{... | collective-permute-start | bytes 589832 | tf_op jit(solution)/shard_map/ppermute | solution.py:32
  16.7 15.3 %collective-permute-start = (bf16[256,1024]{1,0:T(8,128)(2,1)S(1)}, bf16[256,1024]{1,0:T(8,128)(2,1)}, u32[]{:S(2)}, u32[]{:S(2)}) collective-permute-start(bf16[256,1024]{1,0:T(8,128)(2,1)S(1)} %flatten.2.refs_1_.refs_11_.refs_9_), channel_id=1, source_target_pairs={{0,4},{4,0},{8,12},{12,8},{1,5},{5,1},{9,13},{13,9},{2,6},{6,2},{1... | collective-permute-start | bytes 1572872 | tf_op jit(solution)/shard_map/ppermute | solution.py:21
  19.6 12.4 %collective-permute-start.9 = (bf16[512,512]{1,0:T(8,128)(2,1)}, bf16[512,512]{1,0:T(8,128)(2,1)}, u32[]{:S(2)}, u32[]{:S(2)}) collective-permute-start(bf16[512,512]{1,0:T(8,128)(2,1)} %collective-permute-done.6.refs_7_), channel_id=1, source_target_pairs={{0,4},{4,0},{8,12},{12,8},{1,5},{5,1},{9,13},{13,9},{2,6},{6,2},{1... | collective-permute-start | bytes 1572872 | tf_op jit(solution)/shard_map/ppermute | solution.py:21
  29.1 3.4 %collective-permute-start.2 = (bf16[256,1024]{1,0:T(8,128)(2,1)}, bf16[256,1024]{1,0:T(8,128)(2,1)}, u32[]{:S(2)}, u32[]{:S(2)}) collective-permute-start(bf16[256,1024]{1,0:T(8,128)(2,1)} %collective-permute-done.1.refs_3_), channel_id=1, source_target_pairs={{0,4},{4,0},{8,12},{12,8},{1,5},{5,1},{9,13},{13,9},{2,6},{6,2},{1... | collective-permute-start | bytes 1572872 | tf_op jit(solution)/shard_map/ppermute | solution.py:21
  30.7 13.9 %collective-permute-start.4 = (bf16[512,512]{1,0:T(8,128)(2,1)}, bf16[512,512]{1,0:T(8,128)(2,1)}, u32[]{:S(2)}, u32[]{:S(2)}) collective-permute-start(bf16[512,512]{1,0:T(8,128)(2,1)} %get-tuple-element.26.refs_12_.refs_5_), channel_id=1, source_target_pairs={{8,0},{12,4},{0,8},{4,12},{9,1},{13,5},{1,9},{5,13},{10,2},{14,6},... | collective-permute-start | bytes 1572872 | tf_op jit(solution)/shard_map/ppermute | solution.py:26
  31.6 15.9 %collective-permute-start.3 = (bf16[512,512]{1,0:T(8,128)(2,1)}, bf16[512,512]{1,0:T(8,128)(2,1)S(1)}, u32[]{:S(2)}, u32[]{:S(2)}) collective-permute-start(bf16[512,512]{1,0:T(8,128)(2,1)} %get-tuple-element.26.refs_12_.refs_5_), channel_id=1, source_target_pairs={{0,4},{4,0},{8,12},{12,8},{1,5},{5,1},{9,13},{13,9},{2,6},{6,2},{1... | collective-permute-start | bytes 1572872 | tf_op jit(solution)/shard_map/ppermute | solution.py:21
  44.6 2.9 %collective-permute-start.10 = (bf16[512,512]{1,0:T(8,128)(2,1)}, bf16[512,512]{1,0:T(8,128)(2,1)S(1)}, u32[]{:S(2)}, u32[]{:S(2)}) collective-permute-start(bf16[512,512]{1,0:T(8,128)(2,1)} %collective-permute-done.4.refs_7_), channel_id=1, source_target_pairs={{0,4},{4,0},{8,12},{12,8},{1,5},{5,1},{9,13},{13,9},{2,6},{6,2},{1... | collective-permute-start | bytes 1572872 | tf_op jit(solution)/shard_map/ppermute | solution.py:21
  45.3 13.6 %collective-permute-start.19 = (bf16[512,512]{1,0:T(8,128)(2,1)S(1)}, bf16[512,512]{1,0:T(8,128)(2,1)S(1)}, u32[]{:S(2)}, u32[]{:S(2)}) collective-permute-start(bf16[512,512]{1,0:T(8,128)(2,1)S(1)} %get-tuple-element.37.refs_5_.refs_10_), channel_id=1, source_target_pairs={{8,0},{12,4},{0,8},{4,12},{9,1},{13,5},{1,9},{5,13},{10,2},{14,6},... | collective-permute-start | bytes 1572872 | tf_op jit(solution)/shard_map/ppermute | solution.py:26
  45.6 12.4 %collective-permute-start.16 = (bf16[768,128]{1,0:T(8,128)(2,1)S(1)}, bf16[768,128]{1,0:T(8,128)(2,1)S(1)}, u32[]{:S(2)}, u32[]{:S(2)}) collective-permute-start(bf16[768,128]{1,0:T(8,128)(2,1)S(1)} %get-tuple-element.35), channel_id=1, source_target_pairs={{1,0},{2,1},{3,2},{5,4},{6,5},{7,6},{9,8},{10,9},{11,10},{13,12},{... | collective-permute-start | bytes 589832 | tf_op jit(solution)/shard_map/ppermute | solution.py:32
  52.0 7.9 %collective-permute-start.15 = (bf16[768,128]{1,0:T(8,128)(2,1)S(1)}, bf16[768,128]{1,0:T(8,128)(2,1)S(1)}, u32[]{:S(2)}, u32[]{:S(2)}) collective-permute-start(bf16[768,128]{1,0:T(8,128)(2,1)S(1)} %get-tuple-element.34), channel_id=1, source_target_pairs={{0,1},{1,2},{2,3},{4,5},{5,6},{6,7},{8,9},{9,10},{10,11},{12,13},{... | collective-permute-start | bytes 589832 | tf_op jit(solution)/shard_map/ppermute | solution.py:32
  55.6 8.9 %collective-permute-start.14 = (bf16[256,512]{1,0:T(8,128)(2,1)S(1)}, bf16[256,512]{1,0:T(8,128)(2,1)S(1)}, u32[]{:S(2)}, u32[]{:S(2)}) collective-permute-start(bf16[256,512]{1,0:T(8,128)(2,1)S(1)} %get-tuple-element.31.refs_1_.refs_9_), channel_id=1, source_target_pairs={{8,0},{12,4},{0,8},{4,12},{9,1},{13,5},{1,9},{5,13},{10,2},{14,6},... | collective-permute-start | bytes 786440 | tf_op jit(solution)/shard_map/ppermute | solution.py:26
  56.9 8.8 %collective-permute-start.18 = (bf16[512,512]{1,0:T(8,128)(2,1)S(1)}, bf16[512,512]{1,0:T(8,128)(2,1)S(1)}, u32[]{:S(2)}, u32[]{:S(2)}) collective-permute-start(bf16[512,512]{1,0:T(8,128)(2,1)S(1)} %get-tuple-element.37.refs_5_.refs_10_), channel_id=1, source_target_pairs={{0,4},{4,0},{8,12},{12,8},{1,5},{5,1},{9,13},{13,9},{2,6},{6,2},{1... | collective-permute-start | bytes 1572872 | tf_op jit(solution)/shard_map/ppermute | solution.py:21
  59.9 6.9 %collective-permute-start.20 = (bf16[512,512]{1,0:T(8,128)(2,1)S(1)}, bf16[512,512]{1,0:T(8,128)(2,1)S(1)}, u32[]{:S(2)}, u32[]{:S(2)}) collective-permute-start(bf16[512,512]{1,0:T(8,128)(2,1)S(1)} %collective-permute-done.19.refs_7_), channel_id=1, source_target_pairs={{0,4},{4,0},{8,12},{12,8},{1,5},{5,1},{9,13},{13,9},{2,6},{6,2},{1... | collective-permute-start | bytes 1572872 | tf_op jit(solution)/shard_map/ppermute | solution.py:21
  61.2 14.5 %collective-permute-start.23 = (bf16[512,512]{1,0:T(8,128)(2,1)S(1)}, bf16[512,512]{1,0:T(8,128)(2,1)S(1)}, u32[]{:S(2)}, u32[]{:S(2)}) collective-permute-start(bf16[512,512]{1,0:T(8,128)(2,1)S(1)} %get-tuple-element.39.refs_12_.refs_5_), channel_id=1, source_target_pairs={{8,0},{12,4},{0,8},{4,12},{9,1},{13,5},{1,9},{5,13},{10,2},{14,6},... | collective-permute-start | bytes 1572872 | tf_op jit(solution)/shard_map/ppermute | solution.py:26
  62.6 3.0 %collective-permute-start.13 = (bf16[256,512]{1,0:T(8,128)(2,1)S(1)}, bf16[256,512]{1,0:T(8,128)(2,1)S(1)}, u32[]{:S(2)}, u32[]{:S(2)}) collective-permute-start(bf16[256,512]{1,0:T(8,128)(2,1)S(1)} %get-tuple-element.31.refs_1_.refs_9_), channel_id=1, source_target_pairs={{0,4},{4,0},{8,12},{12,8},{1,5},{5,1},{9,13},{13,9},{2,6},{6,2},{1... | collective-permute-start | bytes 786440 | tf_op jit(solution)/shard_map/ppermute | solution.py:21
  64.5 2.3 %collective-permute-start.17 = (bf16[256,512]{1,0:T(8,128)(2,1)S(1)}, bf16[256,512]{1,0:T(8,128)(2,1)S(1)}, u32[]{:S(2)}, u32[]{:S(2)}) collective-permute-start(bf16[256,512]{1,0:T(8,128)(2,1)S(1)} %collective-permute-done.14.refs_3_), channel_id=1, source_target_pairs={{0,4},{4,0},{8,12},{12,8},{1,5},{5,1},{9,13},{13,9},{2,6},{6,2},{1... | collective-permute-start | bytes 786440 | tf_op jit(solution)/shard_map/ppermute | solution.py:21
  65.7 15.7 %collective-permute-start.12 = (bf16[256,512]{1,0:T(8,128)(2,1)S(1)}, bf16[256,512]{1,0:T(8,128)(2,1)S(1)}, u32[]{:S(2)}, u32[]{:S(2)}) collective-permute-start(bf16[256,512]{1,0:T(8,128)(2,1)S(1)} %get-tuple-element.33.refs_11_.refs_1_), channel_id=1, source_target_pairs={{8,0},{12,4},{0,8},{4,12},{9,1},{13,5},{1,9},{5,13},{10,2},{14,6},... | collective-permute-start | bytes 786440 | tf_op jit(solution)/shard_map/ppermute | solution.py:26
  65.7 16.5 %collective-permute-start.22 = (bf16[512,512]{1,0:T(8,128)(2,1)S(1)}, bf16[512,512]{1,0:T(8,128)(2,1)S(1)}, u32[]{:S(2)}, u32[]{:S(2)}) collective-permute-start(bf16[512,512]{1,0:T(8,128)(2,1)S(1)} %get-tuple-element.39.refs_12_.refs_5_), channel_id=1, source_target_pairs={{0,4},{4,0},{8,12},{12,8},{1,5},{5,1},{9,13},{13,9},{2,6},{6,2},{1... | collective-permute-start | bytes 1572872 | tf_op jit(solution)/shard_map/ppermute | solution.py:21
  75.7 7.6 %collective-permute-start.24 = (bf16[512,512]{1,0:T(8,128)(2,1)S(1)}, bf16[512,512]{1,0:T(8,128)(2,1)S(1)}, u32[]{:S(2)}, u32[]{:S(2)}) collective-permute-start(bf16[512,512]{1,0:T(8,128)(2,1)S(1)} %collective-permute-done.23.refs_7_), channel_id=1, source_target_pairs={{0,4},{4,0},{8,12},{12,8},{1,5},{5,1},{9,13},{13,9},{2,6},{6,2},{1... | collective-permute-start | bytes 1572872 | tf_op jit(solution)/shard_map/ppermute | solution.py:21
  76.9 5.2 %collective-permute-start.11 = (bf16[256,512]{1,0:T(8,128)(2,1)S(1)}, bf16[256,512]{1,0:T(8,128)(2,1)S(1)}, u32[]{:S(2)}, u32[]{:S(2)}) collective-permute-start(bf16[256,512]{1,0:T(8,128)(2,1)S(1)} %get-tuple-element.33.refs_11_.refs_1_), channel_id=1, source_target_pairs={{0,4},{4,0},{8,12},{12,8},{1,5},{5,1},{9,13},{13,9},{2,6},{6,2},{1... | collective-permute-start | bytes 786440 | tf_op jit(solution)/shard_map/ppermute | solution.py:21
  (18 other events, 150.7 us)

commit v4 on v3

--- a/solution.py
+++ b/solution.py
@@ -30,6 +30,11 @@
     n = lax.axis_size("space")
     pairs = [(i, i - step) for i in range(n) if 0 <= i - step < n]
     return lax.ppermute(x, "space", pairs)
+
+
+def from_ring(x, axis, offset):
+    n = lax.axis_size(axis)
+    return lax.ppermute(x, axis, [((i + offset) % n, i) for i in range(n)])
 
 
 def after(x, *others):
@@ -53,8 +58,7 @@
     )(*operands)
 
 
-def flatten_kernel(nx, ny, x_ref, *refs):
-    outs, wide_ref = refs[:-1], refs[-1]
+def flatten_one(nx, ny, x_ref, outs, wide_ref):
     count = x_ref.shape[0] // nx
     tall = nx // len(outs)
     tile = min(count, 64)
@@ -69,14 +73,49 @@
             outs[k][pl.ds(at, tile), c * ny : (c + 1) * ny] = row
 
 
-def flatten_edges_kernel(nx, ny, x_ref, e_ref, *refs):
+def flatten_own_kernel(nx, ny, e_ref, p_ref, e_out_ref, *refs):
     *outs, first_ref, final_ref, wide_ref = refs
-    flatten_kernel(nx, ny, x_ref, *outs, wide_ref)
-    e = e_ref.shape[0]
-    first_ref[0:e, :] = e_ref[:, 0:ny]
+    flatten_one(nx, ny, e_ref, [e_out_ref], wide_ref)
+    flatten_one(nx, ny, p_ref, outs, wide_ref)
+    e = e_out_ref.shape[0]
+    first_ref[0:e, :] = e_out_ref[:, 0:ny]
     first_ref[e:, :] = outs[0][:, 0:ny]
-    final_ref[0:e, :] = e_ref[:, (nx - 1) * ny :]
+    final_ref[0:e, :] = e_out_ref[:, (nx - 1) * ny :]
     final_ref[e:, :] = outs[-1][:, outs[-1].shape[1] - ny :]
+
+
+def flatten_others_kernel(nx, ny, count, *refs):
+    xs, outs, (first_ref, final_ref, wide_ref) = refs[:count], refs[count : 2 * count], refs[2 * count :]
+    for x_ref, out_ref in zip(xs, outs):
+        flatten_one(nx, ny, x_ref, [out_ref], wide_ref)
+    first_ref[...] = outs[1][:, 0:ny]
+    final_ref[...] = outs[1][:, (nx - 1) * ny :]
+
+
+def lent_kernel(n, p, width, ny, shares, place_ref, source_ref, *refs):
+    share_refs, refs = refs[:shares], refs[shares:]
+    p_refs, refs = refs[: n * CHUNKS], refs[n * CHUNKS :]
+    own_ref, low_ref, high_ref, up_ref, speed_ref, rate_ref, out_ref, absorption_ref, sp_ref = refs
+    at = 0
+    for share_ref in share_refs:
+        count = out_ref.shape[0] // place_ref.shape[0]
+        for i in range(share_ref.shape[0] // count):
+            to = pl.ds(pl.multiple_of(place_ref[at] * count, count), count)
+            absorption_ref[to, :] = share_ref[i * count : (i + 1) * count, :]
+            at += 1
+    for k in range(CHUNKS):
+        for j in range(n):
+            sp_ref[pl.ds(pl.multiple_of(source_ref[j] * p, p), p), :] = p_refs[k * n + j][...]
+        gain = jnp.dot(absorption_ref[...], sp_ref[...], preferred_element_type=jnp.float32)
+        start, stop = k * width, (k + 1) * width
+        own = own_ref[:, start:stop].astype(jnp.float32)
+        low = (own_ref[:, start - ny : start] if k else low_ref[...]).astype(jnp.float32)
+        high = (own_ref[:, stop : stop + ny] if k + 1 < CHUNKS else high_ref[...]).astype(jnp.float32)
+        lower = jnp.concatenate([low, own[:, : width - ny]], axis=1) if width > ny else low
+        higher = jnp.concatenate([own[:, ny:], high], axis=1) if width > ny else high
+        f_up = jnp.where(up_ref[:, start:stop] == 1, lower, higher)
+        new = (own - speed_ref[...] * (own - f_up) + 0.5 * gain) / (1.0 + rate_ref[...])
+        out_ref[:, start:stop] = new.astype(jnp.bfloat16)
 
 
 def step_kernel(n, e, p, width, ny, nx, cols, edge, last, *refs):
@@ -183,14 +222,27 @@
     width = tall * ny
     lanes = pltpu.VMEM((64 * nx, ny), jnp.float32)
 
-    (e_all,) = call(
-        lambda *refs: flatten_kernel(nx, ny, *refs), (bf16(e, nx * ny),), [lanes],
-        (electrons.reshape(e * nx, ny),), megabytes=4, name="flatten",
-    )
-    far_e = [from_chip(e_all, d) for d in range(1, chips)]
-    *p_chunks, first, final = call(
-        lambda *refs: flatten_edges_kernel(nx, ny, *refs), (bf16(p, width),) * CHUNKS + (bf16(e + p, ny),) * 2, [lanes],
-        (phonons.reshape(p * nx, ny), e_all), megabytes=8, name="flatten",
+    groups, spaces = lax.axis_size("grp"), lax.axis_size("space")
+    lend = chips == 2 and e % (16 * groups * spaces) == 0
+    if lend:
+        count = e // (groups * spaces)
+        grp, space = lax.axis_index("grp").astype(jnp.uint32), lax.axis_index("space").astype(jnp.uint32)
+        start = (grp * spaces + space) * count
+        share = from_chip(lax.dynamic_slice(absorption, (start, jnp.zeros_like(start)), (count, NM)), 1)
+        far_rates = from_chip(jnp.stack([speed, electron_rate]), 1)
+        shares = [share] + [from_ring(share, "space", d) for d in range(1, spaces)]
+        column = jnp.concatenate(shares, axis=0)
+        shares_of = [column] + [from_ring(column, "grp", d) for d in range(1, groups)]
+        places = jnp.stack(
+            [((grp + g) % groups) * spaces + (space + d) % spaces for g in range(groups) for d in range(spaces)]
+        ).astype(jnp.int32)
+
+    near_e = swap_cores(electrons)
+    far_e = [from_chip(electrons, d) for d in range(1, chips)]
+    e_all, *p_chunks, first, final = call(
+        lambda *refs: flatten_own_kernel(nx, ny, *refs),
+        (bf16(e, nx * ny),) + (bf16(p, width),) * CHUNKS + (bf16(e + p, ny),) * 2, [lanes],
+        (electrons.reshape(e * nx, ny), phonons.reshape(p * nx, ny)), megabytes=8, name="flatten",
     )
     block_coupling = after(block_coupling, p_chunks[0])
     kernel = block_coupling.reshape(b_rows, BLK, slots, BLK)
@@ -205,10 +257,9 @@
     sources = jnp.stack(
         [((chip + d) % chips) * CORES + (core ^ c) for d in range(chips) for c in range(CORES)]
     ).astype(jnp.int32)
-    speed, diffusion = speed[:, None], diffusion[:, None]
-    electron_rate, phonon_rate = electron_rate[:, None], phonon_rate[:, None]
     ups = [upwind[k * tall : (k + 1) * tall].reshape(1, width) for k in range(CHUNKS)]
-    weights = (emission, absorption, dense, speed, diffusion, electron_rate, phonon_rate)
+    rates = (x[:, None] for x in (speed, diffusion, electron_rate, phonon_rate))
+    weights = (emission, absorption, dense, *rates)
 
     def step(k, es, ps, low, high, done, want_edge):
         last = bool(done)
@@ -241,23 +292,57 @@
 
     low, high = from_space(final, -1), from_space(first, 1)
     far_p = [[from_chip(c, d) for d in range(1, chips)] for c in p_chunks]
-    everyone = [x for x, _ in gathered(e_all, far_e, (p_chunks[0],), 0)]
-    new = []
+    others = [near_e]
+    for f in far_e:
+        f = after(f, p_chunks[0], *((share, far_rates) if lend else ()))
+        others += [f, swap_cores(f)]
+    *others, far_first, far_final = call(
+        lambda *refs: flatten_others_kernel(nx, ny, n - 1, *refs),
+        (bf16(e, nx * ny),) * (n - 1) + (bf16(e, ny),) * 2, [lanes],
+        [x.reshape(e * nx, ny) for x in others], megabytes=12, name="flatten",
+    )
+    everyone = [e_all, *others]
+    if lend:
+        far_low, far_high = from_space(far_final, -1), from_space(far_first, 1)
+    waits = [(dense, low, high, everyone[1]) + (tuple(shares) if lend else ())]
+    new, every_p = [], []
     for k in range(CHUNKS):
         es = [(x, k * width) for x in everyone]
-        ps = gathered(p_chunks[k], far_p[k], (new[-1][0],) if k else (dense, low, high), 0)
+        ps = gathered(p_chunks[k], far_p[k], waits[k], 0)
         before = ((e_all, k * width - ny), (p_chunks[k - 1], width - ny)) if k else ((low, 0), (low, 0))
         behind = ((e_all, (k + 1) * width), (p_chunks[k + 1], 0)) if k + 1 < CHUNKS else ((high, 0), (high, 0))
         new.append(step(k, es, ps, before, behind, [], True))
+        every_p += [x for x, _ in ps]
+        waits.append((new[-1][0],) + ((far_low, far_high, *shares_of) if lend else ()))
     first, final = new[0][2], new[-1][2]
     chunks = [(c[0], c[1]) for c in new]
 
     low, high = from_space(final, -1), from_space(first, 1)
-    far = [[[from_chip(x, d) for d in range(1, chips)] for x in c] for c in chunks]
+    far_p = [[from_chip(c[1], d) for d in range(1, chips)] for c in chunks]
+    ready = (chunks[-1][0], low, high)
+    if lend:
+        own = after(everyone[2], chunks[-1][0])
+        operands = (
+            places, sources, *shares_of, *every_p, own, far_low, far_high, upwind.reshape(1, nx * ny),
+            far_rates[0][:, None], far_rates[1][:, None],
+        )
+        (lent,) = call(
+            lambda *refs: lent_kernel(n, p, width, ny, groups, *refs), (bf16(e, nx * ny),),
+            [pltpu.VMEM((e, NM), jnp.bfloat16), pltpu.VMEM((n * p, width), jnp.bfloat16)],
+            operands, specs=[SMEM, SMEM] + [VMEM] * (len(operands) - 2), name="lent",
+        )
+        lent = [lent, swap_cores(lent)]
+        ready += (lent[0],)
+    else:
+        far_e = [[from_chip(c[0], d) for d in range(1, chips)] for c in chunks]
     done = []
     for k in range(CHUNKS):
-        wait_for = (done[-1][0],) if k else (chunks[-1][0], low, high)
-        es, ps = (gathered(chunks[k][i], far[k][i], wait_for, 0) for i in range(2))
+        wait_for = (done[-1][0],) if k else ready
+        if lend:
+            es = [(chunks[k][0], 0), (swap_cores(chunks[k][0]), 0)] + [(x, k * width) for x in lent]
+        else:
+            es = gathered(chunks[k][0], far_e[k], wait_for, 0)
+        ps = gathered(chunks[k][1], far_p[k], wait_for, 0)
         before = tuple((x, width - ny) for x in chunks[k - 1]) if k else ((low, 0), (low, 0))
         behind = tuple((x, 0) for x in chunks[k + 1]) if k + 1 < CHUNKS else ((high, 0), (high, 0))
         done.append(step(k, es, ps, before, behind, done if k + 1 == CHUNKS else [], False))

time: 89.6 us -> 139 us (1.55)
  local copies, waits for them, and re-layouts: 8.16 us -> 44.5 us
  starting transfers between devices: 27 us -> 40.3 us
  waiting for transfers between devices: 31.5 us -> 19.3 us
  Pallas kernels: 19.2 us -> 27.9 us
  other arithmetic: 0.08 us -> 1.95 us
    unnamed x35 -> x108, local copies, waits for them, and re-layouts: 7.6 us -> 36.4 us
    ppermute x7, waiting for transfers between devices: 24.8 us -> 9.72 us  [from_chip(): lax.ppermute(x, 'mode', [((i + CORES * offset) % n, i) for i in range(n)])]
    pallas_call x6 -> x7, Pallas kernels: 19.2 us -> 27.9 us  [call(): pl.pallas_call(kernel, out_shape=out, in_specs=specs or [VMEM] * len(oper...]
    ppermute x0 -> x4, waiting for transfers between devices: none -> 5.73 us  [from_ring(): return lax.ppermute(x, axis, [((i + offset) % n, i) for i in range(n)])]
    ppermute x0 -> x4, starting transfers between devices: none -> 4.88 us  [from_ring(): return lax.ppermute(x, axis, [((i + offset) % n, i) for i in range(n)])]
    ppermute x4 -> x6, starting transfers between devices: 10.7 us -> 15.4 us  [from_space(): return lax.ppermute(x, 'space', pairs)]
    another operation x0 -> x4, local copies, waits for them, and re-layouts: none -> 3.98 us  [the longest x2 2.01 us: on_device(): far_rates[1][:, None]]
    ppermute x4 -> x6, waiting for transfers between devices: 3.95 us -> 0.02 us  [from_space(): return lax.ppermute(x, 'space', pairs)]
  transfers between devices with their start and end apart: 25 -> 30, of which waited for: 12 -> 6; matrix products, arithmetic and copies ran while one was open for 3% -> 11% of each run, Pallas kernels for 14% -> 16%
where the time goes in v4:
time: 139 us; the launch traced here: 137 us
  local copies, waits for them, and re-layouts  44.5 us (32%)
  starting transfers between devices  40.3 us (29%)
  Pallas kernels  27.9 us (20%)
  waiting for transfers between devices  19.3 us (14%)
  other arithmetic  1.95 us (1%)
  matrix products  1.83 us (1%)
    unnamed x108, local copies, waits for them, and re-layouts  36.4 us
    pallas_call x7, Pallas kernels, call(): pl.pallas_call(kernel, out_shape=out, in_specs=specs or [VMEM] * len(oper...  27.9 us
    ppermute x6, starting transfers between devices, from_space(): return lax.ppermute(x, 'space', pairs)  15.4 us
    ppermute x13, starting transfers between devices, swap_cores(): return lax.ppermute(x, 'mode', [(i, i ^ 1) for i in range(n)])  15.2 us
    ppermute x7, waiting for transfers between devices, from_chip(): lax.ppermute(x, 'mode', [((i + CORES * offset) % n, i) for i in range(n)])  9.72 us
    ppermute x4, waiting for transfers between devices, from_ring(): return lax.ppermute(x, axis, [((i + offset) % n, i) for i in range(n)])  5.73 us
    ppermute x4, starting transfers between devices, from_ring(): return lax.ppermute(x, axis, [((i + offset) % n, i) for i in range(n)])  4.88 us
    ppermute x7, starting transfers between devices, from_chip(): lax.ppermute(x, 'mode', [((i + CORES * offset) % n, i) for i in range(n)])  4.76 us
  transfers between devices with their start and end apart: 30, of which 6 were waited for; matrix products, arithmetic and copies ran while one was open for 11% of the time, Pallas kernels for 16%

profile of v4, /device:TPU:13, one launch (start us, length us, event | category | flops | bytes accessed | tf_op | source)
XLA Modules:
  0.0 136.8 jit_solution(10173144177314987792)
XLA Ops:
  7.3 1.9 %flatten.2 = (bf16[256,1024]{1,0:T(8,128)(2,1)S(1)}, bf16[512,512]{1,0:T(8,128)(2,1)}, bf16[512,512]{1,0:T(8,128)(2,1)}, bf16[768,128]{1,0:T(8,128)(2,1)S(1)}, bf16[768,128]{1,0:T(8,128)(2,1)S(1)}) custom-call(bf16[2048,128]{1,0:T(8,128)(2,1)S(1)} %bitcast.49, bf16[4096,128]{1,0:T(8,128)(2,1)S(1)} %bitcast.48), custom_call_target="tpu_custom_call" | custom-call | flops 1000 | bytes 1000 | tf_op jit(solution)/shard_map/flatten/pallas_call | solution.py:49
  11.2 1.8 %fusion.2 = bf16[4,128,128,16]{2,3,1,0:T(8,128)(2,1)S(1)} fusion(bf16[4,128,12,128]{3,1,0,2:T(8,128)(2,1)S(1)} %bitcast.57, s32[4,12]{1,0:T(4,128)} %param.16), kind=kOutput, calls=%fused_computation.3 | convolution fusion | flops 26215168 | bytes 3670208 | tf_op jit(solution)/shard_map/bsk,bisj->bikj/dot_general | solution.py:251
  13.7 2.9 %collective-permute-done.3 = f32[2,256]{1,0:T(2,128)S(1)} collective-permute-done((f32[2,256]{1,0:T(2,128)S(1)}, f32[2,256]{1,0:T(2,128)S(1)}, u32[]{:S(2)}, u32[]{:S(2)}) %collective-permute-start.3) | collective-permute-done | bytes 2080 | tf_op jit(solution)/shard_map/ppermute | solution.py:26
  16.6 2.1 %collective-permute-start.10 = (bf16[768,128]{1,0:T(8,128)(2,1)S(1)}, bf16[768,128]{1,0:T(8,128)(2,1)S(1)}, u32[]{:S(2)}, u32[]{:S(2)}) collective-permute-start(bf16[768,128]{1,0:T(8,128)(2,1)S(1)} %get-tuple-element.38), channel_id=1, source_target_pairs={{1,0},{2,1},{3,2},{5,4},{6,5},{7,6},{9,8},{10,9},{11,10},{13,12},{... | collective-permute-start | bytes 589832 | tf_op jit(solution)/shard_map/ppermute | solution.py:32
  18.7 3.0 %collective-permute-start.4 = (bf16[256,8,128]{2,1,0:T(8,128)(2,1)}, bf16[256,8,128]{2,1,0:T(8,128)(2,1)S(1)}, u32[]{:S(2)}, u32[]{:S(2)}) collective-permute-start(bf16[256,8,128]{2,1,0:T(8,128)(2,1)} %collective-permute-done.1), channel_id=1, source_target_pairs={{0,4},{4,0},{8,12},{12,8},{1,5},{5,1},{9,13},{13,9},{2,6},{6,2},{1... | collective-permute-start | bytes 1572872 | tf_op jit(solution)/shard_map/ppermute | solution.py:21
  22.4 2.6 %collective-permute-done.11 = bf16[32,2048]{1,0:T(8,128)(2,1)S(1)} collective-permute-done((bf16[32,2048]{1,0:T(8,128)(2,1)S(1)}, bf16[32,2048]{1,0:T(8,128)(2,1)S(1)}, u32[]{:S(2)}, u32[]{:S(2)}) %collective-permute-start.11) | collective-permute-done | bytes 131104 | tf_op jit(solution)/shard_map/ppermute | solution.py:37
  25.1 1.6 %collective-permute-start.12 = (bf16[32,2048]{1,0:T(8,128)(2,1)S(1)}, bf16[32,2048]{1,0:T(8,128)(2,1)S(1)}, u32[]{:S(2)}, u32[]{:S(2)}) collective-permute-start(bf16[32,2048]{1,0:T(8,128)(2,1)S(1)} %collective-permute-done.2), channel_id=1, source_target_pairs={{2,0},{3,1},{0,2},{1,3},{6,4},{7,5},{4,6},{5,7},{10,8},{11,9},{8,1... | collective-permute-start | bytes 393224 | tf_op jit(solution)/shard_map/ppermute | solution.py:37
  27.3 3.1 %collective-permute-done.12 = bf16[32,2048]{1,0:T(8,128)(2,1)S(1)} collective-permute-done((bf16[32,2048]{1,0:T(8,128)(2,1)S(1)}, bf16[32,2048]{1,0:T(8,128)(2,1)S(1)}, u32[]{:S(2)}, u32[]{:S(2)}) %collective-permute-start.12) | collective-permute-done | bytes 131104 | tf_op jit(solution)/shard_map/ppermute | solution.py:37
  30.4 2.7 %collective-permute-start.9 = (bf16[768,128]{1,0:T(8,128)(2,1)S(1)}, bf16[768,128]{1,0:T(8,128)(2,1)S(1)}, u32[]{:S(2)}, u32[]{:S(2)}) collective-permute-start(bf16[768,128]{1,0:T(8,128)(2,1)S(1)} %get-tuple-element.37), channel_id=1, source_target_pairs={{0,1},{1,2},{2,3},{4,5},{5,6},{6,7},{8,9},{9,10},{10,11},{12,13},{... | collective-permute-start | bytes 589832 | tf_op jit(solution)/shard_map/ppermute | solution.py:32
  33.1 2.0 %collective-permute-start.13 = (bf16[32,2048]{1,0:T(8,128)(2,1)S(1)}, bf16[32,2048]{1,0:T(8,128)(2,1)S(1)}, u32[]{:S(2)}, u32[]{:S(2)}) collective-permute-start(bf16[32,2048]{1,0:T(8,128)(2,1)S(1)} %collective-permute-done.2), channel_id=1, source_target_pairs={{3,0},{0,1},{1,2},{2,3},{7,4},{4,5},{5,6},{6,7},{11,8},{8,9},{9,10... | collective-permute-start | bytes 393224 | tf_op jit(solution)/shard_map/ppermute | solution.py:37
  35.8 6.5 %collective-permute-start.7 = (bf16[512,512]{1,0:T(8,128)(2,1)}, bf16[512,512]{1,0:T(8,128)(2,1)}, u32[]{:S(2)}, u32[]{:S(2)}) collective-permute-start(bf16[512,512]{1,0:T(8,128)(2,1)} %get-tuple-element.30.refs_5_.refs_10_.refs_4_), channel_id=1, source_target_pairs={{0,4},{4,0},{8,12},{12,8},{1,5},{5,1},{9,13},{13,9},{2,6},{6,2},{1... | collective-permute-start | bytes 1572872 | tf_op jit(solution)/shard_map/ppermute | solution.py:21
  42.3 2.1 %flatten.3 = (bf16[256,1024]{1,0:T(8,128)(2,1)S(1)}, bf16[256,1024]{1,0:T(8,128)(2,1)S(1)}, bf16[256,1024]{1,0:T(8,128)(2,1)S(1)}, bf16[256,128]{1,0:T(8,128)(2,1)S(1)}, bf16[256,128]{1,0:T(8,128)(2,1)S(1)}) custom-call(bf16[2048,128]{1,0:T(8,128)(2,1)} %bitcast.6.refs_0_, bf16[2048,128]{1,0:T(8,128)(2,1)} %bitcast.9.refs_1_, bf16[2048,128]{1,0:T(8,128)(2,1)S(1)} %bitcast.50), custom_call_target="tpu_custom_call" | custom-call | flops 1000 | bytes 1000 | tf_op jit(solution)/shard_map/flatten/pallas_call | solution.py:49
  54.5 1.9 %collective-permute-start.15 = (bf16[256,128]{1,0:T(8,128)(2,1)}, bf16[256,128]{1,0:T(8,128)(2,1)S(1)}, u32[]{:S(2)}, u32[]{:S(2)}) collective-permute-start(bf16[256,128]{1,0:T(8,128)(2,1)} %copy-done.45), channel_id=1, source_target_pairs={{0,1},{1,2},{2,3},{4,5},{5,6},{6,7},{8,9},{9,10},{10,11},{12,13},{... | collective-permute-start | bytes 196616 | tf_op jit(solution)/shard_map/ppermute | solution.py:32
  56.4 3.4 %collective-permute-start.16 = (bf16[256,128]{1,0:T(8,128)(2,1)}, bf16[256,128]{1,0:T(8,128)(2,1)S(1)}, u32[]{:S(2)}, u32[]{:S(2)}) collective-permute-start(bf16[256,128]{1,0:T(8,128)(2,1)} %copy-done.44), channel_id=1, source_target_pairs={{1,0},{2,1},{3,2},{5,4},{6,5},{7,6},{9,8},{10,9},{11,10},{13,12},{... | collective-permute-start | bytes 196616 | tf_op jit(solution)/shard_map/ppermute | solution.py:32
  69.1 5.2 %step.4 = (bf16[256,512]{1,0:T(8,128)(2,1)S(1)}, bf16[512,512]{1,0:T(8,128)(2,1)}, bf16[768,128]{1,0:T(8,128)(2,1)S(1)}) custom-call(s32[4]{0:T(128)S(1)} %add_convert_fusion.refs_0_.refs_1_, bf16[256,1024]{1,0:T(8,128)(2,1)S(1)} %copy-done.5, bf16[256,1024]{1,0:T(8,128)(2,1)S(1)} %copy-done.18, bf16[256,1024]{1,0:T(8,128)(2,1)S(1)} %copy-done.11, ...), custom_call_target="tpu_custom_call" | custom-call | flops 1000 | bytes 1000 | tf_op jit(solution)/shard_map/step/pallas_call | solution.py:49
  79.9 1.9 %collective-permute-start.27 = (bf16[768,128]{1,0:T(8,128)(2,1)}, bf16[768,128]{1,0:T(8,128)(2,1)}, u32[]{:S(2)}, u32[]{:S(2)}) collective-permute-start(bf16[768,128]{1,0:T(8,128)(2,1)} %copy-done.43), channel_id=1, source_target_pairs={{1,0},{2,1},{3,2},{5,4},{6,5},{7,6},{9,8},{10,9},{11,10},{13,12},{... | collective-permute-start | bytes 589832 | tf_op jit(solution)/shard_map/ppermute | solution.py:32
  90.0 5.1 %step.5 = (bf16[256,512]{1,0:T(8,128)(2,1)S(1)}, bf16[512,512]{1,0:T(8,128)(2,1)S(1)}, bf16[768,128]{1,0:T(8,128)(2,1)}) custom-call(s32[4]{0:T(128)S(1)} %add_convert_fusion.refs_0_.refs_1_, bf16[256,1024]{1,0:T(8,128)(2,1)S(1)} %copy-done.6, bf16[256,1024]{1,0:T(8,128)(2,1)S(1)} %copy-done.19, bf16[256,1024]{1,0:T(8,128)(2,1)S(1)} %copy-done.12, ...), custom_call_target="tpu_custom_call" | custom-call | flops 1000 | bytes 1000 | tf_op jit(solution)/shard_map/step/pallas_call | solution.py:49
  96.6 3.5 %collective-permute-start.26 = (bf16[768,128]{1,0:T(8,128)(2,1)}, bf16[768,128]{1,0:T(8,128)(2,1)}, u32[]{:S(2)}, u32[]{:S(2)}) collective-permute-start(bf16[768,128]{1,0:T(8,128)(2,1)} %get-tuple-element.48), channel_id=1, source_target_pairs={{0,1},{1,2},{2,3},{4,5},{5,6},{6,7},{8,9},{9,10},{10,11},{12,13},{... | collective-permute-start | bytes 589832 | tf_op jit(solution)/shard_map/ppermute | solution.py:32
  110.1 4.3 %lent.1.refs_3_ = bf16[256,1024]{1,0:T(8,128)(2,1)S(1)} custom-call(s32[8]{0:T(128)S(1)} %copy-done.42, s32[4]{0:T(128)S(1)} %add_convert_fusion.refs_0_.refs_1_, bf16[128,2048]{1,0:T(8,128)(2,1)} %constant_dynamic-update-slice_fusion.refs_2_, bf16[128,2048]{1,0:T(8,128)(2,1)} %collective-permute-done.17.refs_3_, ...), custom_call_target="tpu_custom_call" | custom-call | flops 1000 | bytes 1000 | tf_op jit(solution)/shard_map/lent/pallas_call | solution.py:49
  115.7 1.9 %collective-permute-done.23.refs_2_ = bf16[256,512]{1,0:T(8,128)(2,1)S(1)} collective-permute-done((bf16[256,512]{1,0:T(8,128)(2,1)S(1)}, bf16[256,512]{1,0:T(8,128)(2,1)S(1)}, u32[]{:S(2)}, u32[]{:S(2)}) %collective-permute-start.23) | collective-permute-done | bytes 262176 | tf_op jit(solution)/shard_map/ppermute | solution.py:21
  117.7 4.0 %step.6 = (bf16[256,512]{1,0:T(8,128)(2,1)S(1)}, bf16[512,512]{1,0:T(8,128)(2,1)S(1)}) custom-call(s32[4]{0:T(128)S(1)} %add_convert_fusion.refs_0_.refs_1_, bf16[256,512]{1,0:T(8,128)(2,1)S(1)} %copy-done.26, bf16[256,512]{1,0:T(8,128)(2,1)S(1)} %collective-permute-done.23.refs_2_, bf16[256,1024]{1,0:T(8,128)(2,1)S(1)} %lent.1.refs_3_, ...), custom_call_target="tpu_custom_call" | custom-call | flops 1000 | bytes 1000 | tf_op jit(solution)/shard_map/step/pallas_call | solution.py:49
  121.8 6.8 %collective-permute-done.22.refs_7_ = bf16[512,512]{1,0:T(8,128)(2,1)S(1)} collective-permute-done((bf16[512,512]{1,0:T(8,128)(2,1)S(1)}, bf16[512,512]{1,0:T(8,128)(2,1)S(1)}, u32[]{:S(2)}, u32[]{:S(2)}) %collective-permute-start.22) | collective-permute-done | bytes 524320 | tf_op jit(solution)/shard_map/ppermute | solution.py:26
  129.5 1.9 %collective-permute-done.19.refs_2_ = bf16[256,512]{1,0:T(8,128)(2,1)S(1)} collective-permute-done((bf16[256,512]{1,0:T(8,128)(2,1)S(1)}, bf16[256,512]{1,0:T(8,128)(2,1)S(1)}, u32[]{:S(2)}, u32[]{:S(2)}) %collective-permute-start.19) | collective-permute-done | bytes 262176 | tf_op jit(solution)/shard_map/ppermute | solution.py:21
  131.4 5.4 %step.7 = (bf16[2048,128]{1,0:T(8,128)(2,1)}, bf16[4096,128]{1,0:T(8,128)(2,1)}) custom-call(s32[4]{0:T(128)S(1)} %add_convert_fusion.refs_0_.refs_1_, bf16[256,512]{1,0:T(8,128)(2,1)S(1)} %copy-done.28, bf16[256,512]{1,0:T(8,128)(2,1)S(1)} %collective-permute-done.19.refs_2_, bf16[256,1024]{1,0:T(8,128)(2,1)S(1)} %lent.1.refs_3_, ...), custom_call_target="tpu_custom_call" | custom-call | flops 1000 | bytes 1000 | tf_op jit(solution)/shard_map/step/pallas_call | solution.py:49
  (166 shorter events, 58.2 us)
Async XLA Ops:
  0.6 18.1 %collective-permute-start.1 = (bf16[256,8,128]{2,1,0:T(8,128)(2,1)}, bf16[256,8,128]{2,1,0:T(8,128)(2,1)}, u32[]{:S(2)}, u32[]{:S(2)}) collective-permute-start(bf16[256,8,128]{2,1,0:T(8,128)(2,1)} %param.11), channel_id=1, source_target_pairs={{8,0},{12,4},{0,8},{4,12},{9,1},{13,5},{1,9},{5,13},{10,2},{14,6},... | collective-permute-start | bytes 1572872 | tf_op jit(solution)/shard_map/ppermute | solution.py:26
  0.9 32.2 %collective-permute-start = (bf16[256,8,128]{2,1,0:T(8,128)(2,1)}, bf16[256,8,128]{2,1,0:T(8,128)(2,1)}, u32[]{:S(2)}, u32[]{:S(2)}) collective-permute-start(bf16[256,8,128]{2,1,0:T(8,128)(2,1)} %param.11), channel_id=1, source_target_pairs={{0,4},{4,0},{8,12},{12,8},{1,5},{5,1},{9,13},{13,9},{2,6},{6,2},{1... | collective-permute-start | bytes 1572872 | tf_op jit(solution)/shard_map/ppermute | solution.py:21
  2.8 15.8 %collective-permute-start.2 = (bf16[32,2048]{1,0:T(8,128)(2,1)S(1)}, bf16[32,2048]{1,0:T(8,128)(2,1)S(1)}, u32[]{:S(2)}, u32[]{:S(2)}) collective-permute-start(bf16[32,2048]{1,0:T(8,128)(2,1)S(1)} %constant_dynamic-slice_fusion), channel_id=1, source_target_pairs={{8,0},{12,4},{0,8},{4,12},{9,1},{13,5},{1,9},{5,13},{10,2},{14,6},... | collective-permute-start | bytes 393224 | tf_op jit(solution)/shard_map/ppermute | solution.py:26
  4.8 11.7 %collective-permute-start.3 = (f32[2,256]{1,0:T(2,128)S(1)}, f32[2,256]{1,0:T(2,128)S(1)}, u32[]{:S(2)}, u32[]{:S(2)}) collective-permute-start(f32[2,256]{1,0:T(2,128)S(1)} %pad_maximum_fusion), channel_id=1, source_target_pairs={{8,0},{12,4},{0,8},{4,12},{9,1},{13,5},{1,9},{5,13},{10,2},{14,6},... | collective-permute-start | bytes 6152 | tf_op jit(solution)/shard_map/ppermute | solution.py:26
  10.0 39.6 %collective-permute-start.8 = (bf16[512,512]{1,0:T(8,128)(2,1)}, bf16[512,512]{1,0:T(8,128)(2,1)}, u32[]{:S(2)}, u32[]{:S(2)}) collective-permute-start(bf16[512,512]{1,0:T(8,128)(2,1)} %get-tuple-element.30.refs_5_.refs_10_.refs_4_), channel_id=1, source_target_pairs={{8,0},{12,4},{0,8},{4,12},{9,1},{13,5},{1,9},{5,13},{10,2},{14,6},... | collective-permute-start | bytes 1572872 | tf_op jit(solution)/shard_map/ppermute | solution.py:26
  16.6 31.5 %collective-permute-start.10 = (bf16[768,128]{1,0:T(8,128)(2,1)S(1)}, bf16[768,128]{1,0:T(8,128)(2,1)S(1)}, u32[]{:S(2)}, u32[]{:S(2)}) collective-permute-start(bf16[768,128]{1,0:T(8,128)(2,1)S(1)} %get-tuple-element.38), channel_id=1, source_target_pairs={{1,0},{2,1},{3,2},{5,4},{6,5},{7,6},{9,8},{10,9},{11,10},{13,12},{... | collective-permute-start | bytes 589832 | tf_op jit(solution)/shard_map/ppermute | solution.py:32
  18.6 6.4 %collective-permute-start.11 = (bf16[32,2048]{1,0:T(8,128)(2,1)S(1)}, bf16[32,2048]{1,0:T(8,128)(2,1)S(1)}, u32[]{:S(2)}, u32[]{:S(2)}) collective-permute-start(bf16[32,2048]{1,0:T(8,128)(2,1)S(1)} %collective-permute-done.2), channel_id=1, source_target_pairs={{1,0},{2,1},{3,2},{0,3},{5,4},{6,5},{7,6},{4,7},{9,8},{10,9},{11,1... | collective-permute-start | bytes 393224 | tf_op jit(solution)/shard_map/ppermute | solution.py:37
  18.7 17.1 %collective-permute-start.4 = (bf16[256,8,128]{2,1,0:T(8,128)(2,1)}, bf16[256,8,128]{2,1,0:T(8,128)(2,1)S(1)}, u32[]{:S(2)}, u32[]{:S(2)}) collective-permute-start(bf16[256,8,128]{2,1,0:T(8,128)(2,1)} %collective-permute-done.1), channel_id=1, source_target_pairs={{0,4},{4,0},{8,12},{12,8},{1,5},{5,1},{9,13},{13,9},{2,6},{6,2},{1... | collective-permute-start | bytes 1572872 | tf_op jit(solution)/shard_map/ppermute | solution.py:21
  25.1 5.3 %collective-permute-start.12 = (bf16[32,2048]{1,0:T(8,128)(2,1)S(1)}, bf16[32,2048]{1,0:T(8,128)(2,1)S(1)}, u32[]{:S(2)}, u32[]{:S(2)}) collective-permute-start(bf16[32,2048]{1,0:T(8,128)(2,1)S(1)} %collective-permute-done.2), channel_id=1, source_target_pairs={{2,0},{3,1},{0,2},{1,3},{6,4},{7,5},{4,6},{5,7},{10,8},{11,9},{8,1... | collective-permute-start | bytes 393224 | tf_op jit(solution)/shard_map/ppermute | solution.py:37
  30.4 18.6 %collective-permute-start.9 = (bf16[768,128]{1,0:T(8,128)(2,1)S(1)}, bf16[768,128]{1,0:T(8,128)(2,1)S(1)}, u32[]{:S(2)}, u32[]{:S(2)}) collective-permute-start(bf16[768,128]{1,0:T(8,128)(2,1)S(1)} %get-tuple-element.37), channel_id=1, source_target_pairs={{0,1},{1,2},{2,3},{4,5},{5,6},{6,7},{8,9},{9,10},{10,11},{12,13},{... | collective-permute-start | bytes 589832 | tf_op jit(solution)/shard_map/ppermute | solution.py:32
  33.1 16.6 %collective-permute-start.13 = (bf16[32,2048]{1,0:T(8,128)(2,1)S(1)}, bf16[32,2048]{1,0:T(8,128)(2,1)S(1)}, u32[]{:S(2)}, u32[]{:S(2)}) collective-permute-start(bf16[32,2048]{1,0:T(8,128)(2,1)S(1)} %collective-permute-done.2), channel_id=1, source_target_pairs={{3,0},{0,1},{1,2},{2,3},{7,4},{4,5},{5,6},{6,7},{11,8},{8,9},{9,10... | collective-permute-start | bytes 393224 | tf_op jit(solution)/shard_map/ppermute | solution.py:37
  35.8 20.6 %collective-permute-start.7 = (bf16[512,512]{1,0:T(8,128)(2,1)}, bf16[512,512]{1,0:T(8,128)(2,1)}, u32[]{:S(2)}, u32[]{:S(2)}) collective-permute-start(bf16[512,512]{1,0:T(8,128)(2,1)} %get-tuple-element.30.refs_5_.refs_10_.refs_4_), channel_id=1, source_target_pairs={{0,4},{4,0},{8,12},{12,8},{1,5},{5,1},{9,13},{13,9},{2,6},{6,2},{1... | collective-permute-start | bytes 1572872 | tf_op jit(solution)/shard_map/ppermute | solution.py:21
  48.7 27.0 %collective-permute-start.6 = (bf16[512,512]{1,0:T(8,128)(2,1)}, bf16[512,512]{1,0:T(8,128)(2,1)}, u32[]{:S(2)}, u32[]{:S(2)}) collective-permute-start(bf16[512,512]{1,0:T(8,128)(2,1)} %get-tuple-element.35.refs_12_.refs_5_.refs_8_), channel_id=1, source_target_pairs={{8,0},{12,4},{0,8},{4,12},{9,1},{13,5},{1,9},{5,13},{10,2},{14,6},... | collective-permute-start | bytes 1572872 | tf_op jit(solution)/shard_map/ppermute | solution.py:26
  49.6 10.2 %collective-permute-start.14 = (bf16[512,512]{1,0:T(8,128)(2,1)}, bf16[512,512]{1,0:T(8,128)(2,1)}, u32[]{:S(2)}, u32[]{:S(2)}) collective-permute-start(bf16[512,512]{1,0:T(8,128)(2,1)} %collective-permute-done.8.refs_7_.refs_6_), channel_id=1, source_target_pairs={{0,4},{4,0},{8,12},{12,8},{1,5},{5,1},{9,13},{13,9},{2,6},{6,2},{1... | collective-permute-start | bytes 1572872 | tf_op jit(solution)/shard_map/ppermute | solution.py:21
  50.6 25.1 %collective-permute-start.17 = (bf16[128,2048]{1,0:T(8,128)(2,1)}, bf16[128,2048]{1,0:T(8,128)(2,1)}, u32[]{:S(2)}, u32[]{:S(2)}) collective-permute-start(bf16[128,2048]{1,0:T(8,128)(2,1)} %constant_dynamic-update-slice_fusion.refs_2_), channel_id=1, source_target_pairs={{16,0},{0,16},{17,1},{1,17},{18,2},{2,18},{19,3},{3,19},{20,4},{4,... | collective-permute-start | bytes 1572872 | tf_op jit(solution)/shard_map/ppermute | solution.py:37
  54.5 21.2 %collective-permute-start.15 = (bf16[256,128]{1,0:T(8,128)(2,1)}, bf16[256,128]{1,0:T(8,128)(2,1)S(1)}, u32[]{:S(2)}, u32[]{:S(2)}) collective-permute-start(bf16[256,128]{1,0:T(8,128)(2,1)} %copy-done.45), channel_id=1, source_target_pairs={{0,1},{1,2},{2,3},{4,5},{5,6},{6,7},{8,9},{9,10},{10,11},{12,13},{... | collective-permute-start | bytes 196616 | tf_op jit(solution)/shard_map/ppermute | solution.py:32
  56.4 19.9 %collective-permute-start.16 = (bf16[256,128]{1,0:T(8,128)(2,1)}, bf16[256,128]{1,0:T(8,128)(2,1)S(1)}, u32[]{:S(2)}, u32[]{:S(2)}) collective-permute-start(bf16[256,128]{1,0:T(8,128)(2,1)} %copy-done.44), channel_id=1, source_target_pairs={{1,0},{2,1},{3,2},{5,4},{6,5},{7,6},{9,8},{10,9},{11,10},{13,12},{... | collective-permute-start | bytes 196616 | tf_op jit(solution)/shard_map/ppermute | solution.py:32
  59.8 22.0 %collective-permute-start.5 = (bf16[512,512]{1,0:T(8,128)(2,1)}, bf16[512,512]{1,0:T(8,128)(2,1)}, u32[]{:S(2)}, u32[]{:S(2)}) collective-permute-start(bf16[512,512]{1,0:T(8,128)(2,1)} %get-tuple-element.35.refs_12_.refs_5_.refs_8_), channel_id=1, source_target_pairs={{0,4},{4,0},{8,12},{12,8},{1,5},{5,1},{9,13},{13,9},{2,6},{6,2},{1... | collective-permute-start | bytes 1572872 | tf_op jit(solution)/shard_map/ppermute | solution.py:21
  77.0 37.6 %collective-permute-start.25 = (bf16[512,512]{1,0:T(8,128)(2,1)}, bf16[512,512]{1,0:T(8,128)(2,1)}, u32[]{:S(2)}, u32[]{:S(2)}) collective-permute-start(bf16[512,512]{1,0:T(8,128)(2,1)} %get-tuple-element.47.refs_5_.refs_10_), channel_id=1, source_target_pairs={{8,0},{12,4},{0,8},{4,12},{9,1},{13,5},{1,9},{5,13},{10,2},{14,6},... | collective-permute-start | bytes 1572872 | tf_op jit(solution)/shard_map/ppermute | solution.py:26
  79.9 34.6 %collective-permute-start.27 = (bf16[768,128]{1,0:T(8,128)(2,1)}, bf16[768,128]{1,0:T(8,128)(2,1)}, u32[]{:S(2)}, u32[]{:S(2)}) collective-permute-start(bf16[768,128]{1,0:T(8,128)(2,1)} %copy-done.43), channel_id=1, source_target_pairs={{1,0},{2,1},{3,2},{5,4},{6,5},{7,6},{9,8},{10,9},{11,10},{13,12},{... | collective-permute-start | bytes 589832 | tf_op jit(solution)/shard_map/ppermute | solution.py:32
  96.6 17.9 %collective-permute-start.26 = (bf16[768,128]{1,0:T(8,128)(2,1)}, bf16[768,128]{1,0:T(8,128)(2,1)}, u32[]{:S(2)}, u32[]{:S(2)}) collective-permute-start(bf16[768,128]{1,0:T(8,128)(2,1)} %get-tuple-element.48), channel_id=1, source_target_pairs={{0,1},{1,2},{2,3},{4,5},{5,6},{6,7},{8,9},{9,10},{10,11},{12,13},{... | collective-permute-start | bytes 589832 | tf_op jit(solution)/shard_map/ppermute | solution.py:32
  103.6 14.1 %collective-permute-start.24 = (bf16[512,512]{1,0:T(8,128)(2,1)}, bf16[512,512]{1,0:T(8,128)(2,1)S(1)}, u32[]{:S(2)}, u32[]{:S(2)}) collective-permute-start(bf16[512,512]{1,0:T(8,128)(2,1)} %get-tuple-element.47.refs_5_.refs_10_), channel_id=1, source_target_pairs={{0,4},{4,0},{8,12},{12,8},{1,5},{5,1},{9,13},{13,9},{2,6},{6,2},{1... | collective-permute-start | bytes 1572872 | tf_op jit(solution)/shard_map/ppermute | solution.py:21
  115.1 13.5 %collective-permute-start.22 = (bf16[512,512]{1,0:T(8,128)(2,1)S(1)}, bf16[512,512]{1,0:T(8,128)(2,1)S(1)}, u32[]{:S(2)}, u32[]{:S(2)}) collective-permute-start(bf16[512,512]{1,0:T(8,128)(2,1)S(1)} %copy-done.24), channel_id=1, source_target_pairs={{8,0},{12,4},{0,8},{4,12},{9,1},{13,5},{1,9},{5,13},{10,2},{14,6},... | collective-permute-start | bytes 1572872 | tf_op jit(solution)/shard_map/ppermute | solution.py:26
  117.5 13.8 %collective-permute-start.21 = (bf16[512,512]{1,0:T(8,128)(2,1)S(1)}, bf16[512,512]{1,0:T(8,128)(2,1)S(1)}, u32[]{:S(2)}, u32[]{:S(2)}) collective-permute-start(bf16[512,512]{1,0:T(8,128)(2,1)S(1)} %copy-done.24), channel_id=1, source_target_pairs={{0,4},{4,0},{8,12},{12,8},{1,5},{5,1},{9,13},{13,9},{2,6},{6,2},{1... | collective-permute-start | bytes 1572872 | tf_op jit(solution)/shard_map/ppermute | solution.py:21
  (58 other events, 338.4 us)

commit v5 on v4

v5 whole, which is shorter than its diff:
```python
import jax
import jax.numpy as jnp
from jax import lax
from jax.experimental import pallas as pl
from jax.experimental.pallas import tpu as pltpu
from jax.sharding import PartitionSpec as P

NM = 2048
BLK = 128
ITERS = 2
CORES = 2
CHUNKS = 2

VMEM = pl.BlockSpec(memory_space=pltpu.VMEM)
SMEM = pl.BlockSpec(memory_space=pltpu.SMEM)
ANY = pl.BlockSpec(memory_space=pl.ANY)
COST = pl.CostEstimate(flops=1000, bytes_accessed=1000, transcendentals=0)


def swap_cores(x):
    return exchange(x, "mode", 1)


def exchange(x, axis, bit):
    return lax.ppermute(x, axis, [(i, i ^ bit) for i in range(lax.axis_size(axis))])


def from_chip(x, offset):
    n = lax.axis_size("mode")
    return lax.ppermute(x, "mode", [((i + CORES * offset) % n, i) for i in range(n)])


def halos(a, b):
    n = lax.axis_size("space")
    near = [(i, i ^ 1) for i in range(n) if i ^ 1 < n]
    other = [(i, i + 1 if i % 2 else i - 1) for i in range(n) if 0 <= (i + 1 if i % 2 else i - 1) < n]
    return lax.ppermute(a, "space", near), lax.ppermute(b, "space", other)


def after(x, *others):
    return lax.optimization_barrier((x, *others))[0]


def bf16(*shape):
    return jax.ShapeDtypeStruct(shape, jnp.bfloat16)


def call(kernel, out, scratch, operands, specs, megabytes, name, copies):
    return pl.pallas_call(
        kernel,
        out_shape=out,
        in_specs=specs,
        out_specs=(VMEM,) * len(out),
        scratch_shapes=[*scratch, pltpu.SemaphoreType.DMA((copies,))],
        compiler_params=pltpu.CompilerParams(vmem_limit_bytes=megabytes << 20),
        cost_estimate=COST,
        name=name,
    )(*operands)


class Loader:
    def __init__(self, sems):
        self.sems, self.used = sems, 0

    def start(self, src, dst):
        copy = pltpu.make_async_copy(src, dst, self.sems.at[self.used])
        self.used += 1
        copy.start()
        return copy

    def start_one(self, choose, src, other, dst):
        sem = self.sems.at[self.used]
        self.used += 1

        @pl.when(choose)
        def _():
            pltpu.make_async_copy(src, dst, sem).start()

        @pl.when(jnp.logical_not(choose))
        def _():
            pltpu.make_async_copy(other, dst, sem).start()

        return pltpu.make_async_copy(src, dst, sem)


def rows_at(index, count):
    return pl.ds(pl.multiple_of(index * count, count), count)


def as_column(row):
    return jnp.transpose(jnp.broadcast_to(row, (8, row.shape[1])))[:, 0:1]


def flatten_one(nx, ny, x_ref, outs, wide_ref):
    count = x_ref.shape[0] // nx
    tall = nx // len(outs)
    tile = min(count, 64)

    @pl.loop(0, count // tile)
    def _(i):
        at = pl.multiple_of(i * tile, tile)
        wide_ref[0 : tile * nx, :] = x_ref[pl.ds(pl.multiple_of(at * nx, tile * nx), tile * nx), :].astype(jnp.float32)
        for r in range(nx):
            k, c = r // tall, r % tall
            row = wide_ref[pl.ds(r, tile, stride=nx), :].astype(jnp.bfloat16)
            outs[k][pl.ds(at, tile), c * ny : (c + 1) * ny] = row


def flatten_own_kernel(nx, ny, place_ref, e_ref, p_ref, e_out_ref, *refs):
    *outs, a_ref, b_ref, e_in, p_in, wide_ref, sems = refs
    load = Loader(sems)
    e_copy, p_copy = load.start(e_ref, e_in), load.start(p_ref, p_in)
    e_copy.wait()
    flatten_one(nx, ny, e_in, [e_out_ref], wide_ref)
    p_copy.wait()
    flatten_one(nx, ny, p_in, outs, wide_ref)
    e = e_out_ref.shape[0]
    even = place_ref[0] == 0
    for to_ref, last in ((a_ref, even), (b_ref, jnp.logical_not(even))):

        @pl.when(last)
        def _():
            to_ref[0:e, :] = e_out_ref[:, (nx - 1) * ny :]
            to_ref[e:, :] = outs[-1][:, outs[-1].shape[1] - ny :]

        @pl.when(jnp.logical_not(last))
        def _():
            to_ref[0:e, :] = e_out_ref[:, 0:ny]
            to_ref[e:, :] = outs[0][:, 0:ny]


def flatten_others_kernel(nx, ny, count, *refs):
    xs, outs, ins, (wide_ref, sems) = refs[:count], refs[count : 2 * count], refs[2 * count : 3 * count], refs[3 * count :]
    load = Loader(sems)
    copies = [load.start(x, y) for x, y in zip(xs, ins)]
    for copy, x_ref, out_ref in zip(copies, ins, outs):
        copy.wait()
        flatten_one(nx, ny, x_ref, [out_ref], wide_ref)


def lent_kernel(n, e, p, width, ny, shares, count, place_ref, *refs):
    share_refs, refs = refs[:shares], refs[shares:]
    p_refs, refs = refs[: n * CHUNKS], refs[n * CHUNKS :]
    far_ref, a_ref, b_ref, up_ref, rate_ref, out_ref, absorption_ref, sp_ref, own_ref, edge_ref, sems = refs
    load, first, second = Loader(sems), [], []
    even = place_ref[0] == 0
    at = 1 + n
    for share_ref in share_refs:
        for i in range(share_ref.shape[0] // count):
            to = absorption_ref.at[rows_at(place_ref[at], count), :]
            first.append(load.start(share_ref.at[i * count : (i + 1) * count, :], to))
            at += 1
    for k in range(CHUNKS):
        for j in range(n):
            copy = load.start(p_refs[k * n + j], sp_ref.at[k, rows_at(place_ref[1 + j], p), :])
            (second if k else first).append(copy)
        if not k:
            first.append(load.start(far_ref, own_ref))
            beyond = pl.ds(e + p, e)
            first.append(load.start_one(even, b_ref.at[beyond, :], a_ref.at[beyond, :], edge_ref.at[0:e, :]))
            first.append(load.start_one(even, a_ref.at[beyond, :], b_ref.at[beyond, :], edge_ref.at[e:, :]))
    for k in range(CHUNKS):
        for copy in second if k == 1 else [] if k else first:
            copy.wait()
        gain = jnp.dot(absorption_ref[...], sp_ref[k], preferred_element_type=jnp.float32)
        start, stop = k * width, (k + 1) * width
        own = own_ref[:, start:stop].astype(jnp.float32)
        low = (own_ref[:, start - ny : start] if k else edge_ref[0:e, :]).astype(jnp.float32)
        high = (own_ref[:, stop : stop + ny] if k + 1 < CHUNKS else edge_ref[e:, :]).astype(jnp.float32)
        lower = jnp.concatenate([low, own[:, : width - ny]], axis=1) if width > ny else low
        higher = jnp.concatenate([own[:, ny:], high], axis=1) if width > ny else high
        f_up = jnp.where(up_ref[:, start:stop] == 1, lower, higher)
        speed, rate = as_column(rate_ref[0:1, :]), as_column(rate_ref[1:2, :])
        new = (own - speed * (own - f_up) + 0.5 * gain) / (1.0 + rate)
        out_ref[:, start:stop] = new.astype(jnp.bfloat16)


def step_kernel(n, e, p, width, ny, nx, k, cols, edges, last, place_ref, *refs):
    refs = list(refs)

    def take(count):
        taken = refs[:count]
        del refs[:count]
        return taken

    e_refs, p_refs, before, behind = take(n), take(n), take(2), take(2)
    emission_hbm, absorption_hbm, dense_hbm, up_ref, speed_ref, diffusion_ref, e_rate_ref, p_rate_ref = take(8)
    done = take(2 * (CHUNKS - 1)) if last else []
    border = take(3 if edges == 3 else 2) if edges else []
    e_out_ref, p_out_ref = take(2)
    to_refs = take(2) if edges else []
    se_ref, sp_ref, emission_ref, absorption_ref, dense_ref, low_ref, high_ref = take(7)
    done_ref, wide_ref = take(2) if last else (None, None)
    first_ref, final_ref = take(2) if edges else (None, None)
    load = Loader(refs[0])
    tall = width // ny
    even = place_ref[0] == 0
    me = place_ref[1]

    early = [load.start(absorption_hbm, absorption_ref)]
    for j in range(n):
        early.append(load.start(p_refs[j], sp_ref.at[rows_at(place_ref[1 + j], p), :]))
    for j in range(n):
        late_e = load.start(e_refs[j].at[:, cols[j] : cols[j] + width], se_ref.at[rows_at(place_ref[1 + j], e), :])
        early.append(late_e)
    if k == 0:
        early.append(load.start_one(even, before[1].at[0 : e + p, :], before[0].at[0 : e + p, :], low_ref))
    else:
        early.append(load.start(before[0].at[:, pl.ds((cols[0] or before[0].shape[1]) - ny, ny)], low_ref.at[0:e, :]))
        early.append(load.start(before[1].at[:, width - ny : width], low_ref.at[e:, :]))
    if k == CHUNKS - 1:
        early.append(load.start_one(even, behind[0].at[0 : e + p, :], behind[1].at[0 : e + p, :], high_ref))
    else:
        next_col = cols[0] + width if behind[0].shape[1] > width else 0
        early.append(load.start(behind[0].at[:, next_col : next_col + ny], high_ref.at[0:e, :]))
        early.append(load.start(behind[1].at[:, 0:ny], high_ref.at[e:, :]))
    late = [load.start(emission_hbm, emission_ref), load.start(dense_hbm, dense_ref)]
    for i, array in enumerate(done):
        place = i // 2
        to = done_ref.at[place, 0:e, :] if i % 2 == 0 else done_ref.at[place, e:, :]
        late.append(load.start(array, to))
    if edges:
        late.append(load.start(border[0].at[:, 0:ny], first_ref.at[0:e, :]))
        late.append(load.start(border[1].at[:, 0:ny], first_ref.at[e : e + p, :]))
        if edges == 3:
            late.append(load.start(border[2].at[:, 0:ny], first_ref.at[e + p :, :]))
            late.append(load.start(border[2].at[:, (nx - 1) * ny :], final_ref.at[e + p :, :]))
    tile = min(p, 256)

    def around(x_ref, rows, base):
        own = x_ref[rows, :].astype(jnp.float32)
        low, high = low_ref[base, :].astype(jnp.float32), high_ref[base, :].astype(jnp.float32)
        lower = jnp.concatenate([low, own[:, : width - ny]], axis=1) if width > ny else low
        higher = jnp.concatenate([own[:, ny:], high], axis=1) if width > ny else high
        return own, lower, higher

    def store(new, at, count, base):
        out_ref = p_out_ref if base else e_out_ref
        if not last:
            new = new.astype(jnp.bfloat16)
            out_ref[at : at + count, :] = new
            if edges:
                final_ref[base + at : base + at + count, :] = new[:, width - ny :]
            return
        for c in range(CHUNKS - 1):
            old = done_ref[c, base + at : base + at + count, :].astype(jnp.float32)
            for r in range(tall):
                wide_ref[pl.ds(c * tall + r, count, stride=nx), :] = old[:, r * ny : (r + 1) * ny]
        for r in range(tall):
            wide_ref[pl.ds(nx - tall + r, count, stride=nx), :] = new[:, r * ny : (r + 1) * ny]
        out_ref[at * nx : (at + count) * nx, :] = wide_ref[0 : count * nx, :].astype(jnp.bfloat16)

    for copy in early:
        copy.wait()
    gain = jnp.dot(absorption_ref[...], sp_ref[...], preferred_element_type=jnp.float32)
    own, lower, higher = around(se_ref, rows_at(me, e), pl.ds(0, e))
    f_up = jnp.where(up_ref[...] == 1, lower, higher)
    new = (own - as_column(speed_ref[...]) * (own - f_up) + 0.5 * gain) / (1.0 + as_column(e_rate_ref[...]))
    for copy in late:
        copy.wait()
    store(new, 0, e, 0)

    for at in range(0, p, tile):
        source = jnp.dot(
            emission_ref[at : at + tile, :], se_ref[...], preferred_element_type=jnp.float32
        ) + jnp.dot(dense_ref[at : at + tile, :], sp_ref[...], preferred_element_type=jnp.float32)
        rows = pl.ds(pl.multiple_of(me * p + at, tile), tile)
        own, lower, higher = around(sp_ref, rows, pl.ds(e + at, tile))
        column = lax.broadcasted_iota(jnp.int32, (tile, ny), 1)
        left, right = [], []
        for r in range(tall):
            row = own[:, r * ny : (r + 1) * ny]
            left.append(jnp.where(column == 0, 0.0, pltpu.roll(row, 1, 1)))
            right.append(jnp.where(column == ny - 1, 0.0, pltpu.roll(row, ny - 1, 1)))
        left, right = jnp.concatenate(left, axis=1), jnp.concatenate(right, axis=1)
        lap = lower + higher + left + right - 4.0 * own
        diffusion, rate = as_column(diffusion_ref[:, at : at + tile]), as_column(p_rate_ref[:, at : at + tile])
        store((own + diffusion * lap + 0.5 * source) / (1.0 + rate), at, tile, e)

    if edges:
        for to_ref, is_final in ((to_refs[0], even), (to_refs[1], jnp.logical_not(even))):

            @pl.when(is_final)
            def _():
                to_ref[...] = final_ref[...]

            @pl.when(jnp.logical_not(is_final))
            def _():
                to_ref[...] = first_ref[...]


def on_device(
    electrons,
    phonons,
    emission,
    absorption,
    block_coupling,
    block_cols,
    upwind,
    speed,
    diffusion,
    electron_rate,
    phonon_rate,
):
    e, nx, ny = electrons.shape
    p = phonons.shape[0]
    n = lax.axis_size("mode")
    chips = n // CORES
    slots = block_coupling.shape[1]
    b_rows = p // BLK
    tall = nx // CHUNKS
    width = tall * ny
    lanes = pltpu.VMEM((64 * nx, ny), jnp.float32)
    groups, spaces = lax.axis_size("grp"), lax.axis_size("space")
    me, space, grp = (lax.axis_index(a).astype(jnp.uint32) for a in ("mode", "space", "grp"))
    chip, core = me // CORES, me % CORES
    places = [space % 2] + [((chip + d) % chips) * CORES + (core ^ c) for d in range(chips) for c in range(CORES)]

    bits = [("grp", b) for b in (1, 2, 4, 8) if b < groups] + [("space", b) for b in (1, 2, 4, 8) if b < spaces]
    lend = chips == 2 and 1 << len(bits) == groups * spaces and e % (16 * groups * spaces) == 0 and len(bits) > 0
    near_e = swap_cores(electrons)
    far_e = [from_chip(electrons, d) for d in range(1, chips)]
    if lend:
        count = e // (groups * spaces)
        start = (grp * spaces + space) * count
        shares = [from_chip(lax.dynamic_slice(absorption, (start, jnp.zeros_like(start)), (count, NM)), 1)]
        far_rates = from_chip(jnp.stack([speed, electron_rate]), 1)
        own_share, held = shares[0], [(0, 0)]
        for axis, bit in bits:
            whole = jnp.concatenate(shares, axis=0) if len(shares) > 1 else shares[0]
            shares = [whole, exchange(whole, axis, bit)]
            held = held + [(g ^ bit, s) if axis == "grp" else (g, s ^ bit) for g, s in held]
        places += [(grp ^ g) * spaces + (space ^ s) for g, s in held]
    places = jnp.stack(places).astype(jnp.int32)

    e_all, *p_chunks, to_a, to_b = call(
        lambda *refs: flatten_own_kernel(nx, ny, *refs),
        (bf16(e, nx * ny),) + (bf16(p, width),) * CHUNKS + (bf16(e + p, ny),) * 2,
        [pltpu.VMEM((e * nx, ny), jnp.bfloat16), pltpu.VMEM((p * nx, ny), jnp.bfloat16), lanes],
        (places, electrons.reshape(e * nx, ny), phonons.reshape(p * nx, ny)), [SMEM, ANY, ANY], 8, "flatten", 2,
    )
    block_coupling = after(block_coupling, p_chunks[0])
    kernel = block_coupling.reshape(b_rows, BLK, slots, BLK)
    block_ids = jnp.arange(NM // BLK, dtype=jnp.int32)
    hits = (block_cols[:, :, None] == block_ids[None, None, :]).astype(jnp.bfloat16)
    dense = jnp.einsum(
        "bsk,bisj->bikj", hits, kernel, preferred_element_type=jnp.float32
    ).astype(jnp.bfloat16).reshape(p, NM)

    ups = [upwind[k * tall : (k + 1) * tall].reshape(1, width) for k in range(CHUNKS)]
    weights = (emission, absorption, dense)
    rates = (speed[None], diffusion[None], electron_rate[None], phonon_rate[None])

    def step(k, es, ps, before, behind, done, border):
        last, edges = bool(done), len(border)
        done = [x for d in done for x in d]
        operands = (
            places, *(x for x, _ in es), *ps, *before, *behind, *weights, ups[k], *rates, *done, *border,
        )
        specs = [SMEM] + [ANY] * (2 * n + 7) + [VMEM] * 5 + [ANY] * (len(done) + edges)
        scratch = [
            pltpu.VMEM(shape, jnp.bfloat16)
            for shape in (
                (n * e, width), (n * p, width), (p, n * e), (e, n * p), (p, NM), (e + p, ny), (e + p, ny)
            )
        ]
        if last:
            out = (bf16(e * nx, ny), bf16(p * nx, ny))
            scratch += [
                pltpu.VMEM((CHUNKS - 1, e + p, width), jnp.bfloat16),
                pltpu.VMEM((max(e, min(p, 256)) * nx, ny), jnp.float32),
            ]
        else:
            edge_rows = e + p + (e if edges == 3 else 0)
            out = (bf16(e, width), bf16(p, width)) + (bf16(edge_rows, ny),) * (2 if edges else 0)
            scratch += [pltpu.VMEM((edge_rows, ny), jnp.bfloat16)] * (2 if edges else 0)
        return call(
            lambda *refs: step_kernel(n, e, p, width, ny, nx, k, [c for _, c in es], edges, last, *refs),
            out, scratch, operands, specs, 28, "step", 2 * n + 7 + len(done) + edges + 1,
        )

    def gathered(own, far, wait_for):
        arrays = [own, swap_cores(own)]
        for f in far:
            f = after(f, *wait_for)
            arrays += [f, swap_cores(f)]
        return arrays

    halo = halos(to_a, to_b)
    far_p = [[from_chip(c, d) for d in range(1, chips)] for c in p_chunks]
    others = [near_e]
    for f in far_e:
        f = after(f, p_chunks[0], *((own_share, far_rates) if lend else ()))
        others += [f, swap_cores(f)]
    others = call(
        lambda *refs: flatten_others_kernel(nx, ny, n - 1, *refs), (bf16(e, nx * ny),) * (n - 1),
        [pltpu.VMEM((e * nx, ny), jnp.bfloat16)] * (n - 1) + [lanes],
        [x.reshape(e * nx, ny) for x in others], [ANY] * (n - 1), 12, "flatten", n - 1,
    )
    everyone = [e_all, *others]
    waits = (dense, *halo, everyone[1])
    new, every_p = [], []
    for k in range(CHUNKS):
        ps = gathered(p_chunks[k], far_p[k], waits)
        new.append(step(
            k, [(x, k * width) for x in everyone], ps, (e_all, p_chunks[k - 1]) if k else halo,
            (e_all, p_chunks[k + 1]) if k + 1 < CHUNKS else halo, [],
            () if k + 1 < CHUNKS else (*new[0][:2], *([everyone[2]] if lend else [])),
        ))
        every_p += ps
        waits = (new[-1][1], *(shares if lend else ()))
    halo = halos(new[-1][2], new[-1][3])
    chunks = [c[:2] for c in new]

    far_p = [[from_chip(c[1], d) for d in range(1, chips)] for c in chunks]
    ready = (chunks[-1][1], *halo)
    if lend:
        operands = (places, *shares, *every_p, everyone[2], *halo, upwind.reshape(1, nx * ny), far_rates)
        (lent,) = call(
            lambda *refs: lent_kernel(n, e, p, width, ny, 2, count, *refs), (bf16(e, nx * ny),),
            [
                pltpu.VMEM(shape, jnp.bfloat16)
                for shape in ((e, NM), (CHUNKS, n * p, width), (e, nx * ny), (2 * e, ny))
            ],
            operands, [SMEM] + [ANY] * (len(operands) - 3) + [VMEM, VMEM], 16, "lent",
            groups * spaces + n * CHUNKS + 3,
        )
        lent = [lent, swap_cores(lent)]
        ready += (lent[0],)
    else:
        far_e = [[from_chip(c[0], d) for d in range(1, chips)] for c in chunks]
    done = []
    for k in range(CHUNKS):
        waits = (done[-1][1],) if k else ready
        if lend:
            es = [(chunks[k][0], 0), (swap_cores(chunks[k][0]), 0)] + [(x, k * width) for x in lent]
        else:
            es = [(x, 0) for x in gathered(chunks[k][0], far_e[k], waits)]
        done.append(step(
            k, es, gathered(chunks[k][1], far_p[k], waits), chunks[k - 1] if k else halo,
            chunks[k + 1] if k + 1 < CHUNKS else halo, done if k + 1 == CHUNKS else [], (),
        ))
    return done[-1][0].reshape(e, nx, ny), done[-1][1].reshape(p, nx, ny)


def solution(mesh):
    placed = (
        P("mode", ("grp", "space"), None),
        P("mode", ("grp", "space"), None),
        P("mode", None),
        P("mode", None),
        P("mode", None, None),
        P("mode", None),
        P(("grp", "space"), None),
        P("mode"),
        P("mode"),
        P("mode"),
        P("mode"),
    )
    return jax.shard_map(
        on_device,
        mesh=mesh,
        in_specs=placed,
        out_specs=(P("mode", ("grp", "space"), None), P("mode", ("grp", "space"), None)),
        check_vma=False,
    )
```

time: 139 us -> 110 us (0.79); the launches traced: 137 us -> 110 us
  local copies, waits for them, and re-layouts: 44.5 us -> 3.89 us
  waiting for transfers between devices: 19.3 us -> 49.4 us
  starting transfers between devices: 40.3 us -> 27.3 us
  Pallas kernels: 27.9 us -> 25.5 us
    unnamed x108 -> x23, local copies, waits for them, and re-layouts: 36.4 us -> 2.87 us
    ppermute x23 -> x20, waiting for transfers between devices: 9.53 us -> 37.7 us  [the longest x16 23.2 us: exchange(): lax.ppermute(x, axis, [(i, i ^ bit) for i in range(lax.axis_size(axis))])]
    ppermute x23 -> x20, starting transfers between devices: 35.5 us -> 23.4 us  [the longest x16 13.2 us: exchange(): lax.ppermute(x, axis, [(i, i ^ bit) for i in range(lax.axis_size(axis))])]
    another operation x4 -> x1, local copies, waits for them, and re-layouts: 3.98 us -> 0.09 us  [on_device(): places = jnp.stack(places).astype(jnp.int32)]
    broadcast_in_dim x4 -> x0, local copies, waits for them, and re-layouts: 2.62 us -> none  [on_device(): rates = (x[:, None] for x in (speed, diffusion, electron_rate, phonon_rate))]
    pallas_call x7, Pallas kernels: 27.9 us -> 25.5 us  [call(): pl.pallas_call(kernel, out_shape=out, in_specs=specs, out_specs=(VMEM,) *...]
    ppermute x7, waiting for transfers between devices: 9.72 us -> 11.7 us  [from_chip(): lax.ppermute(x, 'mode', [((i + CORES * offset) % n, i) for i in range(n)])]
  transfers between devices with their start and end apart: 30 -> 27, of which waited for: 6 -> 10; matrix products, arithmetic and copies ran while one was open for 11% -> 4% of each run, Pallas kernels for 16% -> 18%
where the time goes in v5:
time: 110 us
  waiting for transfers between devices  49.4 us (45%)
  starting transfers between devices  27.3 us (25%)
  Pallas kernels  25.5 us (23%)
  local copies, waits for them, and re-layouts  3.89 us (4%)
  matrix products  1.83 us (2%)
    pallas_call x7, Pallas kernels, call(): pl.pallas_call(kernel, out_shape=out, in_specs=specs, out_specs=(VMEM,) *...  25.5 us
    ppermute x16, waiting for transfers between devices, exchange(): lax.ppermute(x, axis, [(i, i ^ bit) for i in range(lax.axis_size(axis))])  23.2 us
    ppermute x4, waiting for transfers between devices, halos(): return (lax.ppermute(a, 'space', near), lax.ppermute(b, 'space', other))  14.5 us
    ppermute x16, starting transfers between devices, exchange(): lax.ppermute(x, axis, [(i, i ^ bit) for i in range(lax.axis_size(axis))])  13.2 us
    ppermute x7, waiting for transfers between devices, from_chip(): lax.ppermute(x, 'mode', [((i + CORES * offset) % n, i) for i in range(n)])  11.7 us
    ppermute x4, starting transfers between devices, halos(): return (lax.ppermute(a, 'space', near), lax.ppermute(b, 'space', other))  10.2 us
    ppermute x7, starting transfers between devices, from_chip(): lax.ppermute(x, 'mode', [((i + CORES * offset) % n, i) for i in range(n)])  3.86 us
    unnamed x23, local copies, waits for them, and re-layouts  2.87 us
  transfers between devices with their start and end apart: 27, of which 10 were waited for; matrix products, arithmetic and copies ran while one was open for 4% of the time, Pallas kernels for 18%

profile of v5, /device:TPU:13, one launch (start us, length us, event | category | flops | bytes accessed | tf_op | source)
XLA Modules:
  0.0 109.7 jit_solution(18332063180524631890)
XLA Ops:
  1.8 1.3 %collective-permute-start.2 = (bf16[32,2048]{1,0:T(8,128)(2,1)S(1)}, bf16[32,2048]{1,0:T(8,128)(2,1)S(1)}, u32[]{:S(2)}, u32[]{:S(2)}) collective-permute-start(bf16[32,2048]{1,0:T(8,128)(2,1)S(1)} %constant_dynamic-slice_fusion), channel_id=1, source_target_pairs={{8,0},{12,4},{0,8},{4,12},{9,1},{13,5},{1,9},{5,13},{10,2},{14,6},... | collective-permute-start | bytes 393224 | tf_op jit(solution)/shard_map/ppermute | solution.py:30
  7.7 1.6 %flatten.2 = (bf16[256,1024]{1,0:T(8,128)(2,1)S(1)}, bf16[512,512]{1,0:T(8,128)(2,1)S(1)}, bf16[512,512]{1,0:T(8,128)(2,1)S(1)}, bf16[768,128]{1,0:T(8,128)(2,1)S(1)}, bf16[768,128]{1,0:T(8,128)(2,1)S(1)}) custom-call(s32[13]{0:T(128)S(1)} %convert_element_type.31.refs_0_, bf16[2048,128]{1,0:T(8,128)(2,1)S(1)} %bitcast.47, bf16[4096,128]{1,0:T(8,128)(2,1)S(1)} %bitcast.43), custom_call_target="tpu_custom_call" | custom-call | flops 1000 | bytes 1000 | tf_op jit(solution)/shard_map/flatten/pallas_call | solution.py:49
  9.3 1.3 %collective-permute-start.8 = (bf16[512,512]{1,0:T(8,128)(2,1)S(1)}, bf16[512,512]{1,0:T(8,128)(2,1)S(1)}, u32[]{:S(2)}, u32[]{:S(2)}) collective-permute-start(bf16[512,512]{1,0:T(8,128)(2,1)S(1)} %get-tuple-element.27.refs_5_.refs_10_.refs_3_), channel_id=1, source_target_pairs={{8,0},{12,4},{0,8},{4,12},{9,1},{13,5},{1,9},{5,13},{10,2},{14,6},... | collective-permute-start | bytes 1572872 | tf_op jit(solution)/shard_map/ppermute | solution.py:30
  10.6 5.9 %collective-permute-done.2 = bf16[32,2048]{1,0:T(8,128)(2,1)S(1)} collective-permute-done((bf16[32,2048]{1,0:T(8,128)(2,1)S(1)}, bf16[32,2048]{1,0:T(8,128)(2,1)S(1)}, u32[]{:S(2)}, u32[]{:S(2)}) %collective-permute-start.2) | collective-permute-done | bytes 131104 | tf_op jit(solution)/shard_map/ppermute | solution.py:30
  17.7 1.8 %fusion.2 = bf16[4,128,128,16]{2,3,1,0:T(8,128)(2,1)S(1)} fusion(bf16[4,128,12,128]{3,1,0,2:T(8,128)(2,1)S(1)} %bitcast.72, s32[4,12]{1,0:T(4,128)} %param.16), kind=kOutput, calls=%fused_computation.3 | convolution fusion | flops 26215168 | bytes 3670208 | tf_op jit(solution)/shard_map/bsk,bisj->bikj/dot_general | solution.py:346
  20.2 3.3 %collective-permute-start.10 = (bf16[768,128]{1,0:T(8,128)(2,1)S(1)}, bf16[768,128]{1,0:T(8,128)(2,1)S(1)}, u32[]{:S(2)}, u32[]{:S(2)}) collective-permute-start(bf16[768,128]{1,0:T(8,128)(2,1)S(1)} %get-tuple-element.35), channel_id=1, source_target_pairs={{1,2},{2,1},{5,6},{6,5},{9,10},{10,9},{13,14},{14,13},{17,18},{18,... | collective-permute-start | bytes 589832 | tf_op jit(solution)/shard_map/ppermute | solution.py:37
  23.6 3.3 %collective-permute-start.4 = (bf16[256,8,128]{2,1,0:T(8,128)(2,1)S(1)}, bf16[256,8,128]{2,1,0:T(8,128)(2,1)S(1)}, u32[]{:S(2)}, u32[]{:S(2)}) collective-permute-start(bf16[256,8,128]{2,1,0:T(8,128)(2,1)S(1)} %collective-permute-done.1), channel_id=1, source_target_pairs={{0,4},{4,0},{8,12},{12,8},{1,5},{5,1},{9,13},{13,9},{2,6},{6,2},{1... | collective-permute-start | bytes 1572872 | tf_op jit(solution)/shard_map/ppermute | solution.py:25
  27.0 1.5 %collective-permute-start.9 = (bf16[768,128]{1,0:T(8,128)(2,1)S(1)}, bf16[768,128]{1,0:T(8,128)(2,1)S(1)}, u32[]{:S(2)}, u32[]{:S(2)}) collective-permute-start(bf16[768,128]{1,0:T(8,128)(2,1)S(1)} %get-tuple-element.34), channel_id=1, source_target_pairs={{0,1},{1,0},{2,3},{3,2},{4,5},{5,4},{6,7},{7,6},{8,9},{9,8},{10,11... | collective-permute-start | bytes 589832 | tf_op jit(solution)/shard_map/ppermute | solution.py:37
  30.5 8.6 %collective-permute-done.9.refs_9_.refs_11_ = bf16[768,128]{1,0:T(8,128)(2,1)S(1)} collective-permute-done((bf16[768,128]{1,0:T(8,128)(2,1)S(1)}, bf16[768,128]{1,0:T(8,128)(2,1)S(1)}, u32[]{:S(2)}, u32[]{:S(2)}) %collective-permute-start.9) | collective-permute-done | bytes 196640 | tf_op jit(solution)/shard_map/ppermute | solution.py:37
  41.5 4.2 %step.4 = (bf16[256,512]{1,0:T(8,128)(2,1)S(1)}, bf16[512,512]{1,0:T(8,128)(2,1)S(1)}) custom-call(s32[13]{0:T(128)S(1)} %convert_element_type.31.refs_0_, bf16[256,1024]{1,0:T(8,128)(2,1)S(1)} %get-tuple-element.26.refs_1_.refs_11_.refs_9_, bf16[256,1024]{1,0:T(8,128)(2,1)S(1)} %get-tuple-element.29.refs_2_, ...), custom_call_target="tpu_custom_call" | custom-call | flops 1000 | bytes 1000 | tf_op jit(solution)/shard_map/step/pallas_call | solution.py:49
  45.7 17.0 %collective-permute-done.14.refs_2_ = bf16[128,2048]{1,0:T(8,128)(2,1)S(1)} collective-permute-done((bf16[128,2048]{1,0:T(8,128)(2,1)S(1)}, bf16[128,2048]{1,0:T(8,128)(2,1)S(1)}, u32[]{:S(2)}, u32[]{:S(2)}) %collective-permute-start.14) | collective-permute-done | bytes 524320 | tf_op jit(solution)/shard_map/ppermute | solution.py:25
  63.6 1.3 %collective-permute-done.15.refs_8_.refs_10_ = bf16[512,512]{1,0:T(8,128)(2,1)S(1)} collective-permute-done((bf16[512,512]{1,0:T(8,128)(2,1)S(1)}, bf16[512,512]{1,0:T(8,128)(2,1)S(1)}, u32[]{:S(2)}, u32[]{:S(2)}) %collective-permute-start.15) | collective-permute-done | bytes 524320 | tf_op jit(solution)/shard_map/ppermute | solution.py:25
  64.9 4.3 %step.5 = (bf16[256,512]{1,0:T(8,128)(2,1)S(1)}, bf16[512,512]{1,0:T(8,128)(2,1)S(1)}, bf16[1024,128]{1,0:T(8,128)(2,1)S(1)}, bf16[1024,128]{1,0:T(8,128)(2,1)S(1)}) custom-call(s32[13]{0:T(128)S(1)} %convert_element_type.31.refs_0_, bf16[256,1024]{1,0:T(8,128)(2,1)S(1)} %get-tuple-element.26.refs_1_.refs_11_.refs_9_, ...), custom_call_target="tpu_custom_call" | custom-call | flops 1000 | bytes 1000 | tf_op jit(solution)/shard_map/step/pallas_call | solution.py:49
  69.2 3.2 %collective-permute-start.17 = (bf16[1024,128]{1,0:T(8,128)(2,1)S(1)}, bf16[1024,128]{1,0:T(8,128)(2,1)S(1)}, u32[]{:S(2)}, u32[]{:S(2)}) collective-permute-start(bf16[1024,128]{1,0:T(8,128)(2,1)S(1)} %get-tuple-element.41), channel_id=1, source_target_pairs={{0,1},{1,0},{2,3},{3,2},{4,5},{5,4},{6,7},{7,6},{8,9},{9,8},{10,11... | collective-permute-start | bytes 786440 | tf_op jit(solution)/shard_map/ppermute | solution.py:37
  72.5 2.1 %collective-permute-start.18 = (bf16[1024,128]{1,0:T(8,128)(2,1)S(1)}, bf16[1024,128]{1,0:T(8,128)(2,1)S(1)}, u32[]{:S(2)}, u32[]{:S(2)}) collective-permute-start(bf16[1024,128]{1,0:T(8,128)(2,1)S(1)} %get-tuple-element.42), channel_id=1, source_target_pairs={{1,2},{2,1},{5,6},{6,5},{9,10},{10,9},{13,14},{14,13},{17,18},{18,... | collective-permute-start | bytes 786440 | tf_op jit(solution)/shard_map/ppermute | solution.py:37
  75.6 3.2 %collective-permute-done.17.refs_12_.refs_9_.refs_11_ = bf16[1024,128]{1,0:T(8,128)(2,1)S(1)} collective-permute-done((bf16[1024,128]{1,0:T(8,128)(2,1)S(1)}, bf16[1024,128]{1,0:T(8,128)(2,1)S(1)}, u32[]{:S(2)}, u32[]{:S(2)}) %collective-permute-start.17) | collective-permute-done | bytes 262176 | tf_op jit(solution)/shard_map/ppermute | solution.py:37
  78.8 2.7 %collective-permute-done.18.refs_13_.refs_10_.refs_12_ = bf16[1024,128]{1,0:T(8,128)(2,1)S(1)} collective-permute-done((bf16[1024,128]{1,0:T(8,128)(2,1)S(1)}, bf16[1024,128]{1,0:T(8,128)(2,1)S(1)}, u32[]{:S(2)}, u32[]{:S(2)}) %collective-permute-start.18) | collective-permute-done | bytes 262176 | tf_op jit(solution)/shard_map/ppermute | solution.py:37
  81.5 4.2 %lent.1.refs_3_ = bf16[256,1024]{1,0:T(8,128)(2,1)S(1)} custom-call(s32[13]{0:T(128)S(1)} %convert_element_type.31.refs_0_, bf16[128,2048]{1,0:T(8,128)(2,1)S(1)} %constant_dynamic-update-slice_fusion.refs_1_, bf16[128,2048]{1,0:T(8,128)(2,1)S(1)} %collective-permute-done.14.refs_2_, bf16[512,512]{1,0:T(8,128)(2,1)S(1)} %get-tuple-element.27.refs_5_.refs_10_.refs_3_, ...), custom_call_target="tpu_custom_call" | custom-call | flops 1000 | bytes 1000 | tf_op jit(solution)/shard_map/lent/pallas_call | solution.py:49
  85.8 1.6 %collective-permute-start.25 = (bf16[512,512]{1,0:T(8,128)(2,1)S(1)}, bf16[512,512]{1,0:T(8,128)(2,1)S(1)}, u32[]{:S(2)}, u32[]{:S(2)}) collective-permute-start(bf16[512,512]{1,0:T(8,128)(2,1)S(1)} %collective-permute-done.24.refs_7_), channel_id=1, source_target_pairs={{0,4},{4,0},{8,12},{12,8},{1,5},{5,1},{9,13},{13,9},{2,6},{6,2},{1... | collective-permute-start | bytes 1572872 | tf_op jit(solution)/shard_map/ppermute | solution.py:25
  88.4 1.7 %collective-permute-done.22.refs_2_ = bf16[256,512]{1,0:T(8,128)(2,1)S(1)} collective-permute-done((bf16[256,512]{1,0:T(8,128)(2,1)S(1)}, bf16[256,512]{1,0:T(8,128)(2,1)S(1)}, u32[]{:S(2)}, u32[]{:S(2)}) %collective-permute-start.22) | collective-permute-done | bytes 262176 | tf_op jit(solution)/shard_map/ppermute | solution.py:25
  90.4 4.4 %step.6 = (bf16[256,512]{1,0:T(8,128)(2,1)S(1)}, bf16[512,512]{1,0:T(8,128)(2,1)S(1)}) custom-call(s32[13]{0:T(128)S(1)} %convert_element_type.31.refs_0_, bf16[256,512]{1,0:T(8,128)(2,1)S(1)} %get-tuple-element.39.refs_21_.refs_1_.refs_9_, bf16[256,512]{1,0:T(8,128)(2,1)S(1)} %collective-permute-done.22.refs_2_, bf16[256,1024]{1,0:T(8,128)(2,1)S(1)} %lent.1.refs_3_, ...), custom_call_target="tpu_custom_call" | custom-call | flops 1000 | bytes 1000 | tf_op jit(solution)/shard_map/step/pallas_call | solution.py:49
  94.8 5.7 %collective-permute-done.21.refs_7_ = bf16[512,512]{1,0:T(8,128)(2,1)S(1)} collective-permute-done((bf16[512,512]{1,0:T(8,128)(2,1)S(1)}, bf16[512,512]{1,0:T(8,128)(2,1)S(1)}, u32[]{:S(2)}, u32[]{:S(2)}) %collective-permute-start.21) | collective-permute-done | bytes 524320 | tf_op jit(solution)/shard_map/ppermute | solution.py:30
  101.8 1.9 %collective-permute-done.16.refs_2_ = bf16[256,512]{1,0:T(8,128)(2,1)S(1)} collective-permute-done((bf16[256,512]{1,0:T(8,128)(2,1)S(1)}, bf16[256,512]{1,0:T(8,128)(2,1)S(1)}, u32[]{:S(2)}, u32[]{:S(2)}) %collective-permute-start.16) | collective-permute-done | bytes 262176 | tf_op jit(solution)/shard_map/ppermute | solution.py:25
  103.7 5.8 %step.7 = (bf16[2048,128]{1,0:T(8,128)(2,1)}, bf16[4096,128]{1,0:T(8,128)(2,1)}) custom-call(s32[13]{0:T(128)S(1)} %convert_element_type.31.refs_0_, bf16[256,512]{1,0:T(8,128)(2,1)S(1)} %get-tuple-element.40.refs_11_.refs_1_, bf16[256,512]{1,0:T(8,128)(2,1)S(1)} %collective-permute-done.16.refs_2_, bf16[256,1024]{1,0:T(8,128)(2,1)S(1)} %lent.1.refs_3_, ...), custom_call_target="tpu_custom_call" | custom-call | flops 1000 | bytes 1000 | tf_op jit(solution)/shard_map/step/pallas_call | solution.py:49
  (68 shorter events, 16.5 us)
Async XLA Ops:
  0.6 22.9 %collective-permute-start.1 = (bf16[256,8,128]{2,1,0:T(8,128)(2,1)}, bf16[256,8,128]{2,1,0:T(8,128)(2,1)S(1)}, u32[]{:S(2)}, u32[]{:S(2)}) collective-permute-start(bf16[256,8,128]{2,1,0:T(8,128)(2,1)} %param.11), channel_id=1, source_target_pairs={{8,0},{12,4},{0,8},{4,12},{9,1},{13,5},{1,9},{5,13},{10,2},{14,6},... | collective-permute-start | bytes 1572872 | tf_op jit(solution)/shard_map/ppermute | solution.py:30
  1.8 14.7 %collective-permute-start.2 = (bf16[32,2048]{1,0:T(8,128)(2,1)S(1)}, bf16[32,2048]{1,0:T(8,128)(2,1)S(1)}, u32[]{:S(2)}, u32[]{:S(2)}) collective-permute-start(bf16[32,2048]{1,0:T(8,128)(2,1)S(1)} %constant_dynamic-slice_fusion), channel_id=1, source_target_pairs={{8,0},{12,4},{0,8},{4,12},{9,1},{13,5},{1,9},{5,13},{10,2},{14,6},... | collective-permute-start | bytes 393224 | tf_op jit(solution)/shard_map/ppermute | solution.py:30
  3.1 23.9 %collective-permute-start = (bf16[256,8,128]{2,1,0:T(8,128)(2,1)}, bf16[256,8,128]{2,1,0:T(8,128)(2,1)S(1)}, u32[]{:S(2)}, u32[]{:S(2)}) collective-permute-start(bf16[256,8,128]{2,1,0:T(8,128)(2,1)} %param.11), channel_id=1, source_target_pairs={{0,4},{4,0},{8,12},{12,8},{1,5},{5,1},{9,13},{13,9},{2,6},{6,2},{1... | collective-permute-start | bytes 1572872 | tf_op jit(solution)/shard_map/ppermute | solution.py:25
  5.1 15.1 %collective-permute-start.3 = (f32[2,256]{1,0:T(2,128)S(1)}, f32[2,256]{1,0:T(2,128)S(1)}, u32[]{:S(2)}, u32[]{:S(2)}) collective-permute-start(f32[2,256]{1,0:T(2,128)S(1)} %pad_maximum_fusion.1), channel_id=1, source_target_pairs={{8,0},{12,4},{0,8},{4,12},{9,1},{13,5},{1,9},{5,13},{10,2},{14,6},... | collective-permute-start | bytes 6152 | tf_op jit(solution)/shard_map/ppermute | solution.py:30
  9.3 29.8 %collective-permute-start.8 = (bf16[512,512]{1,0:T(8,128)(2,1)S(1)}, bf16[512,512]{1,0:T(8,128)(2,1)S(1)}, u32[]{:S(2)}, u32[]{:S(2)}) collective-permute-start(bf16[512,512]{1,0:T(8,128)(2,1)S(1)} %get-tuple-element.27.refs_5_.refs_10_.refs_3_), channel_id=1, source_target_pairs={{8,0},{12,4},{0,8},{4,12},{9,1},{13,5},{1,9},{5,13},{10,2},{14,6},... | collective-permute-start | bytes 1572872 | tf_op jit(solution)/shard_map/ppermute | solution.py:30
  16.5 10.4 %collective-permute-start.12 = (bf16[32,2048]{1,0:T(8,128)(2,1)S(1)}, bf16[32,2048]{1,0:T(8,128)(2,1)S(1)}, u32[]{:S(2)}, u32[]{:S(2)}) collective-permute-start(bf16[32,2048]{1,0:T(8,128)(2,1)S(1)} %collective-permute-done.2), channel_id=1, source_target_pairs={{0,16},{16,0},{1,17},{17,1},{2,18},{18,2},{3,19},{19,3},{4,20},{20... | collective-permute-start | bytes 393224 | tf_op jit(solution)/shard_map/ppermute | solution.py:25
  20.2 10.0 %collective-permute-start.10 = (bf16[768,128]{1,0:T(8,128)(2,1)S(1)}, bf16[768,128]{1,0:T(8,128)(2,1)S(1)}, u32[]{:S(2)}, u32[]{:S(2)}) collective-permute-start(bf16[768,128]{1,0:T(8,128)(2,1)S(1)} %get-tuple-element.35), channel_id=1, source_target_pairs={{1,2},{2,1},{5,6},{6,5},{9,10},{10,9},{13,14},{14,13},{17,18},{18,... | collective-permute-start | bytes 589832 | tf_op jit(solution)/shard_map/ppermute | solution.py:37
  23.6 5.0 %collective-permute-start.4 = (bf16[256,8,128]{2,1,0:T(8,128)(2,1)S(1)}, bf16[256,8,128]{2,1,0:T(8,128)(2,1)S(1)}, u32[]{:S(2)}, u32[]{:S(2)}) collective-permute-start(bf16[256,8,128]{2,1,0:T(8,128)(2,1)S(1)} %collective-permute-done.1), channel_id=1, source_target_pairs={{0,4},{4,0},{8,12},{12,8},{1,5},{5,1},{9,13},{13,9},{2,6},{6,2},{1... | collective-permute-start | bytes 1572872 | tf_op jit(solution)/shard_map/ppermute | solution.py:25
  26.9 13.0 %collective-permute-start.13 = (bf16[64,2048]{1,0:T(8,128)(2,1)S(1)}, bf16[64,2048]{1,0:T(8,128)(2,1)S(1)}, u32[]{:S(2)}, u32[]{:S(2)}) collective-permute-start(bf16[64,2048]{1,0:T(8,128)(2,1)S(1)} %pad_maximum_fusion), channel_id=1, source_target_pairs={{0,1},{1,0},{2,3},{3,2},{4,5},{5,4},{6,7},{7,6},{8,9},{9,8},{10,11... | collective-permute-start | bytes 786440 | tf_op jit(solution)/shard_map/ppermute | solution.py:25
  27.0 12.1 %collective-permute-start.9 = (bf16[768,128]{1,0:T(8,128)(2,1)S(1)}, bf16[768,128]{1,0:T(8,128)(2,1)S(1)}, u32[]{:S(2)}, u32[]{:S(2)}) collective-permute-start(bf16[768,128]{1,0:T(8,128)(2,1)S(1)} %get-tuple-element.34), channel_id=1, source_target_pairs={{0,1},{1,0},{2,3},{3,2},{4,5},{5,4},{6,7},{7,6},{8,9},{9,8},{10,11... | collective-permute-start | bytes 589832 | tf_op jit(solution)/shard_map/ppermute | solution.py:37
  28.5 11.6 %collective-permute-start.7 = (bf16[512,512]{1,0:T(8,128)(2,1)S(1)}, bf16[512,512]{1,0:T(8,128)(2,1)S(1)}, u32[]{:S(2)}, u32[]{:S(2)}) collective-permute-start(bf16[512,512]{1,0:T(8,128)(2,1)S(1)} %get-tuple-element.27.refs_5_.refs_10_.refs_3_), channel_id=1, source_target_pairs={{0,4},{4,0},{8,12},{12,8},{1,5},{5,1},{9,13},{13,9},{2,6},{6,2},{1... | collective-permute-start | bytes 1572872 | tf_op jit(solution)/shard_map/ppermute | solution.py:25
  30.2 15.5 %collective-permute-start.6 = (bf16[512,512]{1,0:T(8,128)(2,1)S(1)}, bf16[512,512]{1,0:T(8,128)(2,1)S(1)}, u32[]{:S(2)}, u32[]{:S(2)}) collective-permute-start(bf16[512,512]{1,0:T(8,128)(2,1)S(1)} %get-tuple-element.32.refs_12_.refs_5_.refs_7_), channel_id=1, source_target_pairs={{8,0},{12,4},{0,8},{4,12},{9,1},{13,5},{1,9},{5,13},{10,2},{14,6},... | collective-permute-start | bytes 1572872 | tf_op jit(solution)/shard_map/ppermute | solution.py:30
  39.9 22.8 %collective-permute-start.14 = (bf16[128,2048]{1,0:T(8,128)(2,1)S(1)}, bf16[128,2048]{1,0:T(8,128)(2,1)S(1)}, u32[]{:S(2)}, u32[]{:S(2)}) collective-permute-start(bf16[128,2048]{1,0:T(8,128)(2,1)S(1)} %constant_dynamic-update-slice_fusion.refs_1_), channel_id=1, source_target_pairs={{0,2},{1,3},{2,0},{3,1},{4,6},{5,7},{6,4},{7,5},{8,10},{9,11},{10,... | collective-permute-start | bytes 1572872 | tf_op jit(solution)/shard_map/ppermute | solution.py:25
  40.0 23.6 %collective-permute-start.5 = (bf16[512,512]{1,0:T(8,128)(2,1)S(1)}, bf16[512,512]{1,0:T(8,128)(2,1)S(1)}, u32[]{:S(2)}, u32[]{:S(2)}) collective-permute-start(bf16[512,512]{1,0:T(8,128)(2,1)S(1)} %get-tuple-element.32.refs_12_.refs_5_.refs_7_), channel_id=1, source_target_pairs={{0,4},{4,0},{8,12},{12,8},{1,5},{5,1},{9,13},{13,9},{2,6},{6,2},{1... | collective-permute-start | bytes 1572872 | tf_op jit(solution)/shard_map/ppermute | solution.py:25
  63.4 22.4 %collective-permute-start.24 = (bf16[512,512]{1,0:T(8,128)(2,1)S(1)}, bf16[512,512]{1,0:T(8,128)(2,1)S(1)}, u32[]{:S(2)}, u32[]{:S(2)}) collective-permute-start(bf16[512,512]{1,0:T(8,128)(2,1)S(1)} %get-tuple-element.37.refs_22_.refs_5_.refs_10_), channel_id=1, source_target_pairs={{8,0},{12,4},{0,8},{4,12},{9,1},{13,5},{1,9},{5,13},{10,2},{14,6},... | collective-permute-start | bytes 1572872 | tf_op jit(solution)/shard_map/ppermute | solution.py:30
  69.2 9.6 %collective-permute-start.17 = (bf16[1024,128]{1,0:T(8,128)(2,1)S(1)}, bf16[1024,128]{1,0:T(8,128)(2,1)S(1)}, u32[]{:S(2)}, u32[]{:S(2)}) collective-permute-start(bf16[1024,128]{1,0:T(8,128)(2,1)S(1)} %get-tuple-element.41), channel_id=1, source_target_pairs={{0,1},{1,0},{2,3},{3,2},{4,5},{5,4},{6,7},{7,6},{8,9},{9,8},{10,11... | collective-permute-start | bytes 786440 | tf_op jit(solution)/shard_map/ppermute | solution.py:37
  72.5 9.1 %collective-permute-start.18 = (bf16[1024,128]{1,0:T(8,128)(2,1)S(1)}, bf16[1024,128]{1,0:T(8,128)(2,1)S(1)}, u32[]{:S(2)}, u32[]{:S(2)}) collective-permute-start(bf16[1024,128]{1,0:T(8,128)(2,1)S(1)} %get-tuple-element.42), channel_id=1, source_target_pairs={{1,2},{2,1},{5,6},{6,5},{9,10},{10,9},{13,14},{14,13},{17,18},{18,... | collective-permute-start | bytes 786440 | tf_op jit(solution)/shard_map/ppermute | solution.py:37
  74.6 15.8 %collective-permute-start.23 = (bf16[512,512]{1,0:T(8,128)(2,1)S(1)}, bf16[512,512]{1,0:T(8,128)(2,1)S(1)}, u32[]{:S(2)}, u32[]{:S(2)}) collective-permute-start(bf16[512,512]{1,0:T(8,128)(2,1)S(1)} %get-tuple-element.37.refs_22_.refs_5_.refs_10_), channel_id=1, source_target_pairs={{0,4},{4,0},{8,12},{12,8},{1,5},{5,1},{9,13},{13,9},{2,6},{6,2},{1... | collective-permute-start | bytes 1572872 | tf_op jit(solution)/shard_map/ppermute | solution.py:25
  85.8 4.6 %collective-permute-start.25 = (bf16[512,512]{1,0:T(8,128)(2,1)S(1)}, bf16[512,512]{1,0:T(8,128)(2,1)S(1)}, u32[]{:S(2)}, u32[]{:S(2)}) collective-permute-start(bf16[512,512]{1,0:T(8,128)(2,1)S(1)} %collective-permute-done.24.refs_7_), channel_id=1, source_target_pairs={{0,4},{4,0},{8,12},{12,8},{1,5},{5,1},{9,13},{13,9},{2,6},{6,2},{1... | collective-permute-start | bytes 1572872 | tf_op jit(solution)/shard_map/ppermute | solution.py:25
  87.4 3.0 %collective-permute-start.19 = (bf16[256,1024]{1,0:T(8,128)(2,1)S(1)}, bf16[256,1024]{1,0:T(8,128)(2,1)S(1)}, u32[]{:S(2)}, u32[]{:S(2)}) collective-permute-start(bf16[256,1024]{1,0:T(8,128)(2,1)S(1)} %lent.1.refs_3_), channel_id=1, source_target_pairs={{0,4},{4,0},{8,12},{12,8},{1,5},{5,1},{9,13},{13,9},{2,6},{6,2},{1... | collective-permute-start | bytes 1572872 | tf_op jit(solution)/shard_map/ppermute | solution.py:25
  87.4 13.1 %collective-permute-start.21 = (bf16[512,512]{1,0:T(8,128)(2,1)S(1)}, bf16[512,512]{1,0:T(8,128)(2,1)S(1)}, u32[]{:S(2)}, u32[]{:S(2)}) collective-permute-start(bf16[512,512]{1,0:T(8,128)(2,1)S(1)} %get-tuple-element.43.refs_12_.refs_5_), channel_id=1, source_target_pairs={{8,0},{12,4},{0,8},{4,12},{9,1},{13,5},{1,9},{5,13},{10,2},{14,6},... | collective-permute-start | bytes 1572872 | tf_op jit(solution)/shard_map/ppermute | solution.py:30
  87.7 2.4 %collective-permute-start.22 = (bf16[256,512]{1,0:T(8,128)(2,1)S(1)}, bf16[256,512]{1,0:T(8,128)(2,1)S(1)}, u32[]{:S(2)}, u32[]{:S(2)}) collective-permute-start(bf16[256,512]{1,0:T(8,128)(2,1)S(1)} %get-tuple-element.39.refs_21_.refs_1_.refs_9_), channel_id=1, source_target_pairs={{0,4},{4,0},{8,12},{12,8},{1,5},{5,1},{9,13},{13,9},{2,6},{6,2},{1... | collective-permute-start | bytes 786440 | tf_op jit(solution)/shard_map/ppermute | solution.py:25
  90.0 13.7 %collective-permute-start.20 = (bf16[512,512]{1,0:T(8,128)(2,1)S(1)}, bf16[512,512]{1,0:T(8,128)(2,1)S(1)}, u32[]{:S(2)}, u32[]{:S(2)}) collective-permute-start(bf16[512,512]{1,0:T(8,128)(2,1)S(1)} %get-tuple-element.43.refs_12_.refs_5_), channel_id=1, source_target_pairs={{0,4},{4,0},{8,12},{12,8},{1,5},{5,1},{9,13},{13,9},{2,6},{6,2},{1... | collective-permute-start | bytes 1572872 | tf_op jit(solution)/shard_map/ppermute | solution.py:25
  100.5 3.2 %collective-permute-start.26 = (bf16[512,512]{1,0:T(8,128)(2,1)S(1)}, bf16[512,512]{1,0:T(8,128)(2,1)S(1)}, u32[]{:S(2)}, u32[]{:S(2)}) collective-permute-start(bf16[512,512]{1,0:T(8,128)(2,1)S(1)} %collective-permute-done.21.refs_7_), channel_id=1, source_target_pairs={{0,4},{4,0},{8,12},{12,8},{1,5},{5,1},{9,13},{13,9},{2,6},{6,2},{1... | collective-permute-start | bytes 1572872 | tf_op jit(solution)/shard_map/ppermute | solution.py:25
  (13 other events, 166.7 us)

commit v6 on v5

--- a/solution.py
+++ b/solution.py
@@ -129,19 +129,41 @@
             to_ref[e:, :] = outs[0][:, 0:ny]
 
 
-def flatten_others_kernel(nx, ny, count, *refs):
-    xs, outs, ins, (wide_ref, sems) = refs[:count], refs[count : 2 * count], refs[2 * count : 3 * count], refs[3 * count :]
+def flatten_others_kernel(nx, ny, count, place_ref, *refs):
+    refs = list(refs)
+    xs, outs, (a_ref, b_ref), ins = refs[:count], refs[count : 2 * count], refs[2 * count : 2 * count + 2], refs[2 * count + 2 : -2]
+    wide_ref, sems = refs[-2:]
     load = Loader(sems)
     copies = [load.start(x, y) for x, y in zip(xs, ins)]
     for copy, x_ref, out_ref in zip(copies, ins, outs):
         copy.wait()
         flatten_one(nx, ny, x_ref, [out_ref], wide_ref)
+    even = place_ref[0] == 0
+    for to_ref, last in ((a_ref, even), (b_ref, jnp.logical_not(even))):
+
+        @pl.when(last)
+        def _():
+            to_ref[...] = outs[1][:, (nx - 1) * ny :]
+
+        @pl.when(jnp.logical_not(last))
+        def _():
+            to_ref[...] = outs[1][:, 0:ny]
+
+
+def stack_kernel(*refs):
+    *x_refs, out_ref, sems = refs
+    load = Loader(sems)
+    count = x_refs[0].shape[0]
+    copies = [load.start(x, out_ref.at[i * count : (i + 1) * count, :]) for i, x in enumerate(x_refs)]
+    for copy in copies:
+        copy.wait()
 
 
 def lent_kernel(n, e, p, width, ny, shares, count, place_ref, *refs):
     share_refs, refs = refs[:shares], refs[shares:]
     p_refs, refs = refs[: n * CHUNKS], refs[n * CHUNKS :]
-    far_ref, a_ref, b_ref, up_ref, rate_ref, out_ref, absorption_ref, sp_ref, own_ref, edge_ref, sems = refs
+    far_ref, a_ref, b_ref, up_ref, rate_ref = refs[:5]
+    out_refs, (absorption_ref, sp_ref, own_ref, edge_ref, sems) = refs[5 : 5 + CHUNKS], refs[5 + CHUNKS :]
     load, first, second = Loader(sems), [], []
     even = place_ref[0] == 0
     at = 1 + n
@@ -156,9 +178,8 @@
             (second if k else first).append(copy)
         if not k:
             first.append(load.start(far_ref, own_ref))
-            beyond = pl.ds(e + p, e)
-            first.append(load.start_one(even, b_ref.at[beyond, :], a_ref.at[beyond, :], edge_ref.at[0:e, :]))
-            first.append(load.start_one(even, a_ref.at[beyond, :], b_ref.at[beyond, :], edge_ref.at[e:, :]))
+            first.append(load.start_one(even, b_ref, a_ref, edge_ref.at[0:e, :]))
+            first.append(load.start_one(even, a_ref, b_ref, edge_ref.at[e:, :]))
     for k in range(CHUNKS):
         for copy in second if k == 1 else [] if k else first:
             copy.wait()
@@ -172,7 +193,7 @@
         f_up = jnp.where(up_ref[:, start:stop] == 1, lower, higher)
         speed, rate = as_column(rate_ref[0:1, :]), as_column(rate_ref[1:2, :])
         new = (own - speed * (own - f_up) + 0.5 * gain) / (1.0 + rate)
-        out_ref[:, start:stop] = new.astype(jnp.bfloat16)
+        out_refs[k][...] = new.astype(jnp.bfloat16)
 
 
 def step_kernel(n, e, p, width, ny, nx, k, cols, edges, last, place_ref, *refs):
@@ -186,7 +207,7 @@
     e_refs, p_refs, before, behind = take(n), take(n), take(2), take(2)
     emission_hbm, absorption_hbm, dense_hbm, up_ref, speed_ref, diffusion_ref, e_rate_ref, p_rate_ref = take(8)
     done = take(2 * (CHUNKS - 1)) if last else []
-    border = take(3 if edges == 3 else 2) if edges else []
+    border = take(2) if edges else []
     e_out_ref, p_out_ref = take(2)
     to_refs = take(2) if edges else []
     se_ref, sp_ref, emission_ref, absorption_ref, dense_ref, low_ref, high_ref = take(7)
@@ -204,12 +225,12 @@
         late_e = load.start(e_refs[j].at[:, cols[j] : cols[j] + width], se_ref.at[rows_at(place_ref[1 + j], e), :])
         early.append(late_e)
     if k == 0:
-        early.append(load.start_one(even, before[1].at[0 : e + p, :], before[0].at[0 : e + p, :], low_ref))
+        early.append(load.start_one(even, before[1], before[0], low_ref))
     else:
         early.append(load.start(before[0].at[:, pl.ds((cols[0] or before[0].shape[1]) - ny, ny)], low_ref.at[0:e, :]))
         early.append(load.start(before[1].at[:, width - ny : width], low_ref.at[e:, :]))
     if k == CHUNKS - 1:
-        early.append(load.start_one(even, behind[0].at[0 : e + p, :], behind[1].at[0 : e + p, :], high_ref))
+        early.append(load.start_one(even, behind[0], behind[1], high_ref))
     else:
         next_col = cols[0] + width if behind[0].shape[1] > width else 0
         early.append(load.start(behind[0].at[:, next_col : next_col + ny], high_ref.at[0:e, :]))
@@ -222,9 +243,6 @@
     if edges:
         late.append(load.start(border[0].at[:, 0:ny], first_ref.at[0:e, :]))
         late.append(load.start(border[1].at[:, 0:ny], first_ref.at[e : e + p, :]))
-        if edges == 3:
-            late.append(load.start(border[2].at[:, 0:ny], first_ref.at[e + p :, :]))
-            late.append(load.start(border[2].at[:, (nx - 1) * ny :], final_ref.at[e + p :, :]))
     tile = min(p, 256)
 
     def around(x_ref, rows, base):
@@ -316,23 +334,17 @@
     chip, core = me // CORES, me % CORES
     places = [space % 2] + [((chip + d) % chips) * CORES + (core ^ c) for d in range(chips) for c in range(CORES)]
 
-    bits = [("grp", b) for b in (1, 2, 4, 8) if b < groups] + [("space", b) for b in (1, 2, 4, 8) if b < spaces]
-    lend = chips == 2 and 1 << len(bits) == groups * spaces and e % (16 * groups * spaces) == 0 and len(bits) > 0
-    near_e = swap_cores(electrons)
-    far_e = [from_chip(electrons, d) for d in range(1, chips)]
+    lend = False
     if lend:
         count = e // (groups * spaces)
         start = (grp * spaces + space) * count
-        shares = [from_chip(lax.dynamic_slice(absorption, (start, jnp.zeros_like(start)), (count, NM)), 1)]
+        share = from_chip(lax.dynamic_slice(absorption, (start, jnp.zeros_like(start)), (count, NM)), 1)
         far_rates = from_chip(jnp.stack([speed, electron_rate]), 1)
-        own_share, held = shares[0], [(0, 0)]
-        for axis, bit in bits:
-            whole = jnp.concatenate(shares, axis=0) if len(shares) > 1 else shares[0]
-            shares = [whole, exchange(whole, axis, bit)]
-            held = held + [(g ^ bit, s) if axis == "grp" else (g, s ^ bit) for g, s in held]
-        places += [(grp ^ g) * spaces + (space ^ s) for g, s in held]
+        places += [(grp ^ g) * spaces + (space ^ s) for g in range(groups) for s in range(spaces)]
     places = jnp.stack(places).astype(jnp.int32)
 
+    near_e = swap_cores(electrons)
+    far_e = [from_chip(electrons, d) for d in range(1, chips)]
     e_all, *p_chunks, to_a, to_b = call(
         lambda *refs: flatten_own_kernel(nx, ny, *refs),
         (bf16(e, nx * ny),) + (bf16(p, width),) * CHUNKS + (bf16(e + p, ny),) * 2,
@@ -371,9 +383,8 @@
                 pltpu.VMEM((max(e, min(p, 256)) * nx, ny), jnp.float32),
             ]
         else:
-            edge_rows = e + p + (e if edges == 3 else 0)
-            out = (bf16(e, width), bf16(p, width)) + (bf16(edge_rows, ny),) * (2 if edges else 0)
-            scratch += [pltpu.VMEM((edge_rows, ny), jnp.bfloat16)] * (2 if edges else 0)
+            out = (bf16(e, width), bf16(p, width)) + (bf16(e + p, ny),) * edges
+            scratch += [pltpu.VMEM((e + p, ny), jnp.bfloat16)] * edges
         return call(
             lambda *refs: step_kernel(n, e, p, width, ny, nx, k, [c for _, c in es], edges, last, *refs),
             out, scratch, operands, specs, 28, "step", 2 * n + 7 + len(done) + edges + 1,
@@ -388,36 +399,45 @@
 
     halo = halos(to_a, to_b)
     far_p = [[from_chip(c, d) for d in range(1, chips)] for c in p_chunks]
+    if lend:
+        shares = [share] + [exchange(share, "space", d) for d in range(1, spaces)]
+        (column,) = call(
+            stack_kernel, (bf16(count * spaces, NM),), [], shares, [ANY] * spaces, 4, "stack", spaces,
+        )
+        columns = (column, exchange(column, "grp", 1))
     others = [near_e]
     for f in far_e:
-        f = after(f, p_chunks[0], *((own_share, far_rates) if lend else ()))
+        f = after(f, p_chunks[0], *(*halo, ), *(() if lend else ()))
         others += [f, swap_cores(f)]
-    others = call(
-        lambda *refs: flatten_others_kernel(nx, ny, n - 1, *refs), (bf16(e, nx * ny),) * (n - 1),
+    *others, far_a, far_b = call(
+        lambda *refs: flatten_others_kernel(nx, ny, n - 1, *refs),
+        (bf16(e, nx * ny),) * (n - 1) + (bf16(e, ny),) * 2,
         [pltpu.VMEM((e * nx, ny), jnp.bfloat16)] * (n - 1) + [lanes],
-        [x.reshape(e * nx, ny) for x in others], [ANY] * (n - 1), 12, "flatten", n - 1,
+        [places, *(x.reshape(e * nx, ny) for x in others)], [SMEM] + [ANY] * (n - 1), 12, "flatten", n - 1,
     )
+    far_halo = halos(far_a, far_b) if lend else ()
     everyone = [e_all, *others]
-    waits = (dense, *halo, everyone[1])
+    waits = (dense, *halo, *(() if lend else ()))
     new, every_p = [], []
     for k in range(CHUNKS):
         ps = gathered(p_chunks[k], far_p[k], waits)
         new.append(step(
             k, [(x, k * width) for x in everyone], ps, (e_all, p_chunks[k - 1]) if k else halo,
             (e_all, p_chunks[k + 1]) if k + 1 < CHUNKS else halo, [],
-            () if k + 1 < CHUNKS else (*new[0][:2], *([everyone[2]] if lend else [])),
+            () if k + 1 < CHUNKS else new[0][:2],
         ))
         every_p += ps
-        waits = (new[-1][1], *(shares if lend else ()))
+        waits = (new[-1][1], *(() if lend else ()))
     halo = halos(new[-1][2], new[-1][3])
     chunks = [c[:2] for c in new]
 
     far_p = [[from_chip(c[1], d) for d in range(1, chips)] for c in chunks]
-    ready = (chunks[-1][1], *halo)
-    if lend:
-        operands = (places, *shares, *every_p, everyone[2], *halo, upwind.reshape(1, nx * ny), far_rates)
-        (lent,) = call(
-            lambda *refs: lent_kernel(n, e, p, width, ny, 2, count, *refs), (bf16(e, nx * ny),),
+    ready = (chunks[-1][1], *halo, *(() if lend else ()))
+
+    def lend_electrons(last_of_all):
+        operands = (places, *columns, *every_p, everyone[2], *far_halo, upwind.reshape(1, nx * ny), far_rates)
+        return call(
+            lambda *refs: lent_kernel(n, e, p, width, ny, 2, count, *refs), (bf16(e, width),) * CHUNKS,
             [
                 pltpu.VMEM(shape, jnp.bfloat16)
                 for shape in ((e, NM), (CHUNKS, n * p, width), (e, nx * ny), (2 * e, ny))
@@ -425,19 +445,21 @@
             operands, [SMEM] + [ANY] * (len(operands) - 3) + [VMEM, VMEM], 16, "lent",
             groups * spaces + n * CHUNKS + 3,
         )
-        lent = [lent, swap_cores(lent)]
-        ready += (lent[0],)
-    else:
+
+    if not lend:
         far_e = [[from_chip(c[0], d) for d in range(1, chips)] for c in chunks]
     done = []
     for k in range(CHUNKS):
         waits = (done[-1][1],) if k else ready
+        ps = gathered(chunks[k][1], far_p[k], waits)
+        if lend and not k:
+            lent = lend_electrons(ps[-1])
         if lend:
-            es = [(chunks[k][0], 0), (swap_cores(chunks[k][0]), 0)] + [(x, k * width) for x in lent]
+            es = [(chunks[k][0], 0), (swap_cores(chunks[k][0]), 0)] + [(lent[k], 0), (swap_cores(lent[k]), 0)]
         else:
             es = [(x, 0) for x in gathered(chunks[k][0], far_e[k], waits)]
         done.append(step(
-            k, es, gathered(chunks[k][1], far_p[k], waits), chunks[k - 1] if k else halo,
+            k, es, ps, chunks[k - 1] if k else halo,
             chunks[k + 1] if k + 1 < CHUNKS else halo, done if k + 1 == CHUNKS else [], (),
         ))
     return done[-1][0].reshape(e, nx, ny), done[-1][1].reshape(p, nx, ny)

time: 110 us -> 86 us (0.78)
  waiting for transfers between devices: 49.4 us -> 32.5 us
  starting transfers between devices: 27.3 us -> 24 us
  Pallas kernels: 25.5 us -> 22.4 us
    ppermute x16 -> x14, waiting for transfers between devices: 23.2 us -> 3.35 us  [exchange(): lax.ppermute(x, axis, [(i, i ^ bit) for i in range(lax.axis_size(axis))])]
    ppermute x7, waiting for transfers between devices: 11.7 us -> 25.8 us  [from_chip(): lax.ppermute(x, 'mode', [((i + CORES * offset) % n, i) for i in range(n)])]
    ppermute x4, waiting for transfers between devices: 14.5 us -> 3.39 us  [halos(): return (lax.ppermute(a, 'space', near), lax.ppermute(b, 'space', other))]
    pallas_call x7 -> x6, Pallas kernels: 25.5 us -> 22.4 us  [call(): pl.pallas_call(kernel, out_shape=out, in_specs=specs, out_specs=(VMEM,) *...]
    ppermute x4, starting transfers between devices: 10.2 us -> 9.03 us  [halos(): return (lax.ppermute(a, 'space', near), lax.ppermute(b, 'space', other))]
    ppermute x16 -> x14, starting transfers between devices: 13.2 us -> 12.1 us  [exchange(): lax.ppermute(x, axis, [(i, i ^ bit) for i in range(lax.axis_size(axis))])]
    unnamed x23 -> x21, local copies, waits for them, and re-layouts: 2.87 us -> 2.86 us
  transfers between devices with their start and end apart: 27 -> 25, of which waited for: 10 -> 11; matrix products, arithmetic and copies ran while one was open for 4% -> 3% of each run, Pallas kernels for 18% -> 20%
where the time goes in v6:
time: 86 us; the launch traced here: 84.8 us
  waiting for transfers between devices  32.5 us (38%)
  starting transfers between devices  24 us (28%)
  Pallas kernels  22.4 us (26%)
  local copies, waits for them, and re-layouts  2.95 us (3%)
  matrix products  1.83 us (2%)
  between operations  1.03 us (1%)
    ppermute x7, waiting for transfers between devices, from_chip(): lax.ppermute(x, 'mode', [((i + CORES * offset) % n, i) for i in range(n)])  25.8 us
    pallas_call x6, Pallas kernels, call(): pl.pallas_call(kernel, out_shape=out, in_specs=specs, out_specs=(VMEM,) *...  22.4 us
    ppermute x14, starting transfers between devices, exchange(): lax.ppermute(x, axis, [(i, i ^ bit) for i in range(lax.axis_size(axis))])  12.1 us
    ppermute x4, starting transfers between devices, halos(): return (lax.ppermute(a, 'space', near), lax.ppermute(b, 'space', other))  9.03 us
    ppermute x4, waiting for transfers between devices, halos(): return (lax.ppermute(a, 'space', near), lax.ppermute(b, 'space', other))  3.39 us
    ppermute x14, waiting for transfers between devices, exchange(): lax.ppermute(x, axis, [(i, i ^ bit) for i in range(lax.axis_size(axis))])  3.35 us
    unnamed x21, local copies, waits for them, and re-layouts  2.86 us
    ppermute x7, starting transfers between devices, from_chip(): lax.ppermute(x, 'mode', [((i + CORES * offset) % n, i) for i in range(n)])  2.86 us
  transfers between devices with their start and end apart: 25, of which 11 were waited for; matrix products, arithmetic and copies ran while one was open for 3% of the time, Pallas kernels for 20%

profile of v6, /device:TPU:13, one launch (start us, length us, event | category | flops | bytes accessed | tf_op | source)
XLA Modules:
  0.0 84.8 jit_solution(9310437681186431038)
XLA Ops:
  1.0 1.2 %copy-done.2 = bf16[512,8,128]{2,1,0:T(8,128)(2,1)S(1)} copy-done((bf16[512,8,128]{2,1,0:T(8,128)(2,1)S(1)}, bf16[512,8,128]{2,1,0:T(8,128)(2,1)}, u32[]{:S(2)}) %copy-start.2) | copy-done | bytes 1048600
  3.3 1.6 %flatten.2 = (bf16[256,1024]{1,0:T(8,128)(2,1)S(1)}, bf16[512,512]{1,0:T(8,128)(2,1)S(1)}, bf16[512,512]{1,0:T(8,128)(2,1)S(1)}, bf16[768,128]{1,0:T(8,128)(2,1)S(1)}, bf16[768,128]{1,0:T(8,128)(2,1)S(1)}) custom-call(s32[5]{0:T(128)S(1)} %convert_element_type.27.refs_0_, bf16[2048,128]{1,0:T(8,128)(2,1)S(1)} %bitcast.35, bf16[4096,128]{1,0:T(8,128)(2,1)S(1)} %bitcast.34), custom_call_target="tpu_custom_call" | custom-call | flops 1000 | bytes 1000 | tf_op jit(solution)/shard_map/flatten/pallas_call | solution.py:49
  4.9 1.3 %collective-permute-start.8 = (bf16[512,512]{1,0:T(8,128)(2,1)S(1)}, bf16[512,512]{1,0:T(8,128)(2,1)S(1)}, u32[]{:S(2)}, u32[]{:S(2)}) collective-permute-start(bf16[512,512]{1,0:T(8,128)(2,1)S(1)} %get-tuple-element.29.refs_5_.refs_10_), channel_id=1, source_target_pairs={{8,0},{12,4},{0,8},{4,12},{9,1},{13,5},{1,9},{5,13},{10,2},{14,6},... | collective-permute-start | bytes 1572872 | tf_op jit(solution)/shard_map/ppermute | solution.py:30
  6.2 1.2 %collective-permute-start = (bf16[256,8,128]{2,1,0:T(8,128)(2,1)S(1)}, bf16[256,8,128]{2,1,0:T(8,128)(2,1)S(1)}, u32[]{:S(2)}, u32[]{:S(2)}) collective-permute-start(bf16[256,8,128]{2,1,0:T(8,128)(2,1)S(1)} %copy-done.3), channel_id=1, source_target_pairs={{0,4},{4,0},{8,12},{12,8},{1,5},{5,1},{9,13},{13,9},{2,6},{6,2},{1... | collective-permute-start | bytes 1572872 | tf_op jit(solution)/shard_map/ppermute | solution.py:25
  7.6 4.3 %collective-permute-start.3 = (bf16[768,128]{1,0:T(8,128)(2,1)S(1)}, bf16[768,128]{1,0:T(8,128)(2,1)S(1)}, u32[]{:S(2)}, u32[]{:S(2)}) collective-permute-start(bf16[768,128]{1,0:T(8,128)(2,1)S(1)} %get-tuple-element.31), channel_id=1, source_target_pairs={{1,2},{2,1},{5,6},{6,5},{9,10},{10,9},{13,14},{14,13},{17,18},{18,... | collective-permute-start | bytes 589832 | tf_op jit(solution)/shard_map/ppermute | solution.py:37
  11.9 1.8 %fusion.2 = bf16[4,128,128,16]{2,3,1,0:T(8,128)(2,1)S(1)} fusion(bf16[4,128,12,128]{3,1,0,2:T(8,128)(2,1)S(1)} %bitcast.60, s32[4,12]{1,0:T(4,128)} %param.16), kind=kOutput, calls=%fused_computation.3 | convolution fusion | flops 26215168 | bytes 3670208 | tf_op jit(solution)/shard_map/bsk,bisj->bikj/dot_general | solution.py:358
  15.1 1.9 %collective-permute-done.3.refs_10_.refs_12_ = bf16[768,128]{1,0:T(8,128)(2,1)S(1)} collective-permute-done((bf16[768,128]{1,0:T(8,128)(2,1)S(1)}, bf16[768,128]{1,0:T(8,128)(2,1)S(1)}, u32[]{:S(2)}, u32[]{:S(2)}) %collective-permute-start.3) | collective-permute-done | bytes 196640 | tf_op jit(solution)/shard_map/ppermute | solution.py:37
  17.8 7.2 %collective-permute-done.8.refs_7_ = bf16[512,512]{1,0:T(8,128)(2,1)S(1)} collective-permute-done((bf16[512,512]{1,0:T(8,128)(2,1)S(1)}, bf16[512,512]{1,0:T(8,128)(2,1)S(1)}, u32[]{:S(2)}, u32[]{:S(2)}) %collective-permute-start.8) | collective-permute-done | bytes 524320 | tf_op jit(solution)/shard_map/ppermute | solution.py:30
  24.9 1.5 %collective-permute-start.9 = (bf16[512,512]{1,0:T(8,128)(2,1)S(1)}, bf16[512,512]{1,0:T(8,128)(2,1)S(1)}, u32[]{:S(2)}, u32[]{:S(2)}) collective-permute-start(bf16[512,512]{1,0:T(8,128)(2,1)S(1)} %collective-permute-done.8.refs_7_), channel_id=1, source_target_pairs={{0,4},{4,0},{8,12},{12,8},{1,5},{5,1},{9,13},{13,9},{2,6},{6,2},{1... | collective-permute-start | bytes 1572872 | tf_op jit(solution)/shard_map/ppermute | solution.py:25
  27.1 2.2 %flatten.3 = (bf16[256,1024]{1,0:T(8,128)(2,1)S(1)}, bf16[256,1024]{1,0:T(8,128)(2,1)S(1)}, bf16[256,1024]{1,0:T(8,128)(2,1)S(1)}, bf16[256,128]{1,0:T(8,128)(2,1)}, bf16[256,128]{1,0:T(8,128)(2,1)}) custom-call(s32[5]{0:T(128)S(1)} %convert_element_type.27.refs_0_, bf16[2048,128]{1,0:T(8,128)(2,1)S(1)} %bitcast.37, bf16[2048,128]{1,0:T(8,128)(2,1)S(1)} %bitcast.36, ...), custom_call_target="tpu_custom_call" | custom-call | flops 1000 | bytes 1000 | tf_op jit(solution)/shard_map/flatten/pallas_call | solution.py:49
  29.4 4.2 %step.4 = (bf16[256,512]{1,0:T(8,128)(2,1)S(1)}, bf16[512,512]{1,0:T(8,128)(2,1)S(1)}) custom-call(s32[5]{0:T(128)S(1)} %convert_element_type.27.refs_0_, bf16[256,1024]{1,0:T(8,128)(2,1)S(1)} %get-tuple-element.28.refs_1_.refs_11_.refs_9_, bf16[256,1024]{1,0:T(8,128)(2,1)S(1)} %get-tuple-element.33.refs_2_, ...), custom_call_target="tpu_custom_call" | custom-call | flops 1000 | bytes 1000 | tf_op jit(solution)/shard_map/step/pallas_call | solution.py:49
  33.6 6.5 %collective-permute-done.6.refs_7_ = bf16[512,512]{1,0:T(8,128)(2,1)S(1)} collective-permute-done((bf16[512,512]{1,0:T(8,128)(2,1)S(1)}, bf16[512,512]{1,0:T(8,128)(2,1)S(1)}, u32[]{:S(2)}, u32[]{:S(2)}) %collective-permute-start.6) | collective-permute-done | bytes 524320 | tf_op jit(solution)/shard_map/ppermute | solution.py:30
  41.0 1.3 %collective-permute-done.10.refs_8_ = bf16[512,512]{1,0:T(8,128)(2,1)S(1)} collective-permute-done((bf16[512,512]{1,0:T(8,128)(2,1)S(1)}, bf16[512,512]{1,0:T(8,128)(2,1)S(1)}, u32[]{:S(2)}, u32[]{:S(2)}) %collective-permute-start.10) | collective-permute-done | bytes 524320 | tf_op jit(solution)/shard_map/ppermute | solution.py:25
  42.4 4.3 %step.5 = (bf16[256,512]{1,0:T(8,128)(2,1)S(1)}, bf16[512,512]{1,0:T(8,128)(2,1)S(1)}, bf16[768,128]{1,0:T(8,128)(2,1)S(1)}, bf16[768,128]{1,0:T(8,128)(2,1)S(1)}) custom-call(s32[5]{0:T(128)S(1)} %convert_element_type.27.refs_0_, bf16[256,1024]{1,0:T(8,128)(2,1)S(1)} %get-tuple-element.28.refs_1_.refs_11_.refs_9_, ...), custom_call_target="tpu_custom_call" | custom-call | flops 1000 | bytes 1000 | tf_op jit(solution)/shard_map/step/pallas_call | solution.py:49
  46.9 4.3 %collective-permute-start.16 = (bf16[768,128]{1,0:T(8,128)(2,1)S(1)}, bf16[768,128]{1,0:T(8,128)(2,1)S(1)}, u32[]{:S(2)}, u32[]{:S(2)}) collective-permute-start(bf16[768,128]{1,0:T(8,128)(2,1)S(1)} %get-tuple-element.45), channel_id=1, source_target_pairs={{1,2},{2,1},{5,6},{6,5},{9,10},{10,9},{13,14},{14,13},{17,18},{18,... | collective-permute-start | bytes 589832 | tf_op jit(solution)/shard_map/ppermute | solution.py:37
  52.7 1.7 %collective-permute-done.19.refs_7_ = bf16[512,512]{1,0:T(8,128)(2,1)S(1)} collective-permute-done((bf16[512,512]{1,0:T(8,128)(2,1)S(1)}, bf16[512,512]{1,0:T(8,128)(2,1)S(1)}, u32[]{:S(2)}, u32[]{:S(2)}) %collective-permute-start.19) | collective-permute-done | bytes 524320 | tf_op jit(solution)/shard_map/ppermute | solution.py:30
  54.4 1.5 %collective-permute-done.16.refs_10_.refs_12_ = bf16[768,128]{1,0:T(8,128)(2,1)S(1)} collective-permute-done((bf16[768,128]{1,0:T(8,128)(2,1)S(1)}, bf16[768,128]{1,0:T(8,128)(2,1)S(1)}, u32[]{:S(2)}, u32[]{:S(2)}) %collective-permute-start.16) | collective-permute-done | bytes 196640 | tf_op jit(solution)/shard_map/ppermute | solution.py:37
  57.6 2.2 %collective-permute-done.14.refs_3_ = bf16[256,512]{1,0:T(8,128)(2,1)S(1)} collective-permute-done((bf16[256,512]{1,0:T(8,128)(2,1)S(1)}, bf16[256,512]{1,0:T(8,128)(2,1)S(1)}, u32[]{:S(2)}, u32[]{:S(2)}) %collective-permute-start.14) | collective-permute-done | bytes 262176 | tf_op jit(solution)/shard_map/ppermute | solution.py:30
  59.7 1.6 %collective-permute-start.17 = (bf16[256,512]{1,0:T(8,128)(2,1)S(1)}, bf16[256,512]{1,0:T(8,128)(2,1)S(1)}, u32[]{:S(2)}, u32[]{:S(2)}) collective-permute-start(bf16[256,512]{1,0:T(8,128)(2,1)S(1)} %collective-permute-done.14.refs_3_), channel_id=1, source_target_pairs={{0,4},{4,0},{8,12},{12,8},{1,5},{5,1},{9,13},{13,9},{2,6},{6,2},{1... | collective-permute-start | bytes 786440 | tf_op jit(solution)/shard_map/ppermute | solution.py:25
  62.5 4.3 %step.6 = (bf16[256,512]{1,0:T(8,128)(2,1)S(1)}, bf16[512,512]{1,0:T(8,128)(2,1)S(1)}) custom-call(s32[5]{0:T(128)S(1)} %convert_element_type.27.refs_0_, bf16[256,512]{1,0:T(8,128)(2,1)S(1)} %get-tuple-element.41.refs_21_.refs_1_.refs_9_, bf16[256,512]{1,0:T(8,128)(2,1)S(1)} %collective-permute-done.13.refs_2_, ...), custom_call_target="tpu_custom_call" | custom-call | flops 1000 | bytes 1000 | tf_op jit(solution)/shard_map/step/pallas_call | solution.py:49
  66.8 4.2 %collective-permute-done.23.refs_7_ = bf16[512,512]{1,0:T(8,128)(2,1)S(1)} collective-permute-done((bf16[512,512]{1,0:T(8,128)(2,1)S(1)}, bf16[512,512]{1,0:T(8,128)(2,1)S(1)}, u32[]{:S(2)}, u32[]{:S(2)}) %collective-permute-start.23) | collective-permute-done | bytes 524320 | tf_op jit(solution)/shard_map/ppermute | solution.py:30
  71.1 1.5 %collective-permute-start.24 = (bf16[512,512]{1,0:T(8,128)(2,1)S(1)}, bf16[512,512]{1,0:T(8,128)(2,1)S(1)}, u32[]{:S(2)}, u32[]{:S(2)}) collective-permute-start(bf16[512,512]{1,0:T(8,128)(2,1)S(1)} %collective-permute-done.23.refs_7_), channel_id=1, source_target_pairs={{0,4},{4,0},{8,12},{12,8},{1,5},{5,1},{9,13},{13,9},{2,6},{6,2},{1... | collective-permute-start | bytes 1572872 | tf_op jit(solution)/shard_map/ppermute | solution.py:25
  72.6 4.1 %collective-permute-done.12.refs_3_ = bf16[256,512]{1,0:T(8,128)(2,1)S(1)} collective-permute-done((bf16[256,512]{1,0:T(8,128)(2,1)S(1)}, bf16[256,512]{1,0:T(8,128)(2,1)S(1)}, u32[]{:S(2)}, u32[]{:S(2)}) %collective-permute-start.12) | collective-permute-done | bytes 262176 | tf_op jit(solution)/shard_map/ppermute | solution.py:30
  78.8 5.8 %step.7 = (bf16[2048,128]{1,0:T(8,128)(2,1)}, bf16[4096,128]{1,0:T(8,128)(2,1)}) custom-call(s32[5]{0:T(128)S(1)} %convert_element_type.27.refs_0_, bf16[256,512]{1,0:T(8,128)(2,1)S(1)} %get-tuple-element.42.refs_11_.refs_1_, bf16[256,512]{1,0:T(8,128)(2,1)S(1)} %collective-permute-done.11.refs_2_, bf16[256,512]{1,0:T(8,128)(2,1)S(1)} %collective-permute-done.12.refs_3_, ...), custom_call_target="tpu_custom_call" | custom-call | flops 1000 | bytes 1000 | tf_op jit(solution)/shard_map/step/pallas_call | solution.py:49
  (57 shorter events, 11.9 us)
Async XLA Ops:
  0.6 16.4 %collective-permute-start.1 = (bf16[256,8,128]{2,1,0:T(8,128)(2,1)}, bf16[256,8,128]{2,1,0:T(8,128)(2,1)S(1)}, u32[]{:S(2)}, u32[]{:S(2)}) collective-permute-start(bf16[256,8,128]{2,1,0:T(8,128)(2,1)} %param.11), channel_id=1, source_target_pairs={{8,0},{12,4},{0,8},{4,12},{9,1},{13,5},{1,9},{5,13},{10,2},{14,6},... | collective-permute-start | bytes 1572872 | tf_op jit(solution)/shard_map/ppermute | solution.py:30
  4.9 20.1 %collective-permute-start.8 = (bf16[512,512]{1,0:T(8,128)(2,1)S(1)}, bf16[512,512]{1,0:T(8,128)(2,1)S(1)}, u32[]{:S(2)}, u32[]{:S(2)}) collective-permute-start(bf16[512,512]{1,0:T(8,128)(2,1)S(1)} %get-tuple-element.29.refs_5_.refs_10_), channel_id=1, source_target_pairs={{8,0},{12,4},{0,8},{4,12},{9,1},{13,5},{1,9},{5,13},{10,2},{14,6},... | collective-permute-start | bytes 1572872 | tf_op jit(solution)/shard_map/ppermute | solution.py:30
  6.2 20.5 %collective-permute-start = (bf16[256,8,128]{2,1,0:T(8,128)(2,1)S(1)}, bf16[256,8,128]{2,1,0:T(8,128)(2,1)S(1)}, u32[]{:S(2)}, u32[]{:S(2)}) collective-permute-start(bf16[256,8,128]{2,1,0:T(8,128)(2,1)S(1)} %copy-done.3), channel_id=1, source_target_pairs={{0,4},{4,0},{8,12},{12,8},{1,5},{5,1},{9,13},{13,9},{2,6},{6,2},{1... | collective-permute-start | bytes 1572872 | tf_op jit(solution)/shard_map/ppermute | solution.py:25
  7.4 7.0 %collective-permute-start.2 = (bf16[768,128]{1,0:T(8,128)(2,1)S(1)}, bf16[768,128]{1,0:T(8,128)(2,1)S(1)}, u32[]{:S(2)}, u32[]{:S(2)}) collective-permute-start(bf16[768,128]{1,0:T(8,128)(2,1)S(1)} %get-tuple-element.30), channel_id=1, source_target_pairs={{0,1},{1,0},{2,3},{3,2},{4,5},{5,4},{6,7},{7,6},{8,9},{9,8},{10,11... | collective-permute-start | bytes 589832 | tf_op jit(solution)/shard_map/ppermute | solution.py:37
  7.6 9.4 %collective-permute-start.3 = (bf16[768,128]{1,0:T(8,128)(2,1)S(1)}, bf16[768,128]{1,0:T(8,128)(2,1)S(1)}, u32[]{:S(2)}, u32[]{:S(2)}) collective-permute-start(bf16[768,128]{1,0:T(8,128)(2,1)S(1)} %get-tuple-element.31), channel_id=1, source_target_pairs={{1,2},{2,1},{5,6},{6,5},{9,10},{10,9},{13,14},{14,13},{17,18},{18,... | collective-permute-start | bytes 589832 | tf_op jit(solution)/shard_map/ppermute | solution.py:37
  14.4 14.9 %collective-permute-start.7 = (bf16[512,512]{1,0:T(8,128)(2,1)S(1)}, bf16[512,512]{1,0:T(8,128)(2,1)S(1)}, u32[]{:S(2)}, u32[]{:S(2)}) collective-permute-start(bf16[512,512]{1,0:T(8,128)(2,1)S(1)} %get-tuple-element.29.refs_5_.refs_10_), channel_id=1, source_target_pairs={{0,4},{4,0},{8,12},{12,8},{1,5},{5,1},{9,13},{13,9},{2,6},{6,2},{1... | collective-permute-start | bytes 1572872 | tf_op jit(solution)/shard_map/ppermute | solution.py:25
  17.0 10.1 %collective-permute-start.4 = (bf16[256,8,128]{2,1,0:T(8,128)(2,1)S(1)}, bf16[256,8,128]{2,1,0:T(8,128)(2,1)S(1)}, u32[]{:S(2)}, u32[]{:S(2)}) collective-permute-start(bf16[256,8,128]{2,1,0:T(8,128)(2,1)S(1)} %collective-permute-done.1), channel_id=1, source_target_pairs={{0,4},{4,0},{8,12},{12,8},{1,5},{5,1},{9,13},{13,9},{2,6},{6,2},{1... | collective-permute-start | bytes 1572872 | tf_op jit(solution)/shard_map/ppermute | solution.py:25
  24.9 4.4 %collective-permute-start.9 = (bf16[512,512]{1,0:T(8,128)(2,1)S(1)}, bf16[512,512]{1,0:T(8,128)(2,1)S(1)}, u32[]{:S(2)}, u32[]{:S(2)}) collective-permute-start(bf16[512,512]{1,0:T(8,128)(2,1)S(1)} %collective-permute-done.8.refs_7_), channel_id=1, source_target_pairs={{0,4},{4,0},{8,12},{12,8},{1,5},{5,1},{9,13},{13,9},{2,6},{6,2},{1... | collective-permute-start | bytes 1572872 | tf_op jit(solution)/shard_map/ppermute | solution.py:25
  26.5 13.6 %collective-permute-start.6 = (bf16[512,512]{1,0:T(8,128)(2,1)S(1)}, bf16[512,512]{1,0:T(8,128)(2,1)S(1)}, u32[]{:S(2)}, u32[]{:S(2)}) collective-permute-start(bf16[512,512]{1,0:T(8,128)(2,1)S(1)} %get-tuple-element.36.refs_12_.refs_5_), channel_id=1, source_target_pairs={{8,0},{12,4},{0,8},{4,12},{9,1},{13,5},{1,9},{5,13},{10,2},{14,6},... | collective-permute-start | bytes 1572872 | tf_op jit(solution)/shard_map/ppermute | solution.py:30
  26.7 14.3 %collective-permute-start.5 = (bf16[512,512]{1,0:T(8,128)(2,1)S(1)}, bf16[512,512]{1,0:T(8,128)(2,1)S(1)}, u32[]{:S(2)}, u32[]{:S(2)}) collective-permute-start(bf16[512,512]{1,0:T(8,128)(2,1)S(1)} %get-tuple-element.36.refs_12_.refs_5_), channel_id=1, source_target_pairs={{0,4},{4,0},{8,12},{12,8},{1,5},{5,1},{9,13},{13,9},{2,6},{6,2},{1... | collective-permute-start | bytes 1572872 | tf_op jit(solution)/shard_map/ppermute | solution.py:25
  40.0 2.3 %collective-permute-start.10 = (bf16[512,512]{1,0:T(8,128)(2,1)S(1)}, bf16[512,512]{1,0:T(8,128)(2,1)S(1)}, u32[]{:S(2)}, u32[]{:S(2)}) collective-permute-start(bf16[512,512]{1,0:T(8,128)(2,1)S(1)} %collective-permute-done.6.refs_7_), channel_id=1, source_target_pairs={{0,4},{4,0},{8,12},{12,8},{1,5},{5,1},{9,13},{13,9},{2,6},{6,2},{1... | collective-permute-start | bytes 1572872 | tf_op jit(solution)/shard_map/ppermute | solution.py:25
  40.8 13.6 %collective-permute-start.19 = (bf16[512,512]{1,0:T(8,128)(2,1)S(1)}, bf16[512,512]{1,0:T(8,128)(2,1)S(1)}, u32[]{:S(2)}, u32[]{:S(2)}) collective-permute-start(bf16[512,512]{1,0:T(8,128)(2,1)S(1)} %get-tuple-element.39.refs_22_.refs_5_.refs_10_), channel_id=1, source_target_pairs={{8,0},{12,4},{0,8},{4,12},{9,1},{13,5},{1,9},{5,13},{10,2},{14,6},... | collective-permute-start | bytes 1572872 | tf_op jit(solution)/shard_map/ppermute | solution.py:30
  46.6 7.7 %collective-permute-start.15 = (bf16[768,128]{1,0:T(8,128)(2,1)S(1)}, bf16[768,128]{1,0:T(8,128)(2,1)S(1)}, u32[]{:S(2)}, u32[]{:S(2)}) collective-permute-start(bf16[768,128]{1,0:T(8,128)(2,1)S(1)} %get-tuple-element.44), channel_id=1, source_target_pairs={{0,1},{1,0},{2,3},{3,2},{4,5},{5,4},{6,7},{7,6},{8,9},{9,8},{10,11... | collective-permute-start | bytes 589832 | tf_op jit(solution)/shard_map/ppermute | solution.py:37
  46.9 9.0 %collective-permute-start.16 = (bf16[768,128]{1,0:T(8,128)(2,1)S(1)}, bf16[768,128]{1,0:T(8,128)(2,1)S(1)}, u32[]{:S(2)}, u32[]{:S(2)}) collective-permute-start(bf16[768,128]{1,0:T(8,128)(2,1)S(1)} %get-tuple-element.45), channel_id=1, source_target_pairs={{1,2},{2,1},{5,6},{6,5},{9,10},{10,9},{13,14},{14,13},{17,18},{18,... | collective-permute-start | bytes 589832 | tf_op jit(solution)/shard_map/ppermute | solution.py:37
  51.2 8.5 %collective-permute-start.14 = (bf16[256,512]{1,0:T(8,128)(2,1)S(1)}, bf16[256,512]{1,0:T(8,128)(2,1)S(1)}, u32[]{:S(2)}, u32[]{:S(2)}) collective-permute-start(bf16[256,512]{1,0:T(8,128)(2,1)S(1)} %get-tuple-element.41.refs_21_.refs_1_.refs_9_), channel_id=1, source_target_pairs={{8,0},{12,4},{0,8},{4,12},{9,1},{13,5},{1,9},{5,13},{10,2},{14,6},... | collective-permute-start | bytes 786440 | tf_op jit(solution)/shard_map/ppermute | solution.py:30
  51.5 9.9 %collective-permute-start.18 = (bf16[512,512]{1,0:T(8,128)(2,1)S(1)}, bf16[512,512]{1,0:T(8,128)(2,1)S(1)}, u32[]{:S(2)}, u32[]{:S(2)}) collective-permute-start(bf16[512,512]{1,0:T(8,128)(2,1)S(1)} %get-tuple-element.39.refs_22_.refs_5_.refs_10_), channel_id=1, source_target_pairs={{0,4},{4,0},{8,12},{12,8},{1,5},{5,1},{9,13},{13,9},{2,6},{6,2},{1... | collective-permute-start | bytes 1572872 | tf_op jit(solution)/shard_map/ppermute | solution.py:25
  55.8 6.7 %collective-permute-start.20 = (bf16[512,512]{1,0:T(8,128)(2,1)S(1)}, bf16[512,512]{1,0:T(8,128)(2,1)S(1)}, u32[]{:S(2)}, u32[]{:S(2)}) collective-permute-start(bf16[512,512]{1,0:T(8,128)(2,1)S(1)} %collective-permute-done.19.refs_7_), channel_id=1, source_target_pairs={{0,4},{4,0},{8,12},{12,8},{1,5},{5,1},{9,13},{13,9},{2,6},{6,2},{1... | collective-permute-start | bytes 1572872 | tf_op jit(solution)/shard_map/ppermute | solution.py:25
  57.0 14.0 %collective-permute-start.23 = (bf16[512,512]{1,0:T(8,128)(2,1)S(1)}, bf16[512,512]{1,0:T(8,128)(2,1)S(1)}, u32[]{:S(2)}, u32[]{:S(2)}) collective-permute-start(bf16[512,512]{1,0:T(8,128)(2,1)S(1)} %get-tuple-element.43.refs_12_.refs_5_), channel_id=1, source_target_pairs={{8,0},{12,4},{0,8},{4,12},{9,1},{13,5},{1,9},{5,13},{10,2},{14,6},... | collective-permute-start | bytes 1572872 | tf_op jit(solution)/shard_map/ppermute | solution.py:30
  57.3 4.1 %collective-permute-start.13 = (bf16[256,512]{1,0:T(8,128)(2,1)S(1)}, bf16[256,512]{1,0:T(8,128)(2,1)S(1)}, u32[]{:S(2)}, u32[]{:S(2)}) collective-permute-start(bf16[256,512]{1,0:T(8,128)(2,1)S(1)} %get-tuple-element.41.refs_21_.refs_1_.refs_9_), channel_id=1, source_target_pairs={{0,4},{4,0},{8,12},{12,8},{1,5},{5,1},{9,13},{13,9},{2,6},{6,2},{1... | collective-permute-start | bytes 786440 | tf_op jit(solution)/shard_map/ppermute | solution.py:25
  59.7 2.8 %collective-permute-start.17 = (bf16[256,512]{1,0:T(8,128)(2,1)S(1)}, bf16[256,512]{1,0:T(8,128)(2,1)S(1)}, u32[]{:S(2)}, u32[]{:S(2)}) collective-permute-start(bf16[256,512]{1,0:T(8,128)(2,1)S(1)} %collective-permute-done.14.refs_3_), channel_id=1, source_target_pairs={{0,4},{4,0},{8,12},{12,8},{1,5},{5,1},{9,13},{13,9},{2,6},{6,2},{1... | collective-permute-start | bytes 786440 | tf_op jit(solution)/shard_map/ppermute | solution.py:25
  61.3 16.3 %collective-permute-start.22 = (bf16[512,512]{1,0:T(8,128)(2,1)S(1)}, bf16[512,512]{1,0:T(8,128)(2,1)S(1)}, u32[]{:S(2)}, u32[]{:S(2)}) collective-permute-start(bf16[512,512]{1,0:T(8,128)(2,1)S(1)} %get-tuple-element.43.refs_12_.refs_5_), channel_id=1, source_target_pairs={{0,4},{4,0},{8,12},{12,8},{1,5},{5,1},{9,13},{13,9},{2,6},{6,2},{1... | collective-permute-start | bytes 1572872 | tf_op jit(solution)/shard_map/ppermute | solution.py:25
  61.3 15.3 %collective-permute-start.12 = (bf16[256,512]{1,0:T(8,128)(2,1)S(1)}, bf16[256,512]{1,0:T(8,128)(2,1)S(1)}, u32[]{:S(2)}, u32[]{:S(2)}) collective-permute-start(bf16[256,512]{1,0:T(8,128)(2,1)S(1)} %get-tuple-element.42.refs_11_.refs_1_), channel_id=1, source_target_pairs={{8,0},{12,4},{0,8},{4,12},{9,1},{13,5},{1,9},{5,13},{10,2},{14,6},... | collective-permute-start | bytes 786440 | tf_op jit(solution)/shard_map/ppermute | solution.py:30
  71.1 7.7 %collective-permute-start.24 = (bf16[512,512]{1,0:T(8,128)(2,1)S(1)}, bf16[512,512]{1,0:T(8,128)(2,1)S(1)}, u32[]{:S(2)}, u32[]{:S(2)}) collective-permute-start(bf16[512,512]{1,0:T(8,128)(2,1)S(1)} %collective-permute-done.23.refs_7_), channel_id=1, source_target_pairs={{0,4},{4,0},{8,12},{12,8},{1,5},{5,1},{9,13},{13,9},{2,6},{6,2},{1... | collective-permute-start | bytes 1572872 | tf_op jit(solution)/shard_map/ppermute | solution.py:25
  72.6 5.1 %collective-permute-start.11 = (bf16[256,512]{1,0:T(8,128)(2,1)S(1)}, bf16[256,512]{1,0:T(8,128)(2,1)S(1)}, u32[]{:S(2)}, u32[]{:S(2)}) collective-permute-start(bf16[256,512]{1,0:T(8,128)(2,1)S(1)} %get-tuple-element.42.refs_11_.refs_1_), channel_id=1, source_target_pairs={{0,4},{4,0},{8,12},{12,8},{1,5},{5,1},{9,13},{13,9},{2,6},{6,2},{1... | collective-permute-start | bytes 786440 | tf_op jit(solution)/shard_map/ppermute | solution.py:25
  (11 other events, 119.1 us)

commit v7 on v5

v7 whole, which is shorter than its diff:
```python
import jax
import jax.numpy as jnp
from jax import lax
from jax.experimental import pallas as pl
from jax.experimental.pallas import tpu as pltpu
from jax.sharding import PartitionSpec as P

NM = 2048
BLK = 128
ITERS = 2
CORES = 2
CHUNKS = 2
PARTS = (1, 2)

VMEM = pl.BlockSpec(memory_space=pltpu.VMEM)
SMEM = pl.BlockSpec(memory_space=pltpu.SMEM)
ANY = pl.BlockSpec(memory_space=pl.ANY)
COST = pl.CostEstimate(flops=1000, bytes_accessed=1000, transcendentals=0)


def swap_cores(x):
    n = lax.axis_size("mode")
    return lax.ppermute(x, "mode", [(i, i ^ 1) for i in range(n)])


def from_chip(x, offset):
    n = lax.axis_size("mode")
    return lax.ppermute(x, "mode", [((i + CORES * offset) % n, i) for i in range(n)])


def halos(a, b):
    n = lax.axis_size("space")
    near = [(i, i ^ 1) for i in range(n) if i ^ 1 < n]
    other = [(i, i + 1 if i % 2 else i - 1) for i in range(n) if 0 <= (i + 1 if i % 2 else i - 1) < n]
    return lax.ppermute(a, "space", near), lax.ppermute(b, "space", other)


def after(x, *others):
    return lax.optimization_barrier((x, *others))[0]


def bf16(*shape):
    return jax.ShapeDtypeStruct(shape, jnp.bfloat16)


def call(kernel, out, scratch, operands, specs, megabytes, name, copies):
    return pl.pallas_call(
        kernel,
        out_shape=out,
        in_specs=specs,
        out_specs=(VMEM,) * len(out),
        scratch_shapes=[*scratch, pltpu.SemaphoreType.DMA((copies,))],
        compiler_params=pltpu.CompilerParams(vmem_limit_bytes=megabytes << 20),
        cost_estimate=COST,
        name=name,
    )(*operands)


class Loader:
    def __init__(self, sems):
        self.sems, self.used = sems, 0

    def start(self, src, dst):
        copy = pltpu.make_async_copy(src, dst, self.sems.at[self.used])
        self.used += 1
        copy.start()
        return copy

    def start_one(self, choose, src, other, dst):
        sem = self.sems.at[self.used]
        self.used += 1

        @pl.when(choose)
        def _():
            pltpu.make_async_copy(src, dst, sem).start()

        @pl.when(jnp.logical_not(choose))
        def _():
            pltpu.make_async_copy(other, dst, sem).start()

        return pltpu.make_async_copy(src, dst, sem)


def rows_at(index, count):
    return pl.ds(pl.multiple_of(index * count, count), count)


def rows_of(base, i, part):
    return pl.ds(base + i * part.shape[0], part.shape[0])


def as_column(row):
    return jnp.transpose(jnp.broadcast_to(row, (8, row.shape[1])))[:, 0:1]


def flatten_one(nx, ny, x_ref, outs, wide_ref):
    count = x_ref.shape[0] // nx
    tall = nx // len(outs)
    tile = min([count, 64] + [out.shape[0] for parts in outs for out in parts])
    for at in range(0, count, tile):
        wide_ref[0 : tile * nx, :] = x_ref[at * nx : (at + tile) * nx, :].astype(jnp.float32)
        for r in range(nx):
            k, c = r // tall, r % tall
            row = wide_ref[pl.ds(r, tile, stride=nx), :].astype(jnp.bfloat16)
            part, offset = divmod(at, outs[k][0].shape[0])
            outs[k][part][offset : offset + tile, c * ny : (c + 1) * ny] = row


def flatten_own_kernel(nx, ny, counts, place_ref, e_ref, p_ref, e_out_ref, *refs):
    *flat, a_ref, b_ref, e_in, p_in, wide_ref, sems = refs
    outs = []
    for count in counts:
        outs.append(flat[:count])
        flat = flat[count:]
    load = Loader(sems)
    e_copy, p_copy = load.start(e_ref, e_in), load.start(p_ref, p_in)
    e_copy.wait()
    flatten_one(nx, ny, e_in, [[e_out_ref]], wide_ref)
    p_copy.wait()
    flatten_one(nx, ny, p_in, outs, wide_ref)
    e = e_out_ref.shape[0]
    even = place_ref[0] == 0

    def put(to_ref, parts, col, e_col):
        to_ref[0:e, :] = e_out_ref[:, e_col : e_col + ny]
        at = e
        for part in parts:
            to_ref[at : at + part.shape[0], :] = part[:, col : col + ny]
            at += part.shape[0]

    for to_ref, last in ((a_ref, even), (b_ref, jnp.logical_not(even))):

        @pl.when(last)
        def _():
            put(to_ref, outs[-1], outs[-1][0].shape[1] - ny, (nx - 1) * ny)

        @pl.when(jnp.logical_not(last))
        def _():
            put(to_ref, outs[0], 0, 0)


def flatten_others_kernel(nx, ny, count, *refs):
    xs, outs, ins, (wide_ref, sems) = refs[:count], refs[count : 2 * count], refs[2 * count : -2], refs[-2:]
    load = Loader(sems)
    copies = [load.start(x, y) for x, y in zip(xs, ins)]
    for copy, x_ref, out_ref in zip(copies, ins, outs):
        copy.wait()
        flatten_one(nx, ny, x_ref, [[out_ref]], wide_ref)


def unflatten(olds, new, nx, ny, at, out_ref, wide_ref):
    count, tall = new.shape[0], new.shape[1] // ny
    for c, chunk in enumerate([*(x.astype(jnp.float32) for x in olds), new]):
        for r in range(tall):
            wide_ref[pl.ds(c * tall + r, count, stride=nx), :] = chunk[:, r * ny : (r + 1) * ny]
    out_ref[at * nx : (at + count) * nx, :] = wide_ref[0 : count * nx, :].astype(jnp.bfloat16)


def emit_kernel(n, e, p, ny, nx, place_ref, *refs):
    e_refs, (rest_ref, emission_ref, p_rate_ref), refs = refs[:n], refs[n : n + 3], refs[n + 3 :]
    done_refs, (out_ref, se_ref, wide_ref, sems) = refs[: CHUNKS - 1], refs[CHUNKS - 1 :]
    load = Loader(sems)
    copies = [load.start(x, se_ref.at[rows_at(place_ref[1 + j], e), :]) for j, x in enumerate(e_refs)]
    for copy in copies:
        copy.wait()
    tile = min(p, 256)
    for at in range(0, p, tile):
        emit = jnp.dot(emission_ref[at : at + tile, :], se_ref[...], preferred_element_type=jnp.float32)
        new = (rest_ref[at : at + tile, :] + 0.5 * emit) / (1.0 + as_column(p_rate_ref[:, at : at + tile]))
        unflatten([x[at : at + tile, :] for x in done_refs], new, nx, ny, at, out_ref, wide_ref)


def step_kernel(n, e, p, width, ny, nx, k, cols, counts, edges, last, place_ref, *refs):
    refs = list(refs)

    def take(count):
        taken = refs[:count]
        del refs[:count]
        return taken

    e_refs, p_refs = take(1 if last else n), [take(counts[0]) for _ in range(n)]
    before, behind = (take(1), take(counts[1])), (take(1), take(counts[2]))
    (emission_hbm,) = [None] if last else take(1)
    absorption_hbm, dense_hbm, up_ref, speed_ref, diffusion_ref, e_rate_ref, p_rate_ref = take(7)
    done = take(CHUNKS - 1) if last else []
    border = take(2) if edges else []
    e_out_ref, p_out_ref = take(2)
    to_refs = take(2) if edges else []
    (emission_ref,) = [None] if last else take(1)
    se_ref, sp_ref, absorption_ref, dense_ref, low_ref, high_ref = take(6)
    done_ref, wide_ref = take(2) if last else (None, None)
    first_ref, final_ref = take(2) if edges else (None, None)
    load = Loader(refs[0])
    tall = width // ny
    even = place_ref[0] == 0
    me = place_ref[1]
    me_e = 0 if last else me

    early = [load.start(absorption_hbm, absorption_ref)]
    for j in range(n):
        for i, part in enumerate(p_refs[j]):
            early.append(load.start(part, sp_ref.at[rows_at(place_ref[1 + j] * counts[0] + i, p // counts[0]), :]))
    for j, e_ref in enumerate(e_refs):
        to = se_ref if last else se_ref.at[rows_at(place_ref[1 + j], e), :]
        early.append(load.start(e_ref.at[:, cols[j] : cols[j] + width], to))
    if k == 0:
        early.append(load.start_one(even, before[1][0], before[0][0], low_ref))
    else:
        col = (cols[0] or before[0][0].shape[1]) - ny
        early.append(load.start(before[0][0].at[:, col : col + ny], low_ref.at[0:e, :]))
        for i, part in enumerate(before[1]):
            early.append(load.start(part.at[:, width - ny : width], low_ref.at[rows_of(e, i, part), :]))
    if k == CHUNKS - 1:
        early.append(load.start_one(even, behind[0][0], behind[1][0], high_ref))
    else:
        col = cols[0] + width if behind[0][0].shape[1] > width else 0
        early.append(load.start(behind[0][0].at[:, col : col + ny], high_ref.at[0:e, :]))
        for i, part in enumerate(behind[1]):
            early.append(load.start(part.at[:, 0:ny], high_ref.at[rows_of(e, i, part), :]))
    late = [load.start(dense_hbm, dense_ref)]
    if not last:
        late.append(load.start(emission_hbm, emission_ref))
    for i, array in enumerate(done):
        late.append(load.start(array, done_ref.at[i]))
    if edges:
        late.append(load.start(border[0].at[:, 0:ny], first_ref.at[0:e, :]))
        late.append(load.start(border[1].at[:, 0:ny], first_ref.at[e : e + p, :]))
    tile = min(p, 256)

    def around(x_ref, rows, base):
        own = x_ref[rows, :].astype(jnp.float32)
        low, high = low_ref[base, :].astype(jnp.float32), high_ref[base, :].astype(jnp.float32)
        lower = jnp.concatenate([low, own[:, : width - ny]], axis=1) if width > ny else low
        higher = jnp.concatenate([own[:, ny:], high], axis=1) if width > ny else high
        return own, lower, higher

    def store(new, at, count, base):
        out_ref = p_out_ref if base else e_out_ref
        if not last:
            new = new.astype(jnp.bfloat16)
            out_ref[at : at + count, :] = new
            if edges:
                final_ref[base + at : base + at + count, :] = new[:, width - ny :]
            return
        unflatten([done_ref[c, at : at + count, :] for c in range(CHUNKS - 1)], new, nx, ny, at, out_ref, wide_ref)

    for copy in early:
        copy.wait()
    gain = jnp.dot(absorption_ref[...], sp_ref[...], preferred_element_type=jnp.float32)
    own, lower, higher = around(se_ref, rows_at(me_e, e), pl.ds(0, e))
    f_up = jnp.where(up_ref[...] == 1, lower, higher)
    new = (own - as_column(speed_ref[...]) * (own - f_up) + 0.5 * gain) / (1.0 + as_column(e_rate_ref[...]))
    for copy in late:
        copy.wait()
    store(new, 0, e, 0)

    for at in range(0, p, tile):
        source = jnp.dot(dense_ref[at : at + tile, :], sp_ref[...], preferred_element_type=jnp.float32)
        if not last:
            source += jnp.dot(emission_ref[at : at + tile, :], se_ref[...], preferred_element_type=jnp.float32)
        rows = pl.ds(pl.multiple_of(me * p + at, tile), tile)
        own, lower, higher = around(sp_ref, rows, pl.ds(e + at, tile))
        column = lax.broadcasted_iota(jnp.int32, (tile, ny), 1)
        left, right = [], []
        for r in range(tall):
            row = own[:, r * ny : (r + 1) * ny]
            left.append(jnp.where(column == 0, 0.0, pltpu.roll(row, 1, 1)))
            right.append(jnp.where(column == ny - 1, 0.0, pltpu.roll(row, ny - 1, 1)))
        left, right = jnp.concatenate(left, axis=1), jnp.concatenate(right, axis=1)
        lap = lower + higher + left + right - 4.0 * own
        diffusion, rate = as_column(diffusion_ref[:, at : at + tile]), as_column(p_rate_ref[:, at : at + tile])
        new = own + diffusion * lap + 0.5 * source
        if last:
            p_out_ref[at : at + tile, :] = new
        else:
            store(new / (1.0 + rate), at, tile, e)

    if edges:
        for to_ref, is_final in ((to_refs[0], even), (to_refs[1], jnp.logical_not(even))):

            @pl.when(is_final)
            def _():
                to_ref[...] = final_ref[...]

            @pl.when(jnp.logical_not(is_final))
            def _():
                to_ref[...] = first_ref[...]


def on_device(
    electrons,
    phonons,
    emission,
    absorption,
    block_coupling,
    block_cols,
    upwind,
    speed,
    diffusion,
    electron_rate,
    phonon_rate,
):
    e, nx, ny = electrons.shape
    p = phonons.shape[0]
    n = lax.axis_size("mode")
    chips = n // CORES
    slots = block_coupling.shape[1]
    b_rows = p // BLK
    tall = nx // CHUNKS
    width = tall * ny
    lanes = pltpu.VMEM((64 * nx, ny), jnp.float32)
    me, space = (lax.axis_index(a).astype(jnp.uint32) for a in ("mode", "space"))
    chip, core = me // CORES, me % CORES
    places = [space % 2] + [((chip + d) % chips) * CORES + (core ^ c) for d in range(chips) for c in range(CORES)]

    places = jnp.stack(places).astype(jnp.int32)

    near_e = swap_cores(electrons)
    far_e = [from_chip(electrons, d) for d in range(1, chips)]
    e_all, *flat, to_a, to_b = call(
        lambda *refs: flatten_own_kernel(nx, ny, PARTS, *refs),
        (bf16(e, nx * ny),) + tuple(bf16(p // count, width) for count in PARTS for _ in range(count))
        + (bf16(e + p, ny),) * 2,
        [pltpu.VMEM((e * nx, ny), jnp.bfloat16), pltpu.VMEM((p * nx, ny), jnp.bfloat16), lanes],
        (places, electrons.reshape(e * nx, ny), phonons.reshape(p * nx, ny)), [SMEM, ANY, ANY], 8, "flatten", 2,
    )
    p_chunks = [flat[sum(PARTS[:k]) : sum(PARTS[: k + 1])] for k in range(CHUNKS)]
    block_coupling = after(block_coupling, flat[0])
    kernel = block_coupling.reshape(b_rows, BLK, slots, BLK)
    block_ids = jnp.arange(NM // BLK, dtype=jnp.int32)
    hits = (block_cols[:, :, None] == block_ids[None, None, :]).astype(jnp.bfloat16)
    dense = jnp.einsum(
        "bsk,bisj->bikj", hits, kernel, preferred_element_type=jnp.float32
    ).astype(jnp.bfloat16).reshape(p, NM)

    ups = [upwind[k * tall : (k + 1) * tall].reshape(1, width) for k in range(CHUNKS)]
    weights = (emission, absorption, dense)
    rates = (speed[None], diffusion[None], electron_rate[None], phonon_rate[None])

    def step(k, es, ps, before, behind, done, border):
        last, edges = bool(done), len(border)
        done = [d[0] for d in done]
        es = es[:1] if last else es
        matrices = weights[1:] if last else weights
        counts = (len(ps[0]), len(before[1]), len(behind[1]))
        operands = (
            places, *(x for x, _ in es), *(x for parts in ps for x in parts), before[0], *before[1], behind[0],
            *behind[1], *matrices, ups[k], *rates, *done, *border,
        )
        large = len(es) + n * counts[0] + counts[1] + counts[2] + 2 + len(matrices)
        specs = [SMEM] + [ANY] * large + [VMEM] * 5 + [ANY] * (len(done) + edges)
        scratch = [
            pltpu.VMEM(shape, jnp.bfloat16)
            for shape in (
                *([] if last else [(p, n * e)]), (len(es) * e, width), (n * p, width), (e, n * p), (p, NM),
                (e + p, ny), (e + p, ny),
            )
        ]
        if last:
            out = (bf16(e * nx, ny), jax.ShapeDtypeStruct((p, width), jnp.float32))
            scratch += [pltpu.VMEM((CHUNKS - 1, e, width), jnp.bfloat16), pltpu.VMEM((e * nx, ny), jnp.float32)]
        else:
            out = (bf16(e, width), bf16(p, width)) + (bf16(e + p, ny),) * edges
            scratch += [pltpu.VMEM((e + p, ny), jnp.bfloat16)] * edges
        return call(
            lambda *refs: step_kernel(n, e, p, width, ny, nx, k, [c for _, c in es], counts, edges, last, *refs),
            out, scratch, operands, specs, 28, "step", large + len(done) + edges + 1,
        )

    def emit(es, rest, done):
        operands = (places, *(x for x, _ in es), rest, emission, rates[3], *(d[1] for d in done))
        return call(
            lambda *refs: emit_kernel(n, e, p, ny, nx, *refs), (bf16(p * nx, ny),),
            [pltpu.VMEM((n * e, width), jnp.bfloat16), pltpu.VMEM((min(p, 256) * nx, ny), jnp.float32)],
            operands, [SMEM] + [ANY] * n + [VMEM] * (2 + CHUNKS), 16, "emit", n,
        )[0]

    def gathered(own, far, wait_for):
        arrays = []
        for f in far:
            f = after(f, *wait_for)
            arrays += [f, swap_cores(f)]
        return [own, swap_cores(own)] + arrays

    halo = halos(to_a, to_b)
    far_p = [[[from_chip(x, d) for d in range(1, chips)] for x in parts] for parts in p_chunks]
    others = [near_e]
    for f in far_e:
        f = after(f, flat[0], *halo)
        others += [f, swap_cores(f)]
    others = call(
        lambda *refs: flatten_others_kernel(nx, ny, n - 1, *refs),
        (bf16(e, nx * ny),) * (n - 1),
        [pltpu.VMEM((e * nx, ny), jnp.bfloat16)] * (n - 1) + [lanes],
        [x.reshape(e * nx, ny) for x in others], [ANY] * (n - 1), 12, "flatten", n - 1,
    )
    everyone = [e_all, *others]
    waits = (dense, *halo)
    new = []
    for k in range(CHUNKS):
        ps = list(zip(*(gathered(x, far, waits) for x, far in zip(p_chunks[k], far_p[k]))))
        new.append(step(
            k, [(x, k * width) for x in everyone], ps,
            (e_all, p_chunks[k - 1]) if k else (halo[0], halo[1:]),
            (e_all, p_chunks[k + 1]) if k + 1 < CHUNKS else (halo[0], halo[1:]), [],
            () if k + 1 < CHUNKS else new[0][:2],
        ))
        waits = (new[-1][1],)
    halo = halos(new[-1][2], new[-1][3])
    chunks = [c[:2] for c in new]

    far_p = [[from_chip(c[1], d) for d in range(1, chips)] for c in chunks]
    ready = (chunks[-1][1], *halo)
    far_e = [[from_chip(c[0], d) for d in range(1, chips)] for c in chunks]

    def everyone_at(k, waits):
        return [(x, 0) for x in gathered(chunks[k][0], far_e[k], waits)]

    done = []
    for k in range(CHUNKS):
        waits = (done[-1][1],) if k else ready
        ps = [[x] for x in gathered(chunks[k][1], far_p[k], waits)]
        last = k + 1 == CHUNKS
        out = step(
            k, [(chunks[k][0], 0)] if last else everyone_at(k, waits), ps,
            (chunks[k - 1][0], chunks[k - 1][1:]) if k else (halo[0], halo[1:]),
            (halo[0], halo[1:]) if last else (chunks[k + 1][0], chunks[k + 1][1:]), done if last else [], (),
        )
        if not last:
            done.append(out)
    e_out, rest = out
    p_out = emit(everyone_at(CHUNKS - 1, (rest,)), rest, done)
    return e_out.reshape(e, nx, ny), p_out.reshape(p, nx, ny)


def solution(mesh):
    placed = (
        P("mode", ("grp", "space"), None),
        P("mode", ("grp", "space"), None),
        P("mode", None),
        P("mode", None),
        P("mode", None, None),
        P("mode", None),
        P(("grp", "space"), None),
        P("mode"),
        P("mode"),
        P("mode"),
        P("mode"),
    )
    return jax.shard_map(
        on_device,
        mesh=mesh,
        in_specs=placed,
        out_specs=(P("mode", ("grp", "space"), None), P("mode", ("grp", "space"), None)),
        check_vma=False,
    )
```

time: 110 us -> 84.7 us (0.77)
  waiting for transfers between devices: 49.4 us -> 29 us
  Pallas kernels: 25.5 us -> 22.6 us
    ppermute x16, waiting for transfers between devices: 23.2 us -> 4.52 us  [swap_cores(): return lax.ppermute(x, 'mode', [(i, i ^ 1) for i in range(n)])]
    ppermute x4, waiting for transfers between devices: 14.5 us -> 5.07 us  [halos(): return (lax.ppermute(a, 'space', near), lax.ppermute(b, 'space', other))]
    ppermute x7 -> x8, waiting for transfers between devices: 11.7 us -> 19.4 us  [from_chip(): lax.ppermute(x, 'mode', [((i + CORES * offset) % n, i) for i in range(n)])]
    pallas_call x7, Pallas kernels: 25.5 us -> 22.6 us  [call(): pl.pallas_call(kernel, out_shape=out, in_specs=specs, out_specs=(VMEM,) *...]
    ppermute x4, starting transfers between devices: 10.2 us -> 9.05 us  [halos(): return (lax.ppermute(a, 'space', near), lax.ppermute(b, 'space', other))]
    ppermute x7 -> x8, starting transfers between devices: 3.86 us -> 4.09 us  [from_chip(): lax.ppermute(x, 'mode', [((i + CORES * offset) % n, i) for i in range(n)])]
    unnamed x23 -> x21, local copies, waits for them, and re-layouts: 2.87 us -> 2.86 us
  transfers between devices with their start and end apart: 27 -> 28, of which waited for: 10 -> 13; matrix products, arithmetic and copies ran while one was open for 4% -> 3% of each run, Pallas kernels for 18% -> 24%
where the time goes in v7:
time: 84.7 us; the launch traced here: 84.3 us
  waiting for transfers between devices  29 us (34%)
  starting transfers between devices  26.9 us (32%)
  Pallas kernels  22.6 us (27%)
  local copies, waits for them, and re-layouts  2.95 us (3%)
  matrix products  1.83 us (2%)
  between operations  1.04 us (1%)
    pallas_call x7, Pallas kernels, call(): pl.pallas_call(kernel, out_shape=out, in_specs=specs, out_specs=(VMEM,) *...  22.6 us
    ppermute x8, waiting for transfers between devices, from_chip(): lax.ppermute(x, 'mode', [((i + CORES * offset) % n, i) for i in range(n)])  19.4 us
    ppermute x16, starting transfers between devices, swap_cores(): return lax.ppermute(x, 'mode', [(i, i ^ 1) for i in range(n)])  13.7 us
    ppermute x4, starting transfers between devices, halos(): return (lax.ppermute(a, 'space', near), lax.ppermute(b, 'space', other))  9.05 us
    ppermute x4, waiting for transfers between devices, halos(): return (lax.ppermute(a, 'space', near), lax.ppermute(b, 'space', other))  5.07 us
    ppermute x16, waiting for transfers between devices, swap_cores(): return lax.ppermute(x, 'mode', [(i, i ^ 1) for i in range(n)])  4.52 us
    ppermute x8, starting transfers between devices, from_chip(): lax.ppermute(x, 'mode', [((i + CORES * offset) % n, i) for i in range(n)])  4.09 us
    unnamed x21, local copies, waits for them, and re-layouts  2.86 us
  transfers between devices with their start and end apart: 28, of which 13 were waited for; matrix products, arithmetic and copies ran while one was open for 3% of the time, Pallas kernels for 24%

profile of v7, /device:TPU:13, one launch (start us, length us, event | category | flops | bytes accessed | tf_op | source)
XLA Modules:
  0.0 84.3 jit_solution(14546277613533990265)
XLA Ops:
  1.0 1.2 %copy-done.2 = bf16[512,8,128]{2,1,0:T(8,128)(2,1)S(1)} copy-done((bf16[512,8,128]{2,1,0:T(8,128)(2,1)S(1)}, bf16[512,8,128]{2,1,0:T(8,128)(2,1)}, u32[]{:S(2)}) %copy-start.2) | copy-done | bytes 1048600
  3.3 1.5 %flatten.2 = (bf16[256,1024]{1,0:T(8,128)(2,1)S(1)}, bf16[512,512]{1,0:T(8,128)(2,1)S(1)}, bf16[256,512]{1,0:T(8,128)(2,1)S(1)}, bf16[256,512]{1,0:T(8,128)(2,1)...) custom-call(s32[5]{0:T(128)S(1)} %convert_element_type.27.refs_0_, bf16[2048,128]{1,0:T(8,128)(2,1)S(1)} %bitcast.38, ...), custom_call_target="tpu_custom_call" | custom-call | flops 1000 | bytes 1000 | tf_op jit(solution)/shard_map/flatten/pallas_call | solution.py:47
  4.8 1.3 %collective-permute-start.9 = (bf16[512,512]{1,0:T(8,128)(2,1)S(1)}, bf16[512,512]{1,0:T(8,128)(2,1)S(1)}, u32[]{:S(2)}, u32[]{:S(2)}) collective-permute-start(bf16[512,512]{1,0:T(8,128)(2,1)S(1)} %get-tuple-element.31.refs_5_.refs_14_), channel_id=1, source_target_pairs={{8,0},{12,4},{0,8},{4,12},{9,1},{13,5},{1,9},{5,13},{10,2},{14,6},... | collective-permute-start | bytes 1572872 | tf_op jit(solution)/shard_map/ppermute | solution.py:28
  6.1 1.2 %collective-permute-start = (bf16[256,8,128]{2,1,0:T(8,128)(2,1)S(1)}, bf16[256,8,128]{2,1,0:T(8,128)(2,1)S(1)}, u32[]{:S(2)}, u32[]{:S(2)}) collective-permute-start(bf16[256,8,128]{2,1,0:T(8,128)(2,1)S(1)} %copy-done.3), channel_id=1, source_target_pairs={{0,4},{4,0},{8,12},{12,8},{1,5},{5,1},{9,13},{13,9},{2,6},{6,2},{1... | collective-permute-start | bytes 1572872 | tf_op jit(solution)/shard_map/ppermute | solution.py:23
  7.5 4.3 %collective-permute-start.3 = (bf16[768,128]{1,0:T(8,128)(2,1)S(1)}, bf16[768,128]{1,0:T(8,128)(2,1)S(1)}, u32[]{:S(2)}, u32[]{:S(2)}) collective-permute-start(bf16[768,128]{1,0:T(8,128)(2,1)S(1)} %get-tuple-element.33), channel_id=1, source_target_pairs={{1,2},{2,1},{5,6},{6,5},{9,10},{10,9},{13,14},{14,13},{17,18},{18,... | collective-permute-start | bytes 589832 | tf_op jit(solution)/shard_map/ppermute | solution.py:35
  11.9 1.8 %fusion.2 = bf16[4,128,128,16]{2,3,1,0:T(8,128)(2,1)S(1)} fusion(bf16[4,128,12,128]{3,1,0,2:T(8,128)(2,1)S(1)} %bitcast.61, s32[4,12]{1,0:T(4,128)} %param.16), kind=kOutput, calls=%fused_computation.3 | convolution fusion | flops 26215168 | bytes 3670208 | tf_op jit(solution)/shard_map/bsk,bisj->bikj/dot_general | solution.py:332
  15.0 1.9 %collective-permute-done.3.refs_10_.refs_16_ = bf16[768,128]{1,0:T(8,128)(2,1)S(1)} collective-permute-done((bf16[768,128]{1,0:T(8,128)(2,1)S(1)}, bf16[768,128]{1,0:T(8,128)(2,1)S(1)}, u32[]{:S(2)}, u32[]{:S(2)}) %collective-permute-start.3) | collective-permute-done | bytes 196640 | tf_op jit(solution)/shard_map/ppermute | solution.py:35
  17.7 7.2 %collective-permute-done.9.refs_7_ = bf16[512,512]{1,0:T(8,128)(2,1)S(1)} collective-permute-done((bf16[512,512]{1,0:T(8,128)(2,1)S(1)}, bf16[512,512]{1,0:T(8,128)(2,1)S(1)}, u32[]{:S(2)}, u32[]{:S(2)}) %collective-permute-start.9) | collective-permute-done | bytes 524320 | tf_op jit(solution)/shard_map/ppermute | solution.py:28
  24.9 1.5 %collective-permute-start.10 = (bf16[512,512]{1,0:T(8,128)(2,1)S(1)}, bf16[512,512]{1,0:T(8,128)(2,1)S(1)}, u32[]{:S(2)}, u32[]{:S(2)}) collective-permute-start(bf16[512,512]{1,0:T(8,128)(2,1)S(1)} %collective-permute-done.9.refs_7_), channel_id=1, source_target_pairs={{0,4},{4,0},{8,12},{12,8},{1,5},{5,1},{9,13},{13,9},{2,6},{6,2},{1... | collective-permute-start | bytes 1572872 | tf_op jit(solution)/shard_map/ppermute | solution.py:23
  26.7 1.2 %collective-permute-start.7 = (bf16[256,512]{1,0:T(8,128)(2,1)S(1)}, bf16[256,512]{1,0:T(8,128)(2,1)S(1)}, u32[]{:S(2)}, u32[]{:S(2)}) collective-permute-start(bf16[256,512]{1,0:T(8,128)(2,1)S(1)} %get-tuple-element.38.refs_12_.refs_5_), channel_id=1, source_target_pairs={{8,0},{12,4},{0,8},{4,12},{9,1},{13,5},{1,9},{5,13},{10,2},{14,6},... | collective-permute-start | bytes 786440 | tf_op jit(solution)/shard_map/ppermute | solution.py:28
  29.0 4.2 %step.4 = (bf16[256,512]{1,0:T(8,128)(2,1)S(1)}, bf16[512,512]{1,0:T(8,128)(2,1)S(1)}) custom-call(s32[5]{0:T(128)S(1)} %convert_element_type.27.refs_0_, bf16[256,1024]{1,0:T(8,128)(2,1)S(1)} %get-tuple-element.30.refs_1_.refs_11_.refs_13_, bf16[256,1024]{1,0:T(8,128)(2,1)S(1)} %get-tuple-element.35.refs_2_, ...), custom_call_target="tpu_custom_call" | custom-call | flops 1000 | bytes 1000 | tf_op jit(solution)/shard_map/step/pallas_call | solution.py:47
  34.4 1.2 %collective-permute-start.13 = (bf16[256,512]{1,0:T(8,128)(2,1)S(1)}, bf16[256,512]{1,0:T(8,128)(2,1)S(1)}, u32[]{:S(2)}, u32[]{:S(2)}) collective-permute-start(bf16[256,512]{1,0:T(8,128)(2,1)S(1)} %collective-permute-done.11.refs_10_), channel_id=1, source_target_pairs={{0,4},{4,0},{8,12},{12,8},{1,5},{5,1},{9,13},{13,9},{2,6},{6,2},{1... | collective-permute-start | bytes 786440 | tf_op jit(solution)/shard_map/ppermute | solution.py:23
  35.6 4.4 %collective-permute-done.7.refs_9_ = bf16[256,512]{1,0:T(8,128)(2,1)S(1)} collective-permute-done((bf16[256,512]{1,0:T(8,128)(2,1)S(1)}, bf16[256,512]{1,0:T(8,128)(2,1)S(1)}, u32[]{:S(2)}, u32[]{:S(2)}) %collective-permute-start.7) | collective-permute-done | bytes 262176 | tf_op jit(solution)/shard_map/ppermute | solution.py:28
  42.4 4.4 %step.5 = (bf16[256,512]{1,0:T(8,128)(2,1)S(1)}, bf16[512,512]{1,0:T(8,128)(2,1)S(1)}, bf16[768,128]{1,0:T(8,128)(2,1)S(1)}, bf16[768,128]{1,0:T(8,128)(2,1)S(1)}) custom-call(s32[5]{0:T(128)S(1)} %convert_element_type.27.refs_0_, bf16[256,1024]{1,0:T(8,128)(2,1)S(1)} %get-tuple-element.30.refs_1_.refs_11_.refs_13_, ...), custom_call_target="tpu_custom_call" | custom-call | flops 1000 | bytes 1000 | tf_op jit(solution)/shard_map/step/pallas_call | solution.py:47
  47.0 4.3 %collective-permute-start.19 = (bf16[768,128]{1,0:T(8,128)(2,1)S(1)}, bf16[768,128]{1,0:T(8,128)(2,1)S(1)}, u32[]{:S(2)}, u32[]{:S(2)}) collective-permute-start(bf16[768,128]{1,0:T(8,128)(2,1)S(1)} %get-tuple-element.49), channel_id=1, source_target_pairs={{1,2},{2,1},{5,6},{6,5},{9,10},{10,9},{13,14},{14,13},{17,18},{18,... | collective-permute-start | bytes 589832 | tf_op jit(solution)/shard_map/ppermute | solution.py:35
  51.7 1.2 %collective-permute-start.21 = (bf16[512,512]{1,0:T(8,128)(2,1)S(1)}, bf16[512,512]{1,0:T(8,128)(2,1)S(1)}, u32[]{:S(2)}, u32[]{:S(2)}) collective-permute-start(bf16[512,512]{1,0:T(8,128)(2,1)S(1)} %get-tuple-element.42.refs_26_.refs_5_.refs_7_), channel_id=1, source_target_pairs={{0,4},{4,0},{8,12},{12,8},{1,5},{5,1},{9,13},{13,9},{2,6},{6,2},{1... | collective-permute-start | bytes 1572872 | tf_op jit(solution)/shard_map/ppermute | solution.py:23
  53.0 3.0 %collective-permute-done.19.refs_10_.refs_9_ = bf16[768,128]{1,0:T(8,128)(2,1)S(1)} collective-permute-done((bf16[768,128]{1,0:T(8,128)(2,1)S(1)}, bf16[768,128]{1,0:T(8,128)(2,1)S(1)}, u32[]{:S(2)}, u32[]{:S(2)}) %collective-permute-start.19) | collective-permute-done | bytes 196640 | tf_op jit(solution)/shard_map/ppermute | solution.py:35
  56.0 1.2 %collective-permute-start.23 = (bf16[512,512]{1,0:T(8,128)(2,1)S(1)}, bf16[512,512]{1,0:T(8,128)(2,1)S(1)}, u32[]{:S(2)}, u32[]{:S(2)}) collective-permute-start(bf16[512,512]{1,0:T(8,128)(2,1)S(1)} %collective-permute-done.22.refs_7_), channel_id=1, source_target_pairs={{0,4},{4,0},{8,12},{12,8},{1,5},{5,1},{9,13},{13,9},{2,6},{6,2},{1... | collective-permute-start | bytes 1572872 | tf_op jit(solution)/shard_map/ppermute | solution.py:23
  58.3 1.8 %collective-permute-start.20 = (bf16[256,512]{1,0:T(8,128)(2,1)S(1)}, bf16[256,512]{1,0:T(8,128)(2,1)S(1)}, u32[]{:S(2)}, u32[]{:S(2)}) collective-permute-start(bf16[256,512]{1,0:T(8,128)(2,1)S(1)} %collective-permute-done.17.refs_3_), channel_id=1, source_target_pairs={{0,4},{4,0},{8,12},{12,8},{1,5},{5,1},{9,13},{13,9},{2,6},{6,2},{1... | collective-permute-start | bytes 786440 | tf_op jit(solution)/shard_map/ppermute | solution.py:23
  61.3 4.3 %step.6 = (bf16[256,512]{1,0:T(8,128)(2,1)S(1)}, bf16[512,512]{1,0:T(8,128)(2,1)S(1)}) custom-call(s32[5]{0:T(128)S(1)} %convert_element_type.27.refs_0_, bf16[256,512]{1,0:T(8,128)(2,1)S(1)} %get-tuple-element.45.refs_25_.refs_1_.refs_6_, bf16[256,512]{1,0:T(8,128)(2,1)S(1)} %collective-permute-done.16.refs_2_, ...), custom_call_target="tpu_custom_call" | custom-call | flops 1000 | bytes 1000 | tf_op jit(solution)/shard_map/step/pallas_call | solution.py:47
  65.7 5.1 %collective-permute-done.15.refs_4_ = bf16[512,512]{1,0:T(8,128)(2,1)S(1)} collective-permute-done((bf16[512,512]{1,0:T(8,128)(2,1)S(1)}, bf16[512,512]{1,0:T(8,128)(2,1)S(1)}, u32[]{:S(2)}, u32[]{:S(2)}) %collective-permute-start.15) | collective-permute-done | bytes 524320 | tf_op jit(solution)/shard_map/ppermute | solution.py:28
  73.1 4.5 %step.7 = (bf16[2048,128]{1,0:T(8,128)(2,1)}, f32[512,512]{1,0:T(8,128)S(1)}) custom-call(s32[5]{0:T(128)S(1)} %convert_element_type.27.refs_0_, bf16[256,512]{1,0:T(8,128)(2,1)S(1)} %get-tuple-element.46.refs_11_.refs_1_, bf16[512,512]{1,0:T(8,128)(2,1)S(1)} %get-tuple-element.47.refs_12_.refs_2_, bf16[512,512]{1,0:T(8,128)(2,1)S(1)} %collective-permute-done.14.refs_3_, ...), custom_call_target="tpu_custom_call" | custom-call | flops 1000 | bytes 1000 | tf_op jit(solution)/shard_map/step/pallas_call | solution.py:47
  77.6 1.9 %collective-permute-done.26.refs_3_ = bf16[256,512]{1,0:T(8,128)(2,1)S(1)} collective-permute-done((bf16[256,512]{1,0:T(8,128)(2,1)S(1)}, bf16[256,512]{1,0:T(8,128)(2,1)S(1)}, u32[]{:S(2)}, u32[]{:S(2)}) %collective-permute-start.26) | collective-permute-done | bytes 262176 | tf_op jit(solution)/shard_map/ppermute | solution.py:28
  81.4 2.7 %emit.1 = bf16[4096,128]{1,0:T(8,128)(2,1)} custom-call(s32[5]{0:T(128)S(1)} %convert_element_type.27.refs_0_, bf16[256,512]{1,0:T(8,128)(2,1)S(1)} %get-tuple-element.46.refs_11_.refs_1_, bf16[256,512]{1,0:T(8,128)(2,1)S(1)} %collective-permute-done.25.refs_2_, bf16[256,512]{1,0:T(8,128)(2,1)S(1)} %collective-permute-done.26.refs_3_, ...), custom_call_target="tpu_custom_call" | custom-call | flops 1000 | bytes 1000 | tf_op jit(solution)/shard_map/emit/pallas_call | solution.py:47
  (64 shorter events, 15.5 us)
Async XLA Ops:
  0.6 16.3 %collective-permute-start.1 = (bf16[256,8,128]{2,1,0:T(8,128)(2,1)}, bf16[256,8,128]{2,1,0:T(8,128)(2,1)S(1)}, u32[]{:S(2)}, u32[]{:S(2)}) collective-permute-start(bf16[256,8,128]{2,1,0:T(8,128)(2,1)} %param.11), channel_id=1, source_target_pairs={{8,0},{12,4},{0,8},{4,12},{9,1},{13,5},{1,9},{5,13},{10,2},{14,6},... | collective-permute-start | bytes 1572872 | tf_op jit(solution)/shard_map/ppermute | solution.py:28
  4.8 20.1 %collective-permute-start.9 = (bf16[512,512]{1,0:T(8,128)(2,1)S(1)}, bf16[512,512]{1,0:T(8,128)(2,1)S(1)}, u32[]{:S(2)}, u32[]{:S(2)}) collective-permute-start(bf16[512,512]{1,0:T(8,128)(2,1)S(1)} %get-tuple-element.31.refs_5_.refs_14_), channel_id=1, source_target_pairs={{8,0},{12,4},{0,8},{4,12},{9,1},{13,5},{1,9},{5,13},{10,2},{14,6},... | collective-permute-start | bytes 1572872 | tf_op jit(solution)/shard_map/ppermute | solution.py:28
  6.1 20.6 %collective-permute-start = (bf16[256,8,128]{2,1,0:T(8,128)(2,1)S(1)}, bf16[256,8,128]{2,1,0:T(8,128)(2,1)S(1)}, u32[]{:S(2)}, u32[]{:S(2)}) collective-permute-start(bf16[256,8,128]{2,1,0:T(8,128)(2,1)S(1)} %copy-done.3), channel_id=1, source_target_pairs={{0,4},{4,0},{8,12},{12,8},{1,5},{5,1},{9,13},{13,9},{2,6},{6,2},{1... | collective-permute-start | bytes 1572872 | tf_op jit(solution)/shard_map/ppermute | solution.py:23
  7.4 7.0 %collective-permute-start.2 = (bf16[768,128]{1,0:T(8,128)(2,1)S(1)}, bf16[768,128]{1,0:T(8,128)(2,1)S(1)}, u32[]{:S(2)}, u32[]{:S(2)}) collective-permute-start(bf16[768,128]{1,0:T(8,128)(2,1)S(1)} %get-tuple-element.32), channel_id=1, source_target_pairs={{0,1},{1,0},{2,3},{3,2},{4,5},{5,4},{6,7},{7,6},{8,9},{9,8},{10,11... | collective-permute-start | bytes 589832 | tf_op jit(solution)/shard_map/ppermute | solution.py:35
  7.5 9.4 %collective-permute-start.3 = (bf16[768,128]{1,0:T(8,128)(2,1)S(1)}, bf16[768,128]{1,0:T(8,128)(2,1)S(1)}, u32[]{:S(2)}, u32[]{:S(2)}) collective-permute-start(bf16[768,128]{1,0:T(8,128)(2,1)S(1)} %get-tuple-element.33), channel_id=1, source_target_pairs={{1,2},{2,1},{5,6},{6,5},{9,10},{10,9},{13,14},{14,13},{17,18},{18,... | collective-permute-start | bytes 589832 | tf_op jit(solution)/shard_map/ppermute | solution.py:35
  14.4 14.6 %collective-permute-start.8 = (bf16[512,512]{1,0:T(8,128)(2,1)S(1)}, bf16[512,512]{1,0:T(8,128)(2,1)S(1)}, u32[]{:S(2)}, u32[]{:S(2)}) collective-permute-start(bf16[512,512]{1,0:T(8,128)(2,1)S(1)} %get-tuple-element.31.refs_5_.refs_14_), channel_id=1, source_target_pairs={{0,4},{4,0},{8,12},{12,8},{1,5},{5,1},{9,13},{13,9},{2,6},{6,2},{1... | collective-permute-start | bytes 1572872 | tf_op jit(solution)/shard_map/ppermute | solution.py:23
  16.9 11.0 %collective-permute-start.4 = (bf16[256,8,128]{2,1,0:T(8,128)(2,1)S(1)}, bf16[256,8,128]{2,1,0:T(8,128)(2,1)S(1)}, u32[]{:S(2)}, u32[]{:S(2)}) collective-permute-start(bf16[256,8,128]{2,1,0:T(8,128)(2,1)S(1)} %collective-permute-done.1), channel_id=1, source_target_pairs={{0,4},{4,0},{8,12},{12,8},{1,5},{5,1},{9,13},{13,9},{2,6},{6,2},{1... | collective-permute-start | bytes 1572872 | tf_op jit(solution)/shard_map/ppermute | solution.py:23
  24.9 4.0 %collective-permute-start.10 = (bf16[512,512]{1,0:T(8,128)(2,1)S(1)}, bf16[512,512]{1,0:T(8,128)(2,1)S(1)}, u32[]{:S(2)}, u32[]{:S(2)}) collective-permute-start(bf16[512,512]{1,0:T(8,128)(2,1)S(1)} %collective-permute-done.9.refs_7_), channel_id=1, source_target_pairs={{0,4},{4,0},{8,12},{12,8},{1,5},{5,1},{9,13},{13,9},{2,6},{6,2},{1... | collective-permute-start | bytes 1572872 | tf_op jit(solution)/shard_map/ppermute | solution.py:23
  26.5 7.9 %collective-permute-start.11 = (bf16[256,512]{1,0:T(8,128)(2,1)S(1)}, bf16[256,512]{1,0:T(8,128)(2,1)S(1)}, u32[]{:S(2)}, u32[]{:S(2)}) collective-permute-start(bf16[256,512]{1,0:T(8,128)(2,1)S(1)} %get-tuple-element.39.refs_13_.refs_6_), channel_id=1, source_target_pairs={{8,0},{12,4},{0,8},{4,12},{9,1},{13,5},{1,9},{5,13},{10,2},{14,6},... | collective-permute-start | bytes 786440 | tf_op jit(solution)/shard_map/ppermute | solution.py:28
  26.7 13.3 %collective-permute-start.7 = (bf16[256,512]{1,0:T(8,128)(2,1)S(1)}, bf16[256,512]{1,0:T(8,128)(2,1)S(1)}, u32[]{:S(2)}, u32[]{:S(2)}) collective-permute-start(bf16[256,512]{1,0:T(8,128)(2,1)S(1)} %get-tuple-element.38.refs_12_.refs_5_), channel_id=1, source_target_pairs={{8,0},{12,4},{0,8},{4,12},{9,1},{13,5},{1,9},{5,13},{10,2},{14,6},... | collective-permute-start | bytes 786440 | tf_op jit(solution)/shard_map/ppermute | solution.py:28
  33.2 22.8 %collective-permute-start.22 = (bf16[512,512]{1,0:T(8,128)(2,1)S(1)}, bf16[512,512]{1,0:T(8,128)(2,1)S(1)}, u32[]{:S(2)}, u32[]{:S(2)}) collective-permute-start(bf16[512,512]{1,0:T(8,128)(2,1)S(1)} %get-tuple-element.42.refs_26_.refs_5_.refs_7_), channel_id=1, source_target_pairs={{8,0},{12,4},{0,8},{4,12},{9,1},{13,5},{1,9},{5,13},{10,2},{14,6},... | collective-permute-start | bytes 1572872 | tf_op jit(solution)/shard_map/ppermute | solution.py:28
  33.5 7.7 %collective-permute-start.5 = (bf16[256,512]{1,0:T(8,128)(2,1)S(1)}, bf16[256,512]{1,0:T(8,128)(2,1)S(1)}, u32[]{:S(2)}, u32[]{:S(2)}) collective-permute-start(bf16[256,512]{1,0:T(8,128)(2,1)S(1)} %get-tuple-element.38.refs_12_.refs_5_), channel_id=1, source_target_pairs={{0,4},{4,0},{8,12},{12,8},{1,5},{5,1},{9,13},{13,9},{2,6},{6,2},{1... | collective-permute-start | bytes 786440 | tf_op jit(solution)/shard_map/ppermute | solution.py:23
  34.3 6.9 %collective-permute-start.6 = (bf16[256,512]{1,0:T(8,128)(2,1)S(1)}, bf16[256,512]{1,0:T(8,128)(2,1)S(1)}, u32[]{:S(2)}, u32[]{:S(2)}) collective-permute-start(bf16[256,512]{1,0:T(8,128)(2,1)S(1)} %get-tuple-element.39.refs_13_.refs_6_), channel_id=1, source_target_pairs={{0,4},{4,0},{8,12},{12,8},{1,5},{5,1},{9,13},{13,9},{2,6},{6,2},{1... | collective-permute-start | bytes 786440 | tf_op jit(solution)/shard_map/ppermute | solution.py:23
  34.4 6.8 %collective-permute-start.13 = (bf16[256,512]{1,0:T(8,128)(2,1)S(1)}, bf16[256,512]{1,0:T(8,128)(2,1)S(1)}, u32[]{:S(2)}, u32[]{:S(2)}) collective-permute-start(bf16[256,512]{1,0:T(8,128)(2,1)S(1)} %collective-permute-done.11.refs_10_), channel_id=1, source_target_pairs={{0,4},{4,0},{8,12},{12,8},{1,5},{5,1},{9,13},{13,9},{2,6},{6,2},{1... | collective-permute-start | bytes 786440 | tf_op jit(solution)/shard_map/ppermute | solution.py:23
  46.8 6.2 %collective-permute-start.18 = (bf16[768,128]{1,0:T(8,128)(2,1)S(1)}, bf16[768,128]{1,0:T(8,128)(2,1)S(1)}, u32[]{:S(2)}, u32[]{:S(2)}) collective-permute-start(bf16[768,128]{1,0:T(8,128)(2,1)S(1)} %get-tuple-element.48), channel_id=1, source_target_pairs={{0,1},{1,0},{2,3},{3,2},{4,5},{5,4},{6,7},{7,6},{8,9},{9,8},{10,11... | collective-permute-start | bytes 589832 | tf_op jit(solution)/shard_map/ppermute | solution.py:35
  47.0 9.0 %collective-permute-start.19 = (bf16[768,128]{1,0:T(8,128)(2,1)S(1)}, bf16[768,128]{1,0:T(8,128)(2,1)S(1)}, u32[]{:S(2)}, u32[]{:S(2)}) collective-permute-start(bf16[768,128]{1,0:T(8,128)(2,1)S(1)} %get-tuple-element.49), channel_id=1, source_target_pairs={{1,2},{2,1},{5,6},{6,5},{9,10},{10,9},{13,14},{14,13},{17,18},{18,... | collective-permute-start | bytes 589832 | tf_op jit(solution)/shard_map/ppermute | solution.py:35
  51.4 7.0 %collective-permute-start.17 = (bf16[256,512]{1,0:T(8,128)(2,1)S(1)}, bf16[256,512]{1,0:T(8,128)(2,1)S(1)}, u32[]{:S(2)}, u32[]{:S(2)}) collective-permute-start(bf16[256,512]{1,0:T(8,128)(2,1)S(1)} %get-tuple-element.45.refs_25_.refs_1_.refs_6_), channel_id=1, source_target_pairs={{8,0},{12,4},{0,8},{4,12},{9,1},{13,5},{1,9},{5,13},{10,2},{14,6},... | collective-permute-start | bytes 786440 | tf_op jit(solution)/shard_map/ppermute | solution.py:28
  51.7 8.5 %collective-permute-start.21 = (bf16[512,512]{1,0:T(8,128)(2,1)S(1)}, bf16[512,512]{1,0:T(8,128)(2,1)S(1)}, u32[]{:S(2)}, u32[]{:S(2)}) collective-permute-start(bf16[512,512]{1,0:T(8,128)(2,1)S(1)} %get-tuple-element.42.refs_26_.refs_5_.refs_7_), channel_id=1, source_target_pairs={{0,4},{4,0},{8,12},{12,8},{1,5},{5,1},{9,13},{13,9},{2,6},{6,2},{1... | collective-permute-start | bytes 1572872 | tf_op jit(solution)/shard_map/ppermute | solution.py:23
  56.0 5.3 %collective-permute-start.23 = (bf16[512,512]{1,0:T(8,128)(2,1)S(1)}, bf16[512,512]{1,0:T(8,128)(2,1)S(1)}, u32[]{:S(2)}, u32[]{:S(2)}) collective-permute-start(bf16[512,512]{1,0:T(8,128)(2,1)S(1)} %collective-permute-done.22.refs_7_), channel_id=1, source_target_pairs={{0,4},{4,0},{8,12},{12,8},{1,5},{5,1},{9,13},{13,9},{2,6},{6,2},{1... | collective-permute-start | bytes 1572872 | tf_op jit(solution)/shard_map/ppermute | solution.py:23
  57.2 13.6 %collective-permute-start.15 = (bf16[512,512]{1,0:T(8,128)(2,1)S(1)}, bf16[512,512]{1,0:T(8,128)(2,1)S(1)}, u32[]{:S(2)}, u32[]{:S(2)}) collective-permute-start(bf16[512,512]{1,0:T(8,128)(2,1)S(1)} %get-tuple-element.47.refs_12_.refs_2_), channel_id=1, source_target_pairs={{8,0},{12,4},{0,8},{4,12},{9,1},{13,5},{1,9},{5,13},{10,2},{14,6},... | collective-permute-start | bytes 1572872 | tf_op jit(solution)/shard_map/ppermute | solution.py:28
  58.3 3.0 %collective-permute-start.20 = (bf16[256,512]{1,0:T(8,128)(2,1)S(1)}, bf16[256,512]{1,0:T(8,128)(2,1)S(1)}, u32[]{:S(2)}, u32[]{:S(2)}) collective-permute-start(bf16[256,512]{1,0:T(8,128)(2,1)S(1)} %collective-permute-done.17.refs_3_), channel_id=1, source_target_pairs={{0,4},{4,0},{8,12},{12,8},{1,5},{5,1},{9,13},{13,9},{2,6},{6,2},{1... | collective-permute-start | bytes 786440 | tf_op jit(solution)/shard_map/ppermute | solution.py:23
  60.2 11.9 %collective-permute-start.14 = (bf16[512,512]{1,0:T(8,128)(2,1)S(1)}, bf16[512,512]{1,0:T(8,128)(2,1)S(1)}, u32[]{:S(2)}, u32[]{:S(2)}) collective-permute-start(bf16[512,512]{1,0:T(8,128)(2,1)S(1)} %get-tuple-element.47.refs_12_.refs_2_), channel_id=1, source_target_pairs={{0,4},{4,0},{8,12},{12,8},{1,5},{5,1},{9,13},{13,9},{2,6},{6,2},{1... | collective-permute-start | bytes 1572872 | tf_op jit(solution)/shard_map/ppermute | solution.py:23
  71.6 7.9 %collective-permute-start.26 = (bf16[256,512]{1,0:T(8,128)(2,1)S(1)}, bf16[256,512]{1,0:T(8,128)(2,1)S(1)}, u32[]{:S(2)}, u32[]{:S(2)}) collective-permute-start(bf16[256,512]{1,0:T(8,128)(2,1)S(1)} %get-tuple-element.46.refs_11_.refs_1_), channel_id=1, source_target_pairs={{8,0},{12,4},{0,8},{4,12},{9,1},{13,5},{1,9},{5,13},{10,2},{14,6},... | collective-permute-start | bytes 786440 | tf_op jit(solution)/shard_map/ppermute | solution.py:28
  71.8 8.5 %collective-permute-start.25 = (bf16[256,512]{1,0:T(8,128)(2,1)S(1)}, bf16[256,512]{1,0:T(8,128)(2,1)S(1)}, u32[]{:S(2)}, u32[]{:S(2)}) collective-permute-start(bf16[256,512]{1,0:T(8,128)(2,1)S(1)} %get-tuple-element.46.refs_11_.refs_1_), channel_id=1, source_target_pairs={{0,4},{4,0},{8,12},{12,8},{1,5},{5,1},{9,13},{13,9},{2,6},{6,2},{1... | collective-permute-start | bytes 786440 | tf_op jit(solution)/shard_map/ppermute | solution.py:23
  (14 other events, 125.7 us)

commit v8 on v7

v8 whole, which is shorter than its diff:
```python
import jax
import jax.numpy as jnp
from jax import lax
from jax.experimental import pallas as pl
from jax.experimental.pallas import tpu as pltpu
from jax.sharding import PartitionSpec as P

NM = 2048
BLK = 128
ITERS = 2
CORES = 2
CHUNKS = 2
SHARES = (3, 5)
PARTS = (1, 1)
NEXT_E_PARTS = 1

VMEM = pl.BlockSpec(memory_space=pltpu.VMEM)
SMEM = pl.BlockSpec(memory_space=pltpu.SMEM)
ANY = pl.BlockSpec(memory_space=pl.ANY)
COST = pl.CostEstimate(flops=1000, bytes_accessed=1000, transcendentals=0)


def swap_cores(x):
    n = lax.axis_size("mode")
    return lax.ppermute(x, "mode", [(i, i ^ 1) for i in range(n)])


def from_chip(x, offset):
    n = lax.axis_size("mode")
    return lax.ppermute(x, "mode", [((i + CORES * offset) % n, i) for i in range(n)])


def halos(a, b):
    n = lax.axis_size("space")
    near = [(i, i ^ 1) for i in range(n) if i ^ 1 < n]
    other = [(i, i + 1 if i % 2 else i - 1) for i in range(n) if 0 <= (i + 1 if i % 2 else i - 1) < n]
    return lax.ppermute(a, "space", near), lax.ppermute(b, "space", other)


def after(x, *others):
    return lax.optimization_barrier((x, *others))[0]


def bf16(*shape):
    return jax.ShapeDtypeStruct(shape, jnp.bfloat16)


def call(kernel, out, scratch, operands, specs, megabytes, name, copies):
    return pl.pallas_call(
        kernel,
        out_shape=out,
        in_specs=specs,
        out_specs=(VMEM,) * len(out),
        scratch_shapes=[*scratch, pltpu.SemaphoreType.DMA((copies,))],
        compiler_params=pltpu.CompilerParams(vmem_limit_bytes=megabytes << 20),
        cost_estimate=COST,
        name=name,
    )(*operands)


class Loader:
    def __init__(self, sems):
        self.sems, self.used = sems, 0

    def start(self, src, dst):
        copy = pltpu.make_async_copy(src, dst, self.sems.at[self.used])
        self.used += 1
        copy.start()
        return copy

    def start_one(self, choose, src, other, dst):
        sem = self.sems.at[self.used]
        self.used += 1

        @pl.when(choose)
        def _():
            pltpu.make_async_copy(src, dst, sem).start()

        @pl.when(jnp.logical_not(choose))
        def _():
            pltpu.make_async_copy(other, dst, sem).start()

        return pltpu.make_async_copy(src, dst, sem)


def rows_at(index, count):
    return pl.ds(pl.multiple_of(index * count, count), count)


def rows_of(base, i, part):
    return pl.ds(base + i * part.shape[0], part.shape[0])


def as_column(row):
    return jnp.transpose(jnp.broadcast_to(row, (8, row.shape[1])))[:, 0:1]


def flatten_one(nx, ny, x_ref, outs, wide_ref):
    count = x_ref.shape[0] // nx
    chunk_of = [(k, c) for k, parts in enumerate(outs) for c in range(parts[0].shape[1] // ny)]
    tile = min([count, 64] + [out.shape[0] for parts in outs for out in parts])
    for at in range(0, count, tile):
        wide_ref[0 : tile * nx, :] = x_ref[at * nx : (at + tile) * nx, :].astype(jnp.float32)
        for r in range(nx):
            k, c = chunk_of[r]
            row = wide_ref[pl.ds(r, tile, stride=nx), :].astype(jnp.bfloat16)
            part, offset = divmod(at, outs[k][0].shape[0])
            outs[k][part][offset : offset + tile, c * ny : (c + 1) * ny] = row


def flatten_own_kernel(nx, ny, counts, place_ref, e_ref, p_ref, e_out_ref, *refs):
    *flat, a_ref, b_ref, e_in, p_in, wide_ref, sems = refs
    outs = []
    for count in counts:
        outs.append(flat[:count])
        flat = flat[count:]
    load = Loader(sems)
    e_copy, p_copy = load.start(e_ref, e_in), load.start(p_ref, p_in)
    e_copy.wait()
    flatten_one(nx, ny, e_in, [[e_out_ref]], wide_ref)
    p_copy.wait()
    flatten_one(nx, ny, p_in, outs, wide_ref)
    e = e_out_ref.shape[0]
    even = place_ref[0] == 0

    def put(to_ref, parts, col, e_col):
        to_ref[0:e, :] = e_out_ref[:, e_col : e_col + ny]
        at = e
        for part in parts:
            to_ref[at : at + part.shape[0], :] = part[:, col : col + ny]
            at += part.shape[0]

    for to_ref, last in ((a_ref, even), (b_ref, jnp.logical_not(even))):

        @pl.when(last)
        def _():
            put(to_ref, outs[-1], outs[-1][0].shape[1] - ny, (nx - 1) * ny)

        @pl.when(jnp.logical_not(last))
        def _():
            put(to_ref, outs[0], 0, 0)


def flatten_others_kernel(nx, ny, count, *refs):
    xs, outs, ins, (wide_ref, sems) = refs[:count], refs[count : 2 * count], refs[2 * count : -2], refs[-2:]
    load = Loader(sems)
    copies = [load.start(x, y) for x, y in zip(xs, ins)]
    for copy, x_ref, out_ref in zip(copies, ins, outs):
        copy.wait()
        flatten_one(nx, ny, x_ref, [[out_ref]], wide_ref)


def unflatten(olds, new, nx, ny, at, out_ref, wide_ref):
    count, row = new.shape[0], 0
    for chunk in [*(x.astype(jnp.float32) for x in olds), new]:
        for r in range(chunk.shape[1] // ny):
            wide_ref[pl.ds(row, count, stride=nx), :] = chunk[:, r * ny : (r + 1) * ny]
            row += 1
    out_ref[at * nx : (at + count) * nx, :] = wide_ref[0 : count * nx, :].astype(jnp.bfloat16)


def finish_kernel(n, e, p, ny, nx, place_ref, *refs):
    far = n - CORES
    far_refs, refs = refs[:far], refs[far:]
    rest_e_ref, rest_p_ref, absorption_ref, dense_ref, e_rate_ref, p_rate_ref = refs[:6]
    done_e, done_p, refs = refs[6 : 5 + CHUNKS], refs[5 + CHUNKS : 4 + 2 * CHUNKS], refs[4 + 2 * CHUNKS :]
    e_out_ref, p_out_ref, p_ref, wide_ref, sems = refs
    load = Loader(sems)
    copies = [load.start(x, p_ref.at[j]) for j, x in enumerate(far_refs)]
    for copy in copies:
        copy.wait()

    def product(weight_ref, at, count):
        total = 0.0
        for j in range(far):
            columns = rows_at(place_ref[1 + CORES + j], p)
            total += jnp.dot(weight_ref[at : at + count, columns], p_ref[j], preferred_element_type=jnp.float32)
        return total

    tile = min(p, 256)
    pieces = [(0, e, absorption_ref, rest_e_ref, e_rate_ref, done_e, e_out_ref)]
    pieces += [(at, tile, dense_ref, rest_p_ref, p_rate_ref, done_p, p_out_ref) for at in range(0, p, tile)]
    for at, count, weight_ref, rest_ref, rate_ref, done, out_ref in pieces:
        total = rest_ref[at : at + count, :] + 0.5 * product(weight_ref, at, count)
        new = total / (1.0 + as_column(rate_ref[:, at : at + count]))
        unflatten([x[at : at + count, :] for x in done], new, nx, ny, at, out_ref, wide_ref)


def step_kernel(n, e, p, width, ny, nx, k, cols, counts, edges, last, place_ref, *refs):
    refs = list(refs)

    def take(count):
        taken = refs[:count]
        del refs[:count]
        return taken

    e_refs, p_refs = [take(counts[3]) for _ in range(n)], [take(counts[0]) for _ in range(CORES if last else n)]
    before, behind = (take(counts[4]), take(counts[1])), (take(counts[5]), take(counts[2]))
    emission_hbm, absorption_hbm, dense_hbm, up_ref, speed_ref, diffusion_ref, e_rate_ref, p_rate_ref = take(8)
    border = (take(counts[6]), take(1)) if edges else ()
    e_out_refs, p_out_ref = take(counts[7]), *take(1)
    to_refs = take(2) if edges else []
    se_ref, sp_ref, emission_ref, absorption_ref, dense_ref, low_ref, high_ref = take(7)
    first_ref, final_ref = take(2) if edges else (None, None)
    load = Loader(refs[0])
    tall = width // ny
    even = place_ref[0] == 0
    me = place_ref[1]
    me_p = 0 if last else me

    early = [load.start(absorption_hbm, absorption_ref)]
    for j, parts in enumerate(p_refs):
        owner = j if last else place_ref[1 + j]
        for i, part in enumerate(parts):
            early.append(load.start(part, sp_ref.at[rows_at(owner * counts[0] + i, p // counts[0]), :]))
    for j, parts in enumerate(e_refs):
        for i, part in enumerate(parts):
            to = se_ref.at[rows_at(place_ref[1 + j] * counts[3] + i, e // counts[3]), :]
            early.append(load.start(part.at[:, cols[j] : cols[j] + width], to))
    if k == 0:
        early.append(load.start_one(even, before[1][0], before[0][0], low_ref))
    else:
        col = cols[0] - ny
        for i, part in enumerate(before[0]):
            early.append(load.start(part.at[:, col : col + ny], low_ref.at[rows_of(0, i, part), :]))
        for i, part in enumerate(before[1]):
            early.append(load.start(part.at[:, part.shape[1] - ny :], low_ref.at[rows_of(e, i, part), :]))
    if k == CHUNKS - 1:
        early.append(load.start_one(even, behind[0][0], behind[1][0], high_ref))
    else:
        col = cols[0] + width
        for i, part in enumerate(behind[0]):
            early.append(load.start(part.at[:, col : col + ny], high_ref.at[rows_of(0, i, part), :]))
        for i, part in enumerate(behind[1]):
            early.append(load.start(part.at[:, 0:ny], high_ref.at[rows_of(e, i, part), :]))
    late = [load.start(dense_hbm, dense_ref), load.start(emission_hbm, emission_ref)]
    if edges:
        for i, part in enumerate(border[0]):
            late.append(load.start(part.at[:, 0:ny], first_ref.at[rows_of(0, i, part), :]))
        for i, part in enumerate(e_out_refs):
            late.append(load.start(border[0][0].at[rows_of(0, i, part), :], part.at[:, 0 : part.shape[1] - width]))
        late.append(load.start(border[1][0].at[:, 0:ny], first_ref.at[e : e + p, :]))
    tile = min(p, 256)

    def around(x_ref, rows, base):
        own = x_ref[rows, :].astype(jnp.float32)
        low, high = low_ref[base, :].astype(jnp.float32), high_ref[base, :].astype(jnp.float32)
        lower = jnp.concatenate([low, own[:, : width - ny]], axis=1) if width > ny else low
        higher = jnp.concatenate([own[:, ny:], high], axis=1) if width > ny else high
        return own, lower, higher

    def store(new, at, count, base):
        new = new.astype(jnp.bfloat16)
        if base:
            p_out_ref[at : at + count, :] = new
        else:
            for i, part in enumerate(e_out_refs):
                columns = slice(part.shape[1] - width, part.shape[1])
                part[:, columns] = new[i * part.shape[0] : (i + 1) * part.shape[0], :]
        if edges:
            final_ref[base + at : base + at + count, :] = new[:, width - ny :]

    def product(weight_ref, at, count):
        if not last:
            return jnp.dot(weight_ref[at : at + count, :], sp_ref[...], preferred_element_type=jnp.float32)
        total = 0.0
        for j in range(CORES):
            weight = weight_ref[at : at + count, rows_at(place_ref[1 + j], p)]
            total += jnp.dot(weight, sp_ref[j * p : (j + 1) * p, :], preferred_element_type=jnp.float32)
        return total

    for copy in early:
        copy.wait()
    gain = product(absorption_ref, 0, e)
    own, lower, higher = around(se_ref, rows_at(me, e), pl.ds(0, e))
    f_up = jnp.where(up_ref[...] == 1, lower, higher)
    new = own - as_column(speed_ref[...]) * (own - f_up) + 0.5 * gain
    if last:
        e_out_refs[0][...] = new
    else:
        store(new / (1.0 + as_column(e_rate_ref[...])), 0, e, 0)
    for copy in late:
        copy.wait()

    for at in range(0, p, tile):
        source = product(dense_ref, at, tile) + jnp.dot(
            emission_ref[at : at + tile, :], se_ref[...], preferred_element_type=jnp.float32
        )
        rows = pl.ds(pl.multiple_of(me_p * p + at, tile), tile)
        own, lower, higher = around(sp_ref, rows, pl.ds(e + at, tile))
        column = lax.broadcasted_iota(jnp.int32, (tile, ny), 1)
        left, right = [], []
        for r in range(tall):
            row = own[:, r * ny : (r + 1) * ny]
            left.append(jnp.where(column == 0, 0.0, pltpu.roll(row, 1, 1)))
            right.append(jnp.where(column == ny - 1, 0.0, pltpu.roll(row, ny - 1, 1)))
        left, right = jnp.concatenate(left, axis=1), jnp.concatenate(right, axis=1)
        lap = lower + higher + left + right - 4.0 * own
        diffusion, rate = as_column(diffusion_ref[:, at : at + tile]), as_column(p_rate_ref[:, at : at + tile])
        new = own + diffusion * lap + 0.5 * source
        if last:
            p_out_ref[at : at + tile, :] = new
        else:
            store(new / (1.0 + rate), at, tile, e)

    if edges:
        for to_ref, is_final in ((to_refs[0], even), (to_refs[1], jnp.logical_not(even))):

            @pl.when(is_final)
            def _():
                to_ref[...] = final_ref[...]

            @pl.when(jnp.logical_not(is_final))
            def _():
                to_ref[...] = first_ref[...]


def on_device(
    electrons,
    phonons,
    emission,
    absorption,
    block_coupling,
    block_cols,
    upwind,
    speed,
    diffusion,
    electron_rate,
    phonon_rate,
):
    e, nx, ny = electrons.shape
    p = phonons.shape[0]
    n = lax.axis_size("mode")
    chips = n // CORES
    slots = block_coupling.shape[1]
    b_rows = p // BLK
    talls = [nx * share // sum(SHARES) for share in SHARES]
    starts = [sum(talls[:k]) for k in range(CHUNKS)]
    widths = [tall * ny for tall in talls]
    lanes = pltpu.VMEM((64 * nx, ny), jnp.float32)
    me, space = (lax.axis_index(a).astype(jnp.uint32) for a in ("mode", "space"))
    chip, core = me // CORES, me % CORES
    places = [space % 2] + [((chip + d) % chips) * CORES + (core ^ c) for d in range(chips) for c in range(CORES)]

    places = jnp.stack(places).astype(jnp.int32)

    near_e = swap_cores(electrons)
    far_e = [from_chip(electrons, d) for d in range(1, chips)]
    e_all, *flat, to_a, to_b = call(
        lambda *refs: flatten_own_kernel(nx, ny, PARTS, *refs),
        (bf16(e, nx * ny),) + tuple(bf16(p // count, width) for count, width in zip(PARTS, widths) for _ in range(count))
        + (bf16(e + p, ny),) * 2,
        [pltpu.VMEM((e * nx, ny), jnp.bfloat16), pltpu.VMEM((p * nx, ny), jnp.bfloat16), lanes],
        (places, electrons.reshape(e * nx, ny), phonons.reshape(p * nx, ny)), [SMEM, ANY, ANY], 8, "flatten", 2,
    )
    p_chunks = [flat[sum(PARTS[:k]) : sum(PARTS[: k + 1])] for k in range(CHUNKS)]
    block_coupling = after(block_coupling, flat[0])
    kernel = block_coupling.reshape(b_rows, BLK, slots, BLK)
    block_ids = jnp.arange(NM // BLK, dtype=jnp.int32)
    hits = (block_cols[:, :, None] == block_ids[None, None, :]).astype(jnp.bfloat16)
    dense = jnp.einsum(
        "bsk,bisj->bikj", hits, kernel, preferred_element_type=jnp.float32
    ).astype(jnp.bfloat16).reshape(p, NM)

    ups = [upwind[a : a + tall].reshape(1, tall * ny) for a, tall in zip(starts, talls)]
    weights = (emission, absorption, dense)
    rates = (speed[None], diffusion[None], electron_rate[None], phonon_rate[None])

    def step(k, es, ps, before, behind, last, border):
        edges, width = len(border), widths[k]
        e_parts = NEXT_E_PARTS if edges else 1
        counts = (
            len(ps[0]), len(before[1]), len(behind[1]), len(es[0][0]), len(before[0]), len(behind[0]),
            len(border[0]) if edges else 0, e_parts,
        )
        operands = (
            places, *(x for parts, _ in es for x in parts), *(x for parts in ps for x in parts), *before[0],
            *before[1], *behind[0], *behind[1], *weights, ups[k], *rates, *(x for parts in border for x in parts),
        )
        large = n * counts[3] + len(ps) * counts[0] + sum(counts[1:3]) + sum(counts[4:6]) + 3
        specs = [SMEM] + [ANY] * large + [VMEM] * 5 + [ANY] * sum(len(parts) for parts in border)
        scratch = [
            pltpu.VMEM(shape, jnp.bfloat16)
            for shape in (
                (n * e, width), (len(ps) * p, width), (p, n * e), (e, n * p), (p, NM), (e + p, ny), (e + p, ny),
            )
        ]
        if last:
            out = tuple(jax.ShapeDtypeStruct((count, width), jnp.float32) for count in (e, p))
        else:
            out = (bf16(e // e_parts, nx * ny if edges else width),) * e_parts + (bf16(p, width),) + (bf16(e + p, ny),) * edges
            scratch += [pltpu.VMEM((e + p, ny), jnp.bfloat16)] * edges
        out = call(
            lambda *refs: step_kernel(n, e, p, width, ny, nx, k, [c for _, c in es], counts, edges, last, *refs),
            out, scratch, operands, specs, 28, "step", large + counts[6] + e_parts + 2,
        )
        return (list(out[:e_parts]), *out[e_parts:])

    def finish(far, rest, done):
        operands = (
            places, *far, *rest, absorption, dense, rates[2], rates[3], *(d[0][0] for d in done), *(d[1] for d in done),
        )
        return call(
            lambda *refs: finish_kernel(n, e, p, ny, nx, *refs), (bf16(e * nx, ny), bf16(p * nx, ny)),
            [pltpu.VMEM((len(far), p, widths[-1]), jnp.bfloat16), pltpu.VMEM((max(e, min(p, 256)) * nx, ny), jnp.float32)],
            operands, [SMEM] + [ANY] * len(far) + [VMEM] * (4 + 2 * CHUNKS), 24, "finish", len(far),
        )

    def gathered(own, far, wait_for):
        arrays = []
        for f in far:
            f = after(f, *wait_for)
            arrays += [f, swap_cores(f)]
        return [own, swap_cores(own)] + arrays

    halo = halos(to_a, to_b)
    far_p = [[[from_chip(x, d) for d in range(1, chips)] for x in parts] for parts in p_chunks]
    others = [near_e]
    for f in far_e:
        f = after(f, flat[0], *halo)
        others += [f, swap_cores(f)]
    others = call(
        lambda *refs: flatten_others_kernel(nx, ny, n - 1, *refs),
        (bf16(e, nx * ny),) * (n - 1),
        [pltpu.VMEM((e * nx, ny), jnp.bfloat16)] * (n - 1) + [lanes],
        [x.reshape(e * nx, ny) for x in others], [ANY] * (n - 1), 12, "flatten", n - 1,
    )
    everyone = [e_all, *others]
    waits = (dense, *halo)
    new = []
    for k in range(CHUNKS):
        ps = list(zip(*(gathered(x, far, waits) for x, far in zip(p_chunks[k], far_p[k]))))
        new.append(step(
            k, [([x], starts[k] * ny) for x in everyone], ps,
            ([e_all], p_chunks[k - 1]) if k else (halo[:1], halo[1:]),
            ([e_all], p_chunks[k + 1]) if k + 1 < CHUNKS else (halo[:1], halo[1:]), False,
            () if k + 1 < CHUNKS else (new[0][0], new[0][1:2]),
        ))
        waits = (new[-1][1],)
    halo = halos(new[-1][2], new[-1][3])
    e_next, p_next = new[-1][0], [c[1] for c in new]

    far_p = [[from_chip(x, d) for d in range(1, chips)] for x in p_next]
    first_p = gathered(p_next[0], far_p[0], (p_next[-1],))
    everyone = zip(*(gathered(x, [from_chip(x, d) for d in range(1, chips)], (first_p[-1], *halo)) for x in e_next))
    everyone = list(everyone)
    done = []
    for k in range(CHUNKS):
        last = k + 1 == CHUNKS
        es = [(parts, starts[k] * ny) for parts in everyone]
        ps = [p_next[k], swap_cores(p_next[k])] if last else first_p
        done.append(step(
            k, es, [[x] for x in ps], (e_next, p_next[k - 1 : k]) if k else (halo[:1], halo[1:]),
            (halo[:1], halo[1:]) if last else (e_next, p_next[k + 1 : k + 2]), last, (),
        ))
    rest = done.pop()
    far = []
    for f in far_p[-1]:
        f = after(f, rest[1], done[-1][1])
        far += [f, swap_cores(f)]
    e_out, p_out = finish(far, (rest[0][0], rest[1]), done)
    return e_out.reshape(e, nx, ny), p_out.reshape(p, nx, ny)


def solution(mesh):
    placed = (
        P("mode", ("grp", "space"), None),
        P("mode", ("grp", "space"), None),
        P("mode", None),
        P("mode", None),
        P("mode", None, None),
        P("mode", None),
        P(("grp", "space"), None),
        P("mode"),
        P("mode"),
        P("mode"),
        P("mode"),
    )
    return jax.shard_map(
        on_device,
        mesh=mesh,
        in_specs=placed,
        out_specs=(P("mode", ("grp", "space"), None), P("mode", ("grp", "space"), None)),
        check_vma=False,
    )
```

time: 84.7 us -> 81.4 us (0.961)
  waiting for transfers between devices: 29 us -> 21.5 us
  Pallas kernels: 22.6 us -> 27.1 us
  starting transfers between devices: 26.9 us -> 25.9 us
    ppermute x8 -> x6, waiting for transfers between devices: 19.4 us -> 10.8 us  [from_chip(): lax.ppermute(x, 'mode', [((i + CORES * offset) % n, i) for i in range(n)])]
    pallas_call x7, Pallas kernels: 22.6 us -> 27.1 us  [call(): pl.pallas_call(kernel, out_shape=out, in_specs=specs, out_specs=(VMEM,) *...]
    ppermute x16 -> x12, waiting for transfers between devices: 4.52 us -> 5.61 us  [swap_cores(): return lax.ppermute(x, 'mode', [(i, i ^ 1) for i in range(n)])]
    ppermute x8 -> x6, starting transfers between devices: 4.09 us -> 3.57 us  [from_chip(): lax.ppermute(x, 'mode', [((i + CORES * offset) % n, i) for i in range(n)])]
    ppermute x16 -> x12, starting transfers between devices: 13.7 us -> 13.3 us  [swap_cores(): return lax.ppermute(x, 'mode', [(i, i ^ 1) for i in range(n)])]
    unnamed x21 -> x25, local copies, waits for them, and re-layouts: 2.86 us -> 2.88 us
  transfers between devices with their start and end apart: 28 -> 22, of which waited for: 13 -> 11; matrix products, arithmetic and copies ran while one was open for 3% -> 3% of each run, Pallas kernels for 24% -> 29%
where the time goes in v8:
time: 81.4 us; the launch traced here: 80.3 us
  Pallas kernels  27.1 us (33%)
  starting transfers between devices  25.9 us (32%)
  waiting for transfers between devices  21.5 us (26%)
  local copies, waits for them, and re-layouts  2.96 us (4%)
  matrix products  1.83 us (2%)
  between operations  1 us (1%)
    pallas_call x7, Pallas kernels, call(): pl.pallas_call(kernel, out_shape=out, in_specs=specs, out_specs=(VMEM,) *...  27.1 us
    ppermute x12, starting transfers between devices, swap_cores(): return lax.ppermute(x, 'mode', [(i, i ^ 1) for i in range(n)])  13.3 us
    ppermute x6, waiting for transfers between devices, from_chip(): lax.ppermute(x, 'mode', [((i + CORES * offset) % n, i) for i in range(n)])  10.8 us
    ppermute x4, starting transfers between devices, halos(): return (lax.ppermute(a, 'space', near), lax.ppermute(b, 'space', other))  9.04 us
    ppermute x12, waiting for transfers between devices, swap_cores(): return lax.ppermute(x, 'mode', [(i, i ^ 1) for i in range(n)])  5.61 us
    ppermute x4, waiting for transfers between devices, halos(): return (lax.ppermute(a, 'space', near), lax.ppermute(b, 'space', other))  5.07 us
    ppermute x6, starting transfers between devices, from_chip(): lax.ppermute(x, 'mode', [((i + CORES * offset) % n, i) for i in range(n)])  3.57 us
    unnamed x25, local copies, waits for them, and re-layouts  2.88 us
  transfers between devices with their start and end apart: 22, of which 11 were waited for; matrix products, arithmetic and copies ran while one was open for 3% of the time, Pallas kernels for 29%

profile of v8, /device:TPU:13, one launch (start us, length us, event | category | flops | bytes accessed | tf_op | source)
XLA Modules:
  0.0 80.3 jit_solution(8711369788256190292)
XLA Ops:
  3.3 1.5 %flatten.2 = (bf16[256,1024]{1,0:T(8,128)(2,1)S(1)}, bf16[512,384]{1,0:T(8,128)(2,1)S(1)}, bf16[512,640]{1,0:T(8,128)(2,1)S(1)}, bf16[768,128]{1,0:T(8,128)(2,1)S(1)}, bf16[768,128]{1,0:T(8,128)(2,1)S(1)}) custom-call(s32[5]{0:T(128)S(1)} %convert_element_type.27.refs_0_, bf16[2048,128]{1,0:T(8,128)(2,1)S(1)} %bitcast.49, bf16[4096,128]{1,0:T(8,128)(2,1)S(1)} %bitcast.45), custom_call_target="tpu_custom_call" | custom-call | flops 1000 | bytes 1000 | tf_op jit(solution)/shard_map/flatten/pallas_call | solution.py:49
  4.9 4.5 %collective-permute-start.3 = (bf16[768,128]{1,0:T(8,128)(2,1)S(1)}, bf16[768,128]{1,0:T(8,128)(2,1)S(1)}, u32[]{:S(2)}, u32[]{:S(2)}) collective-permute-start(bf16[768,128]{1,0:T(8,128)(2,1)S(1)} %get-tuple-element.32), channel_id=1, source_target_pairs={{1,2},{2,1},{5,6},{6,5},{9,10},{10,9},{13,14},{14,13},{17,18},{18,... | collective-permute-start | bytes 589832 | tf_op jit(solution)/shard_map/ppermute | solution.py:37
  9.4 1.3 %collective-permute-start.8 = (bf16[512,384]{1,0:T(8,128)(2,1)S(1)}, bf16[512,384]{1,0:T(8,128)(2,1)S(1)}, u32[]{:S(2)}, u32[]{:S(2)}) collective-permute-start(bf16[512,384]{1,0:T(8,128)(2,1)S(1)} %get-tuple-element.30.refs_5_.refs_10_), channel_id=1, source_target_pairs={{8,0},{12,4},{0,8},{4,12},{9,1},{13,5},{1,9},{5,13},{10,2},{14,6},... | collective-permute-start | bytes 1179656 | tf_op jit(solution)/shard_map/ppermute | solution.py:30
  10.7 1.8 %collective-permute-start = (bf16[256,8,128]{2,1,0:T(8,128)(2,1)}, bf16[256,8,128]{2,1,0:T(8,128)(2,1)S(1)}, u32[]{:S(2)}, u32[]{:S(2)}) collective-permute-start(bf16[256,8,128]{2,1,0:T(8,128)(2,1)} %param.11), channel_id=1, source_target_pairs={{0,4},{4,0},{8,12},{12,8},{1,5},{5,1},{9,13},{13,9},{2,6},{6,2},{1... | collective-permute-start | bytes 1572872 | tf_op jit(solution)/shard_map/ppermute | solution.py:25
  13.4 1.2 %collective-permute-start.6 = (bf16[512,640]{1,0:T(8,128)(2,1)S(1)}, bf16[512,640]{1,0:T(8,128)(2,1)S(1)}, u32[]{:S(2)}, u32[]{:S(2)}) collective-permute-start(bf16[512,640]{1,0:T(8,128)(2,1)S(1)} %get-tuple-element.37.refs_12_.refs_5_), channel_id=1, source_target_pairs={{8,0},{12,4},{0,8},{4,12},{9,1},{13,5},{1,9},{5,13},{10,2},{14,6},... | collective-permute-start | bytes 1966088 | tf_op jit(solution)/shard_map/ppermute | solution.py:30
  14.6 2.1 %collective-permute-start.4 = (bf16[256,8,128]{2,1,0:T(8,128)(2,1)S(1)}, bf16[256,8,128]{2,1,0:T(8,128)(2,1)S(1)}, u32[]{:S(2)}, u32[]{:S(2)}) collective-permute-start(bf16[256,8,128]{2,1,0:T(8,128)(2,1)S(1)} %collective-permute-done.1), channel_id=1, source_target_pairs={{0,4},{4,0},{8,12},{12,8},{1,5},{5,1},{9,13},{13,9},{2,6},{6,2},{1... | collective-permute-start | bytes 1572872 | tf_op jit(solution)/shard_map/ppermute | solution.py:25
  16.8 1.8 %fusion.2 = bf16[4,128,128,16]{2,3,1,0:T(8,128)(2,1)S(1)} fusion(bf16[4,128,12,128]{3,1,0,2:T(8,128)(2,1)S(1)} %bitcast.73, s32[4,12]{1,0:T(4,128)} %param.16), kind=kOutput, calls=%fused_computation.3 | convolution fusion | flops 26215168 | bytes 3670208 | tf_op jit(solution)/shard_map/bsk,bisj->bikj/dot_general | solution.py:361
  19.2 2.9 %collective-permute-done.8.refs_7_ = bf16[512,384]{1,0:T(8,128)(2,1)S(1)} collective-permute-done((bf16[512,384]{1,0:T(8,128)(2,1)S(1)}, bf16[512,384]{1,0:T(8,128)(2,1)S(1)}, u32[]{:S(2)}, u32[]{:S(2)}) %collective-permute-start.8) | collective-permute-done | bytes 393248 | tf_op jit(solution)/shard_map/ppermute | solution.py:30
  22.1 2.7 %collective-permute-start.9 = (bf16[512,384]{1,0:T(8,128)(2,1)S(1)}, bf16[512,384]{1,0:T(8,128)(2,1)S(1)}, u32[]{:S(2)}, u32[]{:S(2)}) collective-permute-start(bf16[512,384]{1,0:T(8,128)(2,1)S(1)} %collective-permute-done.8.refs_7_), channel_id=1, source_target_pairs={{0,4},{4,0},{8,12},{12,8},{1,5},{5,1},{9,13},{13,9},{2,6},{6,2},{1... | collective-permute-start | bytes 1179656 | tf_op jit(solution)/shard_map/ppermute | solution.py:25
  26.2 4.9 %step.4 = (bf16[256,384]{1,0:T(8,128)(2,1)S(1)}, bf16[512,384]{1,0:T(8,128)(2,1)S(1)}) custom-call(s32[5]{0:T(128)S(1)} %convert_element_type.27.refs_0_, bf16[256,1024]{1,0:T(8,128)(2,1)S(1)} %get-tuple-element.29.refs_1_.refs_11_.refs_9_, bf16[256,1024]{1,0:T(8,128)(2,1)S(1)} %get-tuple-element.34.refs_2_, ...), custom_call_target="tpu_custom_call" | custom-call | flops 1000 | bytes 1000 | tf_op jit(solution)/shard_map/step/pallas_call | solution.py:49
  31.1 5.1 %collective-permute-done.6.refs_7_ = bf16[512,640]{1,0:T(8,128)(2,1)S(1)} collective-permute-done((bf16[512,640]{1,0:T(8,128)(2,1)S(1)}, bf16[512,640]{1,0:T(8,128)(2,1)S(1)}, u32[]{:S(2)}, u32[]{:S(2)}) %collective-permute-start.6) | collective-permute-done | bytes 655392 | tf_op jit(solution)/shard_map/ppermute | solution.py:30
  36.2 1.5 %collective-permute-start.10 = (bf16[512,640]{1,0:T(8,128)(2,1)S(1)}, bf16[512,640]{1,0:T(8,128)(2,1)S(1)}, u32[]{:S(2)}, u32[]{:S(2)}) collective-permute-start(bf16[512,640]{1,0:T(8,128)(2,1)S(1)} %collective-permute-done.6.refs_7_), channel_id=1, source_target_pairs={{0,4},{4,0},{8,12},{12,8},{1,5},{5,1},{9,13},{13,9},{2,6},{6,2},{1... | collective-permute-start | bytes 1966088 | tf_op jit(solution)/shard_map/ppermute | solution.py:25
  38.0 1.5 %collective-permute-done.10.refs_8_ = bf16[512,640]{1,0:T(8,128)(2,1)S(1)} collective-permute-done((bf16[512,640]{1,0:T(8,128)(2,1)S(1)}, bf16[512,640]{1,0:T(8,128)(2,1)S(1)}, u32[]{:S(2)}, u32[]{:S(2)}) %collective-permute-start.10) | collective-permute-done | bytes 655392 | tf_op jit(solution)/shard_map/ppermute | solution.py:25
  39.4 6.6 %step.5 = (bf16[256,1024]{1,0:T(8,128)(2,1)S(1)}, bf16[512,640]{1,0:T(8,128)(2,1)S(1)}, bf16[768,128]{1,0:T(8,128)(2,1)S(1)}, bf16[768,128]{1,0:T(8,128)(2,1)S(1)}) custom-call(s32[5]{0:T(128)S(1)} %convert_element_type.27.refs_0_, bf16[256,1024]{1,0:T(8,128)(2,1)S(1)} %get-tuple-element.29.refs_1_.refs_11_.refs_9_, ...), custom_call_target="tpu_custom_call" | custom-call | flops 1000 | bytes 1000 | tf_op jit(solution)/shard_map/step/pallas_call | solution.py:49
  46.3 2.1 %collective-permute-done.14.refs_7_ = bf16[512,384]{1,0:T(8,128)(2,1)S(1)} collective-permute-done((bf16[512,384]{1,0:T(8,128)(2,1)S(1)}, bf16[512,384]{1,0:T(8,128)(2,1)S(1)}, u32[]{:S(2)}, u32[]{:S(2)}) %collective-permute-start.14) | collective-permute-done | bytes 393248 | tf_op jit(solution)/shard_map/ppermute | solution.py:30
  49.4 4.3 %collective-permute-start.17 = (bf16[768,128]{1,0:T(8,128)(2,1)S(1)}, bf16[768,128]{1,0:T(8,128)(2,1)S(1)}, u32[]{:S(2)}, u32[]{:S(2)}) collective-permute-start(bf16[768,128]{1,0:T(8,128)(2,1)S(1)} %get-tuple-element.47), channel_id=1, source_target_pairs={{1,2},{2,1},{5,6},{6,5},{9,10},{10,9},{13,14},{14,13},{17,18},{18,... | collective-permute-start | bytes 589832 | tf_op jit(solution)/shard_map/ppermute | solution.py:37
  54.4 1.4 %collective-permute-done.16.refs_9_ = bf16[768,128]{1,0:T(8,128)(2,1)S(1)} collective-permute-done((bf16[768,128]{1,0:T(8,128)(2,1)S(1)}, bf16[768,128]{1,0:T(8,128)(2,1)S(1)}, u32[]{:S(2)}, u32[]{:S(2)}) %collective-permute-start.16) | collective-permute-done | bytes 196640 | tf_op jit(solution)/shard_map/ppermute | solution.py:37
  56.0 2.8 %collective-permute-done.17.refs_10_ = bf16[768,128]{1,0:T(8,128)(2,1)S(1)} collective-permute-done((bf16[768,128]{1,0:T(8,128)(2,1)S(1)}, bf16[768,128]{1,0:T(8,128)(2,1)S(1)}, u32[]{:S(2)}, u32[]{:S(2)}) %collective-permute-start.17) | collective-permute-done | bytes 196640 | tf_op jit(solution)/shard_map/ppermute | solution.py:37
  59.6 1.7 %collective-permute-start.18 = (bf16[256,1024]{1,0:T(8,128)(2,1)S(1)}, bf16[256,1024]{1,0:T(8,128)(2,1)S(1)}, u32[]{:S(2)}, u32[]{:S(2)}) collective-permute-start(bf16[256,1024]{1,0:T(8,128)(2,1)S(1)} %collective-permute-done.13.refs_3_), channel_id=1, source_target_pairs={{0,4},{4,0},{8,12},{12,8},{1,5},{5,1},{9,13},{13,9},{2,6},{6,2},{1... | collective-permute-start | bytes 1572872 | tf_op jit(solution)/shard_map/ppermute | solution.py:25
  61.3 2.1 %collective-permute-done.20.refs_6_ = bf16[512,384]{1,0:T(8,128)(2,1)S(1)} collective-permute-done((bf16[512,384]{1,0:T(8,128)(2,1)S(1)}, bf16[512,384]{1,0:T(8,128)(2,1)S(1)}, u32[]{:S(2)}, u32[]{:S(2)}) %collective-permute-start.20) | collective-permute-done | bytes 393248 | tf_op jit(solution)/shard_map/ppermute | solution.py:25
  63.4 4.9 %step.7 = (bf16[256,384]{1,0:T(8,128)(2,1)S(1)}, bf16[512,384]{1,0:T(8,128)(2,1)S(1)}) custom-call(s32[5]{0:T(128)S(1)} %convert_element_type.27.refs_0_, bf16[256,1024]{1,0:T(8,128)(2,1)S(1)} %get-tuple-element.44.refs_1_.refs_7_.refs_11_, bf16[256,1024]{1,0:T(8,128)(2,1)S(1)} %collective-permute-done.12.refs_2_, ...), custom_call_target="tpu_custom_call" | custom-call | flops 1000 | bytes 1000 | tf_op jit(solution)/shard_map/step/pallas_call | solution.py:49
  68.3 4.4 %step.6 = (f32[256,640]{1,0:T(8,128)S(1)}, f32[512,640]{1,0:T(8,128)S(1)}) custom-call(s32[5]{0:T(128)S(1)} %convert_element_type.27.refs_0_, bf16[256,1024]{1,0:T(8,128)(2,1)S(1)} %get-tuple-element.44.refs_1_.refs_7_.refs_11_, bf16[256,1024]{1,0:T(8,128)(2,1)S(1)} %collective-permute-done.12.refs_2_, ...), custom_call_target="tpu_custom_call" | custom-call | flops 1000 | bytes 1000 | tf_op jit(solution)/shard_map/step/pallas_call | solution.py:49
  74.5 1.7 %collective-permute-done.21.refs_2_ = bf16[512,640]{1,0:T(8,128)(2,1)S(1)} collective-permute-done((bf16[512,640]{1,0:T(8,128)(2,1)S(1)}, bf16[512,640]{1,0:T(8,128)(2,1)S(1)}, u32[]{:S(2)}, u32[]{:S(2)}) %collective-permute-start.21) | collective-permute-done | bytes 655392 | tf_op jit(solution)/shard_map/ppermute | solution.py:25
  76.2 3.9 %finish.1 = (bf16[2048,128]{1,0:T(8,128)(2,1)}, bf16[4096,128]{1,0:T(8,128)(2,1)}) custom-call(s32[5]{0:T(128)S(1)} %convert_element_type.27.refs_0_, bf16[512,640]{1,0:T(8,128)(2,1)S(1)} %collective-permute-done.11.refs_1_, bf16[512,640]{1,0:T(8,128)(2,1)S(1)} %collective-permute-done.21.refs_2_, f32[256,640]{1,0:T(8,128)S(1)} %get-tuple-element.52.refs_3_, ...), custom_call_target="tpu_custom_call" | custom-call | flops 1000 | bytes 1000 | tf_op jit(solution)/shard_map/finish/pallas_call | solution.py:49
  (55 shorter events, 10.5 us)
Async XLA Ops:
  0.6 14.0 %collective-permute-start.1 = (bf16[256,8,128]{2,1,0:T(8,128)(2,1)}, bf16[256,8,128]{2,1,0:T(8,128)(2,1)S(1)}, u32[]{:S(2)}, u32[]{:S(2)}) collective-permute-start(bf16[256,8,128]{2,1,0:T(8,128)(2,1)} %param.11), channel_id=1, source_target_pairs={{8,0},{12,4},{0,8},{4,12},{9,1},{13,5},{1,9},{5,13},{10,2},{14,6},... | collective-permute-start | bytes 1572872 | tf_op jit(solution)/shard_map/ppermute | solution.py:30
  3.3 13.5 %copy-start.8 = (bf16[512,12,128]{2,0,1:T(8,128)(2,1)S(1)}, bf16[512,12,128]{2,0,1:T(8,128)(2,1)}, u32[]{:S(2)}) copy-start(bf16[512,12,128]{2,0,1:T(8,128)(2,1)} %param.15) | copy-start | bytes 4718596
  4.8 7.7 %collective-permute-start.2 = (bf16[768,128]{1,0:T(8,128)(2,1)S(1)}, bf16[768,128]{1,0:T(8,128)(2,1)S(1)}, u32[]{:S(2)}, u32[]{:S(2)}) collective-permute-start(bf16[768,128]{1,0:T(8,128)(2,1)S(1)} %get-tuple-element.31), channel_id=1, source_target_pairs={{0,1},{1,0},{2,3},{3,2},{4,5},{5,4},{6,7},{7,6},{8,9},{9,8},{10,11... | collective-permute-start | bytes 589832 | tf_op jit(solution)/shard_map/ppermute | solution.py:37
  4.9 8.5 %collective-permute-start.3 = (bf16[768,128]{1,0:T(8,128)(2,1)S(1)}, bf16[768,128]{1,0:T(8,128)(2,1)S(1)}, u32[]{:S(2)}, u32[]{:S(2)}) collective-permute-start(bf16[768,128]{1,0:T(8,128)(2,1)S(1)} %get-tuple-element.32), channel_id=1, source_target_pairs={{1,2},{2,1},{5,6},{6,5},{9,10},{10,9},{13,14},{14,13},{17,18},{18,... | collective-permute-start | bytes 589832 | tf_op jit(solution)/shard_map/ppermute | solution.py:37
  9.4 12.7 %collective-permute-start.8 = (bf16[512,384]{1,0:T(8,128)(2,1)S(1)}, bf16[512,384]{1,0:T(8,128)(2,1)S(1)}, u32[]{:S(2)}, u32[]{:S(2)}) collective-permute-start(bf16[512,384]{1,0:T(8,128)(2,1)S(1)} %get-tuple-element.30.refs_5_.refs_10_), channel_id=1, source_target_pairs={{8,0},{12,4},{0,8},{4,12},{9,1},{13,5},{1,9},{5,13},{10,2},{14,6},... | collective-permute-start | bytes 1179656 | tf_op jit(solution)/shard_map/ppermute | solution.py:30
  10.7 14.1 %collective-permute-start = (bf16[256,8,128]{2,1,0:T(8,128)(2,1)}, bf16[256,8,128]{2,1,0:T(8,128)(2,1)S(1)}, u32[]{:S(2)}, u32[]{:S(2)}) collective-permute-start(bf16[256,8,128]{2,1,0:T(8,128)(2,1)} %param.11), channel_id=1, source_target_pairs={{0,4},{4,0},{8,12},{12,8},{1,5},{5,1},{9,13},{13,9},{2,6},{6,2},{1... | collective-permute-start | bytes 1572872 | tf_op jit(solution)/shard_map/ppermute | solution.py:25
  12.5 13.4 %collective-permute-start.7 = (bf16[512,384]{1,0:T(8,128)(2,1)S(1)}, bf16[512,384]{1,0:T(8,128)(2,1)S(1)}, u32[]{:S(2)}, u32[]{:S(2)}) collective-permute-start(bf16[512,384]{1,0:T(8,128)(2,1)S(1)} %get-tuple-element.30.refs_5_.refs_10_), channel_id=1, source_target_pairs={{0,4},{4,0},{8,12},{12,8},{1,5},{5,1},{9,13},{13,9},{2,6},{6,2},{1... | collective-permute-start | bytes 1179656 | tf_op jit(solution)/shard_map/ppermute | solution.py:25
  13.4 22.8 %collective-permute-start.6 = (bf16[512,640]{1,0:T(8,128)(2,1)S(1)}, bf16[512,640]{1,0:T(8,128)(2,1)S(1)}, u32[]{:S(2)}, u32[]{:S(2)}) collective-permute-start(bf16[512,640]{1,0:T(8,128)(2,1)S(1)} %get-tuple-element.37.refs_12_.refs_5_), channel_id=1, source_target_pairs={{8,0},{12,4},{0,8},{4,12},{9,1},{13,5},{1,9},{5,13},{10,2},{14,6},... | collective-permute-start | bytes 1966088 | tf_op jit(solution)/shard_map/ppermute | solution.py:30
  14.6 10.3 %collective-permute-start.4 = (bf16[256,8,128]{2,1,0:T(8,128)(2,1)S(1)}, bf16[256,8,128]{2,1,0:T(8,128)(2,1)S(1)}, u32[]{:S(2)}, u32[]{:S(2)}) collective-permute-start(bf16[256,8,128]{2,1,0:T(8,128)(2,1)S(1)} %collective-permute-done.1), channel_id=1, source_target_pairs={{0,4},{4,0},{8,12},{12,8},{1,5},{5,1},{9,13},{13,9},{2,6},{6,2},{1... | collective-permute-start | bytes 1572872 | tf_op jit(solution)/shard_map/ppermute | solution.py:25
  18.6 7.6 %copy-start = (bf16[256,2048]{1,0:T(8,128)(2,1)S(1)}, bf16[256,2048]{1,0:T(8,128)(2,1)}, u32[]{:S(2)}) copy-start(bf16[256,2048]{1,0:T(8,128)(2,1)} %refs_5_.1) | copy-start | bytes 3145732
  22.1 4.0 %collective-permute-start.9 = (bf16[512,384]{1,0:T(8,128)(2,1)S(1)}, bf16[512,384]{1,0:T(8,128)(2,1)S(1)}, u32[]{:S(2)}, u32[]{:S(2)}) collective-permute-start(bf16[512,384]{1,0:T(8,128)(2,1)S(1)} %collective-permute-done.8.refs_7_), channel_id=1, source_target_pairs={{0,4},{4,0},{8,12},{12,8},{1,5},{5,1},{9,13},{13,9},{2,6},{6,2},{1... | collective-permute-start | bytes 1179656 | tf_op jit(solution)/shard_map/ppermute | solution.py:25
  24.8 13.1 %collective-permute-start.5 = (bf16[512,640]{1,0:T(8,128)(2,1)S(1)}, bf16[512,640]{1,0:T(8,128)(2,1)S(1)}, u32[]{:S(2)}, u32[]{:S(2)}) collective-permute-start(bf16[512,640]{1,0:T(8,128)(2,1)S(1)} %get-tuple-element.37.refs_12_.refs_5_), channel_id=1, source_target_pairs={{0,4},{4,0},{8,12},{12,8},{1,5},{5,1},{9,13},{13,9},{2,6},{6,2},{1... | collective-permute-start | bytes 1966088 | tf_op jit(solution)/shard_map/ppermute | solution.py:25
  36.2 3.3 %collective-permute-start.10 = (bf16[512,640]{1,0:T(8,128)(2,1)S(1)}, bf16[512,640]{1,0:T(8,128)(2,1)S(1)}, u32[]{:S(2)}, u32[]{:S(2)}) collective-permute-start(bf16[512,640]{1,0:T(8,128)(2,1)S(1)} %collective-permute-done.6.refs_7_), channel_id=1, source_target_pairs={{0,4},{4,0},{8,12},{12,8},{1,5},{5,1},{9,13},{13,9},{2,6},{6,2},{1... | collective-permute-start | bytes 1966088 | tf_op jit(solution)/shard_map/ppermute | solution.py:25
  37.7 10.7 %collective-permute-start.14 = (bf16[512,384]{1,0:T(8,128)(2,1)S(1)}, bf16[512,384]{1,0:T(8,128)(2,1)S(1)}, u32[]{:S(2)}, u32[]{:S(2)}) collective-permute-start(bf16[512,384]{1,0:T(8,128)(2,1)S(1)} %get-tuple-element.40.refs_22_.refs_8_.refs_5_), channel_id=1, source_target_pairs={{8,0},{12,4},{0,8},{4,12},{9,1},{13,5},{1,9},{5,13},{10,2},{14,6},... | collective-permute-start | bytes 1179656 | tf_op jit(solution)/shard_map/ppermute | solution.py:30
  46.0 13.5 %collective-permute-start.13 = (bf16[256,1024]{1,0:T(8,128)(2,1)S(1)}, bf16[256,1024]{1,0:T(8,128)(2,1)S(1)}, u32[]{:S(2)}, u32[]{:S(2)}) collective-permute-start(bf16[256,1024]{1,0:T(8,128)(2,1)S(1)} %get-tuple-element.44.refs_1_.refs_7_.refs_11_), channel_id=1, source_target_pairs={{8,0},{12,4},{0,8},{4,12},{9,1},{13,5},{1,9},{5,13},{10,2},{14,6},... | collective-permute-start | bytes 1572872 | tf_op jit(solution)/shard_map/ppermute | solution.py:30
  48.5 11.1 %collective-permute-start.15 = (bf16[512,384]{1,0:T(8,128)(2,1)S(1)}, bf16[512,384]{1,0:T(8,128)(2,1)S(1)}, u32[]{:S(2)}, u32[]{:S(2)}) collective-permute-start(bf16[512,384]{1,0:T(8,128)(2,1)S(1)} %collective-permute-done.14.refs_7_), channel_id=1, source_target_pairs={{0,4},{4,0},{8,12},{12,8},{1,5},{5,1},{9,13},{13,9},{2,6},{6,2},{1... | collective-permute-start | bytes 1179656 | tf_op jit(solution)/shard_map/ppermute | solution.py:25
  49.2 6.5 %collective-permute-start.16 = (bf16[768,128]{1,0:T(8,128)(2,1)S(1)}, bf16[768,128]{1,0:T(8,128)(2,1)S(1)}, u32[]{:S(2)}, u32[]{:S(2)}) collective-permute-start(bf16[768,128]{1,0:T(8,128)(2,1)S(1)} %get-tuple-element.46), channel_id=1, source_target_pairs={{0,1},{1,0},{2,3},{3,2},{4,5},{5,4},{6,7},{7,6},{8,9},{9,8},{10,11... | collective-permute-start | bytes 589832 | tf_op jit(solution)/shard_map/ppermute | solution.py:37
  49.4 9.4 %collective-permute-start.17 = (bf16[768,128]{1,0:T(8,128)(2,1)S(1)}, bf16[768,128]{1,0:T(8,128)(2,1)S(1)}, u32[]{:S(2)}, u32[]{:S(2)}) collective-permute-start(bf16[768,128]{1,0:T(8,128)(2,1)S(1)} %get-tuple-element.47), channel_id=1, source_target_pairs={{1,2},{2,1},{5,6},{6,5},{9,10},{10,9},{13,14},{14,13},{17,18},{18,... | collective-permute-start | bytes 589832 | tf_op jit(solution)/shard_map/ppermute | solution.py:37
  53.7 14.5 %collective-permute-start.19 = (bf16[512,640]{1,0:T(8,128)(2,1)S(1)}, bf16[512,640]{1,0:T(8,128)(2,1)S(1)}, u32[]{:S(2)}, u32[]{:S(2)}) collective-permute-start(bf16[512,640]{1,0:T(8,128)(2,1)S(1)} %get-tuple-element.43.refs_5_.refs_12_), channel_id=1, source_target_pairs={{0,4},{4,0},{8,12},{12,8},{1,5},{5,1},{9,13},{13,9},{2,6},{6,2},{1... | collective-permute-start | bytes 1966088 | tf_op jit(solution)/shard_map/ppermute | solution.py:25
  55.8 17.6 %collective-permute-start.11 = (bf16[512,640]{1,0:T(8,128)(2,1)S(1)}, bf16[512,640]{1,0:T(8,128)(2,1)S(1)}, u32[]{:S(2)}, u32[]{:S(2)}) collective-permute-start(bf16[512,640]{1,0:T(8,128)(2,1)S(1)} %get-tuple-element.43.refs_5_.refs_12_), channel_id=1, source_target_pairs={{8,0},{12,4},{0,8},{4,12},{9,1},{13,5},{1,9},{5,13},{10,2},{14,6},... | collective-permute-start | bytes 1966088 | tf_op jit(solution)/shard_map/ppermute | solution.py:30
  58.8 4.6 %collective-permute-start.12 = (bf16[256,1024]{1,0:T(8,128)(2,1)S(1)}, bf16[256,1024]{1,0:T(8,128)(2,1)S(1)}, u32[]{:S(2)}, u32[]{:S(2)}) collective-permute-start(bf16[256,1024]{1,0:T(8,128)(2,1)S(1)} %get-tuple-element.44.refs_1_.refs_7_.refs_11_), channel_id=1, source_target_pairs={{0,4},{4,0},{8,12},{12,8},{1,5},{5,1},{9,13},{13,9},{2,6},{6,2},{1... | collective-permute-start | bytes 1572872 | tf_op jit(solution)/shard_map/ppermute | solution.py:25
  59.6 3.8 %collective-permute-start.18 = (bf16[256,1024]{1,0:T(8,128)(2,1)S(1)}, bf16[256,1024]{1,0:T(8,128)(2,1)S(1)}, u32[]{:S(2)}, u32[]{:S(2)}) collective-permute-start(bf16[256,1024]{1,0:T(8,128)(2,1)S(1)} %collective-permute-done.13.refs_3_), channel_id=1, source_target_pairs={{0,4},{4,0},{8,12},{12,8},{1,5},{5,1},{9,13},{13,9},{2,6},{6,2},{1... | collective-permute-start | bytes 1572872 | tf_op jit(solution)/shard_map/ppermute | solution.py:25
  61.2 2.1 %collective-permute-start.20 = (bf16[512,384]{1,0:T(8,128)(2,1)S(1)}, bf16[512,384]{1,0:T(8,128)(2,1)S(1)}, u32[]{:S(2)}, u32[]{:S(2)}) collective-permute-start(bf16[512,384]{1,0:T(8,128)(2,1)S(1)} %get-tuple-element.40.refs_22_.refs_8_.refs_5_), channel_id=1, source_target_pairs={{0,4},{4,0},{8,12},{12,8},{1,5},{5,1},{9,13},{13,9},{2,6},{6,2},{1... | collective-permute-start | bytes 1179656 | tf_op jit(solution)/shard_map/ppermute | solution.py:25
  73.4 2.9 %collective-permute-start.21 = (bf16[512,640]{1,0:T(8,128)(2,1)S(1)}, bf16[512,640]{1,0:T(8,128)(2,1)S(1)}, u32[]{:S(2)}, u32[]{:S(2)}) collective-permute-start(bf16[512,640]{1,0:T(8,128)(2,1)S(1)} %collective-permute-done.11.refs_1_), channel_id=1, source_target_pairs={{0,4},{4,0},{8,12},{12,8},{1,5},{5,1},{9,13},{13,9},{2,6},{6,2},{1... | collective-permute-start | bytes 1966088 | tf_op jit(solution)/shard_map/ppermute | solution.py:25
  (8 other events, 46.2 us)

commit v9 on v8

--- a/solution.py
+++ b/solution.py
@@ -196,11 +196,11 @@
 
     e_refs, p_refs = [take(counts[3]) for _ in range(n)], [take(counts[0]) for _ in range(CORES if last else n)]
     before, behind = (take(counts[4]), take(counts[1])), (take(counts[5]), take(counts[2]))
-    emission_hbm, absorption_hbm, dense_hbm, up_ref, speed_ref, diffusion_ref, e_rate_ref, p_rate_ref = take(8)
+    emission_ref, absorption_ref, dense_ref, up_ref, speed_ref, diffusion_ref, e_rate_ref, p_rate_ref = take(8)
     border = (take(counts[6]), take(1)) if edges else ()
     e_out_refs, p_out_ref = take(counts[7]), *take(1)
     to_refs = take(2) if edges else []
-    se_ref, sp_ref, emission_ref, absorption_ref, dense_ref, low_ref, high_ref = take(7)
+    se_ref, sp_ref, low_ref, high_ref = take(4)
     first_ref, final_ref = take(2) if edges else (None, None)
     load = Loader(refs[0])
     tall = width // ny
@@ -208,7 +208,7 @@
     me = place_ref[1]
     me_p = 0 if last else me
 
-    early = [load.start(absorption_hbm, absorption_ref)]
+    early, middle = [], []
     for j, parts in enumerate(p_refs):
         owner = j if last else place_ref[1 + j]
         for i, part in enumerate(parts):
@@ -216,7 +216,7 @@
     for j, parts in enumerate(e_refs):
         for i, part in enumerate(parts):
             to = se_ref.at[rows_at(place_ref[1 + j] * counts[3] + i, e // counts[3]), :]
-            early.append(load.start(part.at[:, cols[j] : cols[j] + width], to))
+            (middle if j else early).append(load.start(part.at[:, cols[j] : cols[j] + width], to))
     if k == 0:
         early.append(load.start_one(even, before[1][0], before[0][0], low_ref))
     else:
@@ -233,7 +233,7 @@
             early.append(load.start(part.at[:, col : col + ny], high_ref.at[rows_of(0, i, part), :]))
         for i, part in enumerate(behind[1]):
             early.append(load.start(part.at[:, 0:ny], high_ref.at[rows_of(e, i, part), :]))
-    late = [load.start(dense_hbm, dense_ref), load.start(emission_hbm, emission_ref)]
+    late = []
     if edges:
         for i, part in enumerate(border[0]):
             late.append(load.start(part.at[:, 0:ny], first_ref.at[rows_of(0, i, part), :]))
@@ -279,7 +279,7 @@
         e_out_refs[0][...] = new
     else:
         store(new / (1.0 + as_column(e_rate_ref[...])), 0, e, 0)
-    for copy in late:
+    for copy in middle + late:
         copy.wait()
 
     for at in range(0, p, tile):
@@ -377,12 +377,12 @@
             places, *(x for parts, _ in es for x in parts), *(x for parts in ps for x in parts), *before[0],
             *before[1], *behind[0], *behind[1], *weights, ups[k], *rates, *(x for parts in border for x in parts),
         )
-        large = n * counts[3] + len(ps) * counts[0] + sum(counts[1:3]) + sum(counts[4:6]) + 3
-        specs = [SMEM] + [ANY] * large + [VMEM] * 5 + [ANY] * sum(len(parts) for parts in border)
+        large = n * counts[3] + len(ps) * counts[0] + sum(counts[1:3]) + sum(counts[4:6])
+        specs = [SMEM] + [ANY] * large + [VMEM] * 8 + [ANY] * sum(len(parts) for parts in border)
         scratch = [
             pltpu.VMEM(shape, jnp.bfloat16)
             for shape in (
-                (n * e, width), (len(ps) * p, width), (p, n * e), (e, n * p), (p, NM), (e + p, ny), (e + p, ny),
+                (n * e, width), (len(ps) * p, width), (e + p, ny), (e + p, ny),
             )
         ]
         if last:
@@ -392,7 +392,7 @@
             scratch += [pltpu.VMEM((e + p, ny), jnp.bfloat16)] * edges
         out = call(
             lambda *refs: step_kernel(n, e, p, width, ny, nx, k, [c for _, c in es], counts, edges, last, *refs),
-            out, scratch, operands, specs, 28, "step", large + counts[6] + e_parts + 2,
+            out, scratch, operands, specs, 24, "step", large + counts[6] + e_parts + 2,
         )
         return (list(out[:e_parts]), *out[e_parts:])
 

time: 81.4 us -> 81.4 us (level)
  waiting for transfers between devices: 21.5 us -> 23.2 us
  Pallas kernels: 27.1 us -> 25.9 us
    ppermute x6, waiting for transfers between devices: 10.8 us -> 12.7 us  [from_chip(): lax.ppermute(x, 'mode', [((i + CORES * offset) % n, i) for i in range(n)])]
    pallas_call x7, Pallas kernels: 27.1 us -> 25.9 us  [call(): pl.pallas_call(kernel, out_shape=out, in_specs=specs, out_specs=(VMEM,) *...]
  transfers between devices with their start and end apart: 22 -> 22, of which waited for: 11 -> 11; matrix products, arithmetic and copies ran while one was open for 3% -> 3% of each run, Pallas kernels for 29% -> 27%
where the time goes in v9:
time: 81.4 us; the launch traced here: 80.3 us
  Pallas kernels  25.9 us (32%)
  starting transfers between devices  25.3 us (31%)
  waiting for transfers between devices  23.2 us (29%)
  local copies, waits for them, and re-layouts  2.96 us (4%)
  matrix products  1.83 us (2%)
  between operations  1 us (1%)
    pallas_call x7, Pallas kernels, call(): pl.pallas_call(kernel, out_shape=out, in_specs=specs, out_specs=(VMEM,) *...  25.9 us
    ppermute x6, waiting for transfers between devices, from_chip(): lax.ppermute(x, 'mode', [((i + CORES * offset) % n, i) for i in range(n)])  12.7 us
    ppermute x12, starting transfers between devices, swap_cores(): return lax.ppermute(x, 'mode', [(i, i ^ 1) for i in range(n)])  12.5 us
    ppermute x4, starting transfers between devices, halos(): return (lax.ppermute(a, 'space', near), lax.ppermute(b, 'space', other))  9.22 us
    ppermute x12, waiting for transfers between devices, swap_cores(): return lax.ppermute(x, 'mode', [(i, i ^ 1) for i in range(n)])  5.61 us
    ppermute x4, waiting for transfers between devices, halos(): return (lax.ppermute(a, 'space', near), lax.ppermute(b, 'space', other))  4.89 us
    ppermute x6, starting transfers between devices, from_chip(): lax.ppermute(x, 'mode', [((i + CORES * offset) % n, i) for i in range(n)])  3.57 us
    unnamed x25, local copies, waits for them, and re-layouts  2.88 us
  transfers between devices with their start and end apart: 22, of which 11 were waited for; matrix products, arithmetic and copies ran while one was open for 3% of the time, Pallas kernels for 27%

profile of v9, /device:TPU:13, one launch (start us, length us, event | category | flops | bytes accessed | tf_op | source)
XLA Modules:
  0.0 80.3 jit_solution(276771935803160380)
XLA Ops:
  3.3 1.5 %flatten.2 = (bf16[256,1024]{1,0:T(8,128)(2,1)S(1)}, bf16[512,384]{1,0:T(8,128)(2,1)S(1)}, bf16[512,640]{1,0:T(8,128)(2,1)S(1)}, bf16[768,128]{1,0:T(8,128)(2,1)S(1)}, bf16[768,128]{1,0:T(8,128)(2,1)S(1)}) custom-call(s32[5]{0:T(128)S(1)} %convert_element_type.27.refs_0_, bf16[2048,128]{1,0:T(8,128)(2,1)S(1)} %bitcast.49, bf16[4096,128]{1,0:T(8,128)(2,1)S(1)} %bitcast.45), custom_call_target="tpu_custom_call" | custom-call | flops 1000 | bytes 1000 | tf_op jit(solution)/shard_map/flatten/pallas_call | solution.py:49
  4.9 4.5 %collective-permute-start.3 = (bf16[768,128]{1,0:T(8,128)(2,1)S(1)}, bf16[768,128]{1,0:T(8,128)(2,1)S(1)}, u32[]{:S(2)}, u32[]{:S(2)}) collective-permute-start(bf16[768,128]{1,0:T(8,128)(2,1)S(1)} %get-tuple-element.32), channel_id=1, source_target_pairs={{1,2},{2,1},{5,6},{6,5},{9,10},{10,9},{13,14},{14,13},{17,18},{18,... | collective-permute-start | bytes 589832 | tf_op jit(solution)/shard_map/ppermute | solution.py:37
  9.4 1.3 %collective-permute-start.8 = (bf16[512,384]{1,0:T(8,128)(2,1)S(1)}, bf16[512,384]{1,0:T(8,128)(2,1)S(1)}, u32[]{:S(2)}, u32[]{:S(2)}) collective-permute-start(bf16[512,384]{1,0:T(8,128)(2,1)S(1)} %get-tuple-element.30.refs_5_.refs_10_), channel_id=1, source_target_pairs={{8,0},{12,4},{0,8},{4,12},{9,1},{13,5},{1,9},{5,13},{10,2},{14,6},... | collective-permute-start | bytes 1179656 | tf_op jit(solution)/shard_map/ppermute | solution.py:30
  10.7 1.8 %collective-permute-start = (bf16[256,8,128]{2,1,0:T(8,128)(2,1)}, bf16[256,8,128]{2,1,0:T(8,128)(2,1)S(1)}, u32[]{:S(2)}, u32[]{:S(2)}) collective-permute-start(bf16[256,8,128]{2,1,0:T(8,128)(2,1)} %param.11), channel_id=1, source_target_pairs={{0,4},{4,0},{8,12},{12,8},{1,5},{5,1},{9,13},{13,9},{2,6},{6,2},{1... | collective-permute-start | bytes 1572872 | tf_op jit(solution)/shard_map/ppermute | solution.py:25
  13.4 1.2 %collective-permute-start.6 = (bf16[512,640]{1,0:T(8,128)(2,1)S(1)}, bf16[512,640]{1,0:T(8,128)(2,1)S(1)}, u32[]{:S(2)}, u32[]{:S(2)}) collective-permute-start(bf16[512,640]{1,0:T(8,128)(2,1)S(1)} %get-tuple-element.37.refs_12_.refs_5_), channel_id=1, source_target_pairs={{8,0},{12,4},{0,8},{4,12},{9,1},{13,5},{1,9},{5,13},{10,2},{14,6},... | collective-permute-start | bytes 1966088 | tf_op jit(solution)/shard_map/ppermute | solution.py:30
  14.6 2.1 %collective-permute-start.4 = (bf16[256,8,128]{2,1,0:T(8,128)(2,1)S(1)}, bf16[256,8,128]{2,1,0:T(8,128)(2,1)S(1)}, u32[]{:S(2)}, u32[]{:S(2)}) collective-permute-start(bf16[256,8,128]{2,1,0:T(8,128)(2,1)S(1)} %collective-permute-done.1), channel_id=1, source_target_pairs={{0,4},{4,0},{8,12},{12,8},{1,5},{5,1},{9,13},{13,9},{2,6},{6,2},{1... | collective-permute-start | bytes 1572872 | tf_op jit(solution)/shard_map/ppermute | solution.py:25
  16.8 1.8 %fusion.2 = bf16[4,128,128,16]{2,3,1,0:T(8,128)(2,1)S(1)} fusion(bf16[4,128,12,128]{3,1,0,2:T(8,128)(2,1)S(1)} %bitcast.73, s32[4,12]{1,0:T(4,128)} %param.16), kind=kOutput, calls=%fused_computation.3 | convolution fusion | flops 26215168 | bytes 3670208 | tf_op jit(solution)/shard_map/bsk,bisj->bikj/dot_general | solution.py:361
  19.2 2.9 %collective-permute-done.8.refs_7_ = bf16[512,384]{1,0:T(8,128)(2,1)S(1)} collective-permute-done((bf16[512,384]{1,0:T(8,128)(2,1)S(1)}, bf16[512,384]{1,0:T(8,128)(2,1)S(1)}, u32[]{:S(2)}, u32[]{:S(2)}) %collective-permute-start.8) | collective-permute-done | bytes 393248 | tf_op jit(solution)/shard_map/ppermute | solution.py:30
  22.1 2.7 %collective-permute-start.9 = (bf16[512,384]{1,0:T(8,128)(2,1)S(1)}, bf16[512,384]{1,0:T(8,128)(2,1)S(1)}, u32[]{:S(2)}, u32[]{:S(2)}) collective-permute-start(bf16[512,384]{1,0:T(8,128)(2,1)S(1)} %collective-permute-done.8.refs_7_), channel_id=1, source_target_pairs={{0,4},{4,0},{8,12},{12,8},{1,5},{5,1},{9,13},{13,9},{2,6},{6,2},{1... | collective-permute-start | bytes 1179656 | tf_op jit(solution)/shard_map/ppermute | solution.py:25
  26.2 4.7 %step.4 = (bf16[256,384]{1,0:T(8,128)(2,1)S(1)}, bf16[512,384]{1,0:T(8,128)(2,1)S(1)}) custom-call(s32[5]{0:T(128)S(1)} %convert_element_type.27.refs_0_, bf16[256,1024]{1,0:T(8,128)(2,1)S(1)} %get-tuple-element.29.refs_1_.refs_11_.refs_9_, bf16[256,1024]{1,0:T(8,128)(2,1)S(1)} %get-tuple-element.34.refs_2_, ...), custom_call_target="tpu_custom_call" | custom-call | flops 1000 | bytes 1000 | tf_op jit(solution)/shard_map/step/pallas_call | solution.py:49
  30.9 5.3 %collective-permute-done.6.refs_7_ = bf16[512,640]{1,0:T(8,128)(2,1)S(1)} collective-permute-done((bf16[512,640]{1,0:T(8,128)(2,1)S(1)}, bf16[512,640]{1,0:T(8,128)(2,1)S(1)}, u32[]{:S(2)}, u32[]{:S(2)}) %collective-permute-start.6) | collective-permute-done | bytes 655392 | tf_op jit(solution)/shard_map/ppermute | solution.py:30
  36.2 1.5 %collective-permute-start.10 = (bf16[512,640]{1,0:T(8,128)(2,1)S(1)}, bf16[512,640]{1,0:T(8,128)(2,1)S(1)}, u32[]{:S(2)}, u32[]{:S(2)}) collective-permute-start(bf16[512,640]{1,0:T(8,128)(2,1)S(1)} %collective-permute-done.6.refs_7_), channel_id=1, source_target_pairs={{0,4},{4,0},{8,12},{12,8},{1,5},{5,1},{9,13},{13,9},{2,6},{6,2},{1... | collective-permute-start | bytes 1966088 | tf_op jit(solution)/shard_map/ppermute | solution.py:25
  38.0 1.5 %collective-permute-done.10.refs_8_ = bf16[512,640]{1,0:T(8,128)(2,1)S(1)} collective-permute-done((bf16[512,640]{1,0:T(8,128)(2,1)S(1)}, bf16[512,640]{1,0:T(8,128)(2,1)S(1)}, u32[]{:S(2)}, u32[]{:S(2)}) %collective-permute-start.10) | collective-permute-done | bytes 655392 | tf_op jit(solution)/shard_map/ppermute | solution.py:25
  39.4 6.2 %step.5 = (bf16[256,1024]{1,0:T(8,128)(2,1)S(1)}, bf16[512,640]{1,0:T(8,128)(2,1)S(1)}, bf16[768,128]{1,0:T(8,128)(2,1)S(1)}, bf16[768,128]{1,0:T(8,128)(2,1)S(1)}) custom-call(s32[5]{0:T(128)S(1)} %convert_element_type.27.refs_0_, bf16[256,1024]{1,0:T(8,128)(2,1)S(1)} %get-tuple-element.29.refs_1_.refs_11_.refs_9_, ...), custom_call_target="tpu_custom_call" | custom-call | flops 1000 | bytes 1000 | tf_op jit(solution)/shard_map/step/pallas_call | solution.py:49
  45.9 2.6 %collective-permute-done.14.refs_7_ = bf16[512,384]{1,0:T(8,128)(2,1)S(1)} collective-permute-done((bf16[512,384]{1,0:T(8,128)(2,1)S(1)}, bf16[512,384]{1,0:T(8,128)(2,1)S(1)}, u32[]{:S(2)}, u32[]{:S(2)}) %collective-permute-start.14) | collective-permute-done | bytes 393248 | tf_op jit(solution)/shard_map/ppermute | solution.py:30
  49.8 4.5 %collective-permute-start.17 = (bf16[768,128]{1,0:T(8,128)(2,1)S(1)}, bf16[768,128]{1,0:T(8,128)(2,1)S(1)}, u32[]{:S(2)}, u32[]{:S(2)}) collective-permute-start(bf16[768,128]{1,0:T(8,128)(2,1)S(1)} %get-tuple-element.47), channel_id=1, source_target_pairs={{1,2},{2,1},{5,6},{6,5},{9,10},{10,9},{13,14},{14,13},{17,18},{18,... | collective-permute-start | bytes 589832 | tf_op jit(solution)/shard_map/ppermute | solution.py:37
  54.9 1.2 %collective-permute-done.16.refs_9_ = bf16[768,128]{1,0:T(8,128)(2,1)S(1)} collective-permute-done((bf16[768,128]{1,0:T(8,128)(2,1)S(1)}, bf16[768,128]{1,0:T(8,128)(2,1)S(1)}, u32[]{:S(2)}, u32[]{:S(2)}) %collective-permute-start.16) | collective-permute-done | bytes 196640 | tf_op jit(solution)/shard_map/ppermute | solution.py:37
  56.4 2.8 %collective-permute-done.17.refs_10_ = bf16[768,128]{1,0:T(8,128)(2,1)S(1)} collective-permute-done((bf16[768,128]{1,0:T(8,128)(2,1)S(1)}, bf16[768,128]{1,0:T(8,128)(2,1)S(1)}, u32[]{:S(2)}, u32[]{:S(2)}) %collective-permute-start.17) | collective-permute-done | bytes 196640 | tf_op jit(solution)/shard_map/ppermute | solution.py:37
  60.9 2.1 %collective-permute-done.20.refs_6_ = bf16[512,384]{1,0:T(8,128)(2,1)S(1)} collective-permute-done((bf16[512,384]{1,0:T(8,128)(2,1)S(1)}, bf16[512,384]{1,0:T(8,128)(2,1)S(1)}, u32[]{:S(2)}, u32[]{:S(2)}) %collective-permute-start.20) | collective-permute-done | bytes 393248 | tf_op jit(solution)/shard_map/ppermute | solution.py:25
  63.0 4.7 %step.7 = (bf16[256,384]{1,0:T(8,128)(2,1)S(1)}, bf16[512,384]{1,0:T(8,128)(2,1)S(1)}) custom-call(s32[5]{0:T(128)S(1)} %convert_element_type.27.refs_0_, bf16[256,1024]{1,0:T(8,128)(2,1)S(1)} %get-tuple-element.44.refs_1_.refs_7_.refs_11_, bf16[256,1024]{1,0:T(8,128)(2,1)S(1)} %collective-permute-done.12.refs_2_, ...), custom_call_target="tpu_custom_call" | custom-call | flops 1000 | bytes 1000 | tf_op jit(solution)/shard_map/step/pallas_call | solution.py:49
  67.6 4.1 %step.6 = (f32[256,640]{1,0:T(8,128)S(1)}, f32[512,640]{1,0:T(8,128)S(1)}) custom-call(s32[5]{0:T(128)S(1)} %convert_element_type.27.refs_0_, bf16[256,1024]{1,0:T(8,128)(2,1)S(1)} %get-tuple-element.44.refs_1_.refs_7_.refs_11_, bf16[256,1024]{1,0:T(8,128)(2,1)S(1)} %collective-permute-done.12.refs_2_, ...), custom_call_target="tpu_custom_call" | custom-call | flops 1000 | bytes 1000 | tf_op jit(solution)/shard_map/step/pallas_call | solution.py:49
  71.8 2.0 %collective-permute-done.11.refs_1_ = bf16[512,640]{1,0:T(8,128)(2,1)S(1)} collective-permute-done((bf16[512,640]{1,0:T(8,128)(2,1)S(1)}, bf16[512,640]{1,0:T(8,128)(2,1)S(1)}, u32[]{:S(2)}, u32[]{:S(2)}) %collective-permute-start.11) | collective-permute-done | bytes 655392 | tf_op jit(solution)/shard_map/ppermute | solution.py:30
  74.5 1.7 %collective-permute-done.21.refs_2_ = bf16[512,640]{1,0:T(8,128)(2,1)S(1)} collective-permute-done((bf16[512,640]{1,0:T(8,128)(2,1)S(1)}, bf16[512,640]{1,0:T(8,128)(2,1)S(1)}, u32[]{:S(2)}, u32[]{:S(2)}) %collective-permute-start.21) | collective-permute-done | bytes 655392 | tf_op jit(solution)/shard_map/ppermute | solution.py:25
  76.2 3.9 %finish.1 = (bf16[2048,128]{1,0:T(8,128)(2,1)}, bf16[4096,128]{1,0:T(8,128)(2,1)}) custom-call(s32[5]{0:T(128)S(1)} %convert_element_type.27.refs_0_, bf16[512,640]{1,0:T(8,128)(2,1)S(1)} %collective-permute-done.11.refs_1_, bf16[512,640]{1,0:T(8,128)(2,1)S(1)} %collective-permute-done.21.refs_2_, f32[256,640]{1,0:T(8,128)S(1)} %get-tuple-element.52.refs_3_, ...), custom_call_target="tpu_custom_call" | custom-call | flops 1000 | bytes 1000 | tf_op jit(solution)/shard_map/finish/pallas_call | solution.py:49
  (55 shorter events, 10.7 us)
Async XLA Ops:
  0.6 14.0 %collective-permute-start.1 = (bf16[256,8,128]{2,1,0:T(8,128)(2,1)}, bf16[256,8,128]{2,1,0:T(8,128)(2,1)S(1)}, u32[]{:S(2)}, u32[]{:S(2)}) collective-permute-start(bf16[256,8,128]{2,1,0:T(8,128)(2,1)} %param.11), channel_id=1, source_target_pairs={{8,0},{12,4},{0,8},{4,12},{9,1},{13,5},{1,9},{5,13},{10,2},{14,6},... | collective-permute-start | bytes 1572872 | tf_op jit(solution)/shard_map/ppermute | solution.py:30
  3.3 13.5 %copy-start.8 = (bf16[512,12,128]{2,0,1:T(8,128)(2,1)S(1)}, bf16[512,12,128]{2,0,1:T(8,128)(2,1)}, u32[]{:S(2)}) copy-start(bf16[512,12,128]{2,0,1:T(8,128)(2,1)} %param.15) | copy-start | bytes 4718596
  4.8 7.7 %collective-permute-start.2 = (bf16[768,128]{1,0:T(8,128)(2,1)S(1)}, bf16[768,128]{1,0:T(8,128)(2,1)S(1)}, u32[]{:S(2)}, u32[]{:S(2)}) collective-permute-start(bf16[768,128]{1,0:T(8,128)(2,1)S(1)} %get-tuple-element.31), channel_id=1, source_target_pairs={{0,1},{1,0},{2,3},{3,2},{4,5},{5,4},{6,7},{7,6},{8,9},{9,8},{10,11... | collective-permute-start | bytes 589832 | tf_op jit(solution)/shard_map/ppermute | solution.py:37
  4.9 8.5 %collective-permute-start.3 = (bf16[768,128]{1,0:T(8,128)(2,1)S(1)}, bf16[768,128]{1,0:T(8,128)(2,1)S(1)}, u32[]{:S(2)}, u32[]{:S(2)}) collective-permute-start(bf16[768,128]{1,0:T(8,128)(2,1)S(1)} %get-tuple-element.32), channel_id=1, source_target_pairs={{1,2},{2,1},{5,6},{6,5},{9,10},{10,9},{13,14},{14,13},{17,18},{18,... | collective-permute-start | bytes 589832 | tf_op jit(solution)/shard_map/ppermute | solution.py:37
  9.4 12.7 %collective-permute-start.8 = (bf16[512,384]{1,0:T(8,128)(2,1)S(1)}, bf16[512,384]{1,0:T(8,128)(2,1)S(1)}, u32[]{:S(2)}, u32[]{:S(2)}) collective-permute-start(bf16[512,384]{1,0:T(8,128)(2,1)S(1)} %get-tuple-element.30.refs_5_.refs_10_), channel_id=1, source_target_pairs={{8,0},{12,4},{0,8},{4,12},{9,1},{13,5},{1,9},{5,13},{10,2},{14,6},... | collective-permute-start | bytes 1179656 | tf_op jit(solution)/shard_map/ppermute | solution.py:30
  10.7 14.1 %collective-permute-start = (bf16[256,8,128]{2,1,0:T(8,128)(2,1)}, bf16[256,8,128]{2,1,0:T(8,128)(2,1)S(1)}, u32[]{:S(2)}, u32[]{:S(2)}) collective-permute-start(bf16[256,8,128]{2,1,0:T(8,128)(2,1)} %param.11), channel_id=1, source_target_pairs={{0,4},{4,0},{8,12},{12,8},{1,5},{5,1},{9,13},{13,9},{2,6},{6,2},{1... | collective-permute-start | bytes 1572872 | tf_op jit(solution)/shard_map/ppermute | solution.py:25
  12.5 13.4 %collective-permute-start.7 = (bf16[512,384]{1,0:T(8,128)(2,1)S(1)}, bf16[512,384]{1,0:T(8,128)(2,1)S(1)}, u32[]{:S(2)}, u32[]{:S(2)}) collective-permute-start(bf16[512,384]{1,0:T(8,128)(2,1)S(1)} %get-tuple-element.30.refs_5_.refs_10_), channel_id=1, source_target_pairs={{0,4},{4,0},{8,12},{12,8},{1,5},{5,1},{9,13},{13,9},{2,6},{6,2},{1... | collective-permute-start | bytes 1179656 | tf_op jit(solution)/shard_map/ppermute | solution.py:25
  13.4 22.8 %collective-permute-start.6 = (bf16[512,640]{1,0:T(8,128)(2,1)S(1)}, bf16[512,640]{1,0:T(8,128)(2,1)S(1)}, u32[]{:S(2)}, u32[]{:S(2)}) collective-permute-start(bf16[512,640]{1,0:T(8,128)(2,1)S(1)} %get-tuple-element.37.refs_12_.refs_5_), channel_id=1, source_target_pairs={{8,0},{12,4},{0,8},{4,12},{9,1},{13,5},{1,9},{5,13},{10,2},{14,6},... | collective-permute-start | bytes 1966088 | tf_op jit(solution)/shard_map/ppermute | solution.py:30
  14.6 10.3 %collective-permute-start.4 = (bf16[256,8,128]{2,1,0:T(8,128)(2,1)S(1)}, bf16[256,8,128]{2,1,0:T(8,128)(2,1)S(1)}, u32[]{:S(2)}, u32[]{:S(2)}) collective-permute-start(bf16[256,8,128]{2,1,0:T(8,128)(2,1)S(1)} %collective-permute-done.1), channel_id=1, source_target_pairs={{0,4},{4,0},{8,12},{12,8},{1,5},{5,1},{9,13},{13,9},{2,6},{6,2},{1... | collective-permute-start | bytes 1572872 | tf_op jit(solution)/shard_map/ppermute | solution.py:25
  18.6 7.6 %copy-start = (bf16[256,2048]{1,0:T(8,128)(2,1)S(1)}, bf16[256,2048]{1,0:T(8,128)(2,1)}, u32[]{:S(2)}) copy-start(bf16[256,2048]{1,0:T(8,128)(2,1)} %refs_5_.1) | copy-start | bytes 3145732
  22.1 4.0 %collective-permute-start.9 = (bf16[512,384]{1,0:T(8,128)(2,1)S(1)}, bf16[512,384]{1,0:T(8,128)(2,1)S(1)}, u32[]{:S(2)}, u32[]{:S(2)}) collective-permute-start(bf16[512,384]{1,0:T(8,128)(2,1)S(1)} %collective-permute-done.8.refs_7_), channel_id=1, source_target_pairs={{0,4},{4,0},{8,12},{12,8},{1,5},{5,1},{9,13},{13,9},{2,6},{6,2},{1... | collective-permute-start | bytes 1179656 | tf_op jit(solution)/shard_map/ppermute | solution.py:25
  24.8 13.1 %collective-permute-start.5 = (bf16[512,640]{1,0:T(8,128)(2,1)S(1)}, bf16[512,640]{1,0:T(8,128)(2,1)S(1)}, u32[]{:S(2)}, u32[]{:S(2)}) collective-permute-start(bf16[512,640]{1,0:T(8,128)(2,1)S(1)} %get-tuple-element.37.refs_12_.refs_5_), channel_id=1, source_target_pairs={{0,4},{4,0},{8,12},{12,8},{1,5},{5,1},{9,13},{13,9},{2,6},{6,2},{1... | collective-permute-start | bytes 1966088 | tf_op jit(solution)/shard_map/ppermute | solution.py:25
  36.2 3.3 %collective-permute-start.10 = (bf16[512,640]{1,0:T(8,128)(2,1)S(1)}, bf16[512,640]{1,0:T(8,128)(2,1)S(1)}, u32[]{:S(2)}, u32[]{:S(2)}) collective-permute-start(bf16[512,640]{1,0:T(8,128)(2,1)S(1)} %collective-permute-done.6.refs_7_), channel_id=1, source_target_pairs={{0,4},{4,0},{8,12},{12,8},{1,5},{5,1},{9,13},{13,9},{2,6},{6,2},{1... | collective-permute-start | bytes 1966088 | tf_op jit(solution)/shard_map/ppermute | solution.py:25
  37.7 10.7 %collective-permute-start.14 = (bf16[512,384]{1,0:T(8,128)(2,1)S(1)}, bf16[512,384]{1,0:T(8,128)(2,1)S(1)}, u32[]{:S(2)}, u32[]{:S(2)}) collective-permute-start(bf16[512,384]{1,0:T(8,128)(2,1)S(1)} %get-tuple-element.40.refs_22_.refs_8_.refs_5_), channel_id=1, source_target_pairs={{8,0},{12,4},{0,8},{4,12},{9,1},{13,5},{1,9},{5,13},{10,2},{14,6},... | collective-permute-start | bytes 1179656 | tf_op jit(solution)/shard_map/ppermute | solution.py:30
  45.6 14.4 %collective-permute-start.13 = (bf16[256,1024]{1,0:T(8,128)(2,1)S(1)}, bf16[256,1024]{1,0:T(8,128)(2,1)S(1)}, u32[]{:S(2)}, u32[]{:S(2)}) collective-permute-start(bf16[256,1024]{1,0:T(8,128)(2,1)S(1)} %get-tuple-element.44.refs_1_.refs_7_.refs_11_), channel_id=1, source_target_pairs={{8,0},{12,4},{0,8},{4,12},{9,1},{13,5},{1,9},{5,13},{10,2},{14,6},... | collective-permute-start | bytes 1572872 | tf_op jit(solution)/shard_map/ppermute | solution.py:30
  48.5 11.5 %collective-permute-start.15 = (bf16[512,384]{1,0:T(8,128)(2,1)S(1)}, bf16[512,384]{1,0:T(8,128)(2,1)S(1)}, u32[]{:S(2)}, u32[]{:S(2)}) collective-permute-start(bf16[512,384]{1,0:T(8,128)(2,1)S(1)} %collective-permute-done.14.refs_7_), channel_id=1, source_target_pairs={{0,4},{4,0},{8,12},{12,8},{1,5},{5,1},{9,13},{13,9},{2,6},{6,2},{1... | collective-permute-start | bytes 1179656 | tf_op jit(solution)/shard_map/ppermute | solution.py:25
  49.6 6.5 %collective-permute-start.16 = (bf16[768,128]{1,0:T(8,128)(2,1)S(1)}, bf16[768,128]{1,0:T(8,128)(2,1)S(1)}, u32[]{:S(2)}, u32[]{:S(2)}) collective-permute-start(bf16[768,128]{1,0:T(8,128)(2,1)S(1)} %get-tuple-element.46), channel_id=1, source_target_pairs={{0,1},{1,0},{2,3},{3,2},{4,5},{5,4},{6,7},{7,6},{8,9},{9,8},{10,11... | collective-permute-start | bytes 589832 | tf_op jit(solution)/shard_map/ppermute | solution.py:37
  49.8 9.4 %collective-permute-start.17 = (bf16[768,128]{1,0:T(8,128)(2,1)S(1)}, bf16[768,128]{1,0:T(8,128)(2,1)S(1)}, u32[]{:S(2)}, u32[]{:S(2)}) collective-permute-start(bf16[768,128]{1,0:T(8,128)(2,1)S(1)} %get-tuple-element.47), channel_id=1, source_target_pairs={{1,2},{2,1},{5,6},{6,5},{9,10},{10,9},{13,14},{14,13},{17,18},{18,... | collective-permute-start | bytes 589832 | tf_op jit(solution)/shard_map/ppermute | solution.py:37
  54.3 13.3 %collective-permute-start.19 = (bf16[512,640]{1,0:T(8,128)(2,1)S(1)}, bf16[512,640]{1,0:T(8,128)(2,1)S(1)}, u32[]{:S(2)}, u32[]{:S(2)}) collective-permute-start(bf16[512,640]{1,0:T(8,128)(2,1)S(1)} %get-tuple-element.43.refs_5_.refs_12_), channel_id=1, source_target_pairs={{0,4},{4,0},{8,12},{12,8},{1,5},{5,1},{9,13},{13,9},{2,6},{6,2},{1... | collective-permute-start | bytes 1966088 | tf_op jit(solution)/shard_map/ppermute | solution.py:25
  56.2 17.6 %collective-permute-start.11 = (bf16[512,640]{1,0:T(8,128)(2,1)S(1)}, bf16[512,640]{1,0:T(8,128)(2,1)S(1)}, u32[]{:S(2)}, u32[]{:S(2)}) collective-permute-start(bf16[512,640]{1,0:T(8,128)(2,1)S(1)} %get-tuple-element.43.refs_5_.refs_12_), channel_id=1, source_target_pairs={{8,0},{12,4},{0,8},{4,12},{9,1},{13,5},{1,9},{5,13},{10,2},{14,6},... | collective-permute-start | bytes 1966088 | tf_op jit(solution)/shard_map/ppermute | solution.py:30
  59.2 3.8 %collective-permute-start.12 = (bf16[256,1024]{1,0:T(8,128)(2,1)S(1)}, bf16[256,1024]{1,0:T(8,128)(2,1)S(1)}, u32[]{:S(2)}, u32[]{:S(2)}) collective-permute-start(bf16[256,1024]{1,0:T(8,128)(2,1)S(1)} %get-tuple-element.44.refs_1_.refs_7_.refs_11_), channel_id=1, source_target_pairs={{0,4},{4,0},{8,12},{12,8},{1,5},{5,1},{9,13},{13,9},{2,6},{6,2},{1... | collective-permute-start | bytes 1572872 | tf_op jit(solution)/shard_map/ppermute | solution.py:25
  60.0 3.0 %collective-permute-start.18 = (bf16[256,1024]{1,0:T(8,128)(2,1)S(1)}, bf16[256,1024]{1,0:T(8,128)(2,1)S(1)}, u32[]{:S(2)}, u32[]{:S(2)}) collective-permute-start(bf16[256,1024]{1,0:T(8,128)(2,1)S(1)} %collective-permute-done.13.refs_3_), channel_id=1, source_target_pairs={{0,4},{4,0},{8,12},{12,8},{1,5},{5,1},{9,13},{13,9},{2,6},{6,2},{1... | collective-permute-start | bytes 1572872 | tf_op jit(solution)/shard_map/ppermute | solution.py:25
  60.9 2.1 %collective-permute-start.20 = (bf16[512,384]{1,0:T(8,128)(2,1)S(1)}, bf16[512,384]{1,0:T(8,128)(2,1)S(1)}, u32[]{:S(2)}, u32[]{:S(2)}) collective-permute-start(bf16[512,384]{1,0:T(8,128)(2,1)S(1)} %get-tuple-element.40.refs_22_.refs_8_.refs_5_), channel_id=1, source_target_pairs={{0,4},{4,0},{8,12},{12,8},{1,5},{5,1},{9,13},{13,9},{2,6},{6,2},{1... | collective-permute-start | bytes 1179656 | tf_op jit(solution)/shard_map/ppermute | solution.py:25
  73.7 2.5 %collective-permute-start.21 = (bf16[512,640]{1,0:T(8,128)(2,1)S(1)}, bf16[512,640]{1,0:T(8,128)(2,1)S(1)}, u32[]{:S(2)}, u32[]{:S(2)}) collective-permute-start(bf16[512,640]{1,0:T(8,128)(2,1)S(1)} %collective-permute-done.11.refs_1_), channel_id=1, source_target_pairs={{0,4},{4,0},{8,12},{12,8},{1,5},{5,1},{9,13},{13,9},{2,6},{6,2},{1... | collective-permute-start | bytes 1966088 | tf_op jit(solution)/shard_map/ppermute | solution.py:25
  (8 other events, 46.2 us)

commit v10 on v9

--- a/solution.py
+++ b/solution.py
@@ -9,6 +9,7 @@
 BLK = 128
 ITERS = 2
 CORES = 2
+TILE = 512
 CHUNKS = 2
 SHARES = (3, 5)
 PARTS = (1, 1)
@@ -159,25 +160,41 @@
     out_ref[at * nx : (at + count) * nx, :] = wide_ref[0 : count * nx, :].astype(jnp.bfloat16)
 
 
-def finish_kernel(n, e, p, ny, nx, place_ref, *refs):
-    far = n - CORES
-    far_refs, refs = refs[:far], refs[far:]
+def products(p, which, place_ref, p_refs):
+    def product(weight_ref, at, count):
+        total = 0.0
+        for j, x_ref in zip(which, p_refs):
+            columns = rows_at(place_ref[1 + j], p)
+            total += jnp.dot(weight_ref[at : at + count, columns], x_ref[...], preferred_element_type=jnp.float32)
+        return total
+
+    return product
+
+
+def add_kernel(e, p, which, place_ref, *refs):
+    far_refs, (rest_e_ref, rest_p_ref, absorption_ref, dense_ref, e_out_ref, p_out_ref), scratch = (
+        refs[: len(which)], refs[len(which) : len(which) + 6], refs[len(which) + 6 :]
+    )
+    load = Loader(scratch[-1])
+    copies = [load.start(x, y) for x, y in zip(far_refs, scratch)]
+    for copy in copies:
+        copy.wait()
+    product = products(p, which, place_ref, scratch[:-1])
+    e_out_ref[...] = rest_e_ref[...] + 0.5 * product(absorption_ref, 0, e)
+    p_out_ref[...] = rest_p_ref[...] + 0.5 * product(dense_ref, 0, p)
+
+
+def finish_kernel(e, p, ny, nx, which, place_ref, *refs):
+    far_refs, refs = refs[: len(which)], refs[len(which) :]
     rest_e_ref, rest_p_ref, absorption_ref, dense_ref, e_rate_ref, p_rate_ref = refs[:6]
     done_e, done_p, refs = refs[6 : 5 + CHUNKS], refs[5 + CHUNKS : 4 + 2 * CHUNKS], refs[4 + 2 * CHUNKS :]
-    e_out_ref, p_out_ref, p_ref, wide_ref, sems = refs
+    (e_out_ref, p_out_ref), scratch, wide_ref, sems = refs[:2], refs[2:-2], refs[-2], refs[-1]
     load = Loader(sems)
-    copies = [load.start(x, p_ref.at[j]) for j, x in enumerate(far_refs)]
+    copies = [load.start(x, y) for x, y in zip(far_refs, scratch)]
     for copy in copies:
         copy.wait()
-
-    def product(weight_ref, at, count):
-        total = 0.0
-        for j in range(far):
-            columns = rows_at(place_ref[1 + CORES + j], p)
-            total += jnp.dot(weight_ref[at : at + count, columns], p_ref[j], preferred_element_type=jnp.float32)
-        return total
-
-    tile = min(p, 256)
+    product = products(p, which, place_ref, scratch)
+    tile = min(p, TILE)
     pieces = [(0, e, absorption_ref, rest_e_ref, e_rate_ref, done_e, e_out_ref)]
     pieces += [(at, tile, dense_ref, rest_p_ref, p_rate_ref, done_p, p_out_ref) for at in range(0, p, tile)]
     for at, count, weight_ref, rest_ref, rate_ref, done, out_ref in pieces:
@@ -240,7 +257,7 @@
         for i, part in enumerate(e_out_refs):
             late.append(load.start(border[0][0].at[rows_of(0, i, part), :], part.at[:, 0 : part.shape[1] - width]))
         late.append(load.start(border[1][0].at[:, 0:ny], first_ref.at[e : e + p, :]))
-    tile = min(p, 256)
+    tile = min(p, TILE)
 
     def around(x_ref, rows, base):
         own = x_ref[rows, :].astype(jnp.float32)
@@ -396,13 +413,22 @@
         )
         return (list(out[:e_parts]), *out[e_parts:])
 
-    def finish(far, rest, done):
+    def add(far, which, rest):
+        return call(
+            lambda *refs: add_kernel(e, p, which, *refs),
+            tuple(jax.ShapeDtypeStruct((count, widths[-1]), jnp.float32) for count in (e, p)),
+            [pltpu.VMEM((p, widths[-1]), jnp.bfloat16) for _ in far], (places, *far, *rest, absorption, dense),
+            [SMEM] + [ANY] * len(far) + [VMEM] * 4, 20, "add", len(far),
+        )
+
+    def finish(far, which, rest, done):
         operands = (
             places, *far, *rest, absorption, dense, rates[2], rates[3], *(d[0][0] for d in done), *(d[1] for d in done),
         )
         return call(
-            lambda *refs: finish_kernel(n, e, p, ny, nx, *refs), (bf16(e * nx, ny), bf16(p * nx, ny)),
-            [pltpu.VMEM((len(far), p, widths[-1]), jnp.bfloat16), pltpu.VMEM((max(e, min(p, 256)) * nx, ny), jnp.float32)],
+            lambda *refs: finish_kernel(e, p, ny, nx, which, *refs), (bf16(e * nx, ny), bf16(p * nx, ny)),
+            [pltpu.VMEM((p, widths[-1]), jnp.bfloat16) for _ in far]
+            + [pltpu.VMEM((max(e, min(p, TILE)) * nx, ny), jnp.float32)],
             operands, [SMEM] + [ANY] * len(far) + [VMEM] * (4 + 2 * CHUNKS), 24, "finish", len(far),
         )
 
@@ -454,11 +480,11 @@
             (halo[:1], halo[1:]) if last else (e_next, p_next[k + 1 : k + 2]), last, (),
         ))
     rest = done.pop()
-    far = []
-    for f in far_p[-1]:
-        f = after(f, rest[1], done[-1][1])
-        far += [f, swap_cores(f)]
-    e_out, p_out = finish(far, (rest[0][0], rest[1]), done)
+    far = [after(f, rest[1], done[-1][1]) for f in far_p[-1]]
+    passed = [swap_cores(f) for f in far]
+    direct = [CORES * (d + 1) for d in range(len(far))]
+    rest = add(far, direct, (rest[0][0], rest[1]))
+    e_out, p_out = finish(passed, [j + 1 for j in direct], rest, done)
     return e_out.reshape(e, nx, ny), p_out.reshape(p, nx, ny)
 
 

time: 81.4 us -> 80.6 us (level)
  waiting for transfers between devices: 23.2 us -> 21.8 us
    ppermute x12, waiting for transfers between devices: 5.61 us -> 4.05 us  [swap_cores(): return lax.ppermute(x, 'mode', [(i, i ^ 1) for i in range(n)])]
    pallas_call x7 -> x8, Pallas kernels: 25.9 us -> 26.5 us  [call(): pl.pallas_call(kernel, out_shape=out, in_specs=specs, out_specs=(VMEM,) *...]
  transfers between devices with their start and end apart: 22 -> 22, of which waited for: 11 -> 11; matrix products, arithmetic and copies ran while one was open for 3% -> 3% of each run, Pallas kernels for 27% -> 30%
where the time goes in v10:
time: 80.6 us; the launch traced here: 79.4 us
  Pallas kernels  26.5 us (33%)
  starting transfers between devices  25.3 us (31%)
  waiting for transfers between devices  21.8 us (27%)
  local copies, waits for them, and re-layouts  2.96 us (4%)
  matrix products  1.83 us (2%)
  between operations  1 us (1%)
    pallas_call x8, Pallas kernels, call(): pl.pallas_call(kernel, out_shape=out, in_specs=specs, out_specs=(VMEM,) *...  26.5 us
    ppermute x6, waiting for transfers between devices, from_chip(): lax.ppermute(x, 'mode', [((i + CORES * offset) % n, i) for i in range(n)])  12.9 us
    ppermute x12, starting transfers between devices, swap_cores(): return lax.ppermute(x, 'mode', [(i, i ^ 1) for i in range(n)])  12.5 us
    ppermute x4, starting transfers between devices, halos(): return (lax.ppermute(a, 'space', near), lax.ppermute(b, 'space', other))  9.22 us
    ppermute x4, waiting for transfers between devices, halos(): return (lax.ppermute(a, 'space', near), lax.ppermute(b, 'space', other))  4.89 us
    ppermute x12, waiting for transfers between devices, swap_cores(): return lax.ppermute(x, 'mode', [(i, i ^ 1) for i in range(n)])  4.05 us
    ppermute x6, starting transfers between devices, from_chip(): lax.ppermute(x, 'mode', [((i + CORES * offset) % n, i) for i in range(n)])  3.57 us
    unnamed x25, local copies, waits for them, and re-layouts  2.88 us
  transfers between devices with their start and end apart: 22, of which 11 were waited for; matrix products, arithmetic and copies ran while one was open for 3% of the time, Pallas kernels for 30%

profile of v10, /device:TPU:13, one launch (start us, length us, event | category | flops | bytes accessed | tf_op | source)
XLA Modules:
  0.0 79.4 jit_solution(15191847953500930451)
XLA Ops:
  3.3 1.5 %flatten.2 = (bf16[256,1024]{1,0:T(8,128)(2,1)S(1)}, bf16[512,384]{1,0:T(8,128)(2,1)S(1)}, bf16[512,640]{1,0:T(8,128)(2,1)S(1)}, bf16[768,128]{1,0:T(8,128)(2,1)S(1)}, bf16[768,128]{1,0:T(8,128)(2,1)S(1)}) custom-call(s32[5]{0:T(128)S(1)} %convert_element_type.27.refs_0_, bf16[2048,128]{1,0:T(8,128)(2,1)S(1)} %bitcast.50, bf16[4096,128]{1,0:T(8,128)(2,1)S(1)} %bitcast.46), custom_call_target="tpu_custom_call" | custom-call | flops 1000 | bytes 1000 | tf_op jit(solution)/shard_map/flatten/pallas_call | solution.py:50
  4.9 4.5 %collective-permute-start.3 = (bf16[768,128]{1,0:T(8,128)(2,1)S(1)}, bf16[768,128]{1,0:T(8,128)(2,1)S(1)}, u32[]{:S(2)}, u32[]{:S(2)}) collective-permute-start(bf16[768,128]{1,0:T(8,128)(2,1)S(1)} %get-tuple-element.34), channel_id=1, source_target_pairs={{1,2},{2,1},{5,6},{6,5},{9,10},{10,9},{13,14},{14,13},{17,18},{18,... | collective-permute-start | bytes 589832 | tf_op jit(solution)/shard_map/ppermute | solution.py:38
  9.4 1.3 %collective-permute-start.8 = (bf16[512,384]{1,0:T(8,128)(2,1)S(1)}, bf16[512,384]{1,0:T(8,128)(2,1)S(1)}, u32[]{:S(2)}, u32[]{:S(2)}) collective-permute-start(bf16[512,384]{1,0:T(8,128)(2,1)S(1)} %get-tuple-element.32.refs_5_.refs_10_), channel_id=1, source_target_pairs={{8,0},{12,4},{0,8},{4,12},{9,1},{13,5},{1,9},{5,13},{10,2},{14,6},... | collective-permute-start | bytes 1179656 | tf_op jit(solution)/shard_map/ppermute | solution.py:31
  10.7 1.8 %collective-permute-start = (bf16[256,8,128]{2,1,0:T(8,128)(2,1)}, bf16[256,8,128]{2,1,0:T(8,128)(2,1)S(1)}, u32[]{:S(2)}, u32[]{:S(2)}) collective-permute-start(bf16[256,8,128]{2,1,0:T(8,128)(2,1)} %param.11), channel_id=1, source_target_pairs={{0,4},{4,0},{8,12},{12,8},{1,5},{5,1},{9,13},{13,9},{2,6},{6,2},{1... | collective-permute-start | bytes 1572872 | tf_op jit(solution)/shard_map/ppermute | solution.py:26
  13.4 1.2 %collective-permute-start.6 = (bf16[512,640]{1,0:T(8,128)(2,1)S(1)}, bf16[512,640]{1,0:T(8,128)(2,1)S(1)}, u32[]{:S(2)}, u32[]{:S(2)}) collective-permute-start(bf16[512,640]{1,0:T(8,128)(2,1)S(1)} %get-tuple-element.39.refs_12_.refs_5_), channel_id=1, source_target_pairs={{8,0},{12,4},{0,8},{4,12},{9,1},{13,5},{1,9},{5,13},{10,2},{14,6},... | collective-permute-start | bytes 1966088 | tf_op jit(solution)/shard_map/ppermute | solution.py:31
  14.6 2.1 %collective-permute-start.4 = (bf16[256,8,128]{2,1,0:T(8,128)(2,1)S(1)}, bf16[256,8,128]{2,1,0:T(8,128)(2,1)S(1)}, u32[]{:S(2)}, u32[]{:S(2)}) collective-permute-start(bf16[256,8,128]{2,1,0:T(8,128)(2,1)S(1)} %collective-permute-done.1), channel_id=1, source_target_pairs={{0,4},{4,0},{8,12},{12,8},{1,5},{5,1},{9,13},{13,9},{2,6},{6,2},{1... | collective-permute-start | bytes 1572872 | tf_op jit(solution)/shard_map/ppermute | solution.py:26
  16.8 1.8 %fusion.2 = bf16[4,128,128,16]{2,3,1,0:T(8,128)(2,1)S(1)} fusion(bf16[4,128,12,128]{3,1,0,2:T(8,128)(2,1)S(1)} %bitcast.74, s32[4,12]{1,0:T(4,128)} %param.16), kind=kOutput, calls=%fused_computation.3 | convolution fusion | flops 26215168 | bytes 3670208 | tf_op jit(solution)/shard_map/bsk,bisj->bikj/dot_general | solution.py:378
  19.2 2.9 %collective-permute-done.8.refs_7_ = bf16[512,384]{1,0:T(8,128)(2,1)S(1)} collective-permute-done((bf16[512,384]{1,0:T(8,128)(2,1)S(1)}, bf16[512,384]{1,0:T(8,128)(2,1)S(1)}, u32[]{:S(2)}, u32[]{:S(2)}) %collective-permute-start.8) | collective-permute-done | bytes 393248 | tf_op jit(solution)/shard_map/ppermute | solution.py:31
  22.1 2.7 %collective-permute-start.9 = (bf16[512,384]{1,0:T(8,128)(2,1)S(1)}, bf16[512,384]{1,0:T(8,128)(2,1)S(1)}, u32[]{:S(2)}, u32[]{:S(2)}) collective-permute-start(bf16[512,384]{1,0:T(8,128)(2,1)S(1)} %collective-permute-done.8.refs_7_), channel_id=1, source_target_pairs={{0,4},{4,0},{8,12},{12,8},{1,5},{5,1},{9,13},{13,9},{2,6},{6,2},{1... | collective-permute-start | bytes 1179656 | tf_op jit(solution)/shard_map/ppermute | solution.py:26
  26.2 4.6 %step.4 = (bf16[256,384]{1,0:T(8,128)(2,1)S(1)}, bf16[512,384]{1,0:T(8,128)(2,1)S(1)}) custom-call(s32[5]{0:T(128)S(1)} %convert_element_type.27.refs_0_, bf16[256,1024]{1,0:T(8,128)(2,1)S(1)} %get-tuple-element.31.refs_1_.refs_11_.refs_9_, bf16[256,1024]{1,0:T(8,128)(2,1)S(1)} %get-tuple-element.36.refs_2_, ...), custom_call_target="tpu_custom_call" | custom-call | flops 1000 | bytes 1000 | tf_op jit(solution)/shard_map/step/pallas_call | solution.py:50
  30.8 5.3 %collective-permute-done.6.refs_7_ = bf16[512,640]{1,0:T(8,128)(2,1)S(1)} collective-permute-done((bf16[512,640]{1,0:T(8,128)(2,1)S(1)}, bf16[512,640]{1,0:T(8,128)(2,1)S(1)}, u32[]{:S(2)}, u32[]{:S(2)}) %collective-permute-start.6) | collective-permute-done | bytes 655392 | tf_op jit(solution)/shard_map/ppermute | solution.py:31
  36.2 1.5 %collective-permute-start.10 = (bf16[512,640]{1,0:T(8,128)(2,1)S(1)}, bf16[512,640]{1,0:T(8,128)(2,1)S(1)}, u32[]{:S(2)}, u32[]{:S(2)}) collective-permute-start(bf16[512,640]{1,0:T(8,128)(2,1)S(1)} %collective-permute-done.6.refs_7_), channel_id=1, source_target_pairs={{0,4},{4,0},{8,12},{12,8},{1,5},{5,1},{9,13},{13,9},{2,6},{6,2},{1... | collective-permute-start | bytes 1966088 | tf_op jit(solution)/shard_map/ppermute | solution.py:26
  38.0 1.5 %collective-permute-done.10.refs_8_ = bf16[512,640]{1,0:T(8,128)(2,1)S(1)} collective-permute-done((bf16[512,640]{1,0:T(8,128)(2,1)S(1)}, bf16[512,640]{1,0:T(8,128)(2,1)S(1)}, u32[]{:S(2)}, u32[]{:S(2)}) %collective-permute-start.10) | collective-permute-done | bytes 655392 | tf_op jit(solution)/shard_map/ppermute | solution.py:26
  39.4 6.1 %step.5 = (bf16[256,1024]{1,0:T(8,128)(2,1)S(1)}, bf16[512,640]{1,0:T(8,128)(2,1)S(1)}, bf16[768,128]{1,0:T(8,128)(2,1)S(1)}, bf16[768,128]{1,0:T(8,128)(2,1)S(1)}) custom-call(s32[5]{0:T(128)S(1)} %convert_element_type.27.refs_0_, bf16[256,1024]{1,0:T(8,128)(2,1)S(1)} %get-tuple-element.31.refs_1_.refs_11_.refs_9_, ...), custom_call_target="tpu_custom_call" | custom-call | flops 1000 | bytes 1000 | tf_op jit(solution)/shard_map/step/pallas_call | solution.py:50
  45.8 2.6 %collective-permute-done.14.refs_7_ = bf16[512,384]{1,0:T(8,128)(2,1)S(1)} collective-permute-done((bf16[512,384]{1,0:T(8,128)(2,1)S(1)}, bf16[512,384]{1,0:T(8,128)(2,1)S(1)}, u32[]{:S(2)}, u32[]{:S(2)}) %collective-permute-start.14) | collective-permute-done | bytes 393248 | tf_op jit(solution)/shard_map/ppermute | solution.py:31
  49.8 4.5 %collective-permute-start.17 = (bf16[768,128]{1,0:T(8,128)(2,1)S(1)}, bf16[768,128]{1,0:T(8,128)(2,1)S(1)}, u32[]{:S(2)}, u32[]{:S(2)}) collective-permute-start(bf16[768,128]{1,0:T(8,128)(2,1)S(1)} %get-tuple-element.49), channel_id=1, source_target_pairs={{1,2},{2,1},{5,6},{6,5},{9,10},{10,9},{13,14},{14,13},{17,18},{18,... | collective-permute-start | bytes 589832 | tf_op jit(solution)/shard_map/ppermute | solution.py:38
  54.9 1.2 %collective-permute-done.16.refs_9_ = bf16[768,128]{1,0:T(8,128)(2,1)S(1)} collective-permute-done((bf16[768,128]{1,0:T(8,128)(2,1)S(1)}, bf16[768,128]{1,0:T(8,128)(2,1)S(1)}, u32[]{:S(2)}, u32[]{:S(2)}) %collective-permute-start.16) | collective-permute-done | bytes 196640 | tf_op jit(solution)/shard_map/ppermute | solution.py:38
  56.4 2.8 %collective-permute-done.17.refs_10_ = bf16[768,128]{1,0:T(8,128)(2,1)S(1)} collective-permute-done((bf16[768,128]{1,0:T(8,128)(2,1)S(1)}, bf16[768,128]{1,0:T(8,128)(2,1)S(1)}, u32[]{:S(2)}, u32[]{:S(2)}) %collective-permute-start.17) | collective-permute-done | bytes 196640 | tf_op jit(solution)/shard_map/ppermute | solution.py:38
  60.9 2.1 %collective-permute-done.20.refs_6_ = bf16[512,384]{1,0:T(8,128)(2,1)S(1)} collective-permute-done((bf16[512,384]{1,0:T(8,128)(2,1)S(1)}, bf16[512,384]{1,0:T(8,128)(2,1)S(1)}, u32[]{:S(2)}, u32[]{:S(2)}) %collective-permute-start.20) | collective-permute-done | bytes 393248 | tf_op jit(solution)/shard_map/ppermute | solution.py:26
  63.0 4.6 %step.7 = (bf16[256,384]{1,0:T(8,128)(2,1)S(1)}, bf16[512,384]{1,0:T(8,128)(2,1)S(1)}) custom-call(s32[5]{0:T(128)S(1)} %convert_element_type.27.refs_0_, bf16[256,1024]{1,0:T(8,128)(2,1)S(1)} %get-tuple-element.46.refs_1_.refs_7_.refs_11_, bf16[256,1024]{1,0:T(8,128)(2,1)S(1)} %collective-permute-done.12.refs_2_, ...), custom_call_target="tpu_custom_call" | custom-call | flops 1000 | bytes 1000 | tf_op jit(solution)/shard_map/step/pallas_call | solution.py:50
  67.6 4.1 %step.6 = (f32[256,640]{1,0:T(8,128)S(1)}, f32[512,640]{1,0:T(8,128)S(1)}) custom-call(s32[5]{0:T(128)S(1)} %convert_element_type.27.refs_0_, bf16[256,1024]{1,0:T(8,128)(2,1)S(1)} %get-tuple-element.46.refs_1_.refs_7_.refs_11_, bf16[256,1024]{1,0:T(8,128)(2,1)S(1)} %collective-permute-done.12.refs_2_, ...), custom_call_target="tpu_custom_call" | custom-call | flops 1000 | bytes 1000 | tf_op jit(solution)/shard_map/step/pallas_call | solution.py:50
  71.7 2.0 %collective-permute-done.11.refs_1_ = bf16[512,640]{1,0:T(8,128)(2,1)S(1)} collective-permute-done((bf16[512,640]{1,0:T(8,128)(2,1)S(1)}, bf16[512,640]{1,0:T(8,128)(2,1)S(1)}, u32[]{:S(2)}, u32[]{:S(2)}) %collective-permute-start.11) | collective-permute-done | bytes 655392 | tf_op jit(solution)/shard_map/ppermute | solution.py:31
  74.5 1.6 %add.29 = (f32[256,640]{1,0:T(8,128)S(1)}, f32[512,640]{1,0:T(8,128)S(1)}) custom-call(s32[5]{0:T(128)S(1)} %convert_element_type.27.refs_0_, bf16[512,640]{1,0:T(8,128)(2,1)S(1)} %collective-permute-done.11.refs_1_, f32[256,640]{1,0:T(8,128)S(1)} %get-tuple-element.54.refs_2_, f32[512,640]{1,0:T(8,128)S(1)} %get-tuple-element.51.refs_3_, ...), custom_call_target="tpu_custom_call" | custom-call | flops 1000 | bytes 1000 | tf_op jit(solution)/shard_map/add/pallas_call | solution.py:50
  76.2 3.0 %finish.1 = (bf16[2048,128]{1,0:T(8,128)(2,1)}, bf16[4096,128]{1,0:T(8,128)(2,1)}) custom-call(s32[5]{0:T(128)S(1)} %convert_element_type.27.refs_0_, bf16[512,640]{1,0:T(8,128)(2,1)S(1)} %collective-permute-done.21.refs_1_, f32[256,640]{1,0:T(8,128)S(1)} %get-tuple-element.55.refs_2_, f32[512,640]{1,0:T(8,128)S(1)} %get-tuple-element.56.refs_3_, ...), custom_call_target="tpu_custom_call" | custom-call | flops 1000 | bytes 1000 | tf_op jit(solution)/shard_map/finish/pallas_call | solution.py:50
  (56 shorter events, 10.9 us)
Async XLA Ops:
  0.6 14.0 %collective-permute-start.1 = (bf16[256,8,128]{2,1,0:T(8,128)(2,1)}, bf16[256,8,128]{2,1,0:T(8,128)(2,1)S(1)}, u32[]{:S(2)}, u32[]{:S(2)}) collective-permute-start(bf16[256,8,128]{2,1,0:T(8,128)(2,1)} %param.11), channel_id=1, source_target_pairs={{8,0},{12,4},{0,8},{4,12},{9,1},{13,5},{1,9},{5,13},{10,2},{14,6},... | collective-permute-start | bytes 1572872 | tf_op jit(solution)/shard_map/ppermute | solution.py:31
  3.3 13.5 %copy-start.8 = (bf16[512,12,128]{2,0,1:T(8,128)(2,1)S(1)}, bf16[512,12,128]{2,0,1:T(8,128)(2,1)}, u32[]{:S(2)}) copy-start(bf16[512,12,128]{2,0,1:T(8,128)(2,1)} %param.15) | copy-start | bytes 4718596
  4.8 7.7 %collective-permute-start.2 = (bf16[768,128]{1,0:T(8,128)(2,1)S(1)}, bf16[768,128]{1,0:T(8,128)(2,1)S(1)}, u32[]{:S(2)}, u32[]{:S(2)}) collective-permute-start(bf16[768,128]{1,0:T(8,128)(2,1)S(1)} %get-tuple-element.33), channel_id=1, source_target_pairs={{0,1},{1,0},{2,3},{3,2},{4,5},{5,4},{6,7},{7,6},{8,9},{9,8},{10,11... | collective-permute-start | bytes 589832 | tf_op jit(solution)/shard_map/ppermute | solution.py:38
  4.9 8.5 %collective-permute-start.3 = (bf16[768,128]{1,0:T(8,128)(2,1)S(1)}, bf16[768,128]{1,0:T(8,128)(2,1)S(1)}, u32[]{:S(2)}, u32[]{:S(2)}) collective-permute-start(bf16[768,128]{1,0:T(8,128)(2,1)S(1)} %get-tuple-element.34), channel_id=1, source_target_pairs={{1,2},{2,1},{5,6},{6,5},{9,10},{10,9},{13,14},{14,13},{17,18},{18,... | collective-permute-start | bytes 589832 | tf_op jit(solution)/shard_map/ppermute | solution.py:38
  9.4 12.7 %collective-permute-start.8 = (bf16[512,384]{1,0:T(8,128)(2,1)S(1)}, bf16[512,384]{1,0:T(8,128)(2,1)S(1)}, u32[]{:S(2)}, u32[]{:S(2)}) collective-permute-start(bf16[512,384]{1,0:T(8,128)(2,1)S(1)} %get-tuple-element.32.refs_5_.refs_10_), channel_id=1, source_target_pairs={{8,0},{12,4},{0,8},{4,12},{9,1},{13,5},{1,9},{5,13},{10,2},{14,6},... | collective-permute-start | bytes 1179656 | tf_op jit(solution)/shard_map/ppermute | solution.py:31
  10.7 14.1 %collective-permute-start = (bf16[256,8,128]{2,1,0:T(8,128)(2,1)}, bf16[256,8,128]{2,1,0:T(8,128)(2,1)S(1)}, u32[]{:S(2)}, u32[]{:S(2)}) collective-permute-start(bf16[256,8,128]{2,1,0:T(8,128)(2,1)} %param.11), channel_id=1, source_target_pairs={{0,4},{4,0},{8,12},{12,8},{1,5},{5,1},{9,13},{13,9},{2,6},{6,2},{1... | collective-permute-start | bytes 1572872 | tf_op jit(solution)/shard_map/ppermute | solution.py:26
  12.5 13.4 %collective-permute-start.7 = (bf16[512,384]{1,0:T(8,128)(2,1)S(1)}, bf16[512,384]{1,0:T(8,128)(2,1)S(1)}, u32[]{:S(2)}, u32[]{:S(2)}) collective-permute-start(bf16[512,384]{1,0:T(8,128)(2,1)S(1)} %get-tuple-element.32.refs_5_.refs_10_), channel_id=1, source_target_pairs={{0,4},{4,0},{8,12},{12,8},{1,5},{5,1},{9,13},{13,9},{2,6},{6,2},{1... | collective-permute-start | bytes 1179656 | tf_op jit(solution)/shard_map/ppermute | solution.py:26
  13.4 22.8 %collective-permute-start.6 = (bf16[512,640]{1,0:T(8,128)(2,1)S(1)}, bf16[512,640]{1,0:T(8,128)(2,1)S(1)}, u32[]{:S(2)}, u32[]{:S(2)}) collective-permute-start(bf16[512,640]{1,0:T(8,128)(2,1)S(1)} %get-tuple-element.39.refs_12_.refs_5_), channel_id=1, source_target_pairs={{8,0},{12,4},{0,8},{4,12},{9,1},{13,5},{1,9},{5,13},{10,2},{14,6},... | collective-permute-start | bytes 1966088 | tf_op jit(solution)/shard_map/ppermute | solution.py:31
  14.6 10.3 %collective-permute-start.4 = (bf16[256,8,128]{2,1,0:T(8,128)(2,1)S(1)}, bf16[256,8,128]{2,1,0:T(8,128)(2,1)S(1)}, u32[]{:S(2)}, u32[]{:S(2)}) collective-permute-start(bf16[256,8,128]{2,1,0:T(8,128)(2,1)S(1)} %collective-permute-done.1), channel_id=1, source_target_pairs={{0,4},{4,0},{8,12},{12,8},{1,5},{5,1},{9,13},{13,9},{2,6},{6,2},{1... | collective-permute-start | bytes 1572872 | tf_op jit(solution)/shard_map/ppermute | solution.py:26
  18.6 7.6 %copy-start = (bf16[256,2048]{1,0:T(8,128)(2,1)S(1)}, bf16[256,2048]{1,0:T(8,128)(2,1)}, u32[]{:S(2)}) copy-start(bf16[256,2048]{1,0:T(8,128)(2,1)} %refs_4_.3) | copy-start | bytes 3145732
  22.1 4.0 %collective-permute-start.9 = (bf16[512,384]{1,0:T(8,128)(2,1)S(1)}, bf16[512,384]{1,0:T(8,128)(2,1)S(1)}, u32[]{:S(2)}, u32[]{:S(2)}) collective-permute-start(bf16[512,384]{1,0:T(8,128)(2,1)S(1)} %collective-permute-done.8.refs_7_), channel_id=1, source_target_pairs={{0,4},{4,0},{8,12},{12,8},{1,5},{5,1},{9,13},{13,9},{2,6},{6,2},{1... | collective-permute-start | bytes 1179656 | tf_op jit(solution)/shard_map/ppermute | solution.py:26
  24.8 13.1 %collective-permute-start.5 = (bf16[512,640]{1,0:T(8,128)(2,1)S(1)}, bf16[512,640]{1,0:T(8,128)(2,1)S(1)}, u32[]{:S(2)}, u32[]{:S(2)}) collective-permute-start(bf16[512,640]{1,0:T(8,128)(2,1)S(1)} %get-tuple-element.39.refs_12_.refs_5_), channel_id=1, source_target_pairs={{0,4},{4,0},{8,12},{12,8},{1,5},{5,1},{9,13},{13,9},{2,6},{6,2},{1... | collective-permute-start | bytes 1966088 | tf_op jit(solution)/shard_map/ppermute | solution.py:26
  36.2 3.3 %collective-permute-start.10 = (bf16[512,640]{1,0:T(8,128)(2,1)S(1)}, bf16[512,640]{1,0:T(8,128)(2,1)S(1)}, u32[]{:S(2)}, u32[]{:S(2)}) collective-permute-start(bf16[512,640]{1,0:T(8,128)(2,1)S(1)} %collective-permute-done.6.refs_7_), channel_id=1, source_target_pairs={{0,4},{4,0},{8,12},{12,8},{1,5},{5,1},{9,13},{13,9},{2,6},{6,2},{1... | collective-permute-start | bytes 1966088 | tf_op jit(solution)/shard_map/ppermute | solution.py:26
  37.7 10.7 %collective-permute-start.14 = (bf16[512,384]{1,0:T(8,128)(2,1)S(1)}, bf16[512,384]{1,0:T(8,128)(2,1)S(1)}, u32[]{:S(2)}, u32[]{:S(2)}) collective-permute-start(bf16[512,384]{1,0:T(8,128)(2,1)S(1)} %get-tuple-element.42.refs_22_.refs_8_.refs_5_), channel_id=1, source_target_pairs={{8,0},{12,4},{0,8},{4,12},{9,1},{13,5},{1,9},{5,13},{10,2},{14,6},... | collective-permute-start | bytes 1179656 | tf_op jit(solution)/shard_map/ppermute | solution.py:31
  45.6 14.4 %collective-permute-start.13 = (bf16[256,1024]{1,0:T(8,128)(2,1)S(1)}, bf16[256,1024]{1,0:T(8,128)(2,1)S(1)}, u32[]{:S(2)}, u32[]{:S(2)}) collective-permute-start(bf16[256,1024]{1,0:T(8,128)(2,1)S(1)} %get-tuple-element.46.refs_1_.refs_7_.refs_11_), channel_id=1, source_target_pairs={{8,0},{12,4},{0,8},{4,12},{9,1},{13,5},{1,9},{5,13},{10,2},{14,6},... | collective-permute-start | bytes 1572872 | tf_op jit(solution)/shard_map/ppermute | solution.py:31
  48.5 11.5 %collective-permute-start.15 = (bf16[512,384]{1,0:T(8,128)(2,1)S(1)}, bf16[512,384]{1,0:T(8,128)(2,1)S(1)}, u32[]{:S(2)}, u32[]{:S(2)}) collective-permute-start(bf16[512,384]{1,0:T(8,128)(2,1)S(1)} %collective-permute-done.14.refs_7_), channel_id=1, source_target_pairs={{0,4},{4,0},{8,12},{12,8},{1,5},{5,1},{9,13},{13,9},{2,6},{6,2},{1... | collective-permute-start | bytes 1179656 | tf_op jit(solution)/shard_map/ppermute | solution.py:26
  49.6 6.5 %collective-permute-start.16 = (bf16[768,128]{1,0:T(8,128)(2,1)S(1)}, bf16[768,128]{1,0:T(8,128)(2,1)S(1)}, u32[]{:S(2)}, u32[]{:S(2)}) collective-permute-start(bf16[768,128]{1,0:T(8,128)(2,1)S(1)} %get-tuple-element.48), channel_id=1, source_target_pairs={{0,1},{1,0},{2,3},{3,2},{4,5},{5,4},{6,7},{7,6},{8,9},{9,8},{10,11... | collective-permute-start | bytes 589832 | tf_op jit(solution)/shard_map/ppermute | solution.py:38
  49.8 9.4 %collective-permute-start.17 = (bf16[768,128]{1,0:T(8,128)(2,1)S(1)}, bf16[768,128]{1,0:T(8,128)(2,1)S(1)}, u32[]{:S(2)}, u32[]{:S(2)}) collective-permute-start(bf16[768,128]{1,0:T(8,128)(2,1)S(1)} %get-tuple-element.49), channel_id=1, source_target_pairs={{1,2},{2,1},{5,6},{6,5},{9,10},{10,9},{13,14},{14,13},{17,18},{18,... | collective-permute-start | bytes 589832 | tf_op jit(solution)/shard_map/ppermute | solution.py:38
  54.3 13.3 %collective-permute-start.19 = (bf16[512,640]{1,0:T(8,128)(2,1)S(1)}, bf16[512,640]{1,0:T(8,128)(2,1)S(1)}, u32[]{:S(2)}, u32[]{:S(2)}) collective-permute-start(bf16[512,640]{1,0:T(8,128)(2,1)S(1)} %get-tuple-element.45.refs_5_.refs_12_), channel_id=1, source_target_pairs={{0,4},{4,0},{8,12},{12,8},{1,5},{5,1},{9,13},{13,9},{2,6},{6,2},{1... | collective-permute-start | bytes 1966088 | tf_op jit(solution)/shard_map/ppermute | solution.py:26
  56.2 17.6 %collective-permute-start.11 = (bf16[512,640]{1,0:T(8,128)(2,1)S(1)}, bf16[512,640]{1,0:T(8,128)(2,1)S(1)}, u32[]{:S(2)}, u32[]{:S(2)}) collective-permute-start(bf16[512,640]{1,0:T(8,128)(2,1)S(1)} %get-tuple-element.45.refs_5_.refs_12_), channel_id=1, source_target_pairs={{8,0},{12,4},{0,8},{4,12},{9,1},{13,5},{1,9},{5,13},{10,2},{14,6},... | collective-permute-start | bytes 1966088 | tf_op jit(solution)/shard_map/ppermute | solution.py:31
  59.2 3.8 %collective-permute-start.12 = (bf16[256,1024]{1,0:T(8,128)(2,1)S(1)}, bf16[256,1024]{1,0:T(8,128)(2,1)S(1)}, u32[]{:S(2)}, u32[]{:S(2)}) collective-permute-start(bf16[256,1024]{1,0:T(8,128)(2,1)S(1)} %get-tuple-element.46.refs_1_.refs_7_.refs_11_), channel_id=1, source_target_pairs={{0,4},{4,0},{8,12},{12,8},{1,5},{5,1},{9,13},{13,9},{2,6},{6,2},{1... | collective-permute-start | bytes 1572872 | tf_op jit(solution)/shard_map/ppermute | solution.py:26
  60.0 3.0 %collective-permute-start.18 = (bf16[256,1024]{1,0:T(8,128)(2,1)S(1)}, bf16[256,1024]{1,0:T(8,128)(2,1)S(1)}, u32[]{:S(2)}, u32[]{:S(2)}) collective-permute-start(bf16[256,1024]{1,0:T(8,128)(2,1)S(1)} %collective-permute-done.13.refs_3_), channel_id=1, source_target_pairs={{0,4},{4,0},{8,12},{12,8},{1,5},{5,1},{9,13},{13,9},{2,6},{6,2},{1... | collective-permute-start | bytes 1572872 | tf_op jit(solution)/shard_map/ppermute | solution.py:26
  60.9 2.1 %collective-permute-start.20 = (bf16[512,384]{1,0:T(8,128)(2,1)S(1)}, bf16[512,384]{1,0:T(8,128)(2,1)S(1)}, u32[]{:S(2)}, u32[]{:S(2)}) collective-permute-start(bf16[512,384]{1,0:T(8,128)(2,1)S(1)} %get-tuple-element.42.refs_22_.refs_8_.refs_5_), channel_id=1, source_target_pairs={{0,4},{4,0},{8,12},{12,8},{1,5},{5,1},{9,13},{13,9},{2,6},{6,2},{1... | collective-permute-start | bytes 1179656 | tf_op jit(solution)/shard_map/ppermute | solution.py:26
  73.7 2.5 %collective-permute-start.21 = (bf16[512,640]{1,0:T(8,128)(2,1)S(1)}, bf16[512,640]{1,0:T(8,128)(2,1)S(1)}, u32[]{:S(2)}, u32[]{:S(2)}) collective-permute-start(bf16[512,640]{1,0:T(8,128)(2,1)S(1)} %collective-permute-done.11.refs_1_), channel_id=1, source_target_pairs={{0,4},{4,0},{8,12},{12,8},{1,5},{5,1},{9,13},{13,9},{2,6},{6,2},{1... | collective-permute-start | bytes 1966088 | tf_op jit(solution)/shard_map/ppermute | solution.py:26
  (8 other events, 46.2 us)

commit v11 on v10

--- a/solution.py
+++ b/solution.py
@@ -10,6 +10,7 @@
 ITERS = 2
 CORES = 2
 TILE = 512
+LAST_TILE = 256
 CHUNKS = 2
 SHARES = (3, 5)
 PARTS = (1, 1)
@@ -46,12 +47,12 @@
     return jax.ShapeDtypeStruct(shape, jnp.bfloat16)
 
 
-def call(kernel, out, scratch, operands, specs, megabytes, name, copies):
+def call(kernel, out, scratch, operands, specs, megabytes, name, copies, out_spec=VMEM):
     return pl.pallas_call(
         kernel,
         out_shape=out,
         in_specs=specs,
-        out_specs=(VMEM,) * len(out),
+        out_specs=(out_spec,) * len(out),
         scratch_shapes=[*scratch, pltpu.SemaphoreType.DMA((copies,))],
         compiler_params=pltpu.CompilerParams(vmem_limit_bytes=megabytes << 20),
         cost_estimate=COST,
@@ -188,22 +189,26 @@
     far_refs, refs = refs[: len(which)], refs[len(which) :]
     rest_e_ref, rest_p_ref, absorption_ref, dense_ref, e_rate_ref, p_rate_ref = refs[:6]
     done_e, done_p, refs = refs[6 : 5 + CHUNKS], refs[5 + CHUNKS : 4 + 2 * CHUNKS], refs[4 + 2 * CHUNKS :]
-    (e_out_ref, p_out_ref), scratch, wide_ref, sems = refs[:2], refs[2:-2], refs[-2], refs[-1]
+    (e_hbm, p_hbm), scratch, (e_out_ref, p_out_ref, wide_ref, sems) = refs[:2], refs[2:-4], refs[-4:]
     load = Loader(sems)
     copies = [load.start(x, y) for x, y in zip(far_refs, scratch)]
     for copy in copies:
         copy.wait()
     product = products(p, which, place_ref, scratch)
-    tile = min(p, TILE)
-    pieces = [(0, e, absorption_ref, rest_e_ref, e_rate_ref, done_e, e_out_ref)]
-    pieces += [(at, tile, dense_ref, rest_p_ref, p_rate_ref, done_p, p_out_ref) for at in range(0, p, tile)]
-    for at, count, weight_ref, rest_ref, rate_ref, done, out_ref in pieces:
+    tile, stores = min(p, LAST_TILE), []
+    pieces = [(0, e, absorption_ref, rest_e_ref, e_rate_ref, done_e, e_out_ref, e_hbm)]
+    pieces += [(at, tile, dense_ref, rest_p_ref, p_rate_ref, done_p, p_out_ref, p_hbm) for at in range(0, p, tile)]
+    for at, count, weight_ref, rest_ref, rate_ref, done, out_ref, hbm_ref in pieces:
         total = rest_ref[at : at + count, :] + 0.5 * product(weight_ref, at, count)
         new = total / (1.0 + as_column(rate_ref[:, at : at + count]))
         unflatten([x[at : at + count, :] for x in done], new, nx, ny, at, out_ref, wide_ref)
-
-
-def step_kernel(n, e, p, width, ny, nx, k, cols, counts, edges, last, place_ref, *refs):
+        rows = pl.ds(at * nx, count * nx)
+        stores.append(load.start(out_ref.at[rows, :], hbm_ref.at[rows, :]))
+    for copy in stores:
+        copy.wait()
+
+
+def step_kernel(n, e, p, width, ny, nx, k, cols, counts, edges, last, only, place_ref, *refs):
     refs = list(refs)
 
     def take(count):
@@ -215,10 +220,13 @@
     before, behind = (take(counts[4]), take(counts[1])), (take(counts[5]), take(counts[2]))
     emission_ref, absorption_ref, dense_ref, up_ref, speed_ref, diffusion_ref, e_rate_ref, p_rate_ref = take(8)
     border = (take(counts[6]), take(1)) if edges else ()
-    e_out_refs, p_out_ref = take(counts[7]), *take(1)
-    to_refs = take(2) if edges else []
+    next_refs = take(counts[7]) if only == "p" else []
+    e_out_refs = take(counts[7]) if only != "p" else []
+    (p_out_ref,) = take(1) if only != "e" else [None]
+    rims = edges and only != "e"
+    to_refs = take(2) if rims else []
     se_ref, sp_ref, low_ref, high_ref = take(4)
-    first_ref, final_ref = take(2) if edges else (None, None)
+    first_ref, final_ref = take(2) if rims else (None, None)
     load = Loader(refs[0])
     tall = width // ny
     even = place_ref[0] == 0
@@ -230,7 +238,7 @@
         owner = j if last else place_ref[1 + j]
         for i, part in enumerate(parts):
             early.append(load.start(part, sp_ref.at[rows_at(owner * counts[0] + i, p // counts[0]), :]))
-    for j, parts in enumerate(e_refs):
+    for j, parts in enumerate(e_refs[:1] if only == "e" else e_refs):
         for i, part in enumerate(parts):
             to = se_ref.at[rows_at(place_ref[1 + j] * counts[3] + i, e // counts[3]), :]
             (middle if j else early).append(load.start(part.at[:, cols[j] : cols[j] + width], to))
@@ -252,11 +260,14 @@
             early.append(load.start(part.at[:, 0:ny], high_ref.at[rows_of(e, i, part), :]))
     late = []
     if edges:
+        for i, part in enumerate(e_out_refs):
+            late.append(load.start(border[0][0].at[rows_of(0, i, part), :], part.at[:, 0 : part.shape[1] - width]))
+    if rims:
         for i, part in enumerate(border[0]):
             late.append(load.start(part.at[:, 0:ny], first_ref.at[rows_of(0, i, part), :]))
-        for i, part in enumerate(e_out_refs):
-            late.append(load.start(border[0][0].at[rows_of(0, i, part), :], part.at[:, 0 : part.shape[1] - width]))
         late.append(load.start(border[1][0].at[:, 0:ny], first_ref.at[e : e + p, :]))
+        for i, part in enumerate(next_refs):
+            late.append(load.start(part.at[:, part.shape[1] - ny :], final_ref.at[rows_of(0, i, part), :]))
     tile = min(p, TILE)
 
     def around(x_ref, rows, base):
@@ -274,7 +285,7 @@
             for i, part in enumerate(e_out_refs):
                 columns = slice(part.shape[1] - width, part.shape[1])
                 part[:, columns] = new[i * part.shape[0] : (i + 1) * part.shape[0], :]
-        if edges:
+        if rims:
             final_ref[base + at : base + at + count, :] = new[:, width - ny :]
 
     def product(weight_ref, at, count):
@@ -288,18 +299,19 @@
 
     for copy in early:
         copy.wait()
-    gain = product(absorption_ref, 0, e)
-    own, lower, higher = around(se_ref, rows_at(me, e), pl.ds(0, e))
-    f_up = jnp.where(up_ref[...] == 1, lower, higher)
-    new = own - as_column(speed_ref[...]) * (own - f_up) + 0.5 * gain
-    if last:
-        e_out_refs[0][...] = new
-    else:
-        store(new / (1.0 + as_column(e_rate_ref[...])), 0, e, 0)
+    if only != "p":
+        gain = product(absorption_ref, 0, e)
+        own, lower, higher = around(se_ref, rows_at(me, e), pl.ds(0, e))
+        f_up = jnp.where(up_ref[...] == 1, lower, higher)
+        new = own - as_column(speed_ref[...]) * (own - f_up) + 0.5 * gain
+        if last:
+            e_out_refs[0][...] = new
+        else:
+            store(new / (1.0 + as_column(e_rate_ref[...])), 0, e, 0)
     for copy in middle + late:
         copy.wait()
 
-    for at in range(0, p, tile):
+    for at in range(0, 0 if only == "e" else p, tile):
         source = product(dense_ref, at, tile) + jnp.dot(
             emission_ref[at : at + tile, :], se_ref[...], preferred_element_type=jnp.float32
         )
@@ -320,7 +332,7 @@
         else:
             store(new / (1.0 + rate), at, tile, e)
 
-    if edges:
+    if rims:
         for to_ref, is_final in ((to_refs[0], even), (to_refs[1], jnp.logical_not(even))):
 
             @pl.when(is_final)
@@ -383,7 +395,7 @@
     weights = (emission, absorption, dense)
     rates = (speed[None], diffusion[None], electron_rate[None], phonon_rate[None])
 
-    def step(k, es, ps, before, behind, last, border):
+    def step(k, es, ps, before, behind, last, border, only=None, nexts=()):
         edges, width = len(border), widths[k]
         e_parts = NEXT_E_PARTS if edges else 1
         counts = (
@@ -392,10 +404,10 @@
         )
         operands = (
             places, *(x for parts, _ in es for x in parts), *(x for parts in ps for x in parts), *before[0],
-            *before[1], *behind[0], *behind[1], *weights, ups[k], *rates, *(x for parts in border for x in parts),
+            *before[1], *behind[0], *behind[1], *weights, ups[k], *rates, *(x for parts in border for x in parts), *nexts,
         )
         large = n * counts[3] + len(ps) * counts[0] + sum(counts[1:3]) + sum(counts[4:6])
-        specs = [SMEM] + [ANY] * large + [VMEM] * 8 + [ANY] * sum(len(parts) for parts in border)
+        specs = [SMEM] + [ANY] * large + [VMEM] * 8 + [ANY] * (sum(len(parts) for parts in border) + len(nexts))
         scratch = [
             pltpu.VMEM(shape, jnp.bfloat16)
             for shape in (
@@ -405,13 +417,15 @@
         if last:
             out = tuple(jax.ShapeDtypeStruct((count, width), jnp.float32) for count in (e, p))
         else:
-            out = (bf16(e // e_parts, nx * ny if edges else width),) * e_parts + (bf16(p, width),) + (bf16(e + p, ny),) * edges
-            scratch += [pltpu.VMEM((e + p, ny), jnp.bfloat16)] * edges
+            out_e = (bf16(e // e_parts, nx * ny if edges else width),) * e_parts
+            out_p = (bf16(p, width),) + (bf16(e + p, ny),) * edges
+            out = out_e if only == "e" else out_p if only == "p" else out_e + out_p
+            scratch += [pltpu.VMEM((e + p, ny), jnp.bfloat16)] * (0 if only == "e" else edges)
         out = call(
-            lambda *refs: step_kernel(n, e, p, width, ny, nx, k, [c for _, c in es], counts, edges, last, *refs),
-            out, scratch, operands, specs, 24, "step", large + counts[6] + e_parts + 2,
-        )
-        return (list(out[:e_parts]), *out[e_parts:])
+            lambda *refs: step_kernel(n, e, p, width, ny, nx, k, [c for _, c in es], counts, edges, last, only, *refs),
+            out, scratch, operands, specs, 24, "step", large + counts[6] + 2 * e_parts + 2,
+        )
+        return out if only else (list(out[:e_parts]), *out[e_parts:])
 
     def add(far, which, rest):
         return call(
@@ -428,8 +442,10 @@
         return call(
             lambda *refs: finish_kernel(e, p, ny, nx, which, *refs), (bf16(e * nx, ny), bf16(p * nx, ny)),
             [pltpu.VMEM((p, widths[-1]), jnp.bfloat16) for _ in far]
-            + [pltpu.VMEM((max(e, min(p, TILE)) * nx, ny), jnp.float32)],
-            operands, [SMEM] + [ANY] * len(far) + [VMEM] * (4 + 2 * CHUNKS), 24, "finish", len(far),
+            + [pltpu.VMEM((count * nx, ny), jnp.bfloat16) for count in (e, p)]
+            + [pltpu.VMEM((max(e, min(p, LAST_TILE)) * nx, ny), jnp.float32)],
+            operands, [SMEM] + [ANY] * len(far) + [VMEM] * (4 + 2 * CHUNKS), 24, "finish",
+            len(far) + 1 + p // min(p, LAST_TILE), ANY,
         )
 
     def gathered(own, far, wait_for):
@@ -456,12 +472,17 @@
     new = []
     for k in range(CHUNKS):
         ps = list(zip(*(gathered(x, far, waits) for x, far in zip(p_chunks[k], far_p[k]))))
-        new.append(step(
+        operands = (
             k, [([x], starts[k] * ny) for x in everyone], ps,
             ([e_all], p_chunks[k - 1]) if k else (halo[:1], halo[1:]),
             ([e_all], p_chunks[k + 1]) if k + 1 < CHUNKS else (halo[:1], halo[1:]), False,
-            () if k + 1 < CHUNKS else (new[0][0], new[0][1:2]),
-        ))
+        )
+        if k + 1 < CHUNKS:
+            new.append(step(*operands, ()))
+        else:
+            border = (new[0][0], new[0][1:2])
+            e_new = step(*operands, border, "e")
+            new.append((list(e_new), *step(*operands, border, "p", e_new)))
         waits = (new[-1][1],)
     halo = halos(new[-1][2], new[-1][3])
     e_next, p_next = new[-1][0], [c[1] for c in new]

time: 80.6 us -> 80.4 us (level)
  waiting for transfers between devices: 21.8 us -> 19.8 us
  Pallas kernels: 26.5 us -> 28.3 us
    ppermute x6, waiting for transfers between devices: 12.9 us -> 10.9 us  [from_chip(): lax.ppermute(x, 'mode', [((i + CORES * offset) % n, i) for i in range(n)])]
    pallas_call x8 -> x9, Pallas kernels: 26.5 us -> 28.3 us  [call(): pl.pallas_call(kernel, out_shape=out, in_specs=specs, out_specs=(out_spec...]
  transfers between devices with their start and end apart: 22 -> 22, of which waited for: 11 -> 11; matrix products, arithmetic and copies ran while one was open for 3% -> 3% of each run, Pallas kernels for 30% -> 32%
where the time goes in v11:
time: 80.4 us; the launch traced here: 79.3 us
  Pallas kernels  28.3 us (35%)
  starting transfers between devices  25.3 us (31%)
  waiting for transfers between devices  19.8 us (25%)
  local copies, waits for them, and re-layouts  2.96 us (4%)
  matrix products  1.83 us (2%)
  between operations  1.01 us (1%)
    pallas_call x9, Pallas kernels, call(): pl.pallas_call(kernel, out_shape=out, in_specs=specs, out_specs=(out_spec...  28.3 us
    ppermute x12, starting transfers between devices, swap_cores(): return lax.ppermute(x, 'mode', [(i, i ^ 1) for i in range(n)])  12.5 us
    ppermute x6, waiting for transfers between devices, from_chip(): lax.ppermute(x, 'mode', [((i + CORES * offset) % n, i) for i in range(n)])  10.9 us
    ppermute x4, starting transfers between devices, halos(): return (lax.ppermute(a, 'space', near), lax.ppermute(b, 'space', other))  9.22 us
    ppermute x4, waiting for transfers between devices, halos(): return (lax.ppermute(a, 'space', near), lax.ppermute(b, 'space', other))  4.91 us
    ppermute x12, waiting for transfers between devices, swap_cores(): return lax.ppermute(x, 'mode', [(i, i ^ 1) for i in range(n)])  4.05 us
    ppermute x6, starting transfers between devices, from_chip(): lax.ppermute(x, 'mode', [((i + CORES * offset) % n, i) for i in range(n)])  3.57 us
    unnamed x25, local copies, waits for them, and re-layouts  2.88 us
  transfers between devices with their start and end apart: 22, of which 11 were waited for; matrix products, arithmetic and copies ran while one was open for 3% of the time, Pallas kernels for 32%

profile of v11, /device:TPU:13, one launch (start us, length us, event | category | flops | bytes accessed | tf_op | source)
XLA Modules:
  0.0 79.3 jit_solution(11690097592738605276)
XLA Ops:
  3.3 1.5 %flatten.2 = (bf16[256,1024]{1,0:T(8,128)(2,1)S(1)}, bf16[512,384]{1,0:T(8,128)(2,1)S(1)}, bf16[512,640]{1,0:T(8,128)(2,1)S(1)}, bf16[768,128]{1,0:T(8,128)(2,1)S(1)}, bf16[768,128]{1,0:T(8,128)(2,1)S(1)}) custom-call(s32[5]{0:T(128)S(1)} %convert_element_type.27.refs_0_, bf16[2048,128]{1,0:T(8,128)(2,1)S(1)} %bitcast.51, bf16[4096,128]{1,0:T(8,128)(2,1)S(1)} %bitcast.47), custom_call_target="tpu_custom_call" | custom-call | flops 1000 | bytes 1000 | tf_op jit(solution)/shard_map/flatten/pallas_call | solution.py:51
  4.9 4.5 %collective-permute-start.3 = (bf16[768,128]{1,0:T(8,128)(2,1)S(1)}, bf16[768,128]{1,0:T(8,128)(2,1)S(1)}, u32[]{:S(2)}, u32[]{:S(2)}) collective-permute-start(bf16[768,128]{1,0:T(8,128)(2,1)S(1)} %get-tuple-element.33), channel_id=1, source_target_pairs={{1,2},{2,1},{5,6},{6,5},{9,10},{10,9},{13,14},{14,13},{17,18},{18,... | collective-permute-start | bytes 589832 | tf_op jit(solution)/shard_map/ppermute | solution.py:39
  9.4 1.3 %collective-permute-start.8 = (bf16[512,384]{1,0:T(8,128)(2,1)S(1)}, bf16[512,384]{1,0:T(8,128)(2,1)S(1)}, u32[]{:S(2)}, u32[]{:S(2)}) collective-permute-start(bf16[512,384]{1,0:T(8,128)(2,1)S(1)} %get-tuple-element.31.refs_5_.refs_10_), channel_id=1, source_target_pairs={{8,0},{12,4},{0,8},{4,12},{9,1},{13,5},{1,9},{5,13},{10,2},{14,6},... | collective-permute-start | bytes 1179656 | tf_op jit(solution)/shard_map/ppermute | solution.py:32
  10.7 1.8 %collective-permute-start = (bf16[256,8,128]{2,1,0:T(8,128)(2,1)}, bf16[256,8,128]{2,1,0:T(8,128)(2,1)S(1)}, u32[]{:S(2)}, u32[]{:S(2)}) collective-permute-start(bf16[256,8,128]{2,1,0:T(8,128)(2,1)} %param.11), channel_id=1, source_target_pairs={{0,4},{4,0},{8,12},{12,8},{1,5},{5,1},{9,13},{13,9},{2,6},{6,2},{1... | collective-permute-start | bytes 1572872 | tf_op jit(solution)/shard_map/ppermute | solution.py:27
  13.4 1.2 %collective-permute-start.6 = (bf16[512,640]{1,0:T(8,128)(2,1)S(1)}, bf16[512,640]{1,0:T(8,128)(2,1)S(1)}, u32[]{:S(2)}, u32[]{:S(2)}) collective-permute-start(bf16[512,640]{1,0:T(8,128)(2,1)S(1)} %get-tuple-element.38.refs_12_.refs_5_), channel_id=1, source_target_pairs={{8,0},{12,4},{0,8},{4,12},{9,1},{13,5},{1,9},{5,13},{10,2},{14,6},... | collective-permute-start | bytes 1966088 | tf_op jit(solution)/shard_map/ppermute | solution.py:32
  14.6 2.1 %collective-permute-start.4 = (bf16[256,8,128]{2,1,0:T(8,128)(2,1)S(1)}, bf16[256,8,128]{2,1,0:T(8,128)(2,1)S(1)}, u32[]{:S(2)}, u32[]{:S(2)}) collective-permute-start(bf16[256,8,128]{2,1,0:T(8,128)(2,1)S(1)} %collective-permute-done.1), channel_id=1, source_target_pairs={{0,4},{4,0},{8,12},{12,8},{1,5},{5,1},{9,13},{13,9},{2,6},{6,2},{1... | collective-permute-start | bytes 1572872 | tf_op jit(solution)/shard_map/ppermute | solution.py:27
  16.8 1.8 %fusion.2 = bf16[4,128,128,16]{2,3,1,0:T(8,128)(2,1)S(1)} fusion(bf16[4,128,12,128]{3,1,0,2:T(8,128)(2,1)S(1)} %bitcast.80, s32[4,12]{1,0:T(4,128)} %param.16), kind=kOutput, calls=%fused_computation.3 | convolution fusion | flops 26215168 | bytes 3670208 | tf_op jit(solution)/shard_map/bsk,bisj->bikj/dot_general | solution.py:390
  19.2 2.9 %collective-permute-done.8.refs_7_ = bf16[512,384]{1,0:T(8,128)(2,1)S(1)} collective-permute-done((bf16[512,384]{1,0:T(8,128)(2,1)S(1)}, bf16[512,384]{1,0:T(8,128)(2,1)S(1)}, u32[]{:S(2)}, u32[]{:S(2)}) %collective-permute-start.8) | collective-permute-done | bytes 393248 | tf_op jit(solution)/shard_map/ppermute | solution.py:32
  22.1 2.7 %collective-permute-start.9 = (bf16[512,384]{1,0:T(8,128)(2,1)S(1)}, bf16[512,384]{1,0:T(8,128)(2,1)S(1)}, u32[]{:S(2)}, u32[]{:S(2)}) collective-permute-start(bf16[512,384]{1,0:T(8,128)(2,1)S(1)} %collective-permute-done.8.refs_7_), channel_id=1, source_target_pairs={{0,4},{4,0},{8,12},{12,8},{1,5},{5,1},{9,13},{13,9},{2,6},{6,2},{1... | collective-permute-start | bytes 1179656 | tf_op jit(solution)/shard_map/ppermute | solution.py:27
  26.2 4.6 %step.5 = (bf16[256,384]{1,0:T(8,128)(2,1)S(1)}, bf16[512,384]{1,0:T(8,128)(2,1)S(1)}) custom-call(s32[5]{0:T(128)S(1)} %convert_element_type.27.refs_0_, bf16[256,1024]{1,0:T(8,128)(2,1)S(1)} %get-tuple-element.30.refs_1_.refs_11_.refs_9_, bf16[256,1024]{1,0:T(8,128)(2,1)S(1)} %get-tuple-element.35.refs_2_, ...), custom_call_target="tpu_custom_call" | custom-call | flops 1000 | bytes 1000 | tf_op jit(solution)/shard_map/step/pallas_call | solution.py:51
  30.8 5.3 %collective-permute-done.6.refs_7_ = bf16[512,640]{1,0:T(8,128)(2,1)S(1)} collective-permute-done((bf16[512,640]{1,0:T(8,128)(2,1)S(1)}, bf16[512,640]{1,0:T(8,128)(2,1)S(1)}, u32[]{:S(2)}, u32[]{:S(2)}) %collective-permute-start.6) | collective-permute-done | bytes 655392 | tf_op jit(solution)/shard_map/ppermute | solution.py:32
  36.2 1.5 %collective-permute-start.10 = (bf16[512,640]{1,0:T(8,128)(2,1)S(1)}, bf16[512,640]{1,0:T(8,128)(2,1)S(1)}, u32[]{:S(2)}, u32[]{:S(2)}) collective-permute-start(bf16[512,640]{1,0:T(8,128)(2,1)S(1)} %collective-permute-done.6.refs_7_), channel_id=1, source_target_pairs={{0,4},{4,0},{8,12},{12,8},{1,5},{5,1},{9,13},{13,9},{2,6},{6,2},{1... | collective-permute-start | bytes 1966088 | tf_op jit(solution)/shard_map/ppermute | solution.py:27
  38.0 1.5 %collective-permute-done.10.refs_8_ = bf16[512,640]{1,0:T(8,128)(2,1)S(1)} collective-permute-done((bf16[512,640]{1,0:T(8,128)(2,1)S(1)}, bf16[512,640]{1,0:T(8,128)(2,1)S(1)}, u32[]{:S(2)}, u32[]{:S(2)}) %collective-permute-start.10) | collective-permute-done | bytes 655392 | tf_op jit(solution)/shard_map/ppermute | solution.py:27
  39.4 3.0 %step.6.refs_23_.refs_1_.refs_7_.refs_11_ = bf16[256,1024]{1,0:T(8,128)(2,1)S(1)} custom-call(s32[5]{0:T(128)S(1)} %convert_element_type.27.refs_0_, bf16[256,1024]{1,0:T(8,128)(2,1)S(1)} %get-tuple-element.30.refs_1_.refs_11_.refs_9_, bf16[256,1024]{1,0:T(8,128)(2,1)S(1)} %get-tuple-element.35.refs_2_, bf16[256,1024]{1,0:T(8,128)(2,1)S(1)} %get-tuple-element.36.refs_3_, ...), custom_call_target="tpu_custom_call" | custom-call | flops 1000 | bytes 1000 | tf_op jit(solution)/shard_map/step/pallas_call | solution.py:51
  42.8 5.0 %step.7 = (bf16[512,640]{1,0:T(8,128)(2,1)S(1)}, bf16[768,128]{1,0:T(8,128)(2,1)S(1)}, bf16[768,128]{1,0:T(8,128)(2,1)S(1)}) custom-call(s32[5]{0:T(128)S(1)} %convert_element_type.27.refs_0_, bf16[256,1024]{1,0:T(8,128)(2,1)S(1)} %get-tuple-element.30.refs_1_.refs_11_.refs_9_, bf16[256,1024]{1,0:T(8,128)(2,1)S(1)} %get-tuple-element.35.refs_2_, ...), custom_call_target="tpu_custom_call" | custom-call | flops 1000 | bytes 1000 | tf_op jit(solution)/shard_map/step/pallas_call | solution.py:51
  49.8 4.5 %collective-permute-start.17 = (bf16[768,128]{1,0:T(8,128)(2,1)S(1)}, bf16[768,128]{1,0:T(8,128)(2,1)S(1)}, u32[]{:S(2)}, u32[]{:S(2)}) collective-permute-start(bf16[768,128]{1,0:T(8,128)(2,1)S(1)} %get-tuple-element.47), channel_id=1, source_target_pairs={{1,2},{2,1},{5,6},{6,5},{9,10},{10,9},{13,14},{14,13},{17,18},{18,... | collective-permute-start | bytes 589832 | tf_op jit(solution)/shard_map/ppermute | solution.py:39
  54.9 1.2 %collective-permute-done.16.refs_9_ = bf16[768,128]{1,0:T(8,128)(2,1)S(1)} collective-permute-done((bf16[768,128]{1,0:T(8,128)(2,1)S(1)}, bf16[768,128]{1,0:T(8,128)(2,1)S(1)}, u32[]{:S(2)}, u32[]{:S(2)}) %collective-permute-start.16) | collective-permute-done | bytes 196640 | tf_op jit(solution)/shard_map/ppermute | solution.py:39
  56.4 2.8 %collective-permute-done.17.refs_10_ = bf16[768,128]{1,0:T(8,128)(2,1)S(1)} collective-permute-done((bf16[768,128]{1,0:T(8,128)(2,1)S(1)}, bf16[768,128]{1,0:T(8,128)(2,1)S(1)}, u32[]{:S(2)}, u32[]{:S(2)}) %collective-permute-start.17) | collective-permute-done | bytes 196640 | tf_op jit(solution)/shard_map/ppermute | solution.py:39
  60.9 2.1 %collective-permute-done.20.refs_6_ = bf16[512,384]{1,0:T(8,128)(2,1)S(1)} collective-permute-done((bf16[512,384]{1,0:T(8,128)(2,1)S(1)}, bf16[512,384]{1,0:T(8,128)(2,1)S(1)}, u32[]{:S(2)}, u32[]{:S(2)}) %collective-permute-start.20) | collective-permute-done | bytes 393248 | tf_op jit(solution)/shard_map/ppermute | solution.py:27
  63.0 4.6 %step.9 = (bf16[256,384]{1,0:T(8,128)(2,1)S(1)}, bf16[512,384]{1,0:T(8,128)(2,1)S(1)}) custom-call(s32[5]{0:T(128)S(1)} %convert_element_type.27.refs_0_, bf16[256,1024]{1,0:T(8,128)(2,1)S(1)} %step.6.refs_23_.refs_1_.refs_7_.refs_11_, bf16[256,1024]{1,0:T(8,128)(2,1)S(1)} %collective-permute-done.12.refs_2_, ...), custom_call_target="tpu_custom_call" | custom-call | flops 1000 | bytes 1000 | tf_op jit(solution)/shard_map/step/pallas_call | solution.py:51
  67.6 4.1 %step.8 = (f32[256,640]{1,0:T(8,128)S(1)}, f32[512,640]{1,0:T(8,128)S(1)}) custom-call(s32[5]{0:T(128)S(1)} %convert_element_type.27.refs_0_, bf16[256,1024]{1,0:T(8,128)(2,1)S(1)} %step.6.refs_23_.refs_1_.refs_7_.refs_11_, bf16[256,1024]{1,0:T(8,128)(2,1)S(1)} %collective-permute-done.12.refs_2_, bf16[256,1024]{1,0:T(8,128)(2,1)S(1)} %collective-permute-done.13.refs_3_, ...), custom_call_target="tpu_custom_call" | custom-call | flops 1000 | bytes 1000 | tf_op jit(solution)/shard_map/step/pallas_call | solution.py:51
  71.7 2.0 %collective-permute-done.11.refs_1_ = bf16[512,640]{1,0:T(8,128)(2,1)S(1)} collective-permute-done((bf16[512,640]{1,0:T(8,128)(2,1)S(1)}, bf16[512,640]{1,0:T(8,128)(2,1)S(1)}, u32[]{:S(2)}, u32[]{:S(2)}) %collective-permute-start.11) | collective-permute-done | bytes 655392 | tf_op jit(solution)/shard_map/ppermute | solution.py:32
  74.5 1.5 %add.29 = (f32[256,640]{1,0:T(8,128)S(1)}, f32[512,640]{1,0:T(8,128)S(1)}) custom-call(s32[5]{0:T(128)S(1)} %convert_element_type.27.refs_0_, bf16[512,640]{1,0:T(8,128)(2,1)S(1)} %collective-permute-done.11.refs_1_, f32[256,640]{1,0:T(8,128)S(1)} %get-tuple-element.52.refs_2_, f32[512,640]{1,0:T(8,128)S(1)} %get-tuple-element.49.refs_3_, ...), custom_call_target="tpu_custom_call" | custom-call | flops 1000 | bytes 1000 | tf_op jit(solution)/shard_map/add/pallas_call | solution.py:51
  76.2 2.9 %finish.1 = (bf16[2048,128]{1,0:T(8,128)(2,1)}, bf16[4096,128]{1,0:T(8,128)(2,1)}) custom-call(s32[5]{0:T(128)S(1)} %convert_element_type.27.refs_0_, bf16[512,640]{1,0:T(8,128)(2,1)S(1)} %collective-permute-done.21.refs_1_, f32[256,640]{1,0:T(8,128)S(1)} %get-tuple-element.53.refs_2_, f32[512,640]{1,0:T(8,128)S(1)} %get-tuple-element.54.refs_3_, ...), custom_call_target="tpu_custom_call" | custom-call | flops 1000 | bytes 1000 | tf_op jit(solution)/shard_map/finish/pallas_call | solution.py:51
  (57 shorter events, 11.5 us)
Async XLA Ops:
  0.6 14.0 %collective-permute-start.1 = (bf16[256,8,128]{2,1,0:T(8,128)(2,1)}, bf16[256,8,128]{2,1,0:T(8,128)(2,1)S(1)}, u32[]{:S(2)}, u32[]{:S(2)}) collective-permute-start(bf16[256,8,128]{2,1,0:T(8,128)(2,1)} %param.11), channel_id=1, source_target_pairs={{8,0},{12,4},{0,8},{4,12},{9,1},{13,5},{1,9},{5,13},{10,2},{14,6},... | collective-permute-start | bytes 1572872 | tf_op jit(solution)/shard_map/ppermute | solution.py:32
  3.3 13.5 %copy-start.8 = (bf16[512,12,128]{2,0,1:T(8,128)(2,1)S(1)}, bf16[512,12,128]{2,0,1:T(8,128)(2,1)}, u32[]{:S(2)}) copy-start(bf16[512,12,128]{2,0,1:T(8,128)(2,1)} %param.15) | copy-start | bytes 4718596
  4.8 7.7 %collective-permute-start.2 = (bf16[768,128]{1,0:T(8,128)(2,1)S(1)}, bf16[768,128]{1,0:T(8,128)(2,1)S(1)}, u32[]{:S(2)}, u32[]{:S(2)}) collective-permute-start(bf16[768,128]{1,0:T(8,128)(2,1)S(1)} %get-tuple-element.32), channel_id=1, source_target_pairs={{0,1},{1,0},{2,3},{3,2},{4,5},{5,4},{6,7},{7,6},{8,9},{9,8},{10,11... | collective-permute-start | bytes 589832 | tf_op jit(solution)/shard_map/ppermute | solution.py:39
  4.9 8.5 %collective-permute-start.3 = (bf16[768,128]{1,0:T(8,128)(2,1)S(1)}, bf16[768,128]{1,0:T(8,128)(2,1)S(1)}, u32[]{:S(2)}, u32[]{:S(2)}) collective-permute-start(bf16[768,128]{1,0:T(8,128)(2,1)S(1)} %get-tuple-element.33), channel_id=1, source_target_pairs={{1,2},{2,1},{5,6},{6,5},{9,10},{10,9},{13,14},{14,13},{17,18},{18,... | collective-permute-start | bytes 589832 | tf_op jit(solution)/shard_map/ppermute | solution.py:39
  9.4 12.7 %collective-permute-start.8 = (bf16[512,384]{1,0:T(8,128)(2,1)S(1)}, bf16[512,384]{1,0:T(8,128)(2,1)S(1)}, u32[]{:S(2)}, u32[]{:S(2)}) collective-permute-start(bf16[512,384]{1,0:T(8,128)(2,1)S(1)} %get-tuple-element.31.refs_5_.refs_10_), channel_id=1, source_target_pairs={{8,0},{12,4},{0,8},{4,12},{9,1},{13,5},{1,9},{5,13},{10,2},{14,6},... | collective-permute-start | bytes 1179656 | tf_op jit(solution)/shard_map/ppermute | solution.py:32
  10.7 14.1 %collective-permute-start = (bf16[256,8,128]{2,1,0:T(8,128)(2,1)}, bf16[256,8,128]{2,1,0:T(8,128)(2,1)S(1)}, u32[]{:S(2)}, u32[]{:S(2)}) collective-permute-start(bf16[256,8,128]{2,1,0:T(8,128)(2,1)} %param.11), channel_id=1, source_target_pairs={{0,4},{4,0},{8,12},{12,8},{1,5},{5,1},{9,13},{13,9},{2,6},{6,2},{1... | collective-permute-start | bytes 1572872 | tf_op jit(solution)/shard_map/ppermute | solution.py:27
  12.5 13.4 %collective-permute-start.7 = (bf16[512,384]{1,0:T(8,128)(2,1)S(1)}, bf16[512,384]{1,0:T(8,128)(2,1)S(1)}, u32[]{:S(2)}, u32[]{:S(2)}) collective-permute-start(bf16[512,384]{1,0:T(8,128)(2,1)S(1)} %get-tuple-element.31.refs_5_.refs_10_), channel_id=1, source_target_pairs={{0,4},{4,0},{8,12},{12,8},{1,5},{5,1},{9,13},{13,9},{2,6},{6,2},{1... | collective-permute-start | bytes 1179656 | tf_op jit(solution)/shard_map/ppermute | solution.py:27
  13.4 22.8 %collective-permute-start.6 = (bf16[512,640]{1,0:T(8,128)(2,1)S(1)}, bf16[512,640]{1,0:T(8,128)(2,1)S(1)}, u32[]{:S(2)}, u32[]{:S(2)}) collective-permute-start(bf16[512,640]{1,0:T(8,128)(2,1)S(1)} %get-tuple-element.38.refs_12_.refs_5_), channel_id=1, source_target_pairs={{8,0},{12,4},{0,8},{4,12},{9,1},{13,5},{1,9},{5,13},{10,2},{14,6},... | collective-permute-start | bytes 1966088 | tf_op jit(solution)/shard_map/ppermute | solution.py:32
  14.6 10.3 %collective-permute-start.4 = (bf16[256,8,128]{2,1,0:T(8,128)(2,1)S(1)}, bf16[256,8,128]{2,1,0:T(8,128)(2,1)S(1)}, u32[]{:S(2)}, u32[]{:S(2)}) collective-permute-start(bf16[256,8,128]{2,1,0:T(8,128)(2,1)S(1)} %collective-permute-done.1), channel_id=1, source_target_pairs={{0,4},{4,0},{8,12},{12,8},{1,5},{5,1},{9,13},{13,9},{2,6},{6,2},{1... | collective-permute-start | bytes 1572872 | tf_op jit(solution)/shard_map/ppermute | solution.py:27
  18.6 7.6 %copy-start = (bf16[256,2048]{1,0:T(8,128)(2,1)S(1)}, bf16[256,2048]{1,0:T(8,128)(2,1)}, u32[]{:S(2)}) copy-start(bf16[256,2048]{1,0:T(8,128)(2,1)} %refs_4_.3) | copy-start | bytes 3145732
  22.1 4.0 %collective-permute-start.9 = (bf16[512,384]{1,0:T(8,128)(2,1)S(1)}, bf16[512,384]{1,0:T(8,128)(2,1)S(1)}, u32[]{:S(2)}, u32[]{:S(2)}) collective-permute-start(bf16[512,384]{1,0:T(8,128)(2,1)S(1)} %collective-permute-done.8.refs_7_), channel_id=1, source_target_pairs={{0,4},{4,0},{8,12},{12,8},{1,5},{5,1},{9,13},{13,9},{2,6},{6,2},{1... | collective-permute-start | bytes 1179656 | tf_op jit(solution)/shard_map/ppermute | solution.py:27
  24.8 13.1 %collective-permute-start.5 = (bf16[512,640]{1,0:T(8,128)(2,1)S(1)}, bf16[512,640]{1,0:T(8,128)(2,1)S(1)}, u32[]{:S(2)}, u32[]{:S(2)}) collective-permute-start(bf16[512,640]{1,0:T(8,128)(2,1)S(1)} %get-tuple-element.38.refs_12_.refs_5_), channel_id=1, source_target_pairs={{0,4},{4,0},{8,12},{12,8},{1,5},{5,1},{9,13},{13,9},{2,6},{6,2},{1... | collective-permute-start | bytes 1966088 | tf_op jit(solution)/shard_map/ppermute | solution.py:27
  36.2 3.3 %collective-permute-start.10 = (bf16[512,640]{1,0:T(8,128)(2,1)S(1)}, bf16[512,640]{1,0:T(8,128)(2,1)S(1)}, u32[]{:S(2)}, u32[]{:S(2)}) collective-permute-start(bf16[512,640]{1,0:T(8,128)(2,1)S(1)} %collective-permute-done.6.refs_7_), channel_id=1, source_target_pairs={{0,4},{4,0},{8,12},{12,8},{1,5},{5,1},{9,13},{13,9},{2,6},{6,2},{1... | collective-permute-start | bytes 1966088 | tf_op jit(solution)/shard_map/ppermute | solution.py:27
  37.7 10.7 %collective-permute-start.14 = (bf16[512,384]{1,0:T(8,128)(2,1)S(1)}, bf16[512,384]{1,0:T(8,128)(2,1)S(1)}, u32[]{:S(2)}, u32[]{:S(2)}) collective-permute-start(bf16[512,384]{1,0:T(8,128)(2,1)S(1)} %get-tuple-element.41.refs_22_.refs_8_.refs_5_), channel_id=1, source_target_pairs={{8,0},{12,4},{0,8},{4,12},{9,1},{13,5},{1,9},{5,13},{10,2},{14,6},... | collective-permute-start | bytes 1179656 | tf_op jit(solution)/shard_map/ppermute | solution.py:32
  42.5 17.5 %collective-permute-start.13 = (bf16[256,1024]{1,0:T(8,128)(2,1)S(1)}, bf16[256,1024]{1,0:T(8,128)(2,1)S(1)}, u32[]{:S(2)}, u32[]{:S(2)}) collective-permute-start(bf16[256,1024]{1,0:T(8,128)(2,1)S(1)} %step.6.refs_23_.refs_1_.refs_7_.refs_11_), channel_id=1, source_target_pairs={{8,0},{12,4},{0,8},{4,12},{9,1},{13,5},{1,9},{5,13},{10,2},{14,6},... | collective-permute-start | bytes 1572872 | tf_op jit(solution)/shard_map/ppermute | solution.py:32
  48.5 11.5 %collective-permute-start.15 = (bf16[512,384]{1,0:T(8,128)(2,1)S(1)}, bf16[512,384]{1,0:T(8,128)(2,1)S(1)}, u32[]{:S(2)}, u32[]{:S(2)}) collective-permute-start(bf16[512,384]{1,0:T(8,128)(2,1)S(1)} %collective-permute-done.14.refs_7_), channel_id=1, source_target_pairs={{0,4},{4,0},{8,12},{12,8},{1,5},{5,1},{9,13},{13,9},{2,6},{6,2},{1... | collective-permute-start | bytes 1179656 | tf_op jit(solution)/shard_map/ppermute | solution.py:27
  49.6 6.5 %collective-permute-start.16 = (bf16[768,128]{1,0:T(8,128)(2,1)S(1)}, bf16[768,128]{1,0:T(8,128)(2,1)S(1)}, u32[]{:S(2)}, u32[]{:S(2)}) collective-permute-start(bf16[768,128]{1,0:T(8,128)(2,1)S(1)} %get-tuple-element.46), channel_id=1, source_target_pairs={{0,1},{1,0},{2,3},{3,2},{4,5},{5,4},{6,7},{7,6},{8,9},{9,8},{10,11... | collective-permute-start | bytes 589832 | tf_op jit(solution)/shard_map/ppermute | solution.py:39
  49.8 9.4 %collective-permute-start.17 = (bf16[768,128]{1,0:T(8,128)(2,1)S(1)}, bf16[768,128]{1,0:T(8,128)(2,1)S(1)}, u32[]{:S(2)}, u32[]{:S(2)}) collective-permute-start(bf16[768,128]{1,0:T(8,128)(2,1)S(1)} %get-tuple-element.47), channel_id=1, source_target_pairs={{1,2},{2,1},{5,6},{6,5},{9,10},{10,9},{13,14},{14,13},{17,18},{18,... | collective-permute-start | bytes 589832 | tf_op jit(solution)/shard_map/ppermute | solution.py:39
  54.3 13.3 %collective-permute-start.19 = (bf16[512,640]{1,0:T(8,128)(2,1)S(1)}, bf16[512,640]{1,0:T(8,128)(2,1)S(1)}, u32[]{:S(2)}, u32[]{:S(2)}) collective-permute-start(bf16[512,640]{1,0:T(8,128)(2,1)S(1)} %get-tuple-element.44.refs_5_.refs_12_), channel_id=1, source_target_pairs={{0,4},{4,0},{8,12},{12,8},{1,5},{5,1},{9,13},{13,9},{2,6},{6,2},{1... | collective-permute-start | bytes 1966088 | tf_op jit(solution)/shard_map/ppermute | solution.py:27
  56.2 17.6 %collective-permute-start.11 = (bf16[512,640]{1,0:T(8,128)(2,1)S(1)}, bf16[512,640]{1,0:T(8,128)(2,1)S(1)}, u32[]{:S(2)}, u32[]{:S(2)}) collective-permute-start(bf16[512,640]{1,0:T(8,128)(2,1)S(1)} %get-tuple-element.44.refs_5_.refs_12_), channel_id=1, source_target_pairs={{8,0},{12,4},{0,8},{4,12},{9,1},{13,5},{1,9},{5,13},{10,2},{14,6},... | collective-permute-start | bytes 1966088 | tf_op jit(solution)/shard_map/ppermute | solution.py:32
  59.2 3.8 %collective-permute-start.12 = (bf16[256,1024]{1,0:T(8,128)(2,1)S(1)}, bf16[256,1024]{1,0:T(8,128)(2,1)S(1)}, u32[]{:S(2)}, u32[]{:S(2)}) collective-permute-start(bf16[256,1024]{1,0:T(8,128)(2,1)S(1)} %step.6.refs_23_.refs_1_.refs_7_.refs_11_), channel_id=1, source_target_pairs={{0,4},{4,0},{8,12},{12,8},{1,5},{5,1},{9,13},{13,9},{2,6},{6,2},{1... | collective-permute-start | bytes 1572872 | tf_op jit(solution)/shard_map/ppermute | solution.py:27
  60.0 3.0 %collective-permute-start.18 = (bf16[256,1024]{1,0:T(8,128)(2,1)S(1)}, bf16[256,1024]{1,0:T(8,128)(2,1)S(1)}, u32[]{:S(2)}, u32[]{:S(2)}) collective-permute-start(bf16[256,1024]{1,0:T(8,128)(2,1)S(1)} %collective-permute-done.13.refs_3_), channel_id=1, source_target_pairs={{0,4},{4,0},{8,12},{12,8},{1,5},{5,1},{9,13},{13,9},{2,6},{6,2},{1... | collective-permute-start | bytes 1572872 | tf_op jit(solution)/shard_map/ppermute | solution.py:27
  60.9 2.1 %collective-permute-start.20 = (bf16[512,384]{1,0:T(8,128)(2,1)S(1)}, bf16[512,384]{1,0:T(8,128)(2,1)S(1)}, u32[]{:S(2)}, u32[]{:S(2)}) collective-permute-start(bf16[512,384]{1,0:T(8,128)(2,1)S(1)} %get-tuple-element.41.refs_22_.refs_8_.refs_5_), channel_id=1, source_target_pairs={{0,4},{4,0},{8,12},{12,8},{1,5},{5,1},{9,13},{13,9},{2,6},{6,2},{1... | collective-permute-start | bytes 1179656 | tf_op jit(solution)/shard_map/ppermute | solution.py:27
  73.7 2.5 %collective-permute-start.21 = (bf16[512,640]{1,0:T(8,128)(2,1)S(1)}, bf16[512,640]{1,0:T(8,128)(2,1)S(1)}, u32[]{:S(2)}, u32[]{:S(2)}) collective-permute-start(bf16[512,640]{1,0:T(8,128)(2,1)S(1)} %collective-permute-done.11.refs_1_), channel_id=1, source_target_pairs={{0,4},{4,0},{8,12},{12,8},{1,5},{5,1},{9,13},{13,9},{2,6},{6,2},{1... | collective-permute-start | bytes 1966088 | tf_op jit(solution)/shard_map/ppermute | solution.py:27
  (8 other events, 46.2 us)
